TPU v7x, 32 devices: a whole 2x2x4 slice. The times are simulated.
32 devices in a mesh: dp: 4 (over z), expert: 8 (over y, x, core).
Axes of the slice: x: 2, y: 2, z: 4, core: 2. Of those that a mesh axis runs over, the one named last changes fastest.
Arguments:
- act_in: float32 [18912, 768], P(('dp', 'expert')), may hold values from -6 to 6
- w_qkv: float32 [2, 768, 2304], P(None, ('dp', 'expert')), may hold values from -0.21875 to 0.21875
- w_proj: float32 [2, 768, 768], P(None, None, ('dp', 'expert')), may hold values from -1.25 to 1.25
- w_up: float32 [768, 3072], P(('dp', 'expert')), may hold values from -0.21875 to 0.21875
- w_down: float32 [3072, 768], P(None, ('dp', 'expert')), may hold values from -0.109375 to 0.109375
- norm_gain: float32 [4, 768], P(None, ('dp', 'expert')), may hold values from 0.1 to 1.9
- norm_shift: float32 [4, 768], P(None, ('dp', 'expert')), may hold values from -3 to 3
- exp_in: float32 [16, 768, 3072], P('expert', 'dp'), may hold values from -0.21875 to 0.21875
- exp_out: float32 [16, 3072, 768], P('expert', None, 'dp'), may hold values from -0.109375 to 0.109375
- gate: float32 [18912, 2], P(('dp', 'expert')), may hold values from 0.2 to 1
- expert_index: int32 [18912, 2], P(('dp', 'expert')), may hold values from 0 to 15, all different within a row; in each aligned block of 591 rows (0 to 590, 591 to 1181, ...) at most 96 rows name the same one
- cotangent: float32 [18912, 768], P(('dp', 'expert')), may hold values from -6 to 6
Outputs:
- act_out: float32 [18912, 768], P(('dp', 'expert'))
- act_grad: float32 [18912, 768], P(('dp', 'expert'))
- grad_qkv: float32 [2, 768, 2304], P(None, ('dp', 'expert'))
- grad_proj: float32 [2, 768, 768], P(None, None, ('dp', 'expert'))
- grad_up: float32 [768, 3072], P(('dp', 'expert'))
- grad_down: float32 [3072, 768], P(None, ('dp', 'expert'))
- grad_gain: float32 [4, 768], P(None, ('dp', 'expert'))
- grad_shift: float32 [4, 768], P(None, ('dp', 'expert'))
- grad_exp_in: float32 [16, 768, 3072], P('expert', 'dp')
- grad_exp_out: float32 [16, 3072, 768], P('expert', None, 'dp')
- grad_gate: float32 [18912, 2], P(('dp', 'expert'))
Inputs may be any that keep to these rules, and one draw needn't show every extreme that they name: `expert_index`: the 2 entries of a row differ. In each aligned block of 591 rows (the tokens of one device) no expert is named more than 96 times, a bound that some block reaches.
All inputs are finite; a program needn't handle non-finite values.
Results may differ from a plain program's by a relative error of at most 0.018.
The roundings to bfloat16 on the way count: a program that leaves them out, or rounds other values in their place, can miss the bound.
Values may be sent and summed in bfloat16 or wider, within the bound.
No kernel may reach another device: no remote copies, remote signals or barrier semaphores. Data moves between devices by JAX's collectives and lax.ppermute only.
A program may use at most 320 MiB of HBM per device.

v0:
```python
import math

import jax
import jax.numpy as jnp
from jax import lax
from jax.sharding import PartitionSpec as P

D = 768
HEADS = 12
HEAD = 64
SEQ = 197
TOP = 2
EXP_DEV = 2
TOK_DEV = 591


def norm_rows(inputs, gain_row, shift_row):
    average = jnp.mean(inputs, axis=-1, keepdims=True)
    centred = inputs - average
    spread = jnp.mean(centred * centred, axis=-1, keepdims=True)
    return centred * lax.rsqrt(spread + 1e-06) * gain_row + shift_row


def gelu_exact(inputs):
    return jax.nn.gelu(inputs, approximate=False)


def gelu_grad(inputs, upstream):
    _, pull_back = jax.vjp(gelu_exact, inputs)
    return pull_back(upstream)[0]


def norm_grad(inputs, gain_row, shift_row, upstream):
    _, pull_back = jax.vjp(norm_rows, inputs, gain_row, shift_row)
    return pull_back(upstream)


def matmul_low(left, right):
    return jnp.dot(left, right, preferred_element_type=jnp.float32)


def fetch_dense(qkv_part, proj_part, up_part, down_part, gain_part, shift_part):
    fetched = (
        lax.all_gather(qkv_part, ("dp", "expert"), axis=1, tiled=True),
        lax.all_gather(proj_part, ("dp", "expert"), axis=2, tiled=True),
        lax.all_gather(up_part, ("dp", "expert"), axis=0, tiled=True),
        lax.all_gather(down_part, ("dp", "expert"), axis=1, tiled=True),
        lax.all_gather(gain_part, ("dp", "expert"), axis=1, tiled=True),
        lax.all_gather(shift_part, ("dp", "expert"), axis=1, tiled=True),
    )
    return fetched


def reduce_dense(qkv_grad, proj_grad, up_grad, down_grad, gain_grad, shift_grad):
    reduced = (
        lax.psum_scatter(qkv_grad, ("dp", "expert"), scatter_dimension=1, tiled=True),
        lax.psum_scatter(proj_grad, ("dp", "expert"), scatter_dimension=2, tiled=True),
        lax.psum_scatter(up_grad, ("dp", "expert"), scatter_dimension=0, tiled=True),
        lax.psum_scatter(down_grad, ("dp", "expert"), scatter_dimension=1, tiled=True),
        lax.psum_scatter(gain_grad, ("dp", "expert"), scatter_dimension=1, tiled=True),
        lax.psum_scatter(shift_grad, ("dp", "expert"), scatter_dimension=1, tiled=True),
    )
    return reduced


def split_heads(packed_rows):
    images = packed_rows.shape[0] // SEQ
    shaped = packed_rows.reshape(images, SEQ, 3, HEADS, HEAD)
    return (shaped[:, :, 0], shaped[:, :, 1], shaped[:, :, 2])


def attend_forward(normed_low, qkv_weight, proj_weight):
    score_scale = 1.0 / math.sqrt(HEAD)
    packed = matmul_low(normed_low, qkv_weight).astype(jnp.bfloat16)
    query_rows, key_rows, value_rows = split_heads(packed)
    scores = (
        jnp.einsum("bqhd,bkhd->bhqk", query_rows, key_rows, preferred_element_type=jnp.float32)
        * score_scale
    )
    row_peak = jnp.max(scores, axis=-1, keepdims=True)
    raised = jnp.exp(scores - row_peak)
    row_total = jnp.sum(raised, axis=-1, keepdims=True)
    attn_weights = raised / row_total
    log_total = row_peak + jnp.log(row_total)
    mixed_rows = jnp.einsum(
        "bhqk,bkhd->bqhd",
        attn_weights.astype(jnp.bfloat16),
        value_rows,
        preferred_element_type=jnp.float32,
    )
    mixed_rows = mixed_rows.astype(jnp.bfloat16).reshape(packed.shape[0], D)
    branch = matmul_low(mixed_rows, proj_weight)
    return (branch, (packed, log_total, mixed_rows))


def attend_backward(grad_branch, normed_low, qkv_weight, proj_weight, saved):
    score_scale = 1.0 / math.sqrt(HEAD)
    packed, log_total, mixed_rows = saved
    row_count = packed.shape[0]
    grad_low = grad_branch.astype(jnp.bfloat16)
    grad_proj = jnp.einsum("td,te->de", mixed_rows, grad_low, preferred_element_type=jnp.float32)
    grad_mixed = jnp.einsum("te,de->td", grad_low, proj_weight, preferred_element_type=jnp.float32)
    grad_mixed = grad_mixed.astype(jnp.bfloat16).reshape(row_count // SEQ, SEQ, HEADS, HEAD)
    query_rows, key_rows, value_rows = split_heads(packed)
    scores = (
        jnp.einsum("bqhd,bkhd->bhqk", query_rows, key_rows, preferred_element_type=jnp.float32)
        * score_scale
    )
    attn_weights = jnp.exp(scores - log_total)
    grad_weights = jnp.einsum(
        "bqhd,bkhd->bhqk", grad_mixed, value_rows, preferred_element_type=jnp.float32
    )
    grad_values = jnp.einsum(
        "bhqk,bqhd->bkhd",
        attn_weights.astype(jnp.bfloat16),
        grad_mixed,
        preferred_element_type=jnp.float32,
    )
    grad_scores = attn_weights * (
        grad_weights - jnp.sum(attn_weights * grad_weights, axis=-1, keepdims=True)
    )
    grad_scores = grad_scores.astype(jnp.bfloat16)
    grad_query = (
        jnp.einsum("bhqk,bkhd->bqhd", grad_scores, key_rows, preferred_element_type=jnp.float32)
        * score_scale
    )
    grad_keys = (
        jnp.einsum("bhqk,bqhd->bkhd", grad_scores, query_rows, preferred_element_type=jnp.float32)
        * score_scale
    )
    grad_packed = (
        jnp.stack([grad_query, grad_keys, grad_values], axis=2)
        .reshape(row_count, 3 * D)
        .astype(jnp.bfloat16)
    )
    grad_qkv = jnp.einsum("td,tf->df", normed_low, grad_packed, preferred_element_type=jnp.float32)
    grad_normed = jnp.einsum(
        "tf,df->td", grad_packed, qkv_weight, preferred_element_type=jnp.float32
    )
    return (grad_normed, grad_qkv, grad_proj)


def local(
    act_in,
    w_qkv,
    w_proj,
    w_up,
    w_down,
    norm_gain,
    norm_shift,
    exp_in,
    exp_out,
    gate,
    expert_index,
    cotangent,
):
    row_count = act_in.shape[0]
    experts_all = EXP_DEV * lax.axis_size("expert")
    capacity = (TOP * TOK_DEV * 5 // (4 * experts_all) + 7) // 8 * 8
    dense_low = fetch_dense(
        w_qkv.astype(jnp.bfloat16),
        w_proj.astype(jnp.bfloat16),
        w_up.astype(jnp.bfloat16),
        w_down.astype(jnp.bfloat16),
        norm_gain.astype(jnp.bfloat16),
        norm_shift.astype(jnp.bfloat16),
    )
    qkv_all, proj_all, up_all, down_all, gain_all, shift_all = dense_low
    gain_full = gain_all.astype(jnp.float32)
    shift_full = shift_all.astype(jnp.float32)
    expert_low = (
        lax.all_gather(exp_in.astype(jnp.bfloat16), "dp", axis=1, tiled=True),
        lax.all_gather(exp_out.astype(jnp.bfloat16), "dp", axis=2, tiled=True),
    )
    exp_in_all, exp_out_all = expert_low
    normed_a = norm_rows(act_in, gain_full[0], shift_full[0]).astype(jnp.bfloat16)
    branch_a, saved_a = attend_forward(normed_a, qkv_all[0], proj_all[0])
    after_a = act_in + branch_a
    normed_b = norm_rows(after_a, gain_full[1], shift_full[1]).astype(jnp.bfloat16)
    inner_rows = matmul_low(normed_b, up_all)
    hidden_low = gelu_exact(inner_rows).astype(jnp.bfloat16)
    after_b = after_a + matmul_low(hidden_low, down_all)
    normed_c = norm_rows(after_b, gain_full[2], shift_full[2]).astype(jnp.bfloat16)
    branch_c, saved_c = attend_forward(normed_c, qkv_all[1], proj_all[1])
    after_c = after_b + branch_c
    sent_low = norm_rows(after_c, gain_full[3], shift_full[3]).astype(jnp.bfloat16)
    flat_index = expert_index.reshape(-1)
    onehot = (flat_index[:, None] == jnp.arange(experts_all, dtype=jnp.int32)[None, :]).astype(
        jnp.int32
    )
    before = jnp.cumsum(onehot, axis=0) - onehot
    places = flat_index * capacity + jnp.sum(onehot * before, axis=1)
    repeated = jnp.repeat(sent_low, TOP, axis=0)
    send_buffer = (
        jnp.zeros((experts_all * capacity, D), jnp.bfloat16)
        .at[places]
        .set(repeated)
        .reshape(experts_all, capacity, D)
    )
    arrived = lax.all_to_all(send_buffer, "expert", split_axis=0, concat_axis=1, tiled=True)
    expert_inner = jnp.einsum(
        "erd,edf->erf", arrived, exp_in_all, preferred_element_type=jnp.float32
    )
    expert_hidden = gelu_exact(expert_inner).astype(jnp.bfloat16)
    expert_result = jnp.einsum(
        "erf,efd->erd", expert_hidden, exp_out_all, preferred_element_type=jnp.float32
    ).astype(jnp.bfloat16)
    returned = lax.all_to_all(expert_result, "expert", split_axis=1, concat_axis=0, tiled=True)
    picked = returned.reshape(-1, D)[places].astype(jnp.float32).reshape(row_count, TOP, D)
    act_out = after_c + jnp.sum(gate[:, :, None] * picked, axis=1)
    dense_back = fetch_dense(
        w_qkv.astype(jnp.bfloat16),
        w_proj.astype(jnp.bfloat16),
        w_up.astype(jnp.bfloat16),
        w_down.astype(jnp.bfloat16),
        norm_gain.astype(jnp.bfloat16),
        norm_shift.astype(jnp.bfloat16),
    )
    qkv_back, proj_back, up_back, down_back, gain_back, shift_back = dense_back
    gain_bf = gain_back.astype(jnp.float32)
    shift_bf = shift_back.astype(jnp.float32)
    grad_gate = jnp.sum(cotangent[:, None, :] * picked, axis=2)
    grad_slots = (
        (gate[:, :, None] * cotangent[:, None, :]).astype(jnp.bfloat16).reshape(row_count * TOP, D)
    )
    grad_buffer = (
        jnp.zeros((experts_all * capacity, D), jnp.bfloat16)
        .at[places]
        .set(grad_slots)
        .reshape(experts_all, capacity, D)
    )
    grad_arrived = lax.all_to_all(grad_buffer, "expert", split_axis=0, concat_axis=1, tiled=True)
    local_exp_out = jnp.einsum(
        "erf,erd->efd", expert_hidden, grad_arrived, preferred_element_type=jnp.float32
    )
    grad_hidden = jnp.einsum(
        "erd,efd->erf", grad_arrived, exp_out_all, preferred_element_type=jnp.float32
    )
    grad_inner = gelu_grad(expert_inner, grad_hidden).astype(jnp.bfloat16)
    local_exp_in = jnp.einsum(
        "erd,erf->edf", arrived, grad_inner, preferred_element_type=jnp.float32
    )
    grad_routed = jnp.einsum(
        "erf,edf->erd", grad_inner, exp_in_all, preferred_element_type=jnp.float32
    ).astype(jnp.bfloat16)
    grad_home = lax.all_to_all(grad_routed, "expert", split_axis=1, concat_axis=0, tiled=True)
    grad_sent = jnp.sum(
        grad_home.reshape(-1, D)[places].astype(jnp.float32).reshape(row_count, TOP, D), axis=1
    )
    grad_exp_in, grad_exp_out = (
        lax.psum_scatter(
            local_exp_in.astype(jnp.bfloat16), "dp", scatter_dimension=1, tiled=True
        ).astype(jnp.float32),
        lax.psum_scatter(
            local_exp_out.astype(jnp.bfloat16), "dp", scatter_dimension=2, tiled=True
        ).astype(jnp.float32),
    )
    grad_after_c, gain_d, shift_d = norm_grad(after_c, gain_bf[3], shift_bf[3], grad_sent)
    grad_after_c = cotangent + grad_after_c
    grad_normed_c, qkv_grad_c, proj_grad_c = attend_backward(
        grad_after_c, normed_c, qkv_back[1], proj_back[1], saved_c
    )
    through_c, gain_c, shift_c = norm_grad(after_b, gain_bf[2], shift_bf[2], grad_normed_c)
    grad_after_b = grad_after_c + through_c
    grad_mlp = grad_after_b.astype(jnp.bfloat16)
    down_grad = jnp.einsum("tf,td->fd", hidden_low, grad_mlp, preferred_element_type=jnp.float32)
    grad_hidden_b = jnp.einsum("td,fd->tf", grad_mlp, down_back, preferred_element_type=jnp.float32)
    grad_inner_b = gelu_grad(inner_rows, grad_hidden_b).astype(jnp.bfloat16)
    up_grad = jnp.einsum("td,tf->df", normed_b, grad_inner_b, preferred_element_type=jnp.float32)
    grad_normed_b = jnp.einsum(
        "tf,df->td", grad_inner_b, up_back, preferred_element_type=jnp.float32
    )
    through_b, gain_b, shift_b = norm_grad(after_a, gain_bf[1], shift_bf[1], grad_normed_b)
    grad_after_a = grad_after_b + through_b
    grad_normed_a, qkv_grad_a, proj_grad_a = attend_backward(
        grad_after_a, normed_a, qkv_back[0], proj_back[0], saved_a
    )
    through_a, gain_a, shift_a = norm_grad(act_in, gain_bf[0], shift_bf[0], grad_normed_a)
    act_grad = grad_after_a + through_a
    reduced = reduce_dense(
        jnp.stack([qkv_grad_a, qkv_grad_c]),
        jnp.stack([proj_grad_a, proj_grad_c]),
        up_grad,
        down_grad,
        jnp.stack([gain_a, gain_b, gain_c, gain_d]),
        jnp.stack([shift_a, shift_b, shift_c, shift_d]),
    )
    return (
        act_out,
        act_grad,
        reduced[0],
        reduced[1],
        reduced[2],
        reduced[3],
        reduced[4],
        reduced[5],
        grad_exp_in,
        grad_exp_out,
        grad_gate,
    )


def solution(mesh):
    in_specs = (
        P(("dp", "expert"), None),
        P(None, ("dp", "expert"), None),
        P(None, None, ("dp", "expert")),
        P(("dp", "expert"), None),
        P(None, ("dp", "expert")),
        P(None, ("dp", "expert")),
        P(None, ("dp", "expert")),
        P("expert", "dp", None),
        P("expert", None, "dp"),
        P(("dp", "expert"), None),
        P(("dp", "expert"), None),
        P(("dp", "expert"), None),
    )
    out_specs = (
        P(("dp", "expert"), None),
        P(("dp", "expert"), None),
        P(None, ("dp", "expert"), None),
        P(None, None, ("dp", "expert")),
        P(("dp", "expert"), None),
        P(None, ("dp", "expert")),
        P(None, ("dp", "expert")),
        P(None, ("dp", "expert")),
        P("expert", "dp", None),
        P("expert", None, "dp"),
        P(("dp", "expert"), None),
    )
    return jax.shard_map(local, mesh=mesh, in_specs=in_specs, out_specs=out_specs, check_vma=False)
```

profile of v0, /device:TPU:1, one launch (start us, length us, event | category | flops | bytes accessed | tf_op | source)
XLA Modules:
  0.0 1839.2 jit_solution(3664145385643357674)
XLA Ops:
  19.4 4.5 reduce-window.6
  27.8 5.4 mul.444
  33.3 15.2 scatter_custom_fusion.1
  48.5 5.2 all-to-all-start.2
  53.8 4.3 convert_element_type.208
  59.3 69.2 %all-gather.1 = bf16[32,24,4]{1,2,0:T(4,128)(2,1)S(1)} all-gather(bf16[1,24,4]{1,2,0:T(4,128)(2,1)S(1)} %convert_bitcast_fusion), channel_id=1, replica_groups=mesh['dp'=4,'expert'=8] {'dp','expert'}, dimensions={0}, use_global_device_ids=true | all-gather | bytes 6336 | tf_op jit(solution)/shard_map/all_gather | solution.py:49
  128.6 37.0 %all-gather = bf16[32,24,4]{1,2,0:T(4,128)(2,1)S(1)} all-gather(bf16[1,24,4]{1,2,0:T(4,128)(2,1)S(1)} %convert_bitcast_fusion.1), channel_id=1, replica_groups=mesh['dp'=4,'expert'=8] {'dp','expert'}, dimensions={0}, use_global_device_ids=true | all-gather | bytes 6336 | tf_op jit(solution)/shard_map/all_gather | solution.py:48
  166.2 6.0 convolution_convert_fusion.3
  172.2 9.3 reshape.365
  181.5 6.8 fusion.91
  195.8 4.6 copy.198
  217.3 15.5 all-gather.13.cloned.1.call-done
  232.7 35.6 %multiply_convert_fusion.3 = (bf16[591,3072]{1,0:T(8,128)(2,1)}, f32[591,3072]{1,0:T(8,128)}, f32[591,3072]{1,0:T(8,128)}) fusion(bf16[768,3072]{1,0:T(8,128)(2,1)} %all-gather.13.cloned.1.call-done, f32[591,768]{1,0:T(8,128)} %copy-done.6, f32[768]{0:T(1024)S(1)} %get-tuple-element.76, f32[768]{0:T(1024)S(1)} %get-tuple-element.119, f32[591]{0:T(1024)S(1)} %fusion.75, ...), kind=kOutput, calls=%fused_computation.39 | convolution fusion | flops 2908968192 | bytes 24700536 | tf_op jit(solution)/shard_map/dot_general | solution.py:39
  268.3 30.2 %all-gather.15.cloned.1.call-done = bf16[3072,768]{0,1:T(8,128)(2,1)} async-done(((bf16[3072,24]{0,1:T(8,128)(2,1)}), bf16[3072,768]{0,1:T(8,128)(2,1)}) %all-gather.15.cloned.1.call-update) | async-done | bytes 4718608 | tf_op jit(solution)/shard_map/all_gather | solution.py:47
  298.5 6.6 fusion.93
  306.4 5.0 convolution_convert_fusion.2
  311.4 7.4 reshape.366
  318.8 6.7 fusion.90
  356.2 10.4 scatter_custom_fusion
  373.9 22.6 %all-to-all-done = bf16[16,96,768]{2,1,0:T(8,128)(2,1)S(1)} async-done(((bf16[16,96,768]{2,1,0:T(8,128)(2,1)}), bf16[16,96,768]{2,1,0:T(8,128)(2,1)S(1)}, u32[]{:S(2)}, u32[]{:S(2)}) %all-to-all-start) | async-done | bytes 2359328 | tf_op jit(solution)/shard_map/all_to_all | solution.py:200
  398.0 67.3 %all-gather.17.cloned.1.call-done = bf16[2,768,3072]{2,1,0:T(8,128)(2,1)} async-done(((bf16[2,192,3072]{2,1,0:T(8,128)(2,1)}), bf16[2,768,3072]{2,1,0:T(8,128)(2,1)}) %all-gather.17.cloned.1.call-update) | async-done | bytes 9437200 | tf_op jit(solution)/shard_map/all_gather | solution.py:172
  465.4 22.8 %fusion.17 = (u8[768,3072]{1,0:T(8,128)(4,1)}, u8[768,3072]{1,0:T(8,128)(4,1)}, f32[2,768,3072]{2,1,0:T(8,128)}) fusion(bf16[2,768,768]{2,1,0:T(8,128)(2,1)} %bitcast.200, bf16[2,768,3072]{2,1,0:T(8,128)(2,1)} %all-gather.17.cloned.1.call-done), kind=kOutput, calls=%fused_computation.67 | convolution fusion | flops 7304380416 | bytes 35389440 | tf_op jit(solution)/shard_map/erd,edf->erf/dot_general | solution.py:201
  488.2 143.6 %all-gather.19.cloned.1.call-done = bf16[2,3072,768]{1,2,0:T(8,128)(2,1)} async-done(((bf16[2,3072,192]{1,2,0:T(8,128)(2,1)}), bf16[2,3072,768]{1,2,0:T(8,128)(2,1)}) %all-gather.19.cloned.1.call-update) | async-done | bytes 9437200 | tf_op jit(solution)/shard_map/all_gather | solution.py:173
  631.8 56.1 %add_convert_fusion = (bf16[2,768,3072]{2,1,0:T(8,128)(2,1)}, f32[2,768,3072]{2,1,0:T(8,128)}) fusion(f32[2,768,3072]{2,1,0:T(8,128)} %get-tuple-element.110, u8[768,3072]{1,0:T(8,128)(4,1)} %get-tuple-element.56, u8[768,3072]{1,0:T(8,128)(4,1)} %get-tuple-element.55, bf16[2,768,768]{2,1,0:T(8,128)(2,1)S(1)} %bitcast.203, ...), kind=kOutput, calls=%fused_computation.11 | convolution fusion | flops 7611088896 | bytes 63700992 | tf_op jit(solution)/shard_map/erd,efd->erf/dot_general | solution.py:236
  687.9 13.2 multiply_convert_fusion
  701.1 10.1 convolution_convert_fusion.4
  715.0 4.5 all-to-all-start.3
  719.6 12.9 convolution_convert_fusion.5
  736.3 9.2 all-to-all-done.3
  745.6 7.7 all-to-all-start.1
  755.4 23.8 %all-to-all-done.1 = bf16[2,768,768]{2,0,1:T(2,128)(2,1)} async-done(((bf16[2,768,768]{2,0,1:T(2,128)(2,1)}), bf16[2,768,768]{2,0,1:T(2,128)(2,1)}, u32[]{:S(2)}, u32[]{:S(2)}) %all-to-all-start.1) | async-done | bytes 2359328 | tf_op jit(solution)/shard_map/all_to_all | solution.py:208
  782.7 4.8 gather_fusion.1
  787.5 7.7 gather_fusion
  795.3 5.2 reshape.321
  800.4 10.9 multiply_reduce_fusion.4
  811.3 5.2 reshape.322
  816.5 7.7 reduce_sum.307
  837.2 4.4 copy.156
  841.5 5.0 fusion.32
  854.8 5.6 copy.161
  860.5 10.0 convert_element_type.222
  870.5 5.9 multiply_reduce_fusion.7
  879.5 9.5 add_convert_fusion.1
  898.9 8.2 copy.169
  907.1 13.2 convolution_convert_fusion
  920.4 14.4 convolution_convert_fusion.1
  935.5 8.6 fusion.82
  945.6 8.4 fusion.63
  960.7 4.6 copy.163
  965.2 6.1 multiply_reduce_fusion
  978.6 5.6 copy.168
  984.2 10.1 convert_element_type.230
  994.4 8.7 convolution_bitcast_fusion
  1003.1 5.6 convolution_bitcast_fusion.1
  1008.7 11.0 pad_maximum_fusion
  1022.4 7.5 multiply_reduce_fusion.9
  1030.0 40.6 %all-reduce.4 = (f32[4,768]{1,0:T(4,128)S(1)}, f32[4,768]{1,0:T(4,128)S(1)}) all-reduce(f32[4,768]{1,0:T(4,128)S(1)} %pad_maximum_fusion.2, f32[4,768]{1,0:T(4,128)S(1)} %pad_maximum_fusion.3), channel_id=6, replica_groups=mesh['dp'=4,'expert'=8] {'dp','expert'}, use_global_device_ids=true, to_apply=%region_37.38.clone | all-reduce | flops 6144 | bytes 49152
  1077.2 136.7 %reduce-scatter.16.cloned.1.call-done = bf16[2,3072,192]{1,2,0:T(8,128)(2,1)} async-done(((bf16[2,3072,768]{1,2,0:T(8,128)(2,1)}), bf16[2,3072,192]{1,2,0:T(8,128)(2,1)}) %reduce-scatter.16.cloned.1.call-update) | async-done | bytes 2359312 | tf_op jit(solution)/shard_map/reduce_scatter | solution.py:254
  1213.9 4.4 convert_element_type.235
  1218.3 160.2 %reduce-scatter.14.cloned.1.call-done = bf16[2,192,3072]{2,1,0:T(8,128)(2,1)} async-done(((bf16[2,768,3072]{2,1,0:T(8,128)(2,1)}), bf16[2,192,3072]{2,1,0:T(8,128)(2,1)}) %reduce-scatter.14.cloned.1.call-update) | async-done | bytes 2359312 | tf_op jit(solution)/shard_map/reduce_scatter | solution.py:251
  1378.5 4.4 convert_element_type.233
  1383.0 138.0 %reduce-scatter.10.cloned.1.call-done = f32[24,3072]{1,0:T(8,128)} async-done(((f32[768,3072]{1,0:T(8,128)}), f32[24,3072]{1,0:T(8,128)}) %reduce-scatter.10.cloned.1.call-update) | async-done | bytes 294928 | tf_op jit(solution)/shard_map/reduce_scatter | solution.py:58
  1521.0 140.9 %reduce-scatter.12.cloned.1.call-done = f32[3072,24]{0,1:T(8,128)} async-done(((f32[3072,768]{0,1:T(8,128)}), f32[3072,24]{0,1:T(8,128)}) %reduce-scatter.12.cloned.1.call-update) | async-done | bytes 294928 | tf_op jit(solution)/shard_map/reduce_scatter | solution.py:59
  1661.9 170.0 %reduce-scatter.8.cloned.1.call-done = f32[2,24,2304]{2,1,0:T(8,128)} async-done(((f32[2,768,2304]{2,1,0:T(8,128)}), f32[2,24,2304]{2,1,0:T(8,128)}) %reduce-scatter.8.cloned.1.call-update) | async-done | bytes 442384 | tf_op jit(solution)/shard_map/reduce_scatter | solution.py:56
  (381 shorter events, 155.1 us)
Async XLA Ops:
  7.2 159.1 %all-gather.9.cloned.1.call-start = ((), (), s32[]{:S(2)}) async-start(), calls=%async_computation.9 | async-start | bytes 7299072 | tf_op jit(solution)/shard_map/all_gather | solution.py:44
  9.0 204.0 %all-gather.11.cloned.1.call-start = ((), (), s32[]{:S(2)}) async-start(), calls=%async_computation.10 | async-start | bytes 2433024 | tf_op jit(solution)/shard_map/all_gather | solution.py:45
  10.6 222.1 %all-gather.13.cloned.1.call-start = ((), (), s32[]{:S(2)}) async-start(), calls=%async_computation.11 | async-start | bytes 4866048 | tf_op jit(solution)/shard_map/all_gather | solution.py:46
  12.3 286.2 %all-gather.15.cloned.1.call-start = ((), (), s32[]{:S(2)}) async-start(), calls=%async_computation.12 | async-start | bytes 4866048 | tf_op jit(solution)/shard_map/all_gather | solution.py:47
  14.1 451.3 %all-gather.17.cloned.1.call-start = ((), (), s32[]{:S(2)}) async-start(), calls=%async_computation.13 | async-start | bytes 11796480 | tf_op jit(solution)/shard_map/all_gather | solution.py:172
  18.2 6.6 copy-start.10
  19.0 8.9 copy-start.45
  33.3 322.9 %copy-start.84 = (s32[1182]{0:T(1024)}, s32[1182]{0:T(1024)S(1)}, u32[]{:S(2)}) copy-start(s32[1182]{0:T(1024)S(1)} %fusion.73) | copy-start | bytes 14188
  48.5 318.1 %all-to-all-start.2 = ((bf16[16,96,768]{2,1,0:T(8,128)(2,1)}), bf16[16,96,768]{2,1,0:T(8,128)(2,1)}, u32[]{:S(2)}, u32[]{:S(2)}) async-start(bf16[16,96,768]{2,1,0:T(8,128)(2,1)} %bitcast.26), calls=%async_computation.2 | async-start | bytes 4718592 | tf_op jit(solution)/shard_map/all_to_all | solution.py:232
  53.8 578.0 %all-gather.19.cloned.1.call-start = ((), (), s32[]{:S(2)}) async-start(), calls=%async_computation.14 | async-start | bytes 11796480 | tf_op jit(solution)/shard_map/all_gather | solution.py:173
  58.3 113.9 %copy-start.72 = (f32[591]{0:T(1024)}, f32[591]{0:T(1024)S(1)}, u32[]{:S(2)}) copy-start(f32[591]{0:T(1024)S(1)} %broadcast_multiply_fusion.4) | copy-start | bytes 7096
  59.3 112.9 %copy-start.91 = (f32[591]{0:T(1024)}, f32[591]{0:T(1024)S(1)}, u32[]{:S(2)}) copy-start(f32[591]{0:T(1024)S(1)} %fusion.74) | copy-start | bytes 7096
  166.2 66.6 %copy-start.56 = (f32[768]{0:T(1024)}, f32[768]{0:T(1024)S(1)}, u32[]{:S(2)}) copy-start(f32[768]{0:T(1024)S(1)} %get-tuple-element.119) | copy-start | bytes 9220
  166.2 66.5 %copy-start.60 = (f32[768]{0:T(1024)}, f32[768]{0:T(1024)S(1)}, u32[]{:S(2)}) copy-start(f32[768]{0:T(1024)S(1)} %get-tuple-element.76) | copy-start | bytes 9220
  166.2 139.3 %copy-start.89 = (f32[768]{0:T(1024)}, f32[768]{0:T(1024)S(1)}, u32[]{:S(2)}) copy-start(f32[768]{0:T(1024)S(1)} %get-tuple-element.120) | copy-start | bytes 9220
  166.2 139.3 %copy-start.99 = (f32[768]{0:T(1024)}, f32[768]{0:T(1024)S(1)}, u32[]{:S(2)}) copy-start(f32[768]{0:T(1024)S(1)} %get-tuple-element.75) | copy-start | bytes 9220
  166.2 184.0 %copy-start.68 = (f32[768]{0:T(1024)}, f32[768]{0:T(1024)S(1)}, u32[]{:S(2)}) copy-start(f32[768]{0:T(1024)S(1)} %get-tuple-element.121) | copy-start | bytes 9220
  195.8 7.1 copy-start.24
  215.7 52.7 %copy-start.54 = (f32[591]{0:T(1024)}, f32[591]{0:T(1024)S(1)}, u32[]{:S(2)}) copy-start(f32[591]{0:T(1024)S(1)} %broadcast_multiply_fusion.3) | copy-start | bytes 7096
  217.2 51.1 %copy-start.78 = (f32[591]{0:T(1024)}, f32[591]{0:T(1024)S(1)}, u32[]{:S(2)}) copy-start(f32[591]{0:T(1024)S(1)} %multiply_reduce_fusion.16) | copy-start | bytes 7096
  217.2 51.1 %copy-start.58 = (f32[591]{0:T(1024)}, f32[591]{0:T(1024)S(1)}, u32[]{:S(2)}) copy-start(f32[591]{0:T(1024)S(1)} %fusion.75) | copy-start | bytes 7096
  232.7 65.8 %copy-start.7 = (f32[591,768]{1,0:T(8,128)S(1)}, f32[591,768]{1,0:T(8,128)}, u32[]{:S(2)}) copy-start(f32[591,768]{1,0:T(8,128)} %copy-done.6) | copy-start | bytes 5446660
  366.6 29.9 %all-to-all-start = ((bf16[16,96,768]{2,1,0:T(8,128)(2,1)}), bf16[16,96,768]{2,1,0:T(8,128)(2,1)S(1)}, u32[]{:S(2)}, u32[]{:S(2)}) async-start(bf16[16,96,768]{2,1,0:T(8,128)(2,1)} %bitcast.19), calls=%async_computation | async-start | bytes 4718592 | tf_op jit(solution)/shard_map/all_to_all | solution.py:200
  465.4 166.4 %copy-start.48 = (bf16[2,8,96,768]{3,2,1,0:T(8,128)(2,1)S(1)}, bf16[2,8,96,768]{3,2,1,0:T(8,128)(2,1)}, u32[]{:S(2)}) copy-start(bf16[2,8,96,768]{3,2,1,0:T(8,128)(2,1)} %copy.152) | copy-start | bytes 7077892
  631.8 56.1 %copy-start.9 = (f32[2,768,3072]{2,1,0:T(8,128)S(1)}, f32[2,768,3072]{2,1,0:T(8,128)}, u32[]{:S(2)}) copy-start(f32[2,768,3072]{2,1,0:T(8,128)} %get-tuple-element.110) | copy-start | bytes 56623108
  687.9 13.2 copy-start.103
  715.0 30.5 %all-to-all-start.3 = ((bf16[2,768,768]{2,0,1:T(2,128)(2,1)}), bf16[2,768,768]{2,0,1:T(2,128)(2,1)S(1)}, u32[]{:S(2)}, u32[]{:S(2)}) async-start(bf16[2,768,768]{2,0,1:T(2,128)(2,1)} %copy.153), calls=%async_computation.3 | async-start | bytes 4718592 | tf_op jit(solution)/shard_map/all_to_all | solution.py:246
  732.4 20.8 %copy-start.85 = (s32[1182]{0:T(1024)S(1)}, s32[1182]{0:T(1024)}, u32[]{:S(2)}) copy-start(s32[1182]{0:T(1024)} %copy-done.84) | copy-start | bytes 14188
  732.5 20.8 %copy-start.53 = (f32[3,12,197]{2,1,0:T(8,128)S(1)}, f32[3,12,197]{2,1,0:T(8,128)}, u32[]{:S(2)}) copy-start(f32[3,12,197]{2,1,0:T(8,128)} %copy-done.52) | copy-start | bytes 85108
  732.5 20.8 %copy-start.65 = (f32[3,12,197]{2,1,0:T(8,128)S(1)}, f32[3,12,197]{2,1,0:T(8,128)}, u32[]{:S(2)}) copy-start(f32[3,12,197]{2,1,0:T(8,128)} %copy-done.64) | copy-start | bytes 85108
  745.6 7.8 copy-start.31
  745.6 33.7 %all-to-all-start.1 = ((bf16[2,768,768]{2,0,1:T(2,128)(2,1)}), bf16[2,768,768]{2,0,1:T(2,128)(2,1)}, u32[]{:S(2)}, u32[]{:S(2)}) async-start(bf16[2,768,768]{2,0,1:T(2,128)(2,1)} %copy.149), calls=%async_computation.1 | async-start | bytes 4718592 | tf_op jit(solution)/shard_map/all_to_all | solution.py:208
  753.3 322.3 %all-reduce.7.cloned.1.call-start = ((), (), s32[]{:S(2)}) async-start(), calls=%async_computation.20 | async-start | bytes 9437184
  816.5 7.7 copy-start.3
  816.5 7.7 copy-start.67
  816.5 7.7 copy-start.69
  816.5 7.7 copy-start.71
  816.5 10.6 copy-start.83
  837.2 9.4 slice-start.2
  860.4 10.0 copy-start.15
  860.4 10.0 copy-start.75
  860.5 10.0 copy-start.90
  860.5 10.0 copy-start.94
  877.8 11.2 slice-start.4
  878.1 15.2 copy-start.37
  879.5 9.5 copy-start.8
  879.5 9.5 copy-start.55
  879.5 9.5 copy-start.57
  879.5 9.6 copy-start.59
  879.5 9.6 slice-start.5
  907.1 306.8 %reduce-scatter.16.cloned.1.call-start = ((), (), s32[]{:S(2)}) async-start(), calls=%async_computation.19 | async-start | bytes 11796480 | tf_op jit(solution)/shard_map/reduce_scatter | solution.py:254
  920.4 458.2 %reduce-scatter.14.cloned.1.call-start = ((), (), s32[]{:S(2)}) async-start(), calls=%async_computation.18 | async-start | bytes 11796480 | tf_op jit(solution)/shard_map/reduce_scatter | solution.py:251
  934.8 586.1 %reduce-scatter.10.cloned.1.call-start = ((), (), s32[]{:S(2)}) async-start(), calls=%async_computation.16 | async-start | bytes 9732096 | tf_op jit(solution)/shard_map/reduce_scatter | solution.py:58
  944.1 717.8 %reduce-scatter.12.cloned.1.call-start = ((), (), s32[]{:S(2)}) async-start(), calls=%async_computation.17 | async-start | bytes 9732096 | tf_op jit(solution)/shard_map/reduce_scatter | solution.py:59
  954.1 877.9 %reduce-scatter.8.cloned.1.call-start = ((), (), s32[]{:S(2)}) async-start(), calls=%async_computation.15 | async-start | bytes 14598144 | tf_op jit(solution)/shard_map/reduce_scatter | solution.py:56
  960.7 10.7 slice-start
  984.2 10.1 copy-start.100
  994.3 8.8 copy-start.5
  994.4 8.8 copy-start.44
  994.4 8.7 copy-start.73
  994.4 8.7 copy-start.88
  994.4 8.7 copy-start.92
  994.4 8.7 copy-start.98
  1022.4 49.5 %copy-start.77 = (f32[591]{0:T(1024)S(1)}, f32[591]{0:T(1024)}, u32[]{:S(2)}) copy-start(f32[591]{0:T(1024)} %copy-done.76) | copy-start | bytes 7096
  (64 other events, 204.5 us)
Sparse Core Ops, SparseCore 0:
  11.5 89.1 all-gather.8
  104.2 62.3 all-gather.10
  170.1 62.5 all-gather.12
  236.0 62.4 all-gather.14
  299.9 165.3 all-gather.16
  466.8 164.9 all-gather.18
  907.2 142.7 all-reduce.6
  1052.5 161.3 reduce-scatter.15
  1216.4 162.1 reduce-scatter.13
  1385.9 135.0 reduce-scatter.9
  1527.4 134.4 reduce-scatter.11
  1669.4 162.5 reduce-scatter.7
where the time goes:
time: 1850 us; the launch traced here: 1840 us
  waiting for transfers between devices  1060 us (57%)
  matrix products  279 us (15%)
  local copies, waits for them, and re-layouts  204 us (11%)
  blocking collectives  147 us (8%)
  other arithmetic  113 us (6%)
  starting transfers between devices  21.9 us (1%)
    reduce_scatter x1, waiting for transfers between devices, reduce_dense(): lax.psum_scatter(qkv_grad, ('dp', 'expert'), scatter_dimension=1, tiled=T...  170 us
    reduce_scatter x1, waiting for transfers between devices, local(): lax.psum_scatter(local_exp_in.astype(jnp.bfloat16), 'dp', scatter_dimensi...  160 us
    all_gather x1, waiting for transfers between devices, local(): lax.all_gather(exp_out.astype(jnp.bfloat16), 'dp', axis=2, tiled=True)  144 us
    reduce_scatter x1, waiting for transfers between devices, reduce_dense(): lax.psum_scatter(down_grad, ('dp', 'expert'), scatter_dimension=1, tiled=...  141 us
    reduce_scatter x1, waiting for transfers between devices, reduce_dense(): lax.psum_scatter(up_grad, ('dp', 'expert'), scatter_dimension=0, tiled=True)  138 us
    reduce_scatter x1, waiting for transfers between devices, local(): lax.psum_scatter(local_exp_out.astype(jnp.bfloat16), 'dp', scatter_dimens...  137 us
    all_gather x1, blocking collectives, fetch_dense(): lax.all_gather(shift_part, ('dp', 'expert'), axis=1, tiled=True)  69.2 us
    all_gather x1, waiting for transfers between devices, local(): lax.all_gather(exp_in.astype(jnp.bfloat16), 'dp', axis=1, tiled=True)  67.3 us
  transfers between devices with their start and end apart: 16, of which 12 were waited for; matrix products, arithmetic and copies ran while one was open for 20% of the time, Pallas kernels for 0%

commit v1 on v0

v1 whole, which is shorter than its diff:
```python
import math

import jax
import jax.numpy as jnp
from jax import lax
from jax.sharding import Mesh, PartitionSpec as P

D = 768
FF = 3072
HEADS = 12
HEAD = 64
SEQ = 197
TOP = 2
EXP_DEV = 2
TOK_DEV = 591
DP_AXES = ("dh", "dl")
ALL_AXES = ("dh", "dl", "expert")
TOKEN_AXES = ("dl", "expert")


def norm_rows(inputs, gain_row, shift_row):
    average = jnp.mean(inputs, axis=-1, keepdims=True)
    centred = inputs - average
    spread = jnp.mean(centred * centred, axis=-1, keepdims=True)
    return centred * lax.rsqrt(spread + 1e-06) * gain_row + shift_row


def gelu_exact(inputs):
    return jax.nn.gelu(inputs, approximate=False)


def gelu_grad(inputs, upstream):
    _, pull_back = jax.vjp(gelu_exact, inputs)
    return pull_back(upstream)[0]


def norm_grad(inputs, gain_row, shift_row, upstream):
    _, pull_back = jax.vjp(norm_rows, inputs, gain_row, shift_row)
    return pull_back(upstream)


def matmul_low(left, right):
    return jnp.dot(left, right, preferred_element_type=jnp.float32)


def gather_rows(part):
    return lax.all_gather(part, ALL_AXES, axis=0, tiled=True)


def scatter_rows(full):
    return lax.psum_scatter(
        full.astype(jnp.bfloat16), ALL_AXES, scatter_dimension=0, tiled=True
    ).astype(jnp.float32)


def split_heads(packed_rows):
    images = packed_rows.shape[0] // SEQ
    shaped = packed_rows.reshape(images, SEQ, 3, HEADS, HEAD)
    return (shaped[:, :, 0], shaped[:, :, 1], shaped[:, :, 2])


def attend_forward(normed_low, qkv_weight, proj_weight):
    score_scale = 1.0 / math.sqrt(HEAD)
    packed = matmul_low(normed_low, qkv_weight).astype(jnp.bfloat16)
    query_rows, key_rows, value_rows = split_heads(packed)
    scores = (
        jnp.einsum("bqhd,bkhd->bhqk", query_rows, key_rows, preferred_element_type=jnp.float32)
        * score_scale
    )
    row_peak = jnp.max(scores, axis=-1, keepdims=True)
    raised = jnp.exp(scores - row_peak)
    row_total = jnp.sum(raised, axis=-1, keepdims=True)
    attn_weights = raised / row_total
    log_total = row_peak + jnp.log(row_total)
    mixed_rows = jnp.einsum(
        "bhqk,bkhd->bqhd",
        attn_weights.astype(jnp.bfloat16),
        value_rows,
        preferred_element_type=jnp.float32,
    )
    mixed_rows = mixed_rows.astype(jnp.bfloat16).reshape(packed.shape[0], D)
    branch = matmul_low(mixed_rows, proj_weight)
    return (branch, (packed, log_total, mixed_rows))


def attend_backward(grad_branch, normed_low, qkv_weight, proj_weight, saved):
    score_scale = 1.0 / math.sqrt(HEAD)
    packed, log_total, mixed_rows = saved
    row_count = packed.shape[0]
    grad_low = grad_branch.astype(jnp.bfloat16)
    grad_proj = jnp.einsum("td,te->de", mixed_rows, grad_low, preferred_element_type=jnp.float32)
    grad_mixed = jnp.einsum("te,de->td", grad_low, proj_weight, preferred_element_type=jnp.float32)
    grad_mixed = grad_mixed.astype(jnp.bfloat16).reshape(row_count // SEQ, SEQ, HEADS, HEAD)
    query_rows, key_rows, value_rows = split_heads(packed)
    scores = (
        jnp.einsum("bqhd,bkhd->bhqk", query_rows, key_rows, preferred_element_type=jnp.float32)
        * score_scale
    )
    attn_weights = jnp.exp(scores - log_total)
    grad_weights = jnp.einsum(
        "bqhd,bkhd->bhqk", grad_mixed, value_rows, preferred_element_type=jnp.float32
    )
    grad_values = jnp.einsum(
        "bhqk,bqhd->bkhd",
        attn_weights.astype(jnp.bfloat16),
        grad_mixed,
        preferred_element_type=jnp.float32,
    )
    grad_scores = attn_weights * (
        grad_weights - jnp.sum(attn_weights * grad_weights, axis=-1, keepdims=True)
    )
    grad_scores = grad_scores.astype(jnp.bfloat16)
    grad_query = (
        jnp.einsum("bhqk,bkhd->bqhd", grad_scores, key_rows, preferred_element_type=jnp.float32)
        * score_scale
    )
    grad_keys = (
        jnp.einsum("bhqk,bqhd->bkhd", grad_scores, query_rows, preferred_element_type=jnp.float32)
        * score_scale
    )
    grad_packed = (
        jnp.stack([grad_query, grad_keys, grad_values], axis=2)
        .reshape(row_count, 3 * D)
        .astype(jnp.bfloat16)
    )
    grad_qkv = jnp.einsum("td,tf->df", normed_low, grad_packed, preferred_element_type=jnp.float32)
    grad_normed = jnp.einsum(
        "tf,df->td", grad_packed, qkv_weight, preferred_element_type=jnp.float32
    )
    return (grad_normed, grad_qkv, grad_proj)


def local(
    act_in,
    w_qkv,
    w_proj,
    w_up,
    w_down,
    norm_gain,
    norm_shift,
    exp_in,
    exp_out,
    gate,
    expert_index,
    cotangent,
):
    row_count = act_in.shape[0]
    groups = lax.axis_size("expert")
    experts_all = EXP_DEV * groups
    n_dp = lax.axis_size(DP_AXES)
    capacity = (TOP * TOK_DEV * 5 // (4 * experts_all) + 7) // 8 * 8
    low = jnp.bfloat16
    rows = w_up.shape[0]
    proj_t = jnp.swapaxes(w_proj, 1, 2).astype(low)
    qkv_low = w_qkv.astype(low)
    norms = jnp.concatenate([norm_gain.T, norm_shift.T], axis=1).astype(low)
    norms = jnp.pad(norms, ((0, 0), (0, 128 - norms.shape[1])))
    first = gather_rows(jnp.concatenate([qkv_low[0], proj_t[0], norms], axis=1))
    second = gather_rows(
        jnp.concatenate(
            [w_up.astype(low), w_down.T.astype(low), qkv_low[1], proj_t[1]], axis=1
        )
    )
    qkv_all = (first[:, : 3 * D], second[:, 2 * FF : 2 * FF + 3 * D])
    proj_all = (first[:, 3 * D : 4 * D].T, second[:, 2 * FF + 3 * D :].T)
    up_all, down_all = second[:, :FF], second[:, FF : 2 * FF].T
    norm_all = first[:, 4 * D : 4 * D + 8].astype(jnp.float32).T
    gain_full, shift_full = norm_all[:4], norm_all[4:]

    def fetch_expert(part):
        copies = jnp.tile(part.astype(low), (n_dp // EXP_DEV, 1, 1))
        return lax.all_to_all(copies, DP_AXES, 0, 0, tiled=True).reshape(D, FF)

    exp_in_all = fetch_expert(exp_in)
    exp_out_all = fetch_expert(jnp.swapaxes(exp_out, 1, 2)).T
    normed_a = norm_rows(act_in, gain_full[0], shift_full[0]).astype(jnp.bfloat16)
    branch_a, saved_a = attend_forward(normed_a, qkv_all[0], proj_all[0])
    after_a = act_in + branch_a
    normed_b = norm_rows(after_a, gain_full[1], shift_full[1]).astype(jnp.bfloat16)
    inner_rows = matmul_low(normed_b, up_all)
    hidden_low = gelu_exact(inner_rows).astype(jnp.bfloat16)
    after_b = after_a + matmul_low(hidden_low, down_all)
    normed_c = norm_rows(after_b, gain_full[2], shift_full[2]).astype(jnp.bfloat16)
    branch_c, saved_c = attend_forward(normed_c, qkv_all[1], proj_all[1])
    after_c = after_b + branch_c
    sent_low = norm_rows(after_c, gain_full[3], shift_full[3]).astype(jnp.bfloat16)
    flat_index = expert_index.reshape(-1)
    onehot = (flat_index[:, None] == jnp.arange(experts_all, dtype=jnp.int32)[None, :]).astype(
        jnp.int32
    )
    before = jnp.cumsum(onehot, axis=0) - onehot
    holder = (flat_index % EXP_DEV) * groups + flat_index // EXP_DEV
    places = holder * capacity + jnp.sum(onehot * before, axis=1)
    repeated = jnp.repeat(sent_low, TOP, axis=0)
    send_buffer = (
        jnp.zeros((experts_all * capacity, D), jnp.bfloat16)
        .at[places]
        .set(repeated)
        .reshape(experts_all, capacity, D)
    )
    arrived = lax.all_to_all(send_buffer, TOKEN_AXES, 0, 0, tiled=True).reshape(-1, D)
    expert_inner = jnp.einsum(
        "rd,df->rf", arrived, exp_in_all, preferred_element_type=jnp.float32
    )
    expert_hidden = gelu_exact(expert_inner).astype(jnp.bfloat16)
    expert_result = jnp.einsum(
        "rf,fd->rd", expert_hidden, exp_out_all, preferred_element_type=jnp.float32
    ).astype(jnp.bfloat16)
    returned = lax.all_to_all(
        expert_result.reshape(experts_all, capacity, D), TOKEN_AXES, 0, 0, tiled=True
    )
    picked = returned.reshape(-1, D)[places].astype(jnp.float32).reshape(row_count, TOP, D)
    act_out = after_c + jnp.sum(gate[:, :, None] * picked, axis=1)
    grad_gate = jnp.sum(cotangent[:, None, :] * picked, axis=2)
    grad_slots = (
        (gate[:, :, None] * cotangent[:, None, :]).astype(jnp.bfloat16).reshape(row_count * TOP, D)
    )
    grad_buffer = (
        jnp.zeros((experts_all * capacity, D), jnp.bfloat16)
        .at[places]
        .set(grad_slots)
        .reshape(experts_all, capacity, D)
    )
    grad_arrived = lax.all_to_all(grad_buffer, TOKEN_AXES, 0, 0, tiled=True).reshape(-1, D)
    local_exp_out = jnp.einsum(
        "rf,rd->fd", expert_hidden, grad_arrived, preferred_element_type=jnp.float32
    )
    grad_hidden = jnp.einsum(
        "rd,fd->rf", grad_arrived, exp_out_all, preferred_element_type=jnp.float32
    )
    grad_inner = gelu_grad(expert_inner, grad_hidden).astype(jnp.bfloat16)
    local_exp_in = jnp.einsum(
        "rd,rf->df", arrived, grad_inner, preferred_element_type=jnp.float32
    )
    grad_routed = jnp.einsum(
        "rf,df->rd", grad_inner, exp_in_all, preferred_element_type=jnp.float32
    ).astype(jnp.bfloat16)
    grad_home = lax.all_to_all(
        grad_routed.reshape(experts_all, capacity, D), TOKEN_AXES, 0, 0, tiled=True
    )
    grad_sent = jnp.sum(
        grad_home.reshape(-1, D)[places].astype(jnp.float32).reshape(row_count, TOP, D), axis=1
    )
    def share_expert(partial):
        pieces = partial.astype(low).reshape(n_dp, D // n_dp, FF)
        pieces = lax.all_to_all(pieces, DP_AXES, 0, 0, tiled=True)
        pieces = pieces.reshape(n_dp // EXP_DEV, EXP_DEV, D // n_dp, FF)
        return jnp.sum(pieces.astype(jnp.float32), axis=0)

    grad_exp_out = jnp.swapaxes(share_expert(local_exp_out.T), 1, 2)
    grad_exp_in = share_expert(local_exp_in)
    grad_after_c, gain_d, shift_d = norm_grad(after_c, gain_full[3], shift_full[3], grad_sent)
    grad_after_c = cotangent + grad_after_c
    grad_normed_c, qkv_grad_c, proj_grad_c = attend_backward(
        grad_after_c, normed_c, qkv_all[1], proj_all[1], saved_c
    )
    through_c, gain_c, shift_c = norm_grad(after_b, gain_full[2], shift_full[2], grad_normed_c)
    grad_after_b = grad_after_c + through_c
    grad_mlp = grad_after_b.astype(jnp.bfloat16)
    down_grad = jnp.einsum("tf,td->fd", hidden_low, grad_mlp, preferred_element_type=jnp.float32)
    grad_hidden_b = jnp.einsum("td,fd->tf", grad_mlp, down_all, preferred_element_type=jnp.float32)
    grad_inner_b = gelu_grad(inner_rows, grad_hidden_b).astype(jnp.bfloat16)
    up_grad = jnp.einsum("td,tf->df", normed_b, grad_inner_b, preferred_element_type=jnp.float32)
    grad_normed_b = jnp.einsum(
        "tf,df->td", grad_inner_b, up_all, preferred_element_type=jnp.float32
    )
    through_b, gain_b, shift_b = norm_grad(after_a, gain_full[1], shift_full[1], grad_normed_b)
    grad_after_a = grad_after_b + through_b
    grad_normed_a, qkv_grad_a, proj_grad_a = attend_backward(
        grad_after_a, normed_a, qkv_all[0], proj_all[0], saved_a
    )
    through_a, gain_a, shift_a = norm_grad(act_in, gain_full[0], shift_full[0], grad_normed_a)
    act_grad = grad_after_a + through_a
    late = scatter_rows(
        jnp.concatenate([up_grad, down_grad.T, qkv_grad_c, proj_grad_c.T], axis=1)
    )
    norm_grads = jnp.concatenate(
        [
            jnp.stack([gain_a, gain_b, gain_c, gain_d], axis=1),
            jnp.stack([shift_a, shift_b, shift_c, shift_d], axis=1),
            jnp.zeros((D, 120), jnp.float32),
        ],
        axis=1,
    )
    last = scatter_rows(jnp.concatenate([qkv_grad_a, proj_grad_a.T, norm_grads], axis=1))
    grad_qkv = jnp.stack([last[:, : 3 * D], late[:, 2 * FF : 2 * FF + 3 * D]])
    grad_proj = jnp.swapaxes(
        jnp.stack([last[:, 3 * D : 4 * D], late[:, 2 * FF + 3 * D :]]), 1, 2
    )
    return (
        act_out,
        act_grad,
        grad_qkv,
        grad_proj,
        late[:, :FF],
        late[:, FF : 2 * FF].T,
        last[:, 4 * D : 4 * D + 4].T,
        last[:, 4 * D + 4 : 4 * D + 8].T,
        grad_exp_in,
        grad_exp_out,
        grad_gate,
    )


def solution(mesh):
    n_dp, n_expert = mesh.devices.shape
    mesh = Mesh(mesh.devices.reshape(n_dp // EXP_DEV, EXP_DEV, n_expert), ALL_AXES)
    in_specs = (
        P(ALL_AXES, None),
        P(None, ALL_AXES, None),
        P(None, None, ALL_AXES),
        P(ALL_AXES, None),
        P(None, ALL_AXES),
        P(None, ALL_AXES),
        P(None, ALL_AXES),
        P("expert", DP_AXES, None),
        P("expert", None, DP_AXES),
        P(ALL_AXES, None),
        P(ALL_AXES, None),
        P(ALL_AXES, None),
    )
    out_specs = (
        P(ALL_AXES, None),
        P(ALL_AXES, None),
        P(None, ALL_AXES, None),
        P(None, None, ALL_AXES),
        P(ALL_AXES, None),
        P(None, ALL_AXES),
        P(None, ALL_AXES),
        P(None, ALL_AXES),
        P("expert", DP_AXES, None),
        P("expert", None, DP_AXES),
        P(ALL_AXES, None),
    )
    return jax.shard_map(local, mesh=mesh, in_specs=in_specs, out_specs=out_specs, check_vma=False)
```

time: 1850 us -> 1170 us (0.63)
  waiting for transfers between devices: 1060 us -> 533 us
  blocking collectives: 147 us -> 0 us
  starting transfers between devices: 21.9 us -> 49.4 us
  matrix products: 279 us -> 253 us
    reduce_scatter x5 -> x1, waiting for transfers between devices: 746 us -> 53.2 us  [scatter_rows(): lax.psum_scatter(full.astype(jnp.bfloat16), ALL_AXES, scatter_dimension=0...]
    all_to_all x4 -> x8, waiting for transfers between devices: 55.7 us -> 354 us  [the longest x2 242 us: share_expert(): pieces = lax.all_to_all(pieces, DP_AXES, 0, 0, tiled=True)]
    all_gather x6 -> x2, waiting for transfers between devices: 257 us -> 125 us  [gather_rows(): return lax.all_gather(part, ALL_AXES, axis=0, tiled=True)]
    all_gather x2 -> x0, blocking collectives: 106 us -> none  [the longest x1 69.2 us: fetch_dense(): lax.all_gather(shift_part, ('dp', 'expert'), axis=1, tiled=True)]
    unnamed x1 -> x0, blocking collectives: 40.6 us -> none
    all_to_all x4 -> x8, starting transfers between devices: 21.5 us -> 49.2 us  [the longest x2 10.9 us: fetch_expert(): return lax.all_to_all(copies, DP_AXES, 0, 0, tiled=True).reshape(D, FF)]
    convert_element_type x11 -> x8, other arithmetic: 38.7 us -> 12.9 us  [the longest x2 6.84 us: fetch_expert(): copies = jnp.tile(part.astype(low), (n_dp // EXP_DEV, 1, 1))]
    dot_general x6, matrix products: 58.5 us -> 39.6 us  [matmul_low(): return jnp.dot(left, right, preferred_element_type=jnp.float32)]
  transfers between devices with their start and end apart: 16 -> 12, of which waited for: 12 -> 9; matrix products, arithmetic and copies ran while one was open for 20% -> 29% of each run, Pallas kernels for 0% -> 0%
where the time goes in v1:
time: 1170 us; the launch traced here: 1160 us
  waiting for transfers between devices  533 us (46%)
  matrix products  253 us (22%)
  local copies, waits for them, and re-layouts  195 us (17%)
  other arithmetic  113 us (10%)
  starting transfers between devices  49.4 us (4%)
  between operations  15.8 us (1%)
    all_to_all x2, waiting for transfers between devices, share_expert(): pieces = lax.all_to_all(pieces, DP_AXES, 0, 0, tiled=True)  242 us
    all_gather x2, waiting for transfers between devices, gather_rows(): return lax.all_gather(part, ALL_AXES, axis=0, tiled=True)  125 us
    all_to_all x2, waiting for transfers between devices, fetch_expert(): return lax.all_to_all(copies, DP_AXES, 0, 0, tiled=True).reshape(D, FF)  54.6 us
    reduce_scatter x1, waiting for transfers between devices, scatter_rows(): lax.psum_scatter(full.astype(jnp.bfloat16), ALL_AXES, scatter_dimension=0...  53.2 us
    dot_general x1, matrix products, local(): jnp.einsum('rd,df->rf', arrived, exp_in_all, preferred_element_type=jnp.f...  49.4 us
    dot_general x6, matrix products, matmul_low(): return jnp.dot(left, right, preferred_element_type=jnp.float32)  39.6 us
    unnamed x225, local copies, waits for them, and re-layouts  39.3 us
    all_to_all x1, waiting for transfers between devices, local(): lax.all_to_all(send_buffer, TOKEN_AXES, 0, 0, tiled=True).reshape(-1, D)  29.4 us
  transfers between devices with their start and end apart: 12, of which 9 were waited for; matrix products, arithmetic and copies ran while one was open for 29% of the time, Pallas kernels for 0%

profile of v1, /device:TPU:1, one launch (start us, length us, event | category | flops | bytes accessed | tf_op | source)
XLA Modules:
  0.0 1158.6 jit_solution(3566525716894557025)
XLA Ops:
  14.4 4.5 reduce-window.6
  23.2 5.4 mul.455
  28.7 15.2 %scatter_custom_fusion.1 = bf16[1536,768]{1,0:T(8,128)(2,1)} fusion(s32[1182]{0:T(1024)S(1)} %fusion.100, f32[1182,768]{1,0:T(8,128)} %mul.455, f32[1182]{0:T(1024)S(1)} %mul.452, bf16[]{:T(256)} %constant.48.clone.1), kind=kCustom, calls=%fused_computation.103 | custom fusion | flops 1815552 | bytes 5998594 | tf_op jit(solution)/shard_map/scatter | solution.py:221
  43.9 6.6 all-to-all-start.4
  50.5 4.2 convert_element_type.195
  55.8 44.3 %all-gather.3.cloned.1.call-done = bf16[768,3200]{1,0:T(8,128)(2,1)} async-done(((bf16[24,3200]{1,0:T(8,128)(2,1)}), bf16[768,3200]{1,0:T(8,128)(2,1)}) %all-gather.3.cloned.1.call-update) | async-done | bytes 4915216 | tf_op jit(solution)/shard_map/all_gather | solution.py:47
  102.8 6.0 convolution_convert_fusion.7
  108.7 9.3 reshape.466
  118.1 6.8 fusion.118
  128.2 4.7 copy.154
  132.9 4.4 copy.152
  152.0 4.4 tile.8
  156.4 5.9 all-to-all-start.1
  162.4 81.1 %all-gather.5.cloned.1.call-done = bf16[768,9216]{1,0:T(8,128)(2,1)} async-done(((bf16[24,9216]{1,0:T(8,128)(2,1)}), bf16[768,9216]{1,0:T(8,128)(2,1)}) %all-gather.5.cloned.1.call-update) | async-done | bytes 14155792 | tf_op jit(solution)/shard_map/all_gather | solution.py:47
  243.5 22.8 %multiply_convert_fusion.3 = (bf16[591,3072]{1,0:T(8,128)(2,1)S(1)}, f32[591,3072]{1,0:T(8,128)}, f32[591,3072]{1,0:T(8,128)}) fusion(bf16[768,9216]{1,0:T(8,128)(2,1)} %all-gather.5.cloned.1.call-done, f32[591,768]{1,0:T(8,128)S(1)} %copy-done.10, f32[768]{0:T(1024)S(1)} %get-tuple-element.61, f32[768]{0:T(1024)S(1)} %get-tuple-element.62, ...), kind=kOutput, calls=%fused_computation.37 | convolution fusion | flops 2908968192 | bytes 24700536 | tf_op jit(solution)/shard_map/dot_general | solution.py:43
  273.3 7.2 reshape.467
  280.5 6.6 fusion.117
  294.2 4.2 copy.155
  316.6 10.5 scatter_custom_fusion
  327.1 6.2 all-to-all-start
  336.0 29.4 %all-to-all-done = bf16[16,96,768]{2,1,0:T(8,128)(2,1)} async-done(((bf16[16,96,768]{2,1,0:T(8,128)(2,1)}), bf16[16,96,768]{2,1,0:T(8,128)(2,1)}, u32[]{:S(2)}, u32[]{:S(2)}) %all-to-all-start) | async-done | bytes 2359328 | tf_op jit(solution)/shard_map/all_to_all | solution.py:201
  368.2 5.0 all-to-all-start.2
  373.2 49.4 %multiply_convert_fusion = (bf16[1536,3072]{1,0:T(8,128)(2,1)}, f32[1536,3072]{1,0:T(8,128)}, f32[1536,3072]{1,0:T(8,128)}) fusion(bf16[1536,768]{1,0:T(8,128)(2,1)} %bitcast.19, bf16[768,3072]{1,0:T(8,128)(2,1)} %bitcast.21), kind=kOutput, calls=%fused_computation.7 | convolution fusion | flops 7554465792 | bytes 54263808 | tf_op jit(solution)/shard_map/rd,df->rf/dot_general | solution.py:202
  422.6 54.6 %all-to-all-done.2 = bf16[4,192,3072]{2,1,0:T(8,128)(2,1)} async-done(((bf16[4,192,3072]{2,1,0:T(8,128)(2,1)}), bf16[4,192,3072]{2,1,0:T(8,128)(2,1)}, u32[]{:S(2)}, u32[]{:S(2)}) %all-to-all-start.2) | async-done | bytes 4718624 | tf_op jit(solution)/shard_map/all_to_all | solution.py:172
  477.1 21.6 %add_convert_fusion = bf16[1536,3072]{1,0:T(8,128)(2,1)S(1)} fusion(f32[1536,3072]{1,0:T(8,128)} %get-tuple-element.74, f32[1536,3072]{1,0:T(8,128)} %get-tuple-element.101, bf16[1536,768]{1,0:T(8,128)(2,1)} %bitcast.28, bf16[768,3072]{1,0:T(8,128)(2,1)} %bitcast.24), kind=kOutput, calls=%fused_computation.6 | convolution fusion | flops 7313817600 | bytes 54263808 | tf_op jit(solution)/shard_map/rd,fd->rf/dot_general | solution.py:228
  498.8 14.5 %convolution_convert_fusion.8 = bf16[1536,768]{1,0:T(8,128)(2,1)} fusion(bf16[1536,3072]{1,0:T(8,128)(2,1)S(1)} %add_convert_fusion, bf16[768,3072]{1,0:T(8,128)(2,1)} %bitcast.21), kind=kOutput, calls=%fused_computation.86 | convolution fusion | flops 7248936960 | bytes 16515072 | tf_op jit(solution)/shard_map/rf,df->rd/dot_general | solution.py:235
  513.3 8.4 all-to-all-start.5
  521.7 12.6 %convolution_convert_fusion.9 = bf16[1536,768]{1,0:T(8,128)(2,1)} fusion(bf16[1536,3072]{1,0:T(8,128)(2,1)} %get-tuple-element.73, bf16[768,3072]{1,0:T(8,128)(2,1)} %bitcast.24), kind=kOutput, calls=%fused_computation.87 | convolution fusion | flops 7248936960 | bytes 16515072 | tf_op jit(solution)/shard_map/rf,fd->rd/dot_general | solution.py:206
  534.3 19.3 %all-to-all-done.5 = bf16[16,96,768]{2,1,0:T(8,128)(2,1)S(1)} async-done(((bf16[16,96,768]{2,1,0:T(8,128)(2,1)}), bf16[16,96,768]{2,1,0:T(8,128)(2,1)S(1)}, u32[]{:S(2)}, u32[]{:S(2)}) %all-to-all-start.5) | async-done | bytes 2359328 | tf_op jit(solution)/shard_map/all_to_all | solution.py:238
  555.1 6.6 all-to-all-start.3
  561.8 7.7 gather_fusion.1
  569.5 5.0 reshape.431
  574.6 7.6 reduce_sum.323
  584.9 8.8 all-to-all-done.3
  593.6 4.9 gather_fusion
  598.6 5.2 reshape.430
  603.8 20.2 %multiply_reduce_fusion.4 = (f32[591,2]{1,0:T(8,128)}, f32[591,768]{1,0:T(8,128)S(1)}) fusion(f32[591,2,768]{2,1,0:T(2,128)} %reshape.430, f32[591,768]{1,0:T(8,128)S(1)} %copy-done.8, f32[591,2]{1,0:T(8,128)S(1)} %copy-done.42), kind=kLoop, calls=%fused_computation.82 | loop fusion | flops 3176034 | bytes 7271664 | tf_op jit(solution)/shard_map/reduce_sum | solution.py:214
  632.6 4.4 copy.108
  637.0 6.1 multiply_reduce_fusion.1
  650.6 5.6 copy.113
  656.2 10.0 convert_element_type.211
  666.2 5.8 multiply_reduce_fusion.7
  673.9 10.8 add_convert_fusion.1
  684.8 7.0 multiply_reduce_fusion.8
  699.3 4.4 copy.115
  703.7 6.1 multiply_reduce_fusion
  723.7 5.6 copy.120
  729.4 10.0 convert_element_type.218
  739.4 6.9 convolution_convert_fusion.3
  746.3 6.2 multiply_reduce_fusion.9
  758.6 9.2 concatenate.21
  771.9 5.9 convolution_convert_fusion.2
  777.9 4.1 convolution_convert_fusion
  782.1 4.7 convolution_convert_fusion.1
  786.8 11.4 pad_maximum_fusion
  798.2 12.5 %convolution_convert_fusion.5 = bf16[768,3072]{1,0:T(8,128)(2,1)} fusion(bf16[1536,768]{1,0:T(8,128)(2,1)} %bitcast.19, bf16[1536,3072]{1,0:T(8,128)(2,1)} %copy-done.97), kind=kOutput, calls=%fused_computation.60 | convolution fusion | flops 7250116608 | bytes 16515072 | tf_op jit(solution)/shard_map/rd,rf->df/dot_general | solution.py:232
  810.7 5.4 all-to-all-start.6
  816.1 12.3 %convolution_convert_fusion.4 = bf16[768,3072]{1,0:T(8,128)(2,1)} fusion(bf16[1536,768]{1,0:T(8,128)(2,1)} %bitcast.28, bf16[1536,3072]{1,0:T(8,128)(2,1)} %get-tuple-element.73), kind=kOutput, calls=%fused_computation.59 | convolution fusion | flops 7250116608 | bytes 16515072 | tf_op jit(solution)/shard_map/rf,rd->fd/dot_general | solution.py:225
  828.5 110.3 %all-to-all-done.6 = bf16[4,192,3072]{2,1,0:T(8,128)(2,1)} async-done(((bf16[4,192,3072]{2,1,0:T(8,128)(2,1)}), bf16[4,192,3072]{2,1,0:T(8,128)(2,1)}, u32[]{:S(2)}, u32[]{:S(2)}) %all-to-all-start.6) | async-done | bytes 4718624 | tf_op jit(solution)/shard_map/all_to_all | solution.py:246
  938.8 5.1 all-to-all-start.7
  948.4 6.0 convert_reduce_fusion.1
  954.4 131.5 %all-to-all-done.7 = bf16[4,192,3072]{2,1,0:T(8,128)(2,1)} async-done(((bf16[4,192,3072]{2,1,0:T(8,128)(2,1)}), bf16[4,192,3072]{2,1,0:T(8,128)(2,1)}, u32[]{:S(2)}, u32[]{:S(2)}) %all-to-all-start.7) | async-done | bytes 4718624 | tf_op jit(solution)/shard_map/all_to_all | solution.py:246
  1085.9 6.0 convert_reduce_fusion
  1094.3 53.2 %reduce-scatter.5.cloned.1.call-done = bf16[24,9216]{1,0:T(8,128)(2,1)} async-done(((bf16[768,9216]{1,0:T(8,128)(2,1)}), bf16[24,9216]{1,0:T(8,128)(2,1)}) %reduce-scatter.5.cloned.1.call-update) | async-done | bytes 442384 | tf_op jit(solution)/shard_map/reduce_scatter | solution.py:51
  (348 shorter events, 134.9 us)
Async XLA Ops:
  7.2 6.5 copy-start.89
  7.2 12.5 %copy-start.90 = (f32[591,2]{0,1:T(2,128)S(1)}, f32[591,2]{0,1:T(2,128)}, u32[]{:S(2)}) copy-start(f32[591,2]{0,1:T(2,128)} %param.21) | copy-start | bytes 14188
  7.2 12.9 %copy-start.7 = (f32[591,768]{1,0:T(8,128)S(1)}, f32[591,768]{1,0:T(8,128)}, u32[]{:S(2)}) copy-start(f32[591,768]{1,0:T(8,128)} %param.23) | copy-start | bytes 5446660
  7.2 92.9 %all-gather.3.cloned.1.call-start = ((), (), s32[]{:S(2)}) async-start(), calls=%async_computation.10 | async-start | bytes 5068800 | tf_op jit(solution)/shard_map/all_gather | solution.py:47
  10.9 232.6 %all-gather.5.cloned.1.call-start = ((), (), s32[]{:S(2)}) async-start(), calls=%async_computation.11 | async-start | bytes 14598144 | tf_op jit(solution)/shard_map/all_gather | solution.py:47
  19.9 8.7 copy-start.41
  28.7 287.9 %copy-start.75 = (s32[1182]{0:T(1024)}, s32[1182]{0:T(1024)S(1)}, u32[]{:S(2)}) copy-start(s32[1182]{0:T(1024)S(1)} %fusion.100) | copy-start | bytes 14188
  43.9 108.1 %all-to-all-start.4 = ((bf16[16,96,768]{2,1,0:T(8,128)(2,1)}), bf16[16,96,768]{2,1,0:T(8,128)(2,1)}, u32[]{:S(2)}, u32[]{:S(2)}) async-start(bf16[16,96,768]{2,1,0:T(8,128)(2,1)} %bitcast.27), calls=%async_computation.4 | async-start | bytes 4718592 | tf_op jit(solution)/shard_map/all_to_all | solution.py:224
  54.9 53.8 %copy-start.61 = (f32[591]{0:T(1024)}, f32[591]{0:T(1024)S(1)}, u32[]{:S(2)}) copy-start(f32[591]{0:T(1024)S(1)} %broadcast_multiply_fusion.3) | copy-start | bytes 7096
  55.8 52.9 %copy-start.83 = (f32[591]{0:T(1024)}, f32[591]{0:T(1024)S(1)}, u32[]{:S(2)}) copy-start(f32[591]{0:T(1024)S(1)} %fusion.103) | copy-start | bytes 7096
  102.7 140.8 %copy-start.79 = (f32[768]{0:T(1024)}, f32[768]{0:T(1024)S(1)}, u32[]{:S(2)}) copy-start(f32[768]{0:T(1024)S(1)} %get-tuple-element.62) | copy-start | bytes 9220
  102.7 140.8 %copy-start.91 = (f32[768]{0:T(1024)}, f32[768]{0:T(1024)S(1)}, u32[]{:S(2)}) copy-start(f32[768]{0:T(1024)S(1)} %get-tuple-element.61) | copy-start | bytes 9220
  102.7 167.2 %copy-start.81 = (f32[768]{0:T(1024)}, f32[768]{0:T(1024)S(1)}, u32[]{:S(2)}) copy-start(f32[768]{0:T(1024)S(1)} %get-tuple-element.60) | copy-start | bytes 9220
  102.7 167.2 %copy-start.93 = (f32[768]{0:T(1024)}, f32[768]{0:T(1024)S(1)}, u32[]{:S(2)}) copy-start(f32[768]{0:T(1024)S(1)} %get-tuple-element.59) | copy-start | bytes 9220
  102.8 208.6 %copy-start.57 = (f32[768]{0:T(1024)}, f32[768]{0:T(1024)S(1)}, u32[]{:S(2)}) copy-start(f32[768]{0:T(1024)S(1)} %get-tuple-element.57) | copy-start | bytes 9220
  128.2 11.6 %copy-start.21 = (bf16[3,197,1,12,64]{1,4,3,0,2:T(8,128)(2,1)}, bf16[3,197,1,12,64]{1,4,3,0,2:T(8,128)(2,1)S(1)}, u32[]{:S(2)}) copy-start(bf16[3,197,1,12,64]{1,4,3,0,2:T(8,128)(2,1)S(1)} %copy.153) | copy-start | bytes 2723332
  150.4 93.1 %copy-start.63 = (f32[591]{0:T(1024)}, f32[591]{0:T(1024)S(1)}, u32[]{:S(2)}) copy-start(f32[591]{0:T(1024)S(1)} %broadcast_multiply_fusion.2) | copy-start | bytes 7096
  152.0 91.6 %copy-start.85 = (f32[591]{0:T(1024)}, f32[591]{0:T(1024)S(1)}, u32[]{:S(2)}) copy-start(f32[591]{0:T(1024)S(1)} %fusion.104) | copy-start | bytes 7096
  156.4 87.1 %copy-start.10 = (f32[591,768]{1,0:T(8,128)S(1)}, f32[591,768]{1,0:T(8,128)}, u32[]{:S(2)}) copy-start(f32[591,768]{1,0:T(8,128)} %copy-done.9) | copy-start | bytes 5446660
  156.4 170.7 %all-to-all-start.1 = ((bf16[4,192,3072]{2,1,0:T(8,128)(2,1)}), bf16[4,192,3072]{2,1,0:T(8,128)(2,1)}, u32[]{:S(2)}, u32[]{:S(2)}) async-start(bf16[4,192,3072]{2,1,0:T(8,128)(2,1)} %bitcast.179), calls=%async_computation.1 | async-start | bytes 9437184 | tf_op jit(solution)/shard_map/all_to_all | solution.py:172
  243.5 22.8 %copy-start.56 = (bf16[768,9216]{1,0:T(8,128)(2,1)S(1)}, bf16[768,9216]{1,0:T(8,128)(2,1)}, u32[]{:S(2)}) copy-start(bf16[768,9216]{1,0:T(8,128)(2,1)} %all-gather.5.cloned.1.call-done) | copy-start | bytes 42467332
  290.4 9.2 copy-start.24
  327.1 38.3 %all-to-all-start = ((bf16[16,96,768]{2,1,0:T(8,128)(2,1)}), bf16[16,96,768]{2,1,0:T(8,128)(2,1)}, u32[]{:S(2)}, u32[]{:S(2)}) async-start(bf16[16,96,768]{2,1,0:T(8,128)(2,1)} %bitcast.18), calls=%async_computation | async-start | bytes 4718592 | tf_op jit(solution)/shard_map/all_to_all | solution.py:201
  368.2 108.9 %all-to-all-start.2 = ((bf16[4,192,3072]{2,1,0:T(8,128)(2,1)}), bf16[4,192,3072]{2,1,0:T(8,128)(2,1)}, u32[]{:S(2)}, u32[]{:S(2)}) async-start(bf16[4,192,3072]{2,1,0:T(8,128)(2,1)} %bitcast.180), calls=%async_computation.2 | async-start | bytes 9437184 | tf_op jit(solution)/shard_map/all_to_all | solution.py:172
  498.8 14.5 %copy-start.97 = (bf16[1536,3072]{1,0:T(8,128)(2,1)}, bf16[1536,3072]{1,0:T(8,128)(2,1)S(1)}, u32[]{:S(2)}) copy-start(bf16[1536,3072]{1,0:T(8,128)(2,1)S(1)} %add_convert_fusion) | copy-start | bytes 28311556
  513.3 40.4 %all-to-all-start.5 = ((bf16[16,96,768]{2,1,0:T(8,128)(2,1)}), bf16[16,96,768]{2,1,0:T(8,128)(2,1)S(1)}, u32[]{:S(2)}, u32[]{:S(2)}) async-start(bf16[16,96,768]{2,1,0:T(8,128)(2,1)} %bitcast.185), calls=%async_computation.5 | async-start | bytes 4718592 | tf_op jit(solution)/shard_map/all_to_all | solution.py:238
  534.3 27.4 %copy-start.76 = (s32[1182]{0:T(1024)S(1)}, s32[1182]{0:T(1024)}, u32[]{:S(2)}) copy-start(s32[1182]{0:T(1024)} %copy-done.75) | copy-start | bytes 14188
  534.3 27.4 %copy-start.47 = (f32[3,12,197]{2,1,0:T(8,128)S(1)}, f32[3,12,197]{2,1,0:T(8,128)}, u32[]{:S(2)}) copy-start(f32[3,12,197]{2,1,0:T(8,128)} %copy-done.46) | copy-start | bytes 85108
  534.3 27.4 %copy-start.51 = (f32[3,12,197]{2,1,0:T(8,128)S(1)}, f32[3,12,197]{2,1,0:T(8,128)}, u32[]{:S(2)}) copy-start(f32[3,12,197]{2,1,0:T(8,128)} %copy-done.50) | copy-start | bytes 85108
  534.3 27.5 %copy-start.49 = (f32[3,12,197]{2,1,0:T(8,128)S(1)}, f32[3,12,197]{2,1,0:T(8,128)}, u32[]{:S(2)}) copy-start(f32[3,12,197]{2,1,0:T(8,128)} %copy-done.48) | copy-start | bytes 85108
  534.3 27.5 %copy-start.53 = (f32[3,12,197]{2,1,0:T(8,128)S(1)}, f32[3,12,197]{2,1,0:T(8,128)}, u32[]{:S(2)}) copy-start(f32[3,12,197]{2,1,0:T(8,128)} %copy-done.52) | copy-start | bytes 85108
  555.1 38.6 %all-to-all-start.3 = ((bf16[16,96,768]{2,1,0:T(8,128)(2,1)}), bf16[16,96,768]{2,1,0:T(8,128)(2,1)S(1)}, u32[]{:S(2)}, u32[]{:S(2)}) async-start(bf16[16,96,768]{2,1,0:T(8,128)(2,1)} %bitcast.184), calls=%async_computation.3 | async-start | bytes 4718592 | tf_op jit(solution)/shard_map/all_to_all | solution.py:209
  561.6 530.3 %reduce-scatter.7.cloned.1.call-start = ((), (), s32[]{:S(2)}) async-start(), calls=%async_computation.13 | async-start | bytes 5068800
  574.6 7.6 copy-start.55
  574.6 7.6 copy-start.58
  574.6 7.6 copy-start.60
  574.6 10.3 copy-start.74
  603.8 20.2 %copy-start.4 = (f32[591,768]{1,0:T(8,128)S(1)}, f32[591,768]{1,0:T(8,128)}, u32[]{:S(2)}) copy-start(f32[591,768]{1,0:T(8,128)} %copy-done.3) | copy-start | bytes 5446660
  603.8 20.2 %copy-start.18 = (f32[591,768]{1,0:T(8,128)S(1)}, f32[591,768]{1,0:T(8,128)}, u32[]{:S(2)}) copy-start(f32[591,768]{1,0:T(8,128)} %reduce_sum.323) | copy-start | bytes 5446660
  632.6 10.5 slice-start.2
  637.0 6.1 slice-start.3
  656.2 10.0 copy-start.15
  656.2 10.0 copy-start.66
  656.2 10.0 copy-start.82
  656.2 10.0 copy-start.88
  673.9 18.6 %copy-start.33 = (f32[591,768]{1,0:T(8,128)}, f32[591,768]{1,0:T(8,128)S(1)}, u32[]{:S(2)}) copy-start(f32[591,768]{1,0:T(8,128)S(1)} %add_add_fusion.6) | copy-start | bytes 5446660
  673.9 10.8 copy-start.11
  673.9 10.8 copy-start.64
  673.9 10.8 copy-start.80
  673.9 10.8 copy-start.86
  684.8 7.0 copy-start.100
  684.8 7.0 copy-start.70
  699.3 10.5 slice-start
  703.7 6.1 slice-start.1
  729.3 10.0 copy-start.6
  729.3 10.0 copy-start.62
  729.3 10.0 copy-start.78
  729.3 10.0 copy-start.84
  729.3 10.0 copy-start.96
  739.4 6.9 copy-start.40
  746.3 12.3 %copy-start.45 = (bf16[768,768]{1,0:T(8,128)(2,1)S(1)}, bf16[768,768]{1,0:T(8,128)(2,1)}, u32[]{:S(2)}) copy-start(bf16[768,768]{1,0:T(8,128)(2,1)} %convolution_convert_fusion.11) | copy-start | bytes 3538948
  767.9 379.6 %reduce-scatter.5.cloned.1.call-start = ((), (), s32[]{:S(2)}) async-start(), calls=%async_computation.12 | async-start | bytes 14598144 | tf_op jit(solution)/shard_map/reduce_scatter | solution.py:51
  810.7 128.0 %all-to-all-start.6 = ((bf16[4,192,3072]{2,1,0:T(8,128)(2,1)}), bf16[4,192,3072]{2,1,0:T(8,128)(2,1)}, u32[]{:S(2)}, u32[]{:S(2)}) async-start(bf16[4,192,3072]{2,1,0:T(8,128)(2,1)} %bitcast.183), calls=%async_computation.7 | async-start | bytes 9437184 | tf_op jit(solution)/shard_map/all_to_all | solution.py:246
  938.8 147.1 %all-to-all-start.7 = ((bf16[4,192,3072]{2,1,0:T(8,128)(2,1)}), bf16[4,192,3072]{2,1,0:T(8,128)(2,1)}, u32[]{:S(2)}, u32[]{:S(2)}) async-start(bf16[4,192,3072]{2,1,0:T(8,128)(2,1)} %bitcast.182), calls=%async_computation.8 | async-start | bytes 9437184 | tf_op jit(solution)/shard_map/all_to_all | solution.py:246
  (54 other events, 164.3 us)
Sparse Core Ops, SparseCore 0:
  11.5 88.5 all-gather.2
  103.6 139.8 all-gather.4
  768.0 172.6 reduce-scatter.6
  947.6 199.7 reduce-scatter.4

commit v2 on v1

v2 whole, which is shorter than its diff:
```python
import functools
import math

import jax
import jax.numpy as jnp
from jax import lax
from jax.experimental import pallas as pl
from jax.experimental.pallas import tpu as pltpu
from jax.sharding import Mesh, PartitionSpec as P

D = 768
FF = 3072
HEADS = 12
HEAD = 64
SEQ = 197
LINES = 208
TOP = 2
EXP_DEV = 2
TOK_DEV = 591
EPS = 1e-06
LOW = jnp.bfloat16
WIDE = jnp.float32
SCALE = 1.0 / math.sqrt(HEAD)
RSQRT2 = 1.0 / math.sqrt(2.0)
RSQRT2PI = 1.0 / math.sqrt(2.0 * math.pi)
SLOT_TILE = 256
ROW_TILE = 256
HINT = 4


def mm(left, right):
    return jnp.dot(left, right, preferred_element_type=WIDE)


def mm_t(left, right):
    return lax.dot_general(left, right, (((1,), (1,)), ((), ())), preferred_element_type=WIDE)


def t_mm(left, right):
    return lax.dot_general(left, right, (((0,), (0,)), ((), ())), preferred_element_type=WIDE)


def norm_parts(inputs):
    average = jnp.mean(inputs, axis=-1, keepdims=True)
    centred = inputs - average
    spread = jnp.mean(centred * centred, axis=-1, keepdims=True)
    inverse = lax.rsqrt(spread + EPS)
    return centred * inverse, inverse


def norm_low(inputs, gain_ref, shift_ref):
    xhat, _ = norm_parts(inputs)
    return (xhat * gain_ref[...] + shift_ref[...]).astype(LOW)


def norm_backward(dnormed, xhat, inverse, gain_ref, residual, dx_ref, dgain_ref, dshift_ref):
    scaled = dnormed * gain_ref[...]
    mean = jnp.mean(scaled, axis=-1, keepdims=True)
    tilt = jnp.mean(scaled * xhat, axis=-1, keepdims=True)
    dx_ref[0] = residual + inverse * (scaled - mean - xhat * tilt)

    @pl.when(pl.program_id(0) == 0)
    def _():
        dgain_ref[...] = jnp.zeros_like(dgain_ref)
        dshift_ref[...] = jnp.zeros_like(dshift_ref)

    dgain_ref[...] += jnp.sum(dnormed * xhat, axis=0, keepdims=True)
    dshift_ref[...] += jnp.sum(dnormed, axis=0, keepdims=True)


def gelu_both(inner):
    phi = 0.5 + 0.5 * lax.erf(inner * RSQRT2)
    slope = phi + inner * (RSQRT2PI * jnp.exp(-0.5 * inner * inner))
    return (inner * phi).astype(LOW), slope.astype(LOW)


def softmax_rows(query, key):
    scores = mm_t(query, key) * SCALE
    lane = lax.broadcasted_iota(jnp.int32, scores.shape, 1)
    scores = jnp.where(lane < SEQ, scores, -jnp.inf)
    peak = jnp.max(scores, axis=-1, keepdims=True)
    raised = jnp.exp(scores - peak)
    total = jnp.sum(raised, axis=-1, keepdims=True)
    return raised * (1.0 / total)


def whole(shape):
    return pl.BlockSpec(shape, lambda *_: (0,) * len(shape))


def window(width, at):
    return pl.BlockSpec((D, width), lambda *_: (0, at))


def image(width):
    return pl.BlockSpec((1, LINES, width), lambda i: (i, 0, 0))


def params(megabytes):
    return pltpu.CompilerParams(vmem_limit_bytes=megabytes << 20)


def like(shape, kind):
    return jax.ShapeDtypeStruct(shape, kind)


def cost(flops, moved, raised=0):
    return pl.CostEstimate(
        flops=flops // HINT, bytes_accessed=moved // HINT, transcendentals=raised // HINT
    )


def attend_forward_body(x_ref, gain_ref, shift_ref, qkv_ref, proj_ref, out_ref, packed_ref, mixed_ref):
    x = x_ref[0]
    packed_ref[0] = mm(norm_low(x, gain_ref, shift_ref), qkv_ref[...]).astype(LOW)
    first = lax.broadcasted_iota(jnp.int32, (LINES, 2 * HEAD), 1) < HEAD
    zero = jnp.zeros((LINES, 2 * HEAD), LOW)
    for pair in range(HEADS // 2):
        at = pair * 2 * HEAD
        query = packed_ref[0, :, at : at + 2 * HEAD]
        key = packed_ref[0, :, D + at : D + at + 2 * HEAD]
        value = packed_ref[0, :, 2 * D + at : 2 * D + at + 2 * HEAD]
        low = mm(softmax_rows(jnp.where(first, query, zero), key).astype(LOW), value)
        high = mm(softmax_rows(jnp.where(first, zero, query), key).astype(LOW), value)
        mixed_ref[0, :, at : at + 2 * HEAD] = jnp.where(first, low, high).astype(LOW)
    out_ref[0] = x + mm_t(mixed_ref[0], proj_ref[...])


def attend_forward(x, gain, shift, block):
    images = x.shape[0]
    return pl.pallas_call(
        attend_forward_body,
        grid=(images,),
        in_specs=[image(D), whole((1, D)), whole((1, D)), window(3 * D, 0), window(D, 3)],
        out_specs=[image(D), image(3 * D), image(D)],
        out_shape=[
            like((images, LINES, D), WIDE),
            like((images, LINES, 3 * D), LOW),
            like((images, LINES, D), LOW),
        ],
        compiler_params=params(48),
        cost_estimate=cost(3_700_000_000, 13_000_000, 1_600_000),
        name="attend_forward",
    )(x, gain, shift, block, block)


def attend_backward_body(
    x_ref, dy_ref, packed_ref, gain_ref, shift_ref, qkv_ref, proj_ref,
    dx_ref, dpacked_ref, normed_ref, low_ref, dgain_ref, dshift_ref,
    dmixed_ref,
):
    dy = dy_ref[0]
    grad_low = dy.astype(LOW)
    low_ref[0] = grad_low
    dmixed_ref[...] = mm(grad_low, proj_ref[...]).astype(LOW)
    first = lax.broadcasted_iota(jnp.int32, (LINES, 2 * HEAD), 1) < HEAD
    zero = jnp.zeros((LINES, 2 * HEAD), LOW)

    def one(query, key, value, upstream):
        probs = softmax_rows(query, key)
        dprobs = mm_t(upstream, value)
        inner = jnp.sum(probs * dprobs, axis=-1, keepdims=True)
        dscores = (probs * (dprobs - inner)).astype(LOW)
        return t_mm(probs.astype(LOW), upstream), mm(dscores, key), t_mm(dscores, query)

    for pair in range(HEADS // 2):
        at = pair * 2 * HEAD
        query = packed_ref[0, :, at : at + 2 * HEAD]
        key = packed_ref[0, :, D + at : D + at + 2 * HEAD]
        value = packed_ref[0, :, 2 * D + at : 2 * D + at + 2 * HEAD]
        upstream = dmixed_ref[:, at : at + 2 * HEAD]
        dv0, dq0, dk0 = one(
            jnp.where(first, query, zero), key, value, jnp.where(first, upstream, zero)
        )
        dv1, dq1, dk1 = one(
            jnp.where(first, zero, query), key, value, jnp.where(first, zero, upstream)
        )
        dpacked_ref[0, :, at : at + 2 * HEAD] = (jnp.where(first, dq0, dq1) * SCALE).astype(LOW)
        dpacked_ref[0, :, D + at : D + at + 2 * HEAD] = ((dk0 + dk1) * SCALE).astype(LOW)
        dpacked_ref[0, :, 2 * D + at : 2 * D + at + 2 * HEAD] = (dv0 + dv1).astype(LOW)
    xhat, inverse = norm_parts(x_ref[0])
    normed_ref[0] = (xhat * gain_ref[...] + shift_ref[...]).astype(LOW)
    dnormed = mm_t(dpacked_ref[0], qkv_ref[...])
    norm_backward(dnormed, xhat, inverse, gain_ref, dy, dx_ref, dgain_ref, dshift_ref)


def attend_backward(x, dy, packed, gain, shift, block):
    images = x.shape[0]
    return pl.pallas_call(
        attend_backward_body,
        grid=(images,),
        in_specs=[
            image(D), image(D), image(3 * D), whole((1, D)), whole((1, D)),
            window(3 * D, 0), window(D, 3),
        ],
        out_specs=[image(D), image(3 * D), image(D), image(D), whole((1, D)), whole((1, D))],
        out_shape=[
            like((images, LINES, D), WIDE),
            like((images, LINES, 3 * D), LOW),
            like((images, LINES, D), LOW),
            like((images, LINES, D), LOW),
            like((1, D), WIDE),
            like((1, D), WIDE),
        ],
        scratch_shapes=[pltpu.VMEM((LINES, D), LOW)],
        compiler_params=params(48),
        cost_estimate=cost(4_000_000_000, 22_000_000, 1_600_000),
        name="attend_backward",
    )(x, dy, packed, gain, shift, block, block)


def mlp_forward_body(x_ref, gain_ref, shift_ref, up_ref, down_ref, out_ref, hidden_ref, slope_ref):
    x = x_ref[0]
    normed = norm_low(x, gain_ref, shift_ref)
    total = x
    step = FF // 4
    for at in range(0, FF, step):
        hidden, slope = gelu_both(mm(normed, up_ref[:, at : at + step]))
        hidden_ref[0, :, at : at + step] = hidden
        slope_ref[0, :, at : at + step] = slope
        total = total + mm_t(hidden, down_ref[:, at : at + step])
    out_ref[0] = total


def mlp_forward(x, gain, shift, block):
    images = x.shape[0]
    return pl.pallas_call(
        mlp_forward_body,
        grid=(images,),
        in_specs=[image(D), whole((1, D)), whole((1, D)), window(FF, 0), window(FF, 1)],
        out_specs=[image(D), image(FF), image(FF)],
        out_shape=[
            like((images, LINES, D), WIDE),
            like((images, LINES, FF), LOW),
            like((images, LINES, FF), LOW),
        ],
        compiler_params=params(56),
        cost_estimate=cost(5_900_000_000, 21_000_000, 4_000_000),
        name="mlp_forward",
    )(x, gain, shift, block, block)


def mlp_backward_body(
    x_ref, dy_ref, slope_ref, gain_ref, shift_ref, up_ref, down_ref,
    dx_ref, dinner_ref, normed_ref, low_ref, dgain_ref, dshift_ref,
):
    dy = dy_ref[0]
    grad_low = dy.astype(LOW)
    low_ref[0] = grad_low
    step = FF // 4
    dnormed = jnp.zeros((LINES, D), WIDE)
    for at in range(0, FF, step):
        dhidden = mm(grad_low, down_ref[:, at : at + step])
        dinner = (dhidden * slope_ref[0, :, at : at + step].astype(WIDE)).astype(LOW)
        dinner_ref[0, :, at : at + step] = dinner
        dnormed = dnormed + mm_t(dinner, up_ref[:, at : at + step])
    xhat, inverse = norm_parts(x_ref[0])
    normed_ref[0] = (xhat * gain_ref[...] + shift_ref[...]).astype(LOW)
    norm_backward(dnormed, xhat, inverse, gain_ref, dy, dx_ref, dgain_ref, dshift_ref)


def mlp_backward(x, dy, slope, gain, shift, block):
    images = x.shape[0]
    return pl.pallas_call(
        mlp_backward_body,
        grid=(images,),
        in_specs=[
            image(D), image(D), image(FF), whole((1, D)), whole((1, D)),
            window(FF, 0), window(FF, 1),
        ],
        out_specs=[image(D), image(FF), image(D), image(D), whole((1, D)), whole((1, D))],
        out_shape=[
            like((images, LINES, D), WIDE),
            like((images, LINES, FF), LOW),
            like((images, LINES, D), LOW),
            like((images, LINES, D), LOW),
            like((1, D), WIDE),
            like((1, D), WIDE),
        ],
        compiler_params=params(56),
        cost_estimate=cost(5_900_000_000, 25_000_000),
        name="mlp_backward",
    )(x, dy, slope, gain, shift, block, block)


def chosen(places_ref, tile):
    tokens = places_ref.shape[1]
    slot = pl.program_id(0) * tile + lax.broadcasted_iota(jnp.int32, (tile, tokens), 0)
    return [jnp.where(slot == places_ref[k : k + 1, :], 1.0, 0.0) for k in range(TOP)]


def dispatch_body(places_ref, x_ref, gain_ref, shift_ref, out_ref, sent_ref):
    @pl.when(pl.program_id(0) == 0)
    def _():
        sent_ref[...] = norm_low(x_ref[...], gain_ref, shift_ref)

    picks = chosen(places_ref, SLOT_TILE)
    out_ref[...] = mm((picks[0] + picks[1]).astype(LOW), sent_ref[...]).astype(LOW)


def dispatch(places, x, gain, shift, slots):
    tokens = x.shape[0]
    return pl.pallas_call(
        dispatch_body,
        grid=(slots // SLOT_TILE,),
        in_specs=[whole((TOP, tokens)), whole((tokens, D)), whole((1, D)), whole((1, D))],
        out_specs=pl.BlockSpec((SLOT_TILE, D), lambda i: (i, 0)),
        out_shape=like((slots, D), LOW),
        scratch_shapes=[pltpu.VMEM((tokens, D), LOW)],
        compiler_params=params(32),
        cost_estimate=cost(1_500_000_000, 4_500_000),
        name="dispatch",
    )(places, x, gain, shift)


def dispatch_grad_body(places_ref, gate_ref, cot_ref, out_ref, sent_ref):
    @pl.when(pl.program_id(0) == 0)
    def _():
        for k in range(TOP):
            sent_ref[k] = (gate_ref[:, k : k + 1] * cot_ref[...]).astype(LOW)

    picks = chosen(places_ref, SLOT_TILE)
    total = mm(picks[0].astype(LOW), sent_ref[0]) + mm(picks[1].astype(LOW), sent_ref[1])
    out_ref[...] = total.astype(LOW)


def dispatch_grad(places, gate, cot, slots):
    tokens = cot.shape[0]
    return pl.pallas_call(
        dispatch_grad_body,
        grid=(slots // SLOT_TILE,),
        in_specs=[whole((TOP, tokens)), whole((tokens, TOP)), whole((tokens, D))],
        out_specs=pl.BlockSpec((SLOT_TILE, D), lambda i: (i, 0)),
        out_shape=like((slots, D), LOW),
        scratch_shapes=[pltpu.VMEM((TOP, tokens, D), LOW)],
        compiler_params=params(32),
        cost_estimate=cost(3_000_000_000, 4_500_000),
        name="dispatch_grad",
    )(places, gate, cot)


def picker(places_ref, k, slots):
    lane = lax.broadcasted_iota(jnp.int32, (LINES, slots), 1)
    return jnp.where(lane == places_ref[0, :, k : k + 1], 1.0, 0.0)


def combine_body(places_ref, gate_ref, x_ref, cot_ref, home_ref, out_ref, dgate_ref):
    slots = home_ref.shape[0]
    total = x_ref[0]
    for k in range(TOP):
        picked = mm(picker(places_ref, k, slots).astype(LOW), home_ref[...])
        total = total + gate_ref[0, :, k : k + 1] * picked
        dgate_ref[0, :, k : k + 1] = jnp.sum(cot_ref[0] * picked, axis=-1, keepdims=True)
    out_ref[0] = total


def combine(places, gate, x, cot, home):
    images, slots = x.shape[0], home.shape[0]
    return pl.pallas_call(
        combine_body,
        grid=(images,),
        in_specs=[image(TOP), image(TOP), image(D), image(D), whole((slots, D))],
        out_specs=[image(D), image(TOP)],
        out_shape=[like((images, LINES, D), WIDE), like((images, LINES, TOP), WIDE)],
        compiler_params=params(32),
        cost_estimate=cost(3_000_000_000, 8_000_000),
        name="combine",
    )(places, gate, x, cot, home)


def return_grad_body(places_ref, x_ref, cot_ref, gain_ref, home_ref, dx_ref, dgain_ref, dshift_ref):
    slots = home_ref.shape[0]
    picks = (picker(places_ref, 0, slots) + picker(places_ref, 1, slots)).astype(LOW)
    dsent = mm(picks, home_ref[...])
    xhat, inverse = norm_parts(x_ref[0])
    norm_backward(dsent, xhat, inverse, gain_ref, cot_ref[0], dx_ref, dgain_ref, dshift_ref)


def return_grad(places, x, cot, gain, home):
    images, slots = x.shape[0], home.shape[0]
    return pl.pallas_call(
        return_grad_body,
        grid=(images,),
        in_specs=[image(TOP), image(D), image(D), whole((1, D)), whole((slots, D))],
        out_specs=[image(D), whole((1, D)), whole((1, D))],
        out_shape=[like((images, LINES, D), WIDE), like((1, D), WIDE), like((1, D), WIDE)],
        compiler_params=params(32),
        cost_estimate=cost(1_500_000_000, 8_000_000),
        name="return_grad",
    )(places, x, cot, gain, home)


def expert_forward_body(rows_ref, in_ref, hidden_ref, slope_ref):
    step = FF // 4
    for at in range(0, FF, step):
        hidden, slope = gelu_both(mm(rows_ref[...], in_ref[:, at : at + step]))
        hidden_ref[:, at : at + step] = hidden
        slope_ref[:, at : at + step] = slope


def tiled(width):
    return pl.BlockSpec((ROW_TILE, width), lambda i: (i, 0))


def expert_forward(rows, weight):
    count = rows.shape[0]
    return pl.pallas_call(
        expert_forward_body,
        grid=(count // ROW_TILE,),
        in_specs=[tiled(D), whole((D, FF))],
        out_specs=[tiled(FF), tiled(FF)],
        out_shape=[like((count, FF), LOW), like((count, FF), LOW)],
        compiler_params=params(48),
        cost_estimate=cost(7_200_000_000, 26_000_000, 9_000_000),
        name="expert_forward",
    )(rows, weight)


def expert_backward_body(grad_ref, slope_ref, in_ref, out_ref, dinner_ref, dx_ref):
    step = FF // 4
    total = jnp.zeros((ROW_TILE, D), WIDE)
    for at in range(0, FF, step):
        dhidden = mm(grad_ref[...], out_ref[:, at : at + step])
        dinner = (dhidden * slope_ref[:, at : at + step].astype(WIDE)).astype(LOW)
        dinner_ref[:, at : at + step] = dinner
        total = total + mm_t(dinner, in_ref[:, at : at + step])
    dx_ref[...] = total.astype(LOW)


def expert_backward(grad, slope, weight_in, weight_out_t):
    count = grad.shape[0]
    return pl.pallas_call(
        expert_backward_body,
        grid=(count // ROW_TILE,),
        in_specs=[tiled(D), tiled(FF), whole((D, FF)), whole((D, FF))],
        out_specs=[tiled(FF), tiled(D)],
        out_shape=[like((count, FF), LOW), like((count, D), LOW)],
        compiler_params=params(48),
        cost_estimate=cost(14_400_000_000, 33_000_000),
        name="expert_backward",
    )(grad, slope, weight_in, weight_out_t)


def join_body(at_ref, *refs):
    *parts, out_ref, sem = refs
    for index, part in enumerate(parts):
        rows, width = part.shape[1:]
        for block in range(part.shape[0]):
            down = pl.multiple_of(at_ref[index, 2 * block] * 16, 16)
            right = pl.multiple_of(at_ref[index, 2 * block + 1] * 128, 128)
            target = out_ref.at[pl.ds(down, rows), pl.ds(right, width)]
            pltpu.make_async_copy(part.at[block], target, sem).start()
    pltpu.make_async_copy(out_ref, out_ref, sem).wait()


def join(places, parts, width):
    return pl.pallas_call(
        join_body,
        in_specs=[pl.BlockSpec(memory_space=pltpu.SMEM)]
        + [pl.BlockSpec(memory_space=pl.ANY)] * len(parts),
        out_specs=pl.BlockSpec(memory_space=pltpu.VMEM),
        out_shape=like((D, width), LOW),
        scratch_shapes=[pltpu.SemaphoreType.DMA],
        compiler_params=params(32),
        cost_estimate=cost(0, 4 * D * width),
        name="join",
    )(places, *parts)


def flipped(index, first, second, axis):
    return jnp.where(
        index == 0,
        jnp.concatenate([first, second], axis=axis),
        jnp.concatenate([second, first], axis=axis),
    )


class Plan:
    def __init__(self, mesh):
        n_dp, n_expert = mesh.devices.shape
        self.n_dp, self.groups = n_dp, n_expert
        self.wide = (n_dp, n_expert) == (4, 8)
        expert_shape, expert = ((2, 2, 2), ("y", "x", "c")) if self.wide else ((n_expert,), ("expert",))
        self.dp = ("dh", "dl")
        self.expert = expert
        self.axes = self.dp + expert
        self.mesh = Mesh(mesh.devices.reshape((n_dp // 2, 2) + expert_shape), self.axes)

    def hop(self, value, axes, bit):
        size = lax.axis_size(axes)
        return lax.ppermute(value, axes, [(i, i ^ bit) for i in range(size)])

    def gather_depth(self, part, *gates):
        part = after(part, *gates)
        if not self.wide:
            return part
        half, quarter = self.cut(part)
        core = lax.axis_index("c")
        mine = lax.dynamic_slice_in_dim(part, core * half, half, 1)
        other = lax.dynamic_slice_in_dim(part, (1 - core) * half, half, 1)
        mine = flipped(core, mine, self.hop(other, "c", 1), 0)
        deep = self.deepen(mine)
        return lax.optimization_barrier((deep[:, :, :quarter], deep[:, :, quarter:]))

    def deepen(self, mine):
        pair = jnp.stack([mine, self.hop(mine, "dl", 1)])
        return jnp.concatenate([pair] + [self.hop(pair, "dh", k) for k in range(1, self.n_dp // 2)])

    def cut(self, part):
        return part.shape[1] // 2, part.shape[1] // 512 * 128

    def gather_side(self, pair, step, *gates):
        if not self.wide:
            return pair
        left, right, *_ = lax.optimization_barrier(tuple(pair) + gates)
        axes = ("x", "y") if step == 0 else ("y", "x")
        came = lax.optimization_barrier((self.hop(left, axes[0], 1), self.hop(right, axes[1], 1)))
        return tuple(jnp.concatenate([own, new]) for own, new in zip((left, right), came))

    def gather_core(self, pair, part):
        if not self.wide:
            return lax.all_gather(pair, self.axes, axis=0, tiled=True)
        left, right = pair
        rows, width = part.shape
        half, quarter = self.cut(part)
        core = lax.axis_index("c")
        far = lax.optimization_barrier((self.hop(left, "c", 1), self.hop(right, "c", 1)))
        steps = jnp.arange(16, dtype=jnp.int32)
        me = lax.axis_index(self.dp) * 4 + lax.axis_index("y") * 2 + lax.axis_index("x")
        first, second, turn = steps // 8, steps // 4 % 2, steps % 4
        left_at = (turn * 4 + first * 2 + second) ^ me
        right_at = (turn * 4 + second * 2 + first) ^ me

        def spots(at, side, side_core):
            across = jnp.broadcast_to((side_core * half + side * quarter) // 128, at.shape)
            return jnp.stack([at * (2 * rows // 16), across], axis=1).reshape(-1)

        places = jnp.stack(
            [
                spots(left_at, 0, core),
                spots(right_at, 1, core),
                spots(left_at, 0, 1 - core),
                spots(right_at, 1, 1 - core),
            ]
        ).astype(jnp.int32)
        return join(places, (left, right) + tuple(far), width)

    def scatter(self, full):
        if not self.wide:
            return lax.psum_scatter(full, self.axes, scatter_dimension=0, tiled=True).astype(WIDE)
        height, width = full.shape
        half, quarter = width // 2, width // 512 * 128
        core, y, x = lax.axis_index("c"), lax.axis_index("y"), lax.axis_index("x")
        across = self.hop(lax.dynamic_slice_in_dim(full, (1 - core) * half, half, 1), "c", 1)
        mine = self.plus(lax.dynamic_slice_in_dim(full, core * half, half, 1), across)
        mine = mine.reshape(self.n_dp, 2, 2, height // 16, half)

        def pick(value, at, axis):
            return lax.dynamic_index_in_dim(value, at, axis, keepdims=False)

        left, right = mine[..., :quarter], mine[..., quarter:]
        sent = lax.optimization_barrier((pick(left, 1 - y, 1), pick(right, 1 - x, 2)))
        came = lax.optimization_barrier((self.hop(sent[0], "y", 1), self.hop(sent[1], "x", 1)))
        left, right = self.plus(pick(left, y, 1), came[0]), self.plus(pick(right, x, 2), came[1])
        sent = lax.optimization_barrier((pick(left, 1 - x, 1), pick(right, 1 - y, 1)))
        came = lax.optimization_barrier((self.hop(sent[0], "x", 1), self.hop(sent[1], "y", 1)))
        left, right = self.plus(pick(left, x, 1), came[0]), self.plus(pick(right, y, 1), came[1])
        deep = jnp.concatenate([left, right], axis=2)
        deep = deep.reshape(2, 2, height // 16, half)
        high, low = lax.axis_index("dh"), lax.axis_index("dl")
        deep = self.plus(pick(deep, high, 0), self.hop(pick(deep, 1 - high, 0), "dh", 1))
        total = pick(deep, low, 0).astype(WIDE) + self.hop(pick(deep, 1 - low, 0), "dl", 1).astype(WIDE)
        rows = height // 32
        away = self.hop(lax.dynamic_slice_in_dim(total, (1 - core) * rows, rows, 0), "c", 1)
        return flipped(core, lax.dynamic_slice_in_dim(total, core * rows, rows, 0), away, 1)

    def plus(self, one, two):
        return (one.astype(WIDE) + two.astype(WIDE)).astype(LOW)

    def fetch_near(self, part):
        parity = lax.axis_index("dl")
        same, other = part[0], part[1]
        same, other = jnp.where(parity == 0, same, other), jnp.where(parity == 0, other, same)
        return jnp.stack([same, self.hop(other, "dl", 1)])

    def fetch_far(self, pair):
        return [self.hop(pair, "dh", k) for k in range(1, self.n_dp // 2)]

    def join_expert(self, pairs):
        turn = lax.axis_index(self.dp)
        rows, width = pairs[0].shape[1:]
        spots = []
        for k in range(self.n_dp // 2):
            near, far = turn ^ (2 * k), turn ^ (2 * k + 1)
            spots.append(jnp.stack([near * (rows // 16), 0 * turn, far * (rows // 16), 0 * turn]))
        return join(jnp.stack(spots).astype(jnp.int32), pairs, width)

    def share_far(self, partial, *gates):
        half = self.n_dp // 2
        pieces = after(partial, *gates).reshape(half, 2, D // self.n_dp, FF)
        high = lax.axis_index("dh")
        total = lax.dynamic_index_in_dim(pieces, high, 0, keepdims=False).astype(WIDE)
        for k in range(1, half):
            piece = lax.dynamic_index_in_dim(pieces, high ^ k, 0, keepdims=False)
            total = total + self.hop(piece, "dh", k).astype(WIDE)
        return total.astype(LOW)

    def share_near(self, pair):
        parity = lax.axis_index("dl")
        own = lax.dynamic_index_in_dim(pair, parity, 0).astype(WIDE)
        other = self.hop(lax.dynamic_index_in_dim(pair, 1 - parity, 0), "dl", 1).astype(WIDE)
        return flipped(parity, own, other, 0)

    def to_experts(self, rows):
        chunks = rows.reshape(2 * self.groups, -1, D)
        return lax.all_to_all(chunks, ("dl",) + self.expert, 0, 0, tiled=True).reshape(-1, D)


def after(value, *others):
    return lax.optimization_barrier((value,) + others)[0]


def padded(rows, fill=0):
    shaped = rows.reshape(rows.shape[0] // SEQ, SEQ, rows.shape[1])
    return jnp.pad(shaped, ((0, 0), (0, LINES - SEQ), (0, 0)), constant_values=fill)


def unpadded(lines):
    return lines[:, :SEQ].reshape(-1, lines.shape[2])


def flat(lines):
    return lines.reshape(-1, lines.shape[2])


def local(plan, act_in, w_qkv, w_proj, w_up, w_down, norm_gain, norm_shift, exp_in, exp_out, gate, expert_index, cotangent):
    experts_all = EXP_DEV * plan.groups
    capacity = (TOP * TOK_DEV * 5 // (4 * experts_all) + 7) // 8 * 8
    slots = experts_all * capacity
    proj_t = jnp.swapaxes(w_proj, 1, 2).astype(LOW)
    qkv_low = w_qkv.astype(LOW)
    norms = jnp.concatenate([norm_gain, norm_shift]).T.astype(LOW)
    norms = jnp.pad(norms, ((0, 0), (0, 256 - norms.shape[1])))
    part_a = jnp.concatenate([qkv_low[0], proj_t[0], norms], axis=1)
    part_b = jnp.concatenate([w_up.astype(LOW), w_down.T.astype(LOW)], axis=1)
    part_c = jnp.concatenate([qkv_low[1], proj_t[1]], axis=1)
    deep_a = plan.gather_depth(part_a)
    in_near = plan.fetch_near(after(exp_in.astype(LOW), deep_a))
    out_near = plan.fetch_near(after(jnp.swapaxes(exp_out, 1, 2).astype(LOW), in_near))
    in_far = plan.fetch_far(in_near)
    out_far = plan.fetch_far(after(out_near, in_far))
    deep_b = plan.gather_depth(part_b, deep_a)
    deep_c = plan.gather_depth(part_c, deep_b)
    one_a = plan.gather_side(deep_a, 0)
    two_a = plan.gather_side(one_a, 1)
    block_a = plan.gather_core(two_a, part_a)
    norms = block_a[:, 4 * D : 4 * D + 8].astype(WIDE).T
    gain, shift = norms[:4, None], norms[4:, None]
    one_b = plan.gather_side(deep_b, 0, two_a)

    flat_index = expert_index.reshape(-1)
    onehot = (flat_index[:, None] == jnp.arange(experts_all, dtype=jnp.int32)).astype(jnp.int32)
    before = jnp.cumsum(onehot, axis=0) - onehot
    holder = (flat_index % EXP_DEV) * plan.groups + flat_index // EXP_DEV
    spots = (holder * capacity + jnp.sum(onehot * before, axis=1)).reshape(-1, TOP)
    spots = padded(spots, -1)
    spot_rows = flat(spots).T
    gates, cot, x_a = padded(gate), padded(cotangent), padded(act_in)

    grad_rows = plan.to_experts(dispatch_grad(spot_rows, flat(gates), flat(cot), slots))

    x_b, packed_a, mixed_a = attend_forward(after(x_a, in_near), gain[0], shift[0], block_a)
    two_b = plan.gather_side(one_b, 1, x_b)
    block_b = plan.gather_core(two_b, part_b)
    one_c = plan.gather_side(deep_c, 0, two_b)
    x_c, hidden_b, slope_b = mlp_forward(after(x_b, out_near), gain[1], shift[1], block_b)
    two_c = plan.gather_side(one_c, 1)
    block_c = plan.gather_core(two_c, part_c)
    x_d, packed_c, mixed_c = attend_forward(x_c, gain[2], shift[2], block_c)
    sent = dispatch(spot_rows, flat(after(x_d, in_far, grad_rows)), gain[3], shift[3], slots)
    rows = plan.to_experts(sent)

    weight_in = plan.join_expert([in_near] + in_far)
    hidden, slope = expert_forward(rows, weight_in)
    down_partial = t_mm(grad_rows, hidden).astype(LOW)
    weight_out = plan.join_expert([out_near] + after(out_far, hidden, down_partial))
    dinner, droutes = expert_backward(grad_rows, slope, weight_in, weight_out)
    routes_home = plan.to_experts(droutes)
    result = mm_t(hidden, weight_out).astype(LOW)
    home = plan.to_experts(result)
    down_pair = plan.share_far(down_partial, weight_out)
    in_partial = t_mm(rows, dinner).astype(LOW)
    in_pair = plan.share_far(in_partial)

    act_out, grad_gate = combine(spots, gates, x_d, cot, home)
    dx_d, gain_d, shift_d = return_grad(spots, x_d, cot, gain[3], routes_home)
    dx_c, dpacked_c, normed_c, low_c, gain_c, shift_c = attend_backward(
        x_c, dx_d, packed_c, gain[2], shift[2], block_c
    )
    sum_c = jnp.concatenate(
        [t_mm(flat(normed_c), flat(dpacked_c)), t_mm(flat(low_c), flat(mixed_c))], axis=1
    )
    mine_c = plan.scatter(sum_c.astype(LOW))
    dx_b, dinner_b, normed_b, low_b, gain_b, shift_b = mlp_backward(
        x_b, dx_c, slope_b, gain[1], shift[1], block_b
    )
    sum_b = jnp.concatenate(
        [t_mm(flat(normed_b), flat(dinner_b)), t_mm(flat(low_b), flat(hidden_b))], axis=1
    )
    mine_b = plan.scatter(sum_b.astype(LOW))
    dx_a, dpacked_a, normed_a, low_a, gain_a, shift_a = attend_backward(
        x_a, after(dx_b, mine_c), packed_a, gain[0], shift[0], block_a
    )
    norm_grads = jnp.concatenate(
        [gain_a, gain_b, gain_c, gain_d, shift_a, shift_b, shift_c, shift_d]
    )
    norm_grads = jnp.pad(norm_grads.T, ((0, 0), (0, 248)))
    sum_a = jnp.concatenate(
        [t_mm(flat(normed_a), flat(dpacked_a)), t_mm(flat(low_a), flat(mixed_a)), norm_grads], axis=1
    )
    mine_a = plan.scatter(after(sum_a.astype(LOW), down_pair))
    grad_exp_out = jnp.swapaxes(plan.share_near(down_pair), 1, 2)
    grad_exp_in = plan.share_near(in_pair)

    grad_qkv = jnp.stack([mine_a[:, : 3 * D], mine_c[:, : 3 * D]])
    grad_proj = jnp.stack([mine_a[:, 3 * D : 4 * D], mine_c[:, 3 * D :]])
    return (
        unpadded(act_out),
        unpadded(dx_a),
        grad_qkv,
        jnp.swapaxes(grad_proj, 1, 2),
        mine_b[:, :FF],
        mine_b[:, FF:].T,
        mine_a[:, 4 * D : 4 * D + 4].T,
        mine_a[:, 4 * D + 4 : 4 * D + 8].T,
        grad_exp_in,
        grad_exp_out,
        unpadded(grad_gate),
    )


def solution(mesh):
    plan = Plan(mesh)
    rows, dp, expert = plan.axes, plan.dp, plan.expert
    in_specs = (
        P(rows, None),
        P(None, rows, None),
        P(None, None, rows),
        P(rows, None),
        P(None, rows),
        P(None, rows),
        P(None, rows),
        P(expert, dp, None),
        P(expert, None, dp),
        P(rows, None),
        P(rows, None),
        P(rows, None),
    )
    out_specs = (
        P(rows, None),
        P(rows, None),
        P(None, rows, None),
        P(None, None, rows),
        P(rows, None),
        P(None, rows),
        P(None, rows),
        P(None, rows),
        P(expert, dp, None),
        P(expert, None, dp),
        P(rows, None),
    )
    return jax.shard_map(
        functools.partial(local, plan),
        mesh=plan.mesh,
        in_specs=in_specs,
        out_specs=out_specs,
        check_vma=False,
    )
```

time: 1170 us -> 868 us (0.74)
  matrix products: 253 us -> 60 us
  waiting for transfers between devices: 533 us -> 347 us
  Pallas kernels: 0 us -> 179 us
  local copies, waits for them, and re-layouts: 195 us -> 94.7 us
  starting transfers between devices: 49.4 us -> 98.4 us
  other arithmetic: 113 us -> 76.4 us
  between operations: 15.8 us -> 2.74 us
    all_to_all x8 -> x4, waiting for transfers between devices: 354 us -> 80.7 us  [to_experts(): lax.all_to_all(chunks, ('dl',) + self.expert, 0, 0, tiled=True)]
    ppermute x0 -> x59, waiting for transfers between devices: none -> 267 us  [hop(): return lax.ppermute(value, axes, [(i, i ^ bit) for i in range(size)])]
    dot_general x36 -> x9, matrix products: 253 us -> 60 us  [the longest x8 48.9 us: t_mm(): lax.dot_general(left, right, (((0,), (0,)), ((), ())), preferred_element_...]
    pallas_call x0 -> x17, Pallas kernels: none -> 179 us  [the longest x2 47.9 us: attend_backward(): pl.pallas_call(attend_backward_body, grid=(images,), in_specs=[image(D),...]
    all_gather x2 -> x0, waiting for transfers between devices: 125 us -> none  [gather_rows(): return lax.all_gather(part, ALL_AXES, axis=0, tiled=True)]
    ppermute x0 -> x59, starting transfers between devices: none -> 70.8 us  [hop(): return lax.ppermute(value, axes, [(i, i ^ bit) for i in range(size)])]
    reduce_scatter x1 -> x0, waiting for transfers between devices: 53.2 us -> none  [scatter_rows(): lax.psum_scatter(full.astype(jnp.bfloat16), ALL_AXES, scatter_dimension=0...]
    reduce_sum x18 -> x1, other arithmetic: 53.1 us -> 0.03 us  [local(): jnp.sum(onehot * before, axis=1)]
  transfers between devices with their start and end apart: 12 -> 63, of which waited for: 9 -> 35; matrix products, arithmetic and copies ran while one was open for 29% -> 22% of each run, Pallas kernels for 0% -> 17%
where the time goes in v2:
time: 868 us; the launch traced here: 858 us
  waiting for transfers between devices  347 us (40%)
  Pallas kernels  179 us (21%)
  starting transfers between devices  98.4 us (11%)
  local copies, waits for them, and re-layouts  94.7 us (11%)
  other arithmetic  76.4 us (9%)
  matrix products  60 us (7%)
    ppermute x59, waiting for transfers between devices, hop(): return lax.ppermute(value, axes, [(i, i ^ bit) for i in range(size)])  267 us
    all_to_all x4, waiting for transfers between devices, to_experts(): lax.all_to_all(chunks, ('dl',) + self.expert, 0, 0, tiled=True)  80.7 us
    ppermute x59, starting transfers between devices, hop(): return lax.ppermute(value, axes, [(i, i ^ bit) for i in range(size)])  70.8 us
    dot_general x8, matrix products, t_mm(): lax.dot_general(left, right, (((0,), (0,)), ((), ())), preferred_element_...  48.9 us
    pallas_call x2, Pallas kernels, attend_backward(): pl.pallas_call(attend_backward_body, grid=(images,), in_specs=[image(D),...  47.9 us
    unnamed x151, local copies, waits for them, and re-layouts  42.9 us
    all_to_all x4, starting transfers between devices, to_experts(): lax.all_to_all(chunks, ('dl',) + self.expert, 0, 0, tiled=True)  27.6 us
    pallas_call x2, Pallas kernels, attend_forward(): pl.pallas_call(attend_forward_body, grid=(images,), in_specs=[image(D), w...  24.7 us
  transfers between devices with their start and end apart: 63, of which 35 were waited for; matrix products, arithmetic and copies ran while one was open for 22% of the time, Pallas kernels for 17%

profile of v2, /device:TPU:1, one launch (start us, length us, event | category | flops | bytes accessed | tf_op | source)
XLA Modules:
  0.0 858.0 jit_solution(13962953559757429098)
XLA Ops:
  5.6 4.5 reduce-window.6
  14.7 4.4 collective-permute-done.1
  21.5 13.9 %collective-permute-done.2 = bf16[2,48,1664]{2,1,0:T(8,128)(2,1)S(1)} collective-permute-done((bf16[2,48,1664]{2,1,0:T(8,128)(2,1)S(1)}, bf16[2,48,1664]{2,1,0:T(8,128)(2,1)S(1)}, u32[]{:S(2)}, u32[]{:S(2)}) %collective-permute-start.2) | collective-permute-done | bytes 319520 | tf_op jit(solution)/shard_map/ppermute | solution.py:491
  41.0 4.1 convert_element_type.328
  50.2 5.6 collective-permute-done.4
  63.4 8.3 collective-permute-done.6
  71.6 3.1 collective-permute-done.7
  77.1 10.3 %collective-permute-done.13 = bf16[2,48,3072]{2,1,0:T(8,128)(2,1)S(1)} collective-permute-done((bf16[2,48,3072]{2,1,0:T(8,128)(2,1)S(1)}, bf16[2,48,3072]{2,1,0:T(8,128)(2,1)S(1)}, u32[]{:S(2)}, u32[]{:S(2)}) %collective-permute-start.13) | collective-permute-done | bytes 589856 | tf_op jit(solution)/shard_map/ppermute | solution.py:491
  91.0 8.3 collective-permute-done.3
  112.1 12.4 %attend_forward.2 = (f32[3,208,768]{2,1,0:T(8,128)S(1)}, bf16[3,208,2304]{2,1,0:T(8,128)(2,1)}, bf16[3,208,768]{2,1,0:T(8,128)(2,1)S(1)}) custom-call(f32[3,208,768]{2,1,0:T(8,128)S(1)} %pad.43.x_ref, f32[1,768]{1,0:T(1,128)S(1)} %get-tuple-element.309.gain_ref, f32[1,768]{1,0:T(1,128)S(1)} %get-tuple-element.308.shift_ref, bf16[768,3328]{1,0:T(8,128)(2,1)} %copy-done.1, ...), custom_call_target="tpu_custom_call" | custom-call | flops 925000000 | bytes 3250000 | tf_op jit(solution)/shard_map/attend_forward/pallas_call | solution.py:131
  132.8 4.9 dispatch_grad.1
  139.1 8.5 all-to-all-start
  163.6 22.9 %collective-permute-done.23 = bf16[4,48,768]{2,1,0:T(8,128)(2,1)S(1)} collective-permute-done((bf16[4,48,768]{2,1,0:T(8,128)(2,1)S(1)}, bf16[4,48,768]{2,1,0:T(8,128)(2,1)S(1)}, u32[]{:S(2)}, u32[]{:S(2)}) %collective-permute-start.23) | collective-permute-done | bytes 294944 | tf_op jit(solution)/shard_map/ppermute | solution.py:491
  188.4 5.8 collective-permute-start.18
  194.2 3.1 collective-permute-done.25
  199.0 8.1 collective-permute-done.26
  208.0 5.9 collective-permute-start.27
  214.7 15.7 %collective-permute-done.10 = bf16[192,3072]{1,0:T(8,128)(2,1)S(1)} collective-permute-done((bf16[192,3072]{1,0:T(8,128)(2,1)S(1)}, bf16[192,3072]{1,0:T(8,128)(2,1)S(1)}, u32[]{:S(2)}, u32[]{:S(2)}) %collective-permute-start.10) | collective-permute-done | bytes 1179680 | tf_op jit(solution)/shard_map/ppermute | solution.py:491
  231.5 5.2 collective-permute-start.28
  247.2 3.3 pad_maximum_fusion.1.refs_0_
  250.6 3.0 join.7.qkv_ref.proj_ref
  255.8 4.4 join.6.up_ref.down_ref
  260.2 3.7 copy-done
  263.8 15.1 %mlp_forward.1 = (f32[3,208,768]{2,1,0:T(8,128)}, bf16[3,208,3072]{2,1,0:T(8,128)(2,1)}, bf16[3,208,3072]{2,1,0:T(8,128)(2,1)}) custom-call(f32[3,208,768]{2,1,0:T(8,128)} %copy-done.14, f32[1,768]{1,0:T(1,128)} %get-tuple-element.307.gain_ref, f32[1,768]{1,0:T(1,128)} %get-tuple-element.306.shift_ref, bf16[768,6144]{1,0:T(8,128)(2,1)} %copy-done, ...), custom_call_target="tpu_custom_call" | custom-call | flops 1475000064 | bytes 5250000 | tf_op jit(solution)/shard_map/mlp_forward/pallas_call | solution.py:227
  280.4 12.3 %attend_forward.3 = (f32[3,208,768]{2,1,0:T(8,128)S(1)}, bf16[3,208,2304]{2,1,0:T(8,128)(2,1)}, bf16[3,208,768]{2,1,0:T(8,128)(2,1)S(1)}) custom-call(f32[3,208,768]{2,1,0:T(8,128)S(1)} %copy-done.15, f32[1,768]{1,0:T(1,128)S(1)} %get-tuple-element.305.gain_ref, f32[1,768]{1,0:T(1,128)S(1)} %get-tuple-element.304.shift_ref, bf16[768,3072]{1,0:T(8,128)(2,1)} %copy-done.2, ...), custom_call_target="tpu_custom_call" | custom-call | flops 925000000 | bytes 3250000 | tf_op jit(solution)/shard_map/attend_forward/pallas_call | solution.py:131
  295.0 3.3 collective-permute-done.29.refs_1_
  299.9 3.5 dispatch.1
  304.8 6.1 all-to-all-start.1
  316.2 50.6 %all-to-all-done.1 = bf16[16,96,768]{2,1,0:T(8,128)(2,1)} async-done(((bf16[16,96,768]{2,1,0:T(8,128)(2,1)}), bf16[16,96,768]{2,1,0:T(8,128)(2,1)}, u32[]{:S(2)}, u32[]{:S(2)}) %all-to-all-start.1) | async-done | bytes 2359328 | tf_op jit(solution)/shard_map/all_to_all | solution.py:616
  366.8 18.5 %expert_forward.1 = (bf16[1536,3072]{1,0:T(8,128)(2,1)}, bf16[1536,3072]{1,0:T(8,128)(2,1)}) custom-call(bf16[1536,768]{1,0:T(8,128)(2,1)} %bitcast.31.rows_ref, bf16[768,3072]{1,0:T(8,128)(2,1)} %copy-done.3), custom_call_target="tpu_custom_call" | custom-call | flops 1800000000 | bytes 6500000 | tf_op jit(solution)/shard_map/expert_forward/pallas_call | solution.py:407
  385.3 12.5 %convolution_convert_fusion.1 = bf16[768,3072]{1,0:T(8,128)(2,1)} fusion(bf16[1536,768]{1,0:T(8,128)(2,1)} %bitcast.28.grad_ref, bf16[1536,3072]{1,0:T(8,128)(2,1)} %get-tuple-element.165), kind=kOutput, calls=%fused_computation.16 | convolution fusion | flops 7250116608 | bytes 16515072 | tf_op jit(solution)/shard_map/dot_general | solution.py:40
  397.8 17.7 %collective-permute-done.30.refs_1_ = bf16[2,192,3072]{2,1,0:T(8,128)(2,1)} collective-permute-done((bf16[2,192,3072]{2,1,0:T(8,128)(2,1)}, bf16[2,192,3072]{2,1,0:T(8,128)(2,1)}, u32[]{:S(2)}, u32[]{:S(2)}) %collective-permute-start.30) | collective-permute-done | bytes 2359328 | tf_op jit(solution)/shard_map/ppermute | solution.py:491
  420.4 22.8 %expert_backward.1 = (bf16[1536,3072]{1,0:T(8,128)(2,1)}, bf16[1536,768]{1,0:T(8,128)(2,1)S(1)}) custom-call(bf16[1536,768]{1,0:T(8,128)(2,1)} %bitcast.28.grad_ref, bf16[1536,3072]{1,0:T(8,128)(2,1)} %get-tuple-element.169.slope_ref, bf16[768,3072]{1,0:T(8,128)(2,1)} %copy-done.3, bf16[768,3072]{1,0:T(8,128)(2,1)} %copy-done.4), custom_call_target="tpu_custom_call" | custom-call | flops 3600000000 | bytes 8250000 | tf_op jit(solution)/shard_map/expert_backward/pallas_call | solution.py:432
  444.6 5.5 all-to-all-start.3
  450.1 10.9 %convolution_convert_fusion = bf16[768,3072]{1,0:T(8,128)(2,1)S(1)} fusion(bf16[1536,768]{1,0:T(8,128)(2,1)} %bitcast.31.rows_ref, bf16[1536,3072]{1,0:T(8,128)(2,1)} %get-tuple-element.225), kind=kOutput, calls=%fused_computation.15 | convolution fusion | flops 7250116608 | bytes 16515072 | tf_op jit(solution)/shard_map/dot_general | solution.py:40
  464.5 30.0 %all-to-all-done.3 = bf16[16,96,768]{2,1,0:T(8,128)(2,1)} async-done(((bf16[16,96,768]{2,1,0:T(8,128)(2,1)}), bf16[16,96,768]{2,1,0:T(8,128)(2,1)}, u32[]{:S(2)}, u32[]{:S(2)}) %all-to-all-start.3) | async-done | bytes 2359328 | tf_op jit(solution)/shard_map/all_to_all | solution.py:616
  496.1 5.4 return_grad.1
  502.7 24.0 %attend_backward.2 = (f32[3,208,768]{2,1,0:T(8,128)S(1)}, bf16[3,208,2304]{2,1,0:T(8,128)(2,1)}, bf16[3,208,768]{2,1,0:T(8,128)(2,1)S(1)}, bf16[3,208,768]{2,1,0...) custom-call(f32[3,208,768]{2,1,0:T(8,128)S(1)} %copy-done.16, f32[3,208,768]{2,1,0:T(8,128)} %copy-done.18, ...), custom_call_target="tpu_custom_call" | custom-call | flops 1000000000 | bytes 5500000 | tf_op jit(solution)/shard_map/attend_backward/pallas_call | solution.py:189
  526.7 6.2 bitcast_convert_fusion.3
  537.7 11.1 %convolution_convert_fusion.2 = bf16[1536,768]{1,0:T(8,128)(2,1)} fusion(bf16[1536,3072]{1,0:T(8,128)(2,1)} %get-tuple-element.165, bf16[768,3072]{1,0:T(8,128)(2,1)S(1)} %bitcast.235), kind=kOutput, calls=%fused_computation.29 | convolution fusion | flops 7248936960 | bytes 16515072 | tf_op jit(solution)/shard_map/dot_general | solution.py:36
  548.8 7.5 all-to-all-start.2
  556.3 3.2 dynamic-slice_bitcast_fusion.1
  559.5 8.9 %collective-permute-done.56 = bf16[2,192,3072]{2,1,0:T(8,128)(2,1)} collective-permute-done((bf16[2,192,3072]{2,1,0:T(8,128)(2,1)}, bf16[2,192,3072]{2,1,0:T(8,128)(2,1)}, u32[]{:S(2)}, u32[]{:S(2)}) %collective-permute-start.56) | collective-permute-done | bytes 2359328 | tf_op jit(solution)/shard_map/ppermute | solution.py:491
  568.4 3.3 fusion.5
  573.8 14.8 %mlp_backward.1 = (f32[3,208,768]{2,1,0:T(8,128)}, bf16[3,208,3072]{2,1,0:T(8,128)(2,1)}, bf16[3,208,768]{2,1,0:T(8,128)(2,1)}, bf16[3,208,768]{2,1,0:T(8,128)(2...) custom-call(f32[3,208,768]{2,1,0:T(8,128)} %copy-done.14, f32[3,208,768]{2,1,0:T(8,128)} %copy-done.19, ...), custom_call_target="tpu_custom_call" | custom-call | flops 1475000064 | bytes 6250000 | tf_op jit(solution)/shard_map/mlp_backward/pallas_call | solution.py:264
  594.4 4.1 bitcast_convert_fusion.1
  598.5 20.1 %collective-permute-done.32 = bf16[4,2,48,768]{3,2,0,1:T(8,128)(2,1)S(1)} collective-permute-done((bf16[4,2,48,768]{3,2,0,1:T(8,128)(2,1)S(1)}, bf16[4,2,48,768]{3,2,0,1:T(8,128)(2,1)S(1)}, u32[]{:S(2)}, u32[]{:S(2)}) %collective-permute-start.32) | collective-permute-done | bytes 589856 | tf_op jit(solution)/shard_map/ppermute | solution.py:491
  621.4 4.3 bitcast_convert_fusion
  627.6 4.9 fusion.2
  634.7 47.4 %collective-permute-done.36 = bf16[2,48,1536]{2,1,0:T(8,128)(2,1)S(1)} collective-permute-done((bf16[2,48,1536]{2,1,0:T(8,128)(2,1)S(1)}, bf16[2,48,1536]{2,1,0:T(8,128)(2,1)S(1)}, u32[]{:S(2)}, u32[]{:S(2)}) %collective-permute-start.36) | collective-permute-done | bytes 294944 | tf_op jit(solution)/shard_map/ppermute | solution.py:491
  690.8 3.1 convert_element_type.428
  695.9 23.9 %attend_backward.3 = (f32[3,208,768]{2,1,0:T(8,128)S(1)}, bf16[3,208,2304]{2,1,0:T(8,128)(2,1)}, bf16[3,208,768]{2,1,0:T(8,128)(2,1)S(1)}, bf16[3,208,768]{2,1,0...) custom-call(f32[3,208,768]{2,1,0:T(8,128)S(1)} %copy-done.6, f32[3,208,768]{2,1,0:T(8,128)} %get-tuple-element.188.dy_ref, ...), custom_call_target="tpu_custom_call" | custom-call | flops 1000000000 | bytes 5500000 | tf_op jit(solution)/shard_map/attend_backward/pallas_call | solution.py:189
  719.8 7.5 bitcast_convert_fusion.2
  736.0 7.1 add_convert_fusion
  758.2 5.9 combine.1
  765.5 3.1 reshape.510
  770.9 3.1 reshape.515
  785.0 7.6 collective-permute-done.51
  796.0 10.1 %collective-permute-done.41 = bf16[4,2,48,768]{3,2,0,1:T(8,128)(2,1)S(1)} collective-permute-done((bf16[4,2,48,768]{3,2,0,1:T(8,128)(2,1)S(1)}, bf16[4,2,48,768]{3,2,0,1:T(8,128)(2,1)S(1)}, u32[]{:S(2)}, u32[]{:S(2)}) %collective-permute-start.41) | collective-permute-done | bytes 589856 | tf_op jit(solution)/shard_map/ppermute | solution.py:491
  807.3 14.2 %collective-permute-done.53 = bf16[2,48,3072]{2,1,0:T(8,128)(2,1)S(1)} collective-permute-done((bf16[2,48,3072]{2,1,0:T(8,128)(2,1)S(1)}, bf16[2,48,3072]{2,1,0:T(8,128)(2,1)S(1)}, u32[]{:S(2)}, u32[]{:S(2)}) %collective-permute-start.53) | collective-permute-done | bytes 589856 | tf_op jit(solution)/shard_map/ppermute | solution.py:491
  823.2 5.2 collective-permute-done.54
  832.0 3.6 collective-permute-start.55
  835.6 10.9 %collective-permute-done.45 = bf16[2,48,1664]{2,1,0:T(8,128)(2,1)S(1)} collective-permute-done((bf16[2,48,1664]{2,1,0:T(8,128)(2,1)S(1)}, bf16[2,48,1664]{2,1,0:T(8,128)(2,1)S(1)}, u32[]{:S(2)}, u32[]{:S(2)}) %collective-permute-start.45) | collective-permute-done | bytes 319520 | tf_op jit(solution)/shard_map/ppermute | solution.py:491
  846.8 4.1 collective-permute-done.46
  (425 shorter events, 202.8 us)
Async XLA Ops:
  4.3 7.5 collective-permute-start
  11.8 7.2 collective-permute-start.1
  19.1 16.2 %collective-permute-start.2 = (bf16[2,48,1664]{2,1,0:T(8,128)(2,1)S(1)}, bf16[2,48,1664]{2,1,0:T(8,128)(2,1)S(1)}, u32[]{:S(2)}, u32[]{:S(2)}) collective-permute-start(bf16[2,48,1664]{2,1,0:T(8,128)(2,1)S(1)} %pad_maximum_fusion.17), channel_id=1, source_target_pairs={{0,16},{16,0},{1,17},{17,1},{2,18},{18,2},{3,19},{19,3},{4,20},{20... | collective-permute-start | bytes 958472 | tf_op jit(solution)/shard_map/ppermute | solution.py:491
  35.4 14.2 %collective-permute-start.11 = (bf16[24,3072]{1,0:T(8,128)(2,1)S(1)}, bf16[24,3072]{1,0:T(8,128)(2,1)S(1)}, u32[]{:S(2)}, u32[]{:S(2)}) collective-permute-start(bf16[24,3072]{1,0:T(8,128)(2,1)S(1)} %get-tuple-element.293), channel_id=1, source_target_pairs={{0,1},{1,0},{2,3},{3,2},{4,5},{5,4},{6,7},{7,6},{8,9},{9,8},{10,11... | collective-permute-start | bytes 442376 | tf_op jit(solution)/shard_map/ppermute | solution.py:491
  47.1 65.0 %copy-start.5 = (f32[3,208,768]{2,1,0:T(8,128)}, f32[3,208,768]{2,1,0:T(8,128)S(1)}, u32[]{:S(2)}) copy-start(f32[3,208,768]{2,1,0:T(8,128)S(1)} %pad.43.x_ref) | copy-start | bytes 5750788
  47.1 8.7 %collective-permute-start.4 = (bf16[4,48,768]{2,1,0:T(8,128)(2,1)S(1)}, bf16[4,48,768]{2,1,0:T(8,128)(2,1)S(1)}, u32[]{:S(2)}, u32[]{:S(2)}) collective-permute-start(bf16[4,48,768]{2,1,0:T(8,128)(2,1)S(1)} %pad_maximum_fusion.18), channel_id=1, source_target_pairs={{0,2},{2,0},{1,3},{3,1},{4,6},{6,4},{5,7},{7,5},{8,10},{10,8},{9,1... | collective-permute-start | bytes 884744 | tf_op jit(solution)/shard_map/ppermute | solution.py:491
  48.4 9.4 %collective-permute-start.5 = (bf16[4,48,896]{2,1,0:T(8,128)(2,1)S(1)}, bf16[4,48,896]{2,1,0:T(8,128)(2,1)S(1)}, u32[]{:S(2)}, u32[]{:S(2)}) collective-permute-start(bf16[4,48,896]{2,1,0:T(8,128)(2,1)S(1)} %pad_maximum_fusion.15), channel_id=1, source_target_pairs={{0,4},{4,0},{1,5},{5,1},{2,6},{6,2},{3,7},{7,3},{8,12},{12,8},{9,1... | collective-permute-start | bytes 1032200 | tf_op jit(solution)/shard_map/ppermute | solution.py:491
  49.7 9.8 %collective-permute-start.12 = (bf16[48,3072]{1,0:T(8,128)(2,1)S(1)}, bf16[48,3072]{1,0:T(8,128)(2,1)S(1)}, u32[]{:S(2)}, u32[]{:S(2)}) collective-permute-start(bf16[48,3072]{1,0:T(8,128)(2,1)S(1)} %maximum_select_fusion.5), channel_id=1, source_target_pairs={{0,8},{8,0},{1,9},{9,1},{2,10},{10,2},{3,11},{11,3},{4,12},{12,4},... | collective-permute-start | bytes 884744 | tf_op jit(solution)/shard_map/ppermute | solution.py:491
  57.9 13.8 %collective-permute-start.6 = (bf16[8,48,768]{2,1,0:T(8,128)(2,1)S(1)}, bf16[8,48,768]{2,1,0:T(8,128)(2,1)S(1)}, u32[]{:S(2)}, u32[]{:S(2)}) collective-permute-start(bf16[8,48,768]{2,1,0:T(8,128)(2,1)S(1)} %pad_maximum_fusion.8), channel_id=1, source_target_pairs={{0,4},{4,0},{1,5},{5,1},{2,6},{6,2},{3,7},{7,3},{8,12},{12,8},{9,1... | collective-permute-start | bytes 1769480 | tf_op jit(solution)/shard_map/ppermute | solution.py:491
  59.2 15.5 %collective-permute-start.7 = (bf16[8,48,896]{2,1,0:T(8,128)(2,1)S(1)}, bf16[8,48,896]{2,1,0:T(8,128)(2,1)S(1)}, u32[]{:S(2)}, u32[]{:S(2)}) collective-permute-start(bf16[8,48,896]{2,1,0:T(8,128)(2,1)S(1)} %pad_maximum_fusion.6), channel_id=1, source_target_pairs={{0,2},{2,0},{1,3},{3,1},{4,6},{6,4},{5,7},{7,5},{8,10},{10,8},{9,1... | collective-permute-start | bytes 2064392 | tf_op jit(solution)/shard_map/ppermute | solution.py:491
  59.5 28.0 %collective-permute-start.13 = (bf16[2,48,3072]{2,1,0:T(8,128)(2,1)S(1)}, bf16[2,48,3072]{2,1,0:T(8,128)(2,1)S(1)}, u32[]{:S(2)}, u32[]{:S(2)}) collective-permute-start(bf16[2,48,3072]{2,1,0:T(8,128)(2,1)S(1)} %pad_maximum_fusion.9), channel_id=1, source_target_pairs={{0,16},{16,0},{1,17},{17,1},{2,18},{18,2},{3,19},{19,3},{4,20},{20... | collective-permute-start | bytes 1769480 | tf_op jit(solution)/shard_map/ppermute | solution.py:491
  60.4 38.9 %collective-permute-start.3 = (bf16[192,3072]{1,0:T(8,128)(2,1)S(1)}, bf16[192,3072]{1,0:T(8,128)(2,1)S(1)}, u32[]{:S(2)}, u32[]{:S(2)}) collective-permute-start(bf16[192,3072]{1,0:T(8,128)(2,1)S(1)} %get-tuple-element.273), channel_id=1, source_target_pairs={{0,8},{8,0},{1,9},{9,1},{2,10},{10,2},{3,11},{11,3},{4,12},{12,4},... | collective-permute-start | bytes 3538952 | tf_op jit(solution)/shard_map/ppermute | solution.py:491
  74.8 32.3 %collective-permute-start.8 = (bf16[16,48,768]{2,1,0:T(8,128)(2,1)S(1)}, bf16[16,48,768]{2,1,0:T(8,128)(2,1)S(1)}, u32[]{:S(2)}, u32[]{:S(2)}) collective-permute-start(bf16[16,48,768]{2,1,0:T(8,128)(2,1)S(1)} %constant_dynamic-update-slice_fusion.refs_0_), channel_id=1, source_target_pairs={{0,1},{1,0},{2,3},{3,2},{4,5},{5,4},{6,7},{7,6},{8,9},{9,8},{10,11... | collective-permute-start | bytes 3538952 | tf_op jit(solution)/shard_map/ppermute | solution.py:491
  87.7 3.0 collective-permute-start.20
  89.4 17.7 %collective-permute-start.9 = (bf16[16,48,896]{2,1,0:T(8,128)(2,1)S(1)}, bf16[16,48,896]{2,1,0:T(8,128)(2,1)S(1)}, u32[]{:S(2)}, u32[]{:S(2)}) collective-permute-start(bf16[16,48,896]{2,1,0:T(8,128)(2,1)S(1)} %constant_dynamic-update-slice_fusion.2.refs_1_), channel_id=1, source_target_pairs={{0,1},{1,0},{2,3},{3,2},{4,5},{5,4},{6,7},{7,6},{8,9},{9,8},{10,11... | collective-permute-start | bytes 4128776 | tf_op jit(solution)/shard_map/ppermute | solution.py:491
  89.5 16.0 %collective-permute-start.14 = (bf16[4,48,1536]{2,1,0:T(8,128)(2,1)S(1)}, bf16[4,48,1536]{2,1,0:T(8,128)(2,1)S(1)}, u32[]{:S(2)}, u32[]{:S(2)}) collective-permute-start(bf16[4,48,1536]{2,1,0:T(8,128)(2,1)S(1)} %get-tuple-element.139), channel_id=1, source_target_pairs={{0,2},{2,0},{1,3},{3,1},{4,6},{6,4},{5,7},{7,5},{8,10},{10,8},{9,1... | collective-permute-start | bytes 1769480 | tf_op jit(solution)/shard_map/ppermute | solution.py:491
  90.7 14.7 %collective-permute-start.15 = (bf16[4,48,1536]{2,1,0:T(8,128)(2,1)S(1)}, bf16[4,48,1536]{2,1,0:T(8,128)(2,1)S(1)}, u32[]{:S(2)}, u32[]{:S(2)}) collective-permute-start(bf16[4,48,1536]{2,1,0:T(8,128)(2,1)S(1)} %get-tuple-element.140), channel_id=1, source_target_pairs={{0,4},{4,0},{1,5},{5,1},{2,6},{6,2},{3,7},{7,3},{8,12},{12,8},{9,1... | collective-permute-start | bytes 1769480 | tf_op jit(solution)/shard_map/ppermute | solution.py:491
  99.3 4.3 collective-permute-start.21
  104.3 43.3 %collective-permute-start.22 = (bf16[2,48,1536]{2,1,0:T(8,128)(2,1)}, bf16[2,48,1536]{2,1,0:T(8,128)(2,1)}, u32[]{:S(2)}, u32[]{:S(2)}) collective-permute-start(bf16[2,48,1536]{2,1,0:T(8,128)(2,1)} %pad_maximum_fusion.20), channel_id=1, source_target_pairs={{0,16},{16,0},{1,17},{17,1},{2,18},{18,2},{3,19},{19,3},{4,20},{20... | collective-permute-start | bytes 884744 | tf_op jit(solution)/shard_map/ppermute | solution.py:491
  125.8 27.8 %collective-permute-start.16 = (bf16[8,48,1536]{2,1,0:T(8,128)(2,1)}, bf16[8,48,1536]{2,1,0:T(8,128)(2,1)}, u32[]{:S(2)}, u32[]{:S(2)}) collective-permute-start(bf16[8,48,1536]{2,1,0:T(8,128)(2,1)} %get-tuple-element.143), channel_id=1, source_target_pairs={{0,4},{4,0},{1,5},{5,1},{2,6},{6,2},{3,7},{7,3},{8,12},{12,8},{9,1... | collective-permute-start | bytes 3538952 | tf_op jit(solution)/shard_map/ppermute | solution.py:491
  126.0 27.6 %collective-permute-start.17 = (bf16[8,48,1536]{2,1,0:T(8,128)(2,1)}, bf16[8,48,1536]{2,1,0:T(8,128)(2,1)}, u32[]{:S(2)}, u32[]{:S(2)}) collective-permute-start(bf16[8,48,1536]{2,1,0:T(8,128)(2,1)} %get-tuple-element.144), channel_id=1, source_target_pairs={{0,2},{2,0},{1,3},{3,1},{4,6},{6,4},{5,7},{7,5},{8,10},{10,8},{9,1... | collective-permute-start | bytes 3538952 | tf_op jit(solution)/shard_map/ppermute | solution.py:491
  139.1 159.2 %all-to-all-start = ((bf16[16,96,768]{2,1,0:T(8,128)(2,1)}), bf16[16,96,768]{2,1,0:T(8,128)(2,1)}, u32[]{:S(2)}, u32[]{:S(2)}) async-start(bf16[16,96,768]{2,1,0:T(8,128)(2,1)} %bitcast.237), calls=%async_computation | async-start | bytes 4718592 | tf_op jit(solution)/shard_map/all_to_all | solution.py:616
  158.3 28.1 %collective-permute-start.23 = (bf16[4,48,768]{2,1,0:T(8,128)(2,1)S(1)}, bf16[4,48,768]{2,1,0:T(8,128)(2,1)S(1)}, u32[]{:S(2)}, u32[]{:S(2)}) collective-permute-start(bf16[4,48,768]{2,1,0:T(8,128)(2,1)S(1)} %get-tuple-element.153), channel_id=1, source_target_pairs={{0,2},{2,0},{1,3},{3,1},{4,6},{6,4},{5,7},{7,5},{8,10},{10,8},{9,1... | collective-permute-start | bytes 884744 | tf_op jit(solution)/shard_map/ppermute | solution.py:491
  159.7 26.8 %collective-permute-start.24 = (bf16[4,48,768]{2,1,0:T(8,128)(2,1)S(1)}, bf16[4,48,768]{2,1,0:T(8,128)(2,1)S(1)}, u32[]{:S(2)}, u32[]{:S(2)}) collective-permute-start(bf16[4,48,768]{2,1,0:T(8,128)(2,1)S(1)} %get-tuple-element.154), channel_id=1, source_target_pairs={{0,4},{4,0},{1,5},{5,1},{2,6},{6,2},{3,7},{7,3},{8,12},{12,8},{9,1... | collective-permute-start | bytes 884744 | tf_op jit(solution)/shard_map/ppermute | solution.py:491
  186.6 10.7 %collective-permute-start.25 = (bf16[8,48,768]{2,1,0:T(8,128)(2,1)S(1)}, bf16[8,48,768]{2,1,0:T(8,128)(2,1)S(1)}, u32[]{:S(2)}, u32[]{:S(2)}) collective-permute-start(bf16[8,48,768]{2,1,0:T(8,128)(2,1)S(1)} %pad_maximum_fusion.11), channel_id=1, source_target_pairs={{0,4},{4,0},{1,5},{5,1},{2,6},{6,2},{3,7},{7,3},{8,12},{12,8},{9,1... | collective-permute-start | bytes 1769480 | tf_op jit(solution)/shard_map/ppermute | solution.py:491
  187.8 42.7 %collective-permute-start.10 = (bf16[192,3072]{1,0:T(8,128)(2,1)S(1)}, bf16[192,3072]{1,0:T(8,128)(2,1)S(1)}, u32[]{:S(2)}, u32[]{:S(2)}) collective-permute-start(bf16[192,3072]{1,0:T(8,128)(2,1)S(1)} %get-tuple-element.271), channel_id=1, source_target_pairs={{0,8},{8,0},{1,9},{9,1},{2,10},{10,2},{3,11},{11,3},{4,12},{12,4},... | collective-permute-start | bytes 3538952 | tf_op jit(solution)/shard_map/ppermute | solution.py:491
  188.4 67.4 %collective-permute-start.18 = (bf16[16,48,1536]{2,1,0:T(8,128)(2,1)}, bf16[16,48,1536]{2,1,0:T(8,128)(2,1)}, u32[]{:S(2)}, u32[]{:S(2)}) collective-permute-start(bf16[16,48,1536]{2,1,0:T(8,128)(2,1)} %constant_dynamic-update-slice_fusion.4.refs_0_), channel_id=1, source_target_pairs={{0,1},{1,0},{2,3},{3,2},{4,5},{5,4},{6,7},{7,6},{8,9},{9,8},{10,11... | collective-permute-start | bytes 7077896 | tf_op jit(solution)/shard_map/ppermute | solution.py:491
  194.2 61.6 %collective-permute-start.19 = (bf16[16,48,1536]{2,1,0:T(8,128)(2,1)}, bf16[16,48,1536]{2,1,0:T(8,128)(2,1)}, u32[]{:S(2)}, u32[]{:S(2)}) collective-permute-start(bf16[16,48,1536]{2,1,0:T(8,128)(2,1)} %constant_dynamic-update-slice_fusion.6.refs_1_), channel_id=1, source_target_pairs={{0,1},{1,0},{2,3},{3,2},{4,5},{5,4},{6,7},{7,6},{8,9},{9,8},{10,11... | collective-permute-start | bytes 7077896 | tf_op jit(solution)/shard_map/ppermute | solution.py:491
  194.2 104.1 %collective-permute-start.29 = (bf16[2,192,3072]{2,1,0:T(8,128)(2,1)}, bf16[2,192,3072]{2,1,0:T(8,128)(2,1)}, u32[]{:S(2)}, u32[]{:S(2)}) collective-permute-start(bf16[2,192,3072]{2,1,0:T(8,128)(2,1)} %pad_maximum_fusion.refs_0_), channel_id=1, source_target_pairs={{0,16},{16,0},{1,17},{17,1},{2,18},{18,2},{3,19},{19,3},{4,20},{20... | collective-permute-start | bytes 7077896 | tf_op jit(solution)/shard_map/ppermute | solution.py:491
  197.3 9.9 %collective-permute-start.26 = (bf16[8,48,768]{2,1,0:T(8,128)(2,1)S(1)}, bf16[8,48,768]{2,1,0:T(8,128)(2,1)S(1)}, u32[]{:S(2)}, u32[]{:S(2)}) collective-permute-start(bf16[8,48,768]{2,1,0:T(8,128)(2,1)S(1)} %pad_maximum_fusion.12), channel_id=1, source_target_pairs={{0,2},{2,0},{1,3},{3,1},{4,6},{6,4},{5,7},{7,5},{8,10},{10,8},{9,1... | collective-permute-start | bytes 1769480 | tf_op jit(solution)/shard_map/ppermute | solution.py:491
  208.0 42.5 %collective-permute-start.27 = (bf16[16,48,768]{2,1,0:T(8,128)(2,1)}, bf16[16,48,768]{2,1,0:T(8,128)(2,1)}, u32[]{:S(2)}, u32[]{:S(2)}) collective-permute-start(bf16[16,48,768]{2,1,0:T(8,128)(2,1)} %constant_dynamic-update-slice_fusion.8.refs_0_), channel_id=1, source_target_pairs={{0,1},{1,0},{2,3},{3,2},{4,5},{5,4},{6,7},{7,6},{8,9},{9,8},{10,11... | collective-permute-start | bytes 3538952 | tf_op jit(solution)/shard_map/ppermute | solution.py:491
  231.5 19.0 %collective-permute-start.28 = (bf16[16,48,768]{2,1,0:T(8,128)(2,1)}, bf16[16,48,768]{2,1,0:T(8,128)(2,1)}, u32[]{:S(2)}, u32[]{:S(2)}) collective-permute-start(bf16[16,48,768]{2,1,0:T(8,128)(2,1)} %constant_dynamic-update-slice_fusion.10.refs_1_), channel_id=1, source_target_pairs={{0,1},{1,0},{2,3},{3,2},{4,5},{5,4},{6,7},{7,6},{8,9},{9,8},{10,11... | collective-permute-start | bytes 3538952 | tf_op jit(solution)/shard_map/ppermute | solution.py:491
  304.8 62.0 %all-to-all-start.1 = ((bf16[16,96,768]{2,1,0:T(8,128)(2,1)}), bf16[16,96,768]{2,1,0:T(8,128)(2,1)}, u32[]{:S(2)}, u32[]{:S(2)}) async-start(bf16[16,96,768]{2,1,0:T(8,128)(2,1)} %bitcast.238), calls=%async_computation.1 | async-start | bytes 4718592 | tf_op jit(solution)/shard_map/all_to_all | solution.py:616
  310.9 104.6 %collective-permute-start.30 = (bf16[2,192,3072]{2,1,0:T(8,128)(2,1)}, bf16[2,192,3072]{2,1,0:T(8,128)(2,1)}, u32[]{:S(2)}, u32[]{:S(2)}) collective-permute-start(bf16[2,192,3072]{2,1,0:T(8,128)(2,1)} %pad_maximum_fusion.1.refs_0_), channel_id=1, source_target_pairs={{0,16},{16,0},{1,17},{17,1},{2,18},{18,2},{3,19},{19,3},{4,20},{20... | collective-permute-start | bytes 7077896 | tf_op jit(solution)/shard_map/ppermute | solution.py:491
  444.6 50.0 %all-to-all-start.3 = ((bf16[16,96,768]{2,1,0:T(8,128)(2,1)}), bf16[16,96,768]{2,1,0:T(8,128)(2,1)}, u32[]{:S(2)}, u32[]{:S(2)}) async-start(bf16[16,96,768]{2,1,0:T(8,128)(2,1)} %bitcast.241), calls=%async_computation.3 | async-start | bytes 4718592 | tf_op jit(solution)/shard_map/all_to_all | solution.py:616
  463.9 104.6 %collective-permute-start.56 = (bf16[2,192,3072]{2,1,0:T(8,128)(2,1)}, bf16[2,192,3072]{2,1,0:T(8,128)(2,1)}, u32[]{:S(2)}, u32[]{:S(2)}) collective-permute-start(bf16[2,192,3072]{2,1,0:T(8,128)(2,1)} %dynamic-slice_bitcast_fusion), channel_id=1, source_target_pairs={{0,16},{16,0},{1,17},{17,1},{2,18},{18,2},{3,19},{19,3},{4,20},{20... | collective-permute-start | bytes 7077896 | tf_op jit(solution)/shard_map/ppermute | solution.py:491
  536.8 51.9 %collective-permute-start.31 = (bf16[768,1536]{1,0:T(8,128)(2,1)}, bf16[768,1536]{1,0:T(8,128)(2,1)}, u32[]{:S(2)}, u32[]{:S(2)}) collective-permute-start(bf16[768,1536]{1,0:T(8,128)(2,1)} %fusion.7), channel_id=1, source_target_pairs={{0,1},{1,0},{2,3},{3,2},{4,5},{5,4},{6,7},{7,6},{8,9},{9,8},{10,11... | collective-permute-start | bytes 7077896 | tf_op jit(solution)/shard_map/ppermute | solution.py:491
  548.8 207.9 %all-to-all-start.2 = ((bf16[16,96,768]{2,1,0:T(8,128)(2,1)}), bf16[16,96,768]{2,1,0:T(8,128)(2,1)}, u32[]{:S(2)}, u32[]{:S(2)}) async-start(bf16[16,96,768]{2,1,0:T(8,128)(2,1)} %bitcast.260), calls=%async_computation.2 | async-start | bytes 4718592 | tf_op jit(solution)/shard_map/all_to_all | solution.py:616
  559.5 122.8 %collective-permute-start.39 = (bf16[2,192,3072]{2,1,0:T(8,128)(2,1)}, bf16[2,192,3072]{2,1,0:T(8,128)(2,1)}, u32[]{:S(2)}, u32[]{:S(2)}) collective-permute-start(bf16[2,192,3072]{2,1,0:T(8,128)(2,1)} %dynamic-slice_bitcast_fusion.1), channel_id=1, source_target_pairs={{0,16},{16,0},{1,17},{17,1},{2,18},{18,2},{3,19},{19,3},{4,20},{20... | collective-permute-start | bytes 7077896 | tf_op jit(solution)/shard_map/ppermute | solution.py:491
  573.8 117.0 %collective-permute-start.57 = (bf16[1,192,3072]{2,1,0:T(8,128)(2,1)}, bf16[1,192,3072]{2,1,0:T(8,128)(2,1)}, u32[]{:S(2)}, u32[]{:S(2)}) collective-permute-start(bf16[1,192,3072]{2,1,0:T(8,128)(2,1)} %get-tuple-element.265), channel_id=1, source_target_pairs={{0,8},{8,0},{1,9},{9,1},{2,10},{10,2},{3,11},{11,3},{4,12},{12,4},... | collective-permute-start | bytes 3538952 | tf_op jit(solution)/shard_map/ppermute | solution.py:491
  591.9 26.6 %collective-permute-start.32 = (bf16[4,2,48,768]{3,2,0,1:T(8,128)(2,1)S(1)}, bf16[4,2,48,768]{3,2,0,1:T(8,128)(2,1)S(1)}, u32[]{:S(2)}, u32[]{:S(2)}) collective-permute-start(bf16[4,2,48,768]{3,2,0,1:T(8,128)(2,1)S(1)} %bitcast.276), channel_id=1, source_target_pairs={{0,4},{4,0},{1,5},{5,1},{2,6},{6,2},{3,7},{7,3},{8,12},{12,8},{9,1... | collective-permute-start | bytes 1769480 | tf_op jit(solution)/shard_map/ppermute | solution.py:491
  593.2 25.4 %collective-permute-start.33 = (bf16[4,2,48,768]{3,2,1,0:T(8,128)(2,1)S(1)}, bf16[4,2,48,768]{3,2,1,0:T(8,128)(2,1)S(1)}, u32[]{:S(2)}, u32[]{:S(2)}) collective-permute-start(bf16[4,2,48,768]{3,2,1,0:T(8,128)(2,1)S(1)} %dynamic-slice_bitcast_fusion.7), channel_id=1, source_target_pairs={{0,2},{2,0},{1,3},{3,1},{4,6},{6,4},{5,7},{7,5},{8,10},{10,8},{9,1... | collective-permute-start | bytes 1769480 | tf_op jit(solution)/shard_map/ppermute | solution.py:491
  619.0 8.3 collective-permute-start.34
  619.0 8.2 collective-permute-start.35
  627.5 54.6 %collective-permute-start.36 = (bf16[2,48,1536]{2,1,0:T(8,128)(2,1)S(1)}, bf16[2,48,1536]{2,1,0:T(8,128)(2,1)S(1)}, u32[]{:S(2)}, u32[]{:S(2)}) collective-permute-start(bf16[2,48,1536]{2,1,0:T(8,128)(2,1)S(1)} %dynamic-slice_bitcast_fusion.12), channel_id=1, source_target_pairs={{0,16},{16,0},{1,17},{17,1},{2,18},{18,2},{3,19},{19,3},{4,20},{20... | collective-permute-start | bytes 884744 | tf_op jit(solution)/shard_map/ppermute | solution.py:491
  632.5 103.4 %collective-permute-start.48 = (bf16[768,3072]{1,0:T(8,128)(2,1)}, bf16[768,3072]{1,0:T(8,128)(2,1)}, u32[]{:S(2)}, u32[]{:S(2)}) collective-permute-start(bf16[768,3072]{1,0:T(8,128)(2,1)} %fusion.2), channel_id=1, source_target_pairs={{0,1},{1,0},{2,3},{3,2},{4,5},{5,4},{6,7},{7,6},{8,9},{9,8},{10,11... | collective-permute-start | bytes 14155784 | tf_op jit(solution)/shard_map/ppermute | solution.py:491
  682.2 4.5 collective-permute-start.37
  686.8 8.4 collective-permute-start.38
  690.8 61.3 %collective-permute-start.58 = (bf16[1,192,3072]{2,1,0:T(8,128)(2,1)}, bf16[1,192,3072]{2,1,0:T(8,128)(2,1)}, u32[]{:S(2)}, u32[]{:S(2)}) collective-permute-start(bf16[1,192,3072]{2,1,0:T(8,128)(2,1)} %get-tuple-element.263), channel_id=1, source_target_pairs={{0,8},{8,0},{1,9},{9,1},{2,10},{10,2},{3,11},{11,3},{4,12},{12,4},... | collective-permute-start | bytes 3538952 | tf_op jit(solution)/shard_map/ppermute | solution.py:491
  735.6 45.1 %collective-permute-start.40 = (bf16[768,1664]{1,0:T(8,128)(2,1)}, bf16[768,1664]{1,0:T(8,128)(2,1)}, u32[]{:S(2)}, u32[]{:S(2)}) collective-permute-start(bf16[768,1664]{1,0:T(8,128)(2,1)} %constant_dynamic-slice_fusion.10), channel_id=1, source_target_pairs={{0,1},{1,0},{2,3},{3,2},{4,5},{5,4},{6,7},{7,6},{8,9},{9,8},{10,11... | collective-permute-start | bytes 7667720 | tf_op jit(solution)/shard_map/ppermute | solution.py:491
  747.3 27.7 %collective-permute-start.49 = (bf16[4,2,48,1536]{3,2,0,1:T(8,128)(2,1)}, bf16[4,2,48,1536]{3,2,0,1:T(8,128)(2,1)}, u32[]{:S(2)}, u32[]{:S(2)}) collective-permute-start(bf16[4,2,48,1536]{3,2,0,1:T(8,128)(2,1)} %bitcast.227), channel_id=1, source_target_pairs={{0,4},{4,0},{1,5},{5,1},{2,6},{6,2},{3,7},{7,3},{8,12},{12,8},{9,1... | collective-permute-start | bytes 3538952 | tf_op jit(solution)/shard_map/ppermute | solution.py:491
  748.4 27.3 %collective-permute-start.50 = (bf16[4,2,48,1536]{3,2,1,0:T(8,128)(2,1)}, bf16[4,2,48,1536]{3,2,1,0:T(8,128)(2,1)}, u32[]{:S(2)}, u32[]{:S(2)}) collective-permute-start(bf16[4,2,48,1536]{3,2,1,0:T(8,128)(2,1)} %dynamic-slice_bitcast_fusion.2), channel_id=1, source_target_pairs={{0,2},{2,0},{1,3},{3,1},{4,6},{6,4},{5,7},{7,5},{8,10},{10,8},{9,1... | collective-permute-start | bytes 3538952 | tf_op jit(solution)/shard_map/ppermute | solution.py:491
  779.1 13.5 %collective-permute-start.51 = (bf16[4,48,1536]{2,1,0:T(8,128)(2,1)S(1)}, bf16[4,48,1536]{2,1,0:T(8,128)(2,1)S(1)}, u32[]{:S(2)}, u32[]{:S(2)}) collective-permute-start(bf16[4,48,1536]{2,1,0:T(8,128)(2,1)S(1)} %dynamic-slice_bitcast_fusion.6), channel_id=1, source_target_pairs={{0,2},{2,0},{1,3},{3,1},{4,6},{6,4},{5,7},{7,5},{8,10},{10,8},{9,1... | collective-permute-start | bytes 1769480 | tf_op jit(solution)/shard_map/ppermute | solution.py:491
  780.4 13.1 %collective-permute-start.52 = (bf16[4,48,1536]{2,1,0:T(8,128)(2,1)S(1)}, bf16[4,48,1536]{2,1,0:T(8,128)(2,1)S(1)}, u32[]{:S(2)}, u32[]{:S(2)}) collective-permute-start(bf16[4,48,1536]{2,1,0:T(8,128)(2,1)S(1)} %dynamic-slice_bitcast_fusion.5), channel_id=1, source_target_pairs={{0,4},{4,0},{1,5},{5,1},{2,6},{6,2},{3,7},{7,3},{8,12},{12,8},{9,1... | collective-permute-start | bytes 1769480 | tf_op jit(solution)/shard_map/ppermute | solution.py:491
  783.5 22.6 %collective-permute-start.41 = (bf16[4,2,48,768]{3,2,0,1:T(8,128)(2,1)S(1)}, bf16[4,2,48,768]{3,2,0,1:T(8,128)(2,1)S(1)}, u32[]{:S(2)}, u32[]{:S(2)}) collective-permute-start(bf16[4,2,48,768]{3,2,0,1:T(8,128)(2,1)S(1)} %bitcast.275), channel_id=1, source_target_pairs={{0,4},{4,0},{1,5},{5,1},{2,6},{6,2},{3,7},{7,3},{8,12},{12,8},{9,1... | collective-permute-start | bytes 1769480 | tf_op jit(solution)/shard_map/ppermute | solution.py:491
  784.7 22.6 %collective-permute-start.42 = (bf16[4,2,48,896]{3,2,1,0:T(8,128)(2,1)S(1)}, bf16[4,2,48,896]{3,2,1,0:T(8,128)(2,1)S(1)}, u32[]{:S(2)}, u32[]{:S(2)}) collective-permute-start(bf16[4,2,48,896]{3,2,1,0:T(8,128)(2,1)S(1)} %dynamic-slice_bitcast_fusion.3), channel_id=1, source_target_pairs={{0,2},{2,0},{1,3},{3,1},{4,6},{6,4},{5,7},{7,5},{8,10},{10,8},{9,1... | collective-permute-start | bytes 2064392 | tf_op jit(solution)/shard_map/ppermute | solution.py:491
  794.0 27.5 %collective-permute-start.53 = (bf16[2,48,3072]{2,1,0:T(8,128)(2,1)S(1)}, bf16[2,48,3072]{2,1,0:T(8,128)(2,1)S(1)}, u32[]{:S(2)}, u32[]{:S(2)}) collective-permute-start(bf16[2,48,3072]{2,1,0:T(8,128)(2,1)S(1)} %dynamic-slice_bitcast_fusion.4), channel_id=1, source_target_pairs={{0,16},{16,0},{1,17},{17,1},{2,18},{18,2},{3,19},{19,3},{4,20},{20... | collective-permute-start | bytes 1769480 | tf_op jit(solution)/shard_map/ppermute | solution.py:491
  821.7 6.7 collective-permute-start.54
  822.2 6.7 collective-permute-start.43
  822.5 7.4 collective-permute-start.44
  830.3 16.3 %collective-permute-start.45 = (bf16[2,48,1664]{2,1,0:T(8,128)(2,1)S(1)}, bf16[2,48,1664]{2,1,0:T(8,128)(2,1)S(1)}, u32[]{:S(2)}, u32[]{:S(2)}) collective-permute-start(bf16[2,48,1664]{2,1,0:T(8,128)(2,1)S(1)} %dynamic-slice_bitcast_fusion.9), channel_id=1, source_target_pairs={{0,16},{16,0},{1,17},{17,1},{2,18},{18,2},{3,19},{19,3},{4,20},{20... | collective-permute-start | bytes 958472 | tf_op jit(solution)/shard_map/ppermute | solution.py:491
  832.0 14.8 %collective-permute-start.55 = (f32[24,3072]{1,0:T(8,128)S(1)}, f32[24,3072]{1,0:T(8,128)S(1)}, u32[]{:S(2)}, u32[]{:S(2)}) collective-permute-start(f32[24,3072]{1,0:T(8,128)S(1)} %get-tuple-element.283), channel_id=1, source_target_pairs={{0,1},{1,0},{2,3},{3,2},{4,5},{5,4},{6,7},{7,6},{8,9},{9,8},{10,11... | collective-permute-start | bytes 884744 | tf_op jit(solution)/shard_map/ppermute | solution.py:491
  846.7 4.2 collective-permute-start.46
  851.0 3.7 collective-permute-start.47
  (67 other events, 585.2 us)

commit v3 on v2

--- a/solution.py
+++ b/solution.py
@@ -3,6 +3,7 @@
 
 import jax
 import jax.numpy as jnp
+import numpy as np
 from jax import lax
 from jax.experimental import pallas as pl
 from jax.experimental.pallas import tpu as pltpu
@@ -25,6 +26,7 @@
 RSQRT2PI = 1.0 / math.sqrt(2.0 * math.pi)
 SLOT_TILE = 256
 ROW_TILE = 256
+WIDTH_TILE = 768
 HINT = 4
 
 
@@ -441,6 +443,78 @@
     )(grad, slope, weight_in, weight_out_t)
 
 
+def weight_grad_body(tiles, starts, split, at_ref, *refs):
+    count = len(starts)
+    lefts, rights = refs[:count], refs[count : 2 * count]
+    outs, turned = refs[2 * count : -count], refs[-count:]
+    step = pl.program_id(0)
+    tile = lax.rem(step + at_ref[0], tiles)
+
+    @pl.when(step == 0)
+    def _():
+        for left, scratch in zip(lefts, turned):
+            scratch[...] = left[...].T
+
+    for index, (left, right) in enumerate(zip(turned, rights)):
+        stop = (starts + (tiles,))[index + 1]
+
+        @pl.when((tile >= starts[index]) & (tile < stop))
+        def _(left=left, right=right):
+            value = mm(left[...], right[...]).astype(LOW)
+            if split:
+
+                @pl.when(step < tiles // 2)
+                def _():
+                    outs[0][...] = value
+
+                @pl.when(step >= tiles // 2)
+                def _():
+                    outs[1][...] = value
+            else:
+                outs[0][...] = value
+
+
+def weight_grad(split, core, *pairs):
+    width = WIDTH_TILE
+    tokens = pairs[0][0].shape[0]
+    counts = [right.shape[1] // width for _, right in pairs]
+    starts = tuple(int(n) for n in np.cumsum([0] + counts[:-1]))
+    tiles = sum(counts)
+    first = ((1 - core) * (tiles // 2) if split else 0 * core).astype(jnp.int32).reshape(1)
+
+    def right_spec(start, count):
+        def at(step, at_ref):
+            return 0, jnp.clip(lax.rem(step + at_ref[0], tiles) - start, 0, count - 1)
+
+        return pl.BlockSpec((tokens, width), at)
+
+    half = tiles // 2
+    if split:
+        out_specs = [
+            pl.BlockSpec((D, width), lambda step, _: (0, jnp.minimum(step, half - 1))),
+            pl.BlockSpec((D, width), lambda step, _: (0, jnp.maximum(step - half, 0))),
+        ]
+        out_shape = [like((D, half * width), LOW)] * 2
+    else:
+        out_specs = [pl.BlockSpec((D, width), lambda step, _: (0, step))]
+        out_shape = [like((D, tiles * width), LOW)]
+    return pl.pallas_call(
+        functools.partial(weight_grad_body, tiles, starts, split),
+        grid_spec=pltpu.PrefetchScalarGridSpec(
+            num_scalar_prefetch=1,
+            grid=(tiles,),
+            in_specs=[whole((tokens, D)) for _ in pairs]
+            + [right_spec(start, count) for start, count in zip(starts, counts)],
+            out_specs=out_specs,
+            scratch_shapes=[pltpu.VMEM((D, tokens), LOW) for _ in pairs],
+        ),
+        out_shape=out_shape,
+        compiler_params=params(48),
+        cost_estimate=cost(2 * D * tokens * tiles * width, 3 * D * tiles * width),
+        name="weight_grad",
+    )(first, *[left for left, _ in pairs], *[right for _, right in pairs])
+
+
 def join_body(at_ref, *refs):
     *parts, out_ref, sem = refs
     for index, part in enumerate(parts):
@@ -467,6 +541,10 @@
     )(places, *parts)
 
 
+def pick(value, at, axis):
+    return lax.dynamic_index_in_dim(value, at, axis, keepdims=False)
+
+
 def flipped(index, first, second, axis):
     return jnp.where(
         index == 0,
@@ -490,43 +568,58 @@
         size = lax.axis_size(axes)
         return lax.ppermute(value, axes, [(i, i ^ bit) for i in range(size)])
 
-    def gather_depth(self, part, *gates):
-        part = after(part, *gates)
+    def gather_depth(self, parts):
         if not self.wide:
-            return part
-        half, quarter = self.cut(part)
+            return jnp.concatenate(parts, axis=1)
         core = lax.axis_index("c")
-        mine = lax.dynamic_slice_in_dim(part, core * half, half, 1)
-        other = lax.dynamic_slice_in_dim(part, (1 - core) * half, half, 1)
-        mine = flipped(core, mine, self.hop(other, "c", 1), 0)
-        deep = self.deepen(mine)
-        return lax.optimization_barrier((deep[:, :, :quarter], deep[:, :, quarter:]))
-
-    def deepen(self, mine):
-        pair = jnp.stack([mine, self.hop(mine, "dl", 1)])
-        return jnp.concatenate([pair] + [self.hop(pair, "dh", k) for k in range(1, self.n_dp // 2)])
+        sides = [
+            jnp.concatenate(
+                [
+                    lax.dynamic_slice_in_dim(part, side * self.cut(part)[0], self.cut(part)[0], 1)
+                    for part in parts
+                ],
+                axis=1,
+            )
+            for side in (core, 1 - core)
+        ]
+        mine = flipped(core, sides[0], self.hop(sides[1], "c", 1), 0)
+        return lax.all_gather(mine[None], self.dp, axis=0, tiled=True)
+
+    def gather_split(self, deep, parts):
+        if not self.wide:
+            ends = np.cumsum([part.shape[1] for part in parts])
+            return [deep[:, end - part.shape[1] : end] for end, part in zip(ends, parts)]
+        pairs, at = [], 0
+        for part in parts:
+            half, quarter = self.cut(part)
+            pairs.append((deep[:, :, at : at + quarter], deep[:, :, at + quarter : at + half]))
+            at += half
+        return pairs
 
     def cut(self, part):
         return part.shape[1] // 2, part.shape[1] // 512 * 128
 
-    def gather_side(self, pair, step, *gates):
+    def gather_side(self, pair, step):
         if not self.wide:
             return pair
-        left, right, *_ = lax.optimization_barrier(tuple(pair) + gates)
+        left, right = lax.optimization_barrier(tuple(pair))
         axes = ("x", "y") if step == 0 else ("y", "x")
         came = lax.optimization_barrier((self.hop(left, axes[0], 1), self.hop(right, axes[1], 1)))
         return tuple(jnp.concatenate([own, new]) for own, new in zip((left, right), came))
 
-    def gather_core(self, pair, part):
+    def gather_core(self, pair):
         if not self.wide:
-            return lax.all_gather(pair, self.axes, axis=0, tiled=True)
-        left, right = pair
+            return pair
+        return tuple(pair) + tuple(self.hop(value, "c", 1) for value in pair)
+
+    def gather_join(self, four, part):
+        if not self.wide:
+            return lax.all_gather(four, self.axes, axis=0, tiled=True)
         rows, width = part.shape
         half, quarter = self.cut(part)
         core = lax.axis_index("c")
-        far = lax.optimization_barrier((self.hop(left, "c", 1), self.hop(right, "c", 1)))
         steps = jnp.arange(16, dtype=jnp.int32)
-        me = lax.axis_index(self.dp) * 4 + lax.axis_index("y") * 2 + lax.axis_index("x")
+        me = lax.axis_index("y") * 2 + lax.axis_index("x")
         first, second, turn = steps // 8, steps // 4 % 2, steps % 4
         left_at = (turn * 4 + first * 2 + second) ^ me
         right_at = (turn * 4 + second * 2 + first) ^ me
@@ -543,34 +636,55 @@
                 spots(right_at, 1, 1 - core),
             ]
         ).astype(jnp.int32)
-        return join(places, (left, right) + tuple(far), width)
-
-    def scatter(self, full):
+        return join(places, four, width)
+
+    def scatter_swap(self, halves):
         if not self.wide:
-            return lax.psum_scatter(full, self.axes, scatter_dimension=0, tiled=True).astype(WIDE)
-        height, width = full.shape
-        half, quarter = width // 2, width // 512 * 128
-        core, y, x = lax.axis_index("c"), lax.axis_index("y"), lax.axis_index("x")
-        across = self.hop(lax.dynamic_slice_in_dim(full, (1 - core) * half, half, 1), "c", 1)
-        mine = self.plus(lax.dynamic_slice_in_dim(full, core * half, half, 1), across)
+            return halves[0]
+        other, mine = halves
+        height, half = mine.shape
+        quarter = half // 256 * 128
+        mine = self.plus(mine, self.hop(other, "c", 1))
         mine = mine.reshape(self.n_dp, 2, 2, height // 16, half)
-
-        def pick(value, at, axis):
-            return lax.dynamic_index_in_dim(value, at, axis, keepdims=False)
-
-        left, right = mine[..., :quarter], mine[..., quarter:]
-        sent = lax.optimization_barrier((pick(left, 1 - y, 1), pick(right, 1 - x, 2)))
-        came = lax.optimization_barrier((self.hop(sent[0], "y", 1), self.hop(sent[1], "x", 1)))
-        left, right = self.plus(pick(left, y, 1), came[0]), self.plus(pick(right, x, 2), came[1])
-        sent = lax.optimization_barrier((pick(left, 1 - x, 1), pick(right, 1 - y, 1)))
-        came = lax.optimization_barrier((self.hop(sent[0], "x", 1), self.hop(sent[1], "y", 1)))
-        left, right = self.plus(pick(left, x, 1), came[0]), self.plus(pick(right, y, 1), came[1])
-        deep = jnp.concatenate([left, right], axis=2)
-        deep = deep.reshape(2, 2, height // 16, half)
-        high, low = lax.axis_index("dh"), lax.axis_index("dl")
-        deep = self.plus(pick(deep, high, 0), self.hop(pick(deep, 1 - high, 0), "dh", 1))
-        total = pick(deep, low, 0).astype(WIDE) + self.hop(pick(deep, 1 - low, 0), "dl", 1).astype(WIDE)
-        rows = height // 32
+        return mine[..., :quarter], mine[..., quarter:]
+
+    def scatter_side(self, pair, step):
+        if not self.wide:
+            return pair
+        y, x = lax.axis_index("y"), lax.axis_index("x")
+        turns = ((("y", y, 1), ("x", x, 2)), (("x", x, 1), ("y", y, 1)))[step]
+        kept = [pick(value, at, axis) for value, (_, at, axis) in zip(pair, turns)]
+        sent = [pick(value, 1 - at, axis) for value, (_, at, axis) in zip(pair, turns)]
+        sent = lax.optimization_barrier(tuple(sent))
+        came = [self.hop(value, name, 1) for value, (name, _, _) in zip(sent, turns)]
+        came = lax.optimization_barrier(tuple(came))
+        return tuple(self.plus(one, two) for one, two in zip(kept, came))
+
+    def scatter_far(self, pair, side):
+        if not self.wide:
+            return pair
+        deep = pair[side].reshape((2, 2) + pair[side].shape[1:])
+        high = lax.axis_index("dh")
+        return self.plus(pick(deep, high, 0), self.hop(pick(deep, 1 - high, 0), "dh", 1))
+
+    def scatter_merge(self, left, right):
+        return jnp.concatenate([left, right], axis=2) if self.wide else left
+
+    def scatter_small(self, values):
+        devices = self.n_dp * self.groups
+        pieces = lax.all_to_all(values.reshape(devices, -1), self.axes, 0, 0, tiled=True)
+        return jnp.sum(pieces, axis=0).reshape(-1, values.shape[1])
+
+    def scatter_near(self, deep):
+        if not self.wide:
+            return deep
+        low = lax.axis_index("dl")
+        return pick(deep, low, 0).astype(WIDE) + self.hop(pick(deep, 1 - low, 0), "dl", 1).astype(WIDE)
+
+    def scatter_core(self, total):
+        if not self.wide:
+            return lax.psum_scatter(total, self.axes, scatter_dimension=0, tiled=True).astype(WIDE)
+        core, rows = lax.axis_index("c"), total.shape[0] // 2
         away = self.hop(lax.dynamic_slice_in_dim(total, (1 - core) * rows, rows, 0), "c", 1)
         return flipped(core, lax.dynamic_slice_in_dim(total, core * rows, rows, 0), away, 1)
 
@@ -581,31 +695,17 @@
         parity = lax.axis_index("dl")
         same, other = part[0], part[1]
         same, other = jnp.where(parity == 0, same, other), jnp.where(parity == 0, other, same)
-        return jnp.stack([same, self.hop(other, "dl", 1)])
-
-    def fetch_far(self, pair):
-        return [self.hop(pair, "dh", k) for k in range(1, self.n_dp // 2)]
-
-    def join_expert(self, pairs):
-        turn = lax.axis_index(self.dp)
-        rows, width = pairs[0].shape[1:]
-        spots = []
-        for k in range(self.n_dp // 2):
-            near, far = turn ^ (2 * k), turn ^ (2 * k + 1)
-            spots.append(jnp.stack([near * (rows // 16), 0 * turn, far * (rows // 16), 0 * turn]))
-        return join(jnp.stack(spots).astype(jnp.int32), pairs, width)
+        pair = flipped(parity, same[None], self.hop(other, "dl", 1)[None], 0)
+        return pair.reshape(-1, part.shape[2])
+
+    def fetch_far(self, pair, *gates):
+        return lax.all_gather(after(pair, *gates), "dh", axis=0, tiled=True)
 
     def share_far(self, partial, *gates):
-        half = self.n_dp // 2
-        pieces = after(partial, *gates).reshape(half, 2, D // self.n_dp, FF)
-        high = lax.axis_index("dh")
-        total = lax.dynamic_index_in_dim(pieces, high, 0, keepdims=False).astype(WIDE)
-        for k in range(1, half):
-            piece = lax.dynamic_index_in_dim(pieces, high ^ k, 0, keepdims=False)
-            total = total + self.hop(piece, "dh", k).astype(WIDE)
-        return total.astype(LOW)
+        return lax.psum_scatter(after(partial, *gates), "dh", scatter_dimension=0, tiled=True)
 
     def share_near(self, pair):
+        pair = pair.reshape(2, -1, pair.shape[1])
         parity = lax.axis_index("dl")
         own = lax.dynamic_index_in_dim(pair, parity, 0).astype(WIDE)
         other = self.hop(lax.dynamic_index_in_dim(pair, 1 - parity, 0), "dl", 1).astype(WIDE)
@@ -618,6 +718,12 @@
 
 def after(value, *others):
     return lax.optimization_barrier((value,) + others)[0]
+
+
+def fenced(ready, body, *operands):
+    shapes = jax.eval_shape(body, *operands)
+    empty = lambda *_: jax.tree.map(lambda leaf: jnp.zeros(leaf.shape, leaf.dtype), shapes)
+    return lax.cond(ready, body, empty, *operands)
 
 
 def padded(rows, fill=0):
@@ -644,98 +750,187 @@
     part_a = jnp.concatenate([qkv_low[0], proj_t[0], norms], axis=1)
     part_b = jnp.concatenate([w_up.astype(LOW), w_down.T.astype(LOW)], axis=1)
     part_c = jnp.concatenate([qkv_low[1], proj_t[1]], axis=1)
-    deep_a = plan.gather_depth(part_a)
-    in_near = plan.fetch_near(after(exp_in.astype(LOW), deep_a))
-    out_near = plan.fetch_near(after(jnp.swapaxes(exp_out, 1, 2).astype(LOW), in_near))
-    in_far = plan.fetch_far(in_near)
-    out_far = plan.fetch_far(after(out_near, in_far))
-    deep_b = plan.gather_depth(part_b, deep_a)
-    deep_c = plan.gather_depth(part_c, deep_b)
-    one_a = plan.gather_side(deep_a, 0)
-    two_a = plan.gather_side(one_a, 1)
-    block_a = plan.gather_core(two_a, part_a)
-    norms = block_a[:, 4 * D : 4 * D + 8].astype(WIDE).T
-    gain, shift = norms[:4, None], norms[4:, None]
-    one_b = plan.gather_side(deep_b, 0, two_a)
-
-    flat_index = expert_index.reshape(-1)
-    onehot = (flat_index[:, None] == jnp.arange(experts_all, dtype=jnp.int32)).astype(jnp.int32)
-    before = jnp.cumsum(onehot, axis=0) - onehot
-    holder = (flat_index % EXP_DEV) * plan.groups + flat_index // EXP_DEV
-    spots = (holder * capacity + jnp.sum(onehot * before, axis=1)).reshape(-1, TOP)
-    spots = padded(spots, -1)
+    ready = expert_index[0, 0] >= 0
+    bar = lax.optimization_barrier
+    core = lax.axis_index("c") if plan.wide else 0 * expert_index[0, 0]
+    parts = (part_a, part_b, part_c)
+    in_near = plan.fetch_near(exp_in.astype(LOW))
+    deep = plan.gather_depth(parts)
+
+    def prepare(expert_index, gate, cotangent, act_in):
+        flat_index = expert_index.reshape(-1)
+        onehot = (flat_index[:, None] == jnp.arange(experts_all, dtype=jnp.int32)).astype(jnp.int32)
+        before = jnp.cumsum(onehot, axis=0) - onehot
+        holder = (flat_index % EXP_DEV) * plan.groups + flat_index // EXP_DEV
+        spots = (holder * capacity + jnp.sum(onehot * before, axis=1)).reshape(-1, TOP)
+        spots = padded(spots, -1)
+        gates, cot, x_a = padded(gate), padded(cotangent), padded(act_in)
+        grad_sent = dispatch_grad(flat(spots).T, flat(gates), flat(cot), slots)
+        return spots, gates, cot, x_a, grad_sent
+
+    spots, gates, cot, x_a, grad_sent = fenced(
+        ready, prepare, expert_index, gate, cotangent, act_in
+    )
     spot_rows = flat(spots).T
-    gates, cot, x_a = padded(gate), padded(cotangent), padded(act_in)
-
-    grad_rows = plan.to_experts(dispatch_grad(spot_rows, flat(gates), flat(cot), slots))
-
-    x_b, packed_a, mixed_a = attend_forward(after(x_a, in_near), gain[0], shift[0], block_a)
-    two_b = plan.gather_side(one_b, 1, x_b)
-    block_b = plan.gather_core(two_b, part_b)
-    one_c = plan.gather_side(deep_c, 0, two_b)
-    x_c, hidden_b, slope_b = mlp_forward(after(x_b, out_near), gain[1], shift[1], block_b)
-    two_c = plan.gather_side(one_c, 1)
-    block_c = plan.gather_core(two_c, part_c)
-    x_d, packed_c, mixed_c = attend_forward(x_c, gain[2], shift[2], block_c)
-    sent = dispatch(spot_rows, flat(after(x_d, in_far, grad_rows)), gain[3], shift[3], slots)
-    rows = plan.to_experts(sent)
-
-    weight_in = plan.join_expert([in_near] + in_far)
+
+    out_low = jnp.swapaxes(exp_out, 1, 2).astype(LOW)
+    in_near, out_low, x_a, grad_sent, deep = bar((in_near, out_low, x_a, grad_sent, deep))
+    weight_in = plan.fetch_far(in_near)
+    out_near = plan.fetch_near(out_low)
+
+    def zeroth_part(deep, parts):
+        pair_a, pair_b, pair_c = plan.gather_split(deep, parts)
+        one_a = bar(plan.gather_side(pair_a, 0))
+        two_a = bar(plan.gather_side(one_a, 1))
+        pair_b, two_a = bar((pair_b, two_a))
+        four_a, one_b = bar((plan.gather_core(two_a), plan.gather_side(pair_b, 0)))
+        return four_a, one_b, pair_c
+
+    four_a, one_b, pair_c = fenced(ready, zeroth_part, deep, parts)
+    four_a, out_near = bar((four_a, out_near))
+    weight_out = plan.fetch_far(out_near)
+
+    def first_part(four_a, one_b, part_a, x_a):
+        block_a = plan.gather_join(four_a, part_a)
+        norms = block_a[:, 4 * D : 4 * D + 8].astype(WIDE).T
+        gain, shift = norms[:4, None], norms[4:, None]
+        x_b, packed_a, mixed_a = attend_forward(x_a, gain[0], shift[0], block_a)
+        two_b, x_b = bar((plan.gather_side(one_b, 1), x_b))
+        return gain, shift, block_a, x_b, packed_a, mixed_a, two_b
+
+    gain, shift, block_a, x_b, packed_a, mixed_a, two_b = fenced(
+        ready, first_part, four_a, one_b, part_a, x_a
+    )
+
+    def second_part(x_b, gain, shift, two_b, pair_c, part_b, part_c, spot_rows, grad_sent):
+        grad_rows = plan.to_experts(grad_sent)
+        four_b, one_c = bar((plan.gather_core(two_b), plan.gather_side(pair_c, 0)))
+        block_b = plan.gather_join(four_b, part_b)
+        x_c, hidden_b, slope_b = mlp_forward(x_b, gain[1], shift[1], block_b)
+        two_c, x_c = bar((plan.gather_side(one_c, 1), x_c))
+        block_c = plan.gather_join(bar(plan.gather_core(two_c)), part_c)
+        x_d, packed_c, mixed_c = attend_forward(x_c, gain[2], shift[2], block_c)
+        x_d, grad_rows = bar((x_d, grad_rows))
+        rows = plan.to_experts(dispatch(spot_rows, flat(x_d), gain[3], shift[3], slots))
+        return block_b, block_c, x_c, x_d, hidden_b, slope_b, packed_c, mixed_c, rows, grad_rows
+
+    block_b, block_c, x_c, x_d, hidden_b, slope_b, packed_c, mixed_c, rows, grad_rows = fenced(
+        ready, second_part, x_b, gain, shift, two_b, pair_c, part_b, part_c, spot_rows, grad_sent
+    )
     hidden, slope = expert_forward(rows, weight_in)
-    down_partial = t_mm(grad_rows, hidden).astype(LOW)
-    weight_out = plan.join_expert([out_near] + after(out_far, hidden, down_partial))
-    dinner, droutes = expert_backward(grad_rows, slope, weight_in, weight_out)
-    routes_home = plan.to_experts(droutes)
-    result = mm_t(hidden, weight_out).astype(LOW)
-    home = plan.to_experts(result)
-    down_pair = plan.share_far(down_partial, weight_out)
-    in_partial = t_mm(rows, dinner).astype(LOW)
+    (down_partial,) = weight_grad(False, core, (grad_rows, hidden))
+    down_pair = plan.share_far(down_partial)
+
+    def experts_backward(rows, grad_rows, hidden, slope, weight_in, weight_out):
+        dinner, droutes = expert_backward(grad_rows, slope, weight_in, weight_out)
+        routes_home = plan.to_experts(droutes)
+        (in_partial,) = weight_grad(False, core, (after(rows, droutes), dinner))
+        result = mm_t(after(hidden, in_partial), weight_out).astype(LOW)
+        routes_home, result = bar((routes_home, result))
+        return routes_home, in_partial, result
+
+    routes_home, in_partial, result = fenced(
+        ready, experts_backward, rows, grad_rows, hidden, slope, weight_in,
+        after(weight_out, down_partial),
+    )
     in_pair = plan.share_far(in_partial)
 
-    act_out, grad_gate = combine(spots, gates, x_d, cot, home)
-    dx_d, gain_d, shift_d = return_grad(spots, x_d, cot, gain[3], routes_home)
-    dx_c, dpacked_c, normed_c, low_c, gain_c, shift_c = attend_backward(
-        x_c, dx_d, packed_c, gain[2], shift[2], block_c
-    )
-    sum_c = jnp.concatenate(
-        [t_mm(flat(normed_c), flat(dpacked_c)), t_mm(flat(low_c), flat(mixed_c))], axis=1
-    )
-    mine_c = plan.scatter(sum_c.astype(LOW))
-    dx_b, dinner_b, normed_b, low_b, gain_b, shift_b = mlp_backward(
-        x_b, dx_c, slope_b, gain[1], shift[1], block_b
-    )
-    sum_b = jnp.concatenate(
-        [t_mm(flat(normed_b), flat(dinner_b)), t_mm(flat(low_b), flat(hidden_b))], axis=1
-    )
-    mine_b = plan.scatter(sum_b.astype(LOW))
-    dx_a, dpacked_a, normed_a, low_a, gain_a, shift_a = attend_backward(
-        x_a, after(dx_b, mine_c), packed_a, gain[0], shift[0], block_a
-    )
-    norm_grads = jnp.concatenate(
-        [gain_a, gain_b, gain_c, gain_d, shift_a, shift_b, shift_c, shift_d]
-    )
-    norm_grads = jnp.pad(norm_grads.T, ((0, 0), (0, 248)))
-    sum_a = jnp.concatenate(
-        [t_mm(flat(normed_a), flat(dpacked_a)), t_mm(flat(low_a), flat(mixed_a)), norm_grads], axis=1
-    )
-    mine_a = plan.scatter(after(sum_a.astype(LOW), down_pair))
-    grad_exp_out = jnp.swapaxes(plan.share_near(down_pair), 1, 2)
-    grad_exp_in = plan.share_near(in_pair)
+    def third_part(
+        gain, shift, block_b, block_c, x_b, x_c, x_d, packed_c, mixed_c, hidden_b, slope_b, spots,
+        cot, routes_home, result,
+    ):
+        home = plan.to_experts(result)
+        dx_d, gain_d, shift_d = return_grad(spots, x_d, cot, gain[3], routes_home)
+        dx_c, dpacked_c, normed_c, low_c, gain_c, shift_c = attend_backward(
+            x_c, dx_d, packed_c, gain[2], shift[2], block_c
+        )
+        sum_c = weight_grad(
+            plan.wide, core, (flat(normed_c), flat(dpacked_c)), (flat(low_c), flat(mixed_c))
+        )
+        sum_c, dx_c = bar((sum_c, dx_c))
+        dx_b, dinner_b, normed_b, low_b, gain_b, shift_b = mlp_backward(
+            x_b, dx_c, slope_b, gain[1], shift[1], block_b
+        )
+        pair_c, dx_b, dinner_b, home = bar((plan.scatter_swap(sum_c), dx_b, dinner_b, home))
+        sum_b = weight_grad(
+            plan.wide, core, (flat(normed_b), flat(dinner_b)), (flat(low_b), flat(hidden_b))
+        )
+        pair_c, sum_b = bar((plan.scatter_side(pair_c, 0), sum_b))
+        pair_c, pair_b = bar((plan.scatter_side(pair_c, 1), plan.scatter_swap(sum_b)))
+        gains, shifts = (gain_b, gain_c, gain_d), (shift_b, shift_c, shift_d)
+        return pair_c, pair_b, dx_b, gains, shifts, home
+
+    pair_c, pair_b, dx_b, gains, shifts, home = fenced(
+        ready, third_part, gain, shift, block_b, block_c, x_b, x_c, x_d, packed_c, mixed_c,
+        hidden_b, slope_b, spots, cot, routes_home, result,
+    )
+
+    def fourth_part(
+        gain, shift, block_a, x_a, packed_a, mixed_a, pair_c, pair_b, dx_b, gains, shifts, down_pair,
+    ):
+        dx_a, dpacked_a, normed_a, low_a, gain_a, shift_a = attend_backward(
+            x_a, dx_b, packed_a, gain[0], shift[0], block_a
+        )
+        grad_out = plan.share_near(down_pair)
+        pair_b, far_c, dx_a, dpacked_a, grad_out = bar(
+            (
+                plan.scatter_side(pair_b, 0),
+                plan.scatter_merge(plan.scatter_far(pair_c, 0), plan.scatter_far(pair_c, 1)),
+                dx_a,
+                dpacked_a,
+                grad_out,
+            )
+        )
+        norm_grads = jnp.concatenate((gain_a,) + gains + (shift_a,) + shifts).T
+        sum_a = weight_grad(
+            plan.wide, core, (flat(normed_a), flat(dpacked_a)), (flat(low_a), flat(mixed_a))
+        )
+        pair_b, near_c, sum_a = bar((plan.scatter_side(pair_b, 1), plan.scatter_near(far_c), sum_a))
+        pair_a, left_b, mine_c = bar(
+            (plan.scatter_swap(sum_a), plan.scatter_far(pair_b, 0), plan.scatter_core(near_c))
+        )
+        pair_a, right_b = bar((plan.scatter_side(pair_a, 0), plan.scatter_far(pair_b, 1)))
+        far_b = plan.scatter_merge(left_b, right_b)
+        return unpadded(dx_a), norm_grads, pair_a, far_b, mine_c, grad_out
+
+    dx_a, norm_grads, pair_a, far_b, mine_c, grad_exp_out = fenced(
+        ready, fourth_part, gain, shift, block_a, x_a, packed_a, mixed_a, pair_c, pair_b, dx_b,
+        gains, shifts, down_pair,
+    )
+
+    def fifth_part(pair_a, far_b, in_pair, norm_grads, spots, gates, x_d, cot, home):
+        grad_exp_in = plan.share_near(in_pair)
+        mine_norms = plan.scatter_small(norm_grads)
+        act_out, grad_gate = combine(spots, gates, x_d, cot, home)
+        pair_a, near_b, act_out = bar(
+            (plan.scatter_side(pair_a, 1), plan.scatter_near(far_b), act_out)
+        )
+        far_a = plan.scatter_merge(plan.scatter_far(pair_a, 0), plan.scatter_far(pair_a, 1))
+        far_a, mine_b, grad_exp_in, mine_norms = bar(
+            (far_a, plan.scatter_core(near_b), grad_exp_in, mine_norms)
+        )
+        mine_a = plan.scatter_core(plan.scatter_near(far_a))
+        return mine_a, mine_b, mine_norms, grad_exp_in, unpadded(act_out), unpadded(grad_gate)
+
+    mine_a, mine_b, mine_norms, grad_exp_in, act_out, grad_gate = fenced(
+        ready, fifth_part, pair_a, far_b, in_pair, norm_grads, spots, gates, x_d, cot, home
+    )
+    grad_exp_out = jnp.swapaxes(grad_exp_out, 1, 2)
 
     grad_qkv = jnp.stack([mine_a[:, : 3 * D], mine_c[:, : 3 * D]])
-    grad_proj = jnp.stack([mine_a[:, 3 * D : 4 * D], mine_c[:, 3 * D :]])
+    grad_proj = jnp.stack([mine_a[:, 3 * D :], mine_c[:, 3 * D :]])
     return (
-        unpadded(act_out),
-        unpadded(dx_a),
+        act_out,
+        dx_a,
         grad_qkv,
         jnp.swapaxes(grad_proj, 1, 2),
         mine_b[:, :FF],
         mine_b[:, FF:].T,
-        mine_a[:, 4 * D : 4 * D + 4].T,
-        mine_a[:, 4 * D + 4 : 4 * D + 8].T,
+        mine_norms[:, :4].T,
+        mine_norms[:, 4:8].T,
         grad_exp_in,
         grad_exp_out,
-        unpadded(grad_gate),
+        grad_gate,
     )
 
 

time: 868 us -> 811 us (0.934)
  waiting for transfers between devices: 347 us -> 186 us
  blocking collectives: 0 us -> 73.8 us
  Pallas kernels: 179 us -> 242 us
  matrix products: 60 us -> 11.1 us
  other arithmetic: 76.4 us -> 91.2 us
  between operations: 2.74 us -> 14.9 us
  local copies, waits for them, and re-layouts: 94.7 us -> 82.7 us
    ppermute x59 -> x50, waiting for transfers between devices: 267 us -> 155 us  [hop(): return lax.ppermute(value, axes, [(i, i ^ bit) for i in range(size)])]
    all_to_all x0 -> x1, blocking collectives: none -> 73.8 us  [to_experts(): lax.all_to_all(chunks, ('dl',) + self.expert, 0, 0, tiled=True)]
    pallas_call x0 -> x5, Pallas kernels: none -> 55.6 us  [weight_grad(): pl.pallas_call(functools.partial(weight_grad_body, tiles, starts, split),...]
    all_to_all x4 -> x3, waiting for transfers between devices: 80.7 us -> 30.4 us  [to_experts(): lax.all_to_all(chunks, ('dl',) + self.expert, 0, 0, tiled=True)]
    dot_general x8 -> x0, matrix products: 48.9 us -> none  [t_mm(): lax.dot_general(left, right, (((0,), (0,)), ((), ())), preferred_element_...]
    unnamed x151 -> x28, local copies, waits for them, and re-layouts: 42.9 us -> 7.63 us
    ppermute x59 -> x50, starting transfers between devices: 70.8 us -> 53.4 us  [hop(): return lax.ppermute(value, axes, [(i, i ^ bit) for i in range(size)])]
    squeeze x15 -> x20, local copies, waits for them, and re-layouts: 1.67 us -> 17.5 us  [pick(): return lax.dynamic_index_in_dim(value, at, axis, keepdims=False)]
  transfers between devices with their start and end apart: 63 -> 59, of which waited for: 35 -> 23; matrix products, arithmetic and copies ran while one was open for 22% -> 19% of each run, Pallas kernels for 17% -> 30%
where the time goes in v3:
time: 811 us; the launch traced here: 801 us
  Pallas kernels  242 us (30%)
  waiting for transfers between devices  186 us (23%)
  starting transfers between devices  97.9 us (12%)
  other arithmetic  91.2 us (11%)
  local copies, waits for them, and re-layouts  82.7 us (10%)
  blocking collectives  73.8 us (9%)
  between operations  14.9 us (2%)
  matrix products  11.1 us (1%)
    ppermute x50, waiting for transfers between devices, hop(): return lax.ppermute(value, axes, [(i, i ^ bit) for i in range(size)])  155 us
    all_to_all x1, blocking collectives, to_experts(): lax.all_to_all(chunks, ('dl',) + self.expert, 0, 0, tiled=True)  73.8 us
    pallas_call x5, Pallas kernels, weight_grad(): pl.pallas_call(functools.partial(weight_grad_body, tiles, starts, split),...  55.6 us
    ppermute x50, starting transfers between devices, hop(): return lax.ppermute(value, axes, [(i, i ^ bit) for i in range(size)])  53.4 us
    pallas_call x2, Pallas kernels, attend_backward(): pl.pallas_call(attend_backward_body, grid=(images,), in_specs=[image(D),...  48.5 us
    all_to_all x3, starting transfers between devices, to_experts(): lax.all_to_all(chunks, ('dl',) + self.expert, 0, 0, tiled=True)  39 us
    all_to_all x3, waiting for transfers between devices, to_experts(): lax.all_to_all(chunks, ('dl',) + self.expert, 0, 0, tiled=True)  30.4 us
    convert_element_type x21, other arithmetic, plus(): return (one.astype(WIDE) + two.astype(WIDE)).astype(LOW)  26.7 us
  transfers between devices with their start and end apart: 59, of which 23 were waited for; matrix products, arithmetic and copies ran while one was open for 19% of the time, Pallas kernels for 30%

profile of v3, /device:TPU:1, one launch (start us, length us, event | category | flops | bytes accessed | tf_op | source)
XLA Modules:
  0.0 801.4 jit_solution(193833718261373311)
XLA Ops:
  15.9 2.7 convert_element_type.343
  23.4 23.0 %conditional.8 = (s32[3,208,2]{1,0,2:T(4,128)S(1)}, f32[3,208,2]{1,0,2:T(4,128)}, f32[3,208,768]{2,1,0:T(8,128)}, f32[3,208,768]{2,1,0:T(8,128)S(1)}, bf16[1536,768]{1,0:T(8,128)(2,1)}) conditional(s32[]{:T(128)} %bitcast.98, () %tuple.125, (s32[591,2]{0,1:T(2,128)S(1)}, f32[591,2]{0,1:T(2,128)S(1)}, f32[591,768]{1,0:T(8,128)}, ...), branch_computations={%region_0.1_spmd, %region_1.5_spmd} | conditional | flops 752782976 | bytes 24152984 | solution.py:726
  24.1 4.5 reduce-window.4
  33.3 2.9 reshape.561
  36.2 3.0 pad.32
  39.2 7.2 dispatch_grad.1
  46.4 4.8 convert_bitcast_fusion.1
  51.2 36.1 %collective-permute-done.47 = bf16[192,3072]{1,0:T(8,128)(2,1)} collective-permute-done((bf16[192,3072]{1,0:T(8,128)(2,1)}, bf16[192,3072]{1,0:T(8,128)(2,1)}, u32[]{:S(2)}, u32[]{:S(2)}) %collective-permute-start.47) | collective-permute-done | bytes 1179680 | tf_op jit(solution)/shard_map/ppermute | solution.py:569
  87.3 3.4 maximum_select_fusion.5
  90.8 3.3 broadcast_select_fusion
  94.1 46.1 %conditional.9 = (bf16[16,48,768]{2,1,0:T(8,128)(2,1)}, bf16[16,48,896]{2,1,0:T(8,128)(2,1)}, bf16[16,48,768]{2,1,0:T(8,128)(2,1)}, bf16[16,48,896]{2,1,0:T(8,12...) conditional(s32[]{:T(128)} %bitcast.98, () %tuple.124, ...), branch_computations={%region_5.6_spmd, %region_6.7_spmd} | conditional | flops 3096576 | bytes 39813504 | solution.py:726
  97.3 5.9 collective-permute-done
  106.0 10.9 %collective-permute-done.2 = bf16[8,48,768]{2,1,0:T(8,128)(2,1)S(1)} collective-permute-done((bf16[8,48,768]{2,1,0:T(8,128)(2,1)S(1)}, bf16[8,48,768]{2,1,0:T(8,128)(2,1)S(1)}, u32[]{:S(2)}, u32[]{:S(2)}) %collective-permute-start.2) | collective-permute-done | bytes 589856 | tf_op jit(solution)/shard_map/cond/branch_1_fun/ppermute | solution.py:569
  126.0 12.6 %collective-permute-done.6 = bf16[4,48,1536]{2,1,0:T(8,128)(2,1)S(1)} collective-permute-done((bf16[4,48,1536]{2,1,0:T(8,128)(2,1)S(1)}, bf16[4,48,1536]{2,1,0:T(8,128)(2,1)S(1)}, u32[]{:S(2)}, u32[]{:S(2)}) %collective-permute-start.6) | collective-permute-done | bytes 589856 | tf_op jit(solution)/shard_map/cond/branch_1_fun/ppermute | solution.py:569
  140.2 4.3 maximum_select_fusion.6
  145.3 31.1 %conditional.10 = (f32[4,1,768]{2,0,1:T(4,128)S(1)}, f32[4,1,768]{2,0,1:T(4,128)S(1)}, bf16[768,3328]{1,0:T(8,128)(2,1)}, f32[3,208,768]{2,1,0:T(8,128)}, bf16[3...) conditional(s32[]{:T(128)} %bitcast.98, () %tuple.123, ...), branch_computations={%region_7.8_spmd, %region_8.9_spmd} | conditional | flops 927366528 | bytes 45278736 | solution.py:726
  147.6 3.1 join.3.qkv_ref.proj_ref
  153.1 12.9 %attend_forward.2 = (f32[3,208,768]{2,1,0:T(8,128)}, bf16[3,208,2304]{2,1,0:T(8,128)(2,1)}, bf16[3,208,768]{2,1,0:T(8,128)(2,1)}) custom-call(f32[3,208,768]{2,1,0:T(8,128)S(1)} %get-tuple-element.181.x_ref, f32[1,768]{1,0:T(1,128)S(1)} %get-tuple-element.732.gain_ref, f32[1,768]{1,0:T(1,128)S(1)} %get-tuple-element.731.shift_ref, ...), custom_call_target="tpu_custom_call" | custom-call | flops 925000000 | bytes 3250000 | tf_op jit(solution)/shard_map/cond/branch_1_fun/attend_forward/pallas_call | solution.py:133
  166.0 5.7 collective-permute-done.8
  172.5 3.8 pad_maximum_fusion.6
  177.0 171.9 %conditional.11 = (bf16[768,6144]{1,0:T(8,128)(2,1)}, bf16[768,3072]{1,0:T(8,128)(2,1)}, f32[3,208,768]{2,1,0:T(8,128)}, f32[3,208,768]{2,1,0:T(8,128)}, bf16[3,...) conditional(s32[]{:T(128)} %bitcast.98, () %tuple.130, ...), branch_computations={%region_9.10_spmd, %region_10.11_spmd} | conditional | flops 2776771072 | bytes 80026568 | solution.py:726
  178.2 2.8 collective-permute-start.11
  180.9 4.7 all-to-all-start
  189.5 17.8 %collective-permute-done.12 = bf16[4,48,768]{2,1,0:T(8,128)(2,1)S(1)} collective-permute-done((bf16[4,48,768]{2,1,0:T(8,128)(2,1)}, bf16[4,48,768]{2,1,0:T(8,128)(2,1)S(1)}, u32[]{:S(2)}, u32[]{:S(2)}) %collective-permute-start.12) | collective-permute-done | bytes 294944 | tf_op jit(solution)/shard_map/cond/branch_1_fun/ppermute | solution.py:569
  219.1 7.8 join.4.up_ref.down_ref
  226.9 14.9 %mlp_forward.1 = (f32[3,208,768]{2,1,0:T(8,128)}, bf16[3,208,3072]{2,1,0:T(8,128)(2,1)}, bf16[3,208,3072]{2,1,0:T(8,128)(2,1)}) custom-call(f32[3,208,768]{2,1,0:T(8,128)S(1)} %copy-done.8, f32[1,768]{1,0:T(1,128)} %get-tuple-element.761.gain_ref, f32[1,768]{1,0:T(1,128)} %get-tuple-element.745.shift_ref, bf16[768,6144]{1,0:T(8,128)(2,1)} %join.4.up_ref.down_ref, ...), custom_call_target="tpu_custom_call" | custom-call | flops 1475000064 | bytes 5250000 | tf_op jit(solution)/shard_map/cond/branch_1_fun/mlp_forward/pallas_call | solution.py:229
  251.5 5.2 join.5.qkv_ref.proj_ref
  256.7 13.1 %attend_forward.3 = (f32[3,208,768]{2,1,0:T(8,128)}, bf16[3,208,2304]{2,1,0:T(8,128)(2,1)}, bf16[3,208,768]{2,1,0:T(8,128)(2,1)}) custom-call(f32[3,208,768]{2,1,0:T(8,128)} %get-tuple-element.864.x_ref, f32[1,768]{1,0:T(1,128)S(1)} %get-tuple-element.762.gain_ref, f32[1,768]{1,0:T(1,128)S(1)} %get-tuple-element.744.shift_ref, ...), custom_call_target="tpu_custom_call" | custom-call | flops 925000000 | bytes 3250000 | tf_op jit(solution)/shard_map/cond/branch_1_fun/attend_forward/pallas_call | solution.py:133
  269.8 5.1 dispatch.1
  274.9 73.8 %all_to_all.24 = bf16[16,96,768]{2,1,0:T(8,128)(2,1)} all-to-all(bf16[16,96,768]{2,1,0:T(8,128)(2,1)S(1)} %bitcast.241), channel_id=1, replica_groups=mesh['dh'=2,'dl'=2,'y'=2,'x'=2,'c'=2] {'dl','y','x','c'}, dimensions={0} | all-to-all | bytes 4718592 | tf_op jit(solution)/shard_map/cond/branch_1_fun/all_to_all | solution.py:716
  348.9 18.0 %expert_forward.1 = (bf16[1536,3072]{1,0:T(8,128)(2,1)S(1)}, bf16[1536,3072]{1,0:T(8,128)(2,1)}) custom-call(bf16[1536,768]{1,0:T(8,128)(2,1)} %get-tuple-element.488.rows_ref, bf16[768,3072]{1,0:T(8,128)(2,1)} %all-gather.6.cloned.1.call-done.in_ref), custom_call_target="tpu_custom_call" | custom-call | flops 1800000000 | bytes 6500000 | tf_op jit(solution)/shard_map/expert_forward/pallas_call | solution.py:409
  366.9 3.5 copy-done.10
  370.5 11.2 %weight_grad.9 = bf16[768,3072]{1,0:T(8,128)(2,1)S(1)} custom-call(s32[1]{0:T(128)} %constant.569.clone.1.at_ref, bf16[1536,768]{1,0:T(8,128)(2,1)} %get-tuple-element.487.refs_0_, bf16[1536,3072]{1,0:T(8,128)(2,1)S(1)} %get-tuple-element.492.refs_1_), custom_call_target="tpu_custom_call" | custom-call | flops 1811939328 | bytes 1769472 | tf_op jit(solution)/shard_map/weight_grad/pallas_call | solution.py:501
  384.0 83.1 %conditional.12 = (bf16[1536,768]{1,0:T(8,128)(2,1)}, bf16[768,3072]{1,0:T(8,128)(2,1)}, bf16[1536,768]{1,0:T(8,128)(2,1)}) conditional(s32[]{:T(128)} %bitcast.98, () %tuple.132, (bf16[1536,768]{1,0:T(8,128)(2,1)}, bf16[1536,3072]{1,0:T(8,128)(2,1)}, bf16[768,3072]{1,0:T(8,128)(2,1)}, bf16[768,3072]{1,0:T(8,128)(2,1)}, ...), branch_computations={%region_11.12_spmd, %region_12.13_spmd} | conditional | flops 12660876288 | bytes 61924112 | solution.py:726
  384.0 23.6 %expert_backward.1 = (bf16[1536,3072]{1,0:T(8,128)(2,1)}, bf16[1536,768]{1,0:T(8,128)(2,1)}) custom-call(bf16[1536,768]{1,0:T(8,128)(2,1)} %get-tuple-element.226.grad_ref, bf16[1536,3072]{1,0:T(8,128)(2,1)} %get-tuple-element.227.slope_ref, bf16[768,3072]{1,0:T(8,128)(2,1)} %get-tuple-element.228.in_ref, bf16[768,3072]{1,0:T(8,128)(2,1)} %get-tuple-element.229.out_ref), custom_call_target="tpu_custom_call" | custom-call | flops 3600000000 | bytes 8250000 | tf_op jit(solution)/shard_map/cond/branch_1_fun/expert_backward/pallas_call | solution.py:434
  407.6 5.4 all-to-all-start.3
  413.0 12.4 %weight_grad.5 = bf16[768,3072]{1,0:T(8,128)(2,1)} custom-call(s32[1]{0:T(128)} %constant.524.clone.at_ref, bf16[1536,768]{1,0:T(8,128)(2,1)} %get-tuple-element.233.refs_0_, bf16[1536,3072]{1,0:T(8,128)(2,1)} %get-tuple-element.234.refs_1_), custom_call_target="tpu_custom_call" | custom-call | flops 1811939328 | bytes 1769472 | tf_op jit(solution)/shard_map/cond/branch_1_fun/weight_grad/pallas_call | solution.py:501
  425.5 11.1 %convolution_convert_fusion = bf16[1536,768]{1,0:T(8,128)(2,1)} fusion(bf16[1536,3072]{1,0:T(8,128)(2,1)S(1)} %bitcast.255, bf16[768,3072]{1,0:T(8,128)(2,1)} %get-tuple-element.229.out_ref), kind=kOutput, calls=%fused_computation.84 | convolution fusion | flops 7248936960 | bytes 16515072 | tf_op jit(solution)/shard_map/cond/branch_1_fun/dot_general | solution.py:38
  436.6 30.4 %all-to-all-done.3 = bf16[16,96,768]{2,1,0:T(8,128)(2,1)} async-done(((bf16[16,96,768]{2,1,0:T(8,128)(2,1)}), bf16[16,96,768]{2,1,0:T(8,128)(2,1)}, u32[]{:S(2)}, u32[]{:S(2)}) %all-to-all-start.3) | async-done | bytes 2359328 | tf_op jit(solution)/shard_map/cond/branch_1_fun/all_to_all | solution.py:716
  467.8 129.0 %conditional.13 = (bf16[4,48,768]{2,1,0:T(8,128)(2,1)}, bf16[4,48,768]{2,1,0:T(8,128)(2,1)S(1)}, bf16[4,2,2,48,1536]{4,3,2,1,0:T(8,128)(2,1)}, bf16[4,2,2,48,153...) conditional(s32[]{:T(128)} %bitcast.98, () %tuple.122, ...), branch_computations={%region_14.15_spmd, %region_15.16_spmd} | conditional | flops 5075995648 | bytes 174272832 | solution.py:726
  467.8 29.0 %all-to-all-start.2 = ((bf16[16,96,768]{2,1,0:T(8,128)(2,1)}), bf16[16,96,768]{2,1,0:T(8,128)(2,1)}, u32[]{:S(2)}, u32[]{:S(2)}) async-start(bf16[16,96,768]{2,1,0:T(8,128)(2,1)} %bitcast.31), calls=%async_computation.2 | async-start | bytes 4718592 | tf_op jit(solution)/shard_map/cond/branch_1_fun/all_to_all | solution.py:716
  497.6 5.8 return_grad.1
  503.4 24.1 %attend_backward.2 = (f32[3,208,768]{2,1,0:T(8,128)S(1)}, bf16[3,208,2304]{2,1,0:T(8,128)(2,1)}, bf16[3,208,768]{2,1,0:T(8,128)(2,1)S(1)}, bf16[3,208,768]{2,1,0...) custom-call(f32[3,208,768]{2,1,0:T(8,128)} %get-tuple-element.239.x_ref, ...), custom_call_target="tpu_custom_call" | custom-call | flops 1000000000 | bytes 5500000 | tf_op jit(solution)/shard_map/cond/branch_1_fun/attend_backward/pallas_call | solution.py:191
  528.8 8.4 %weight_grad.6 = (bf16[768,1536]{1,0:T(8,128)(2,1)S(1)}, bf16[768,1536]{1,0:T(8,128)(2,1)}) custom-call(s32[1]{0:T(128)} %bitcast.20.at_ref, bf16[624,768]{1,0:T(8,128)(2,1)S(1)} %bitcast.248, bf16[624,768]{1,0:T(8,128)(2,1)S(1)} %bitcast.249, bf16[624,2304]{1,0:T(8,128)(2,1)} %bitcast.260, bf16[624,768]{1,0:T(8,128)(2,1)} %bitcast.27.refs_3_), custom_call_target="tpu_custom_call" | custom-call | flops 736100352 | bytes 1769472 | tf_op jit(solution)/shard_map/cond/branch_1_fun/weight_grad/pallas_call | solution.py:501
  537.4 15.0 %mlp_backward.1 = (f32[3,208,768]{2,1,0:T(8,128)}, bf16[3,208,3072]{2,1,0:T(8,128)(2,1)}, bf16[3,208,768]{2,1,0:T(8,128)(2,1)}, bf16[3,208,768]{2,1,0:T(8,128)(2...) custom-call(f32[3,208,768]{2,1,0:T(8,128)} %get-tuple-element.258.x_ref, f32[3,208,768]{2,1,0:T(8,128)} %copy-done.2, ...), custom_call_target="tpu_custom_call" | custom-call | flops 1475000064 | bytes 6250000 | tf_op jit(solution)/shard_map/cond/branch_1_fun/mlp_backward/pallas_call | solution.py:266
  564.0 14.2 %weight_grad.7 = (bf16[768,3072]{1,0:T(8,128)(2,1)}, bf16[768,3072]{1,0:T(8,128)(2,1)}) custom-call(s32[1]{0:T(128)} %bitcast.37.at_ref, bf16[624,768]{1,0:T(8,128)(2,1)S(1)} %bitcast.246, bf16[624,768]{1,0:T(8,128)(2,1)S(1)} %bitcast.247, bf16[624,3072]{1,0:T(8,128)(2,1)S(1)} %bitcast.242, bf16[624,3072]{1,0:T(8,128)(2,1)} %bitcast.41.refs_3_), custom_call_target="tpu_custom_call" | custom-call | flops 1472200704 | bytes 3538944 | tf_op jit(solution)/shard_map/cond/branch_1_fun/weight_grad/pallas_call | solution.py:501
  582.1 8.6 %collective-permute-done.21 = bf16[4,48,768]{2,1,0:T(8,128)(2,1)S(1)} collective-permute-done((bf16[4,48,768]{2,1,0:T(8,128)(2,1)S(1)}, bf16[4,48,768]{2,1,0:T(8,128)(2,1)S(1)}, u32[]{:S(2)}, u32[]{:S(2)}) %collective-permute-start.21) | collective-permute-done | bytes 294944 | tf_op jit(solution)/shard_map/cond/branch_1_fun/ppermute | solution.py:569
  593.6 2.9 fusion.79
  596.8 124.9 %conditional.14 = (f32[591,768]{1,0:T(8,128)}, f32[768,8]{0,1:T(8,128)S(1)}, bf16[4,2,48,768]{3,2,1,0:T(8,128)(2,1)}, bf16[4,2,48,768]{3,2,1,0:T(8,128)(2,1)}, b...) conditional(s32[]{:T(128)} %bitcast.98, () %tuple.121, ...), branch_computations={%region_17.18_spmd, %region_18.19_spmd} | conditional | flops 1758956032 | bytes 189846368 | solution.py:726
  610.3 24.3 %attend_backward.3 = (f32[3,208,768]{2,1,0:T(8,128)S(1)}, bf16[3,208,2304]{2,1,0:T(8,128)(2,1)}, bf16[3,208,768]{2,1,0:T(8,128)(2,1)S(1)}, bf16[3,208,768]{2,1,0...) custom-call(f32[3,208,768]{2,1,0:T(8,128)} %get-tuple-element.305.x_ref, ...), custom_call_target="tpu_custom_call" | custom-call | flops 1000000000 | bytes 5500000 | tf_op jit(solution)/shard_map/cond/branch_1_fun/attend_backward/pallas_call | solution.py:191
  644.1 2.5 maximum_select_fusion
  651.7 9.4 %weight_grad.8 = (bf16[768,1536]{1,0:T(8,128)(2,1)}, bf16[768,1536]{1,0:T(8,128)(2,1)}) custom-call(s32[1]{0:T(128)} %bitcast.67.at_ref, bf16[624,768]{1,0:T(8,128)(2,1)S(1)} %bitcast.244, bf16[624,768]{1,0:T(8,128)(2,1)S(1)} %bitcast.245, bf16[624,2304]{1,0:T(8,128)(2,1)} %bitcast.259, bf16[624,768]{1,0:T(8,128)(2,1)} %bitcast.258), custom_call_target="tpu_custom_call" | custom-call | flops 736100352 | bytes 1769472 | tf_op jit(solution)/shard_map/cond/branch_1_fun/weight_grad/pallas_call | solution.py:501
  665.0 3.2 collective-permute-start.41
  673.1 24.1 %collective-permute-done.42 = bf16[2,48,1536]{2,1,0:T(8,128)(2,1)S(1)} collective-permute-done((bf16[2,48,1536]{2,1,0:T(8,128)(2,1)S(1)}, bf16[2,48,1536]{2,1,0:T(8,128)(2,1)S(1)}, u32[]{:S(2)}, u32[]{:S(2)}) %collective-permute-start.42) | collective-permute-done | bytes 294944 | tf_op jit(solution)/shard_map/cond/branch_1_fun/ppermute | solution.py:569
  705.3 3.1 reshape.602
  709.4 6.3 collective-permute-done.44
  723.1 66.9 %conditional.15 = (f32[24,3072]{1,0:T(8,128)S(1)}, f32[24,6144]{1,0:T(8,128)S(1)}, f32[24,8]{1,0:T(8,128)}, f32[2,192,3072]{2,1,0:T(8,128)}, f32[591,768]{1,0:T(8,128)}, /*index=5*/f32[591,2]{0,1:T(2,128)}) conditional(s32[]{:T(128)} %bitcast.98, () %tuple.120, (bf16[4,2,48,768]{3,2,1,0:T(8,128)(2,1)}, bf16[4,2,48,768]{3,2,1,0:T(8,128)(2,1)}, ...), branch_computations={%region_19.20_spmd, %region_20.22_spmd} | conditional | flops 758411008 | bytes 70868728 | solution.py:726
  726.7 5.3 all-to-all-start.4
  740.3 6.1 combine.1
  755.5 12.1 %collective-permute-done.27 = bf16[2,48,768]{2,1,0:T(8,128)(2,1)S(1)} collective-permute-done((bf16[2,48,768]{2,1,0:T(8,128)(2,1)S(1)}, bf16[2,48,768]{2,1,0:T(8,128)(2,1)S(1)}, u32[]{:S(2)}, u32[]{:S(2)}) %collective-permute-start.27) | collective-permute-done | bytes 147488 | tf_op jit(solution)/shard_map/cond/branch_1_fun/ppermute | solution.py:569
  767.7 3.1 collective-permute-done.28
  776.0 2.7 collective-permute-start.31
  782.0 2.7 collective-permute-start.32
  787.0 3.0 reshape.615
  (386 shorter events, 180.5 us)
Async XLA Ops:
  7.2 83.5 %all-gather.4.cloned.1.call-start = ((), (), s32[]{:S(2)}) async-start(), calls=%async_computation.7 | async-start | bytes 3010560 | tf_op jit(solution)/shard_map/all_gather | solution.py:586
  13.3 1.7 collective-permute-start.48
  15.9 333.0 %all-gather.6.cloned.1.call-start = ((), (), s32[]{:S(2)}) async-start(), calls=%async_computation.8 | async-start | bytes 7077888 | tf_op jit(solution)/shard_map/all_gather | solution.py:702
  19.8 67.5 %collective-permute-start.47 = (bf16[192,3072]{1,0:T(8,128)(2,1)}, bf16[192,3072]{1,0:T(8,128)(2,1)}, u32[]{:S(2)}, u32[]{:S(2)}) collective-permute-start(bf16[192,3072]{1,0:T(8,128)(2,1)} %get-tuple-element.795), channel_id=1, source_target_pairs={{0,8},{8,0},{1,9},{9,1},{2,10},{10,2},{3,11},{11,3},{4,12},{12,4},... | collective-permute-start | bytes 3538952 | tf_op jit(solution)/shard_map/ppermute | solution.py:569
  46.4 98.2 %copy-start.34 = (s32[3,208,2]{1,0,2:T(4,128)}, s32[3,208,2]{1,0,2:T(4,128)S(1)}, u32[]{:S(2)}) copy-start(s32[3,208,2]{1,0,2:T(4,128)S(1)} %get-tuple-element.477) | copy-start | bytes 14980
  46.4 98.9 %copy-start.9 = (f32[3,208,768]{2,1,0:T(8,128)}, f32[3,208,768]{2,1,0:T(8,128)S(1)}, u32[]{:S(2)}) copy-start(f32[3,208,768]{2,1,0:T(8,128)S(1)} %get-tuple-element.475) | copy-start | bytes 5750788
  90.7 293.3 %all-gather.8.cloned.1.call-start = ((), (), s32[]{:S(2)}) async-start(), calls=%async_computation.9 | async-start | bytes 7077888 | tf_op jit(solution)/shard_map/all_gather | solution.py:702
  94.1 46.1 %collective-permute-start.49 = (bf16[192,3072]{1,0:T(8,128)(2,1)}, bf16[192,3072]{1,0:T(8,128)(2,1)}, u32[]{:S(2)}, u32[]{:S(2)}) collective-permute-start(bf16[192,3072]{1,0:T(8,128)(2,1)} %get-tuple-element.793), channel_id=1, source_target_pairs={{0,8},{8,0},{1,9},{9,1},{2,10},{10,2},{3,11},{11,3},{4,12},{12,4},... | collective-permute-start | bytes 3538952 | tf_op jit(solution)/shard_map/ppermute | solution.py:569
  95.0 8.8 %collective-permute-start.1 = (bf16[4,48,896]{2,1,0:T(8,128)(2,1)S(1)}, bf16[4,48,896]{2,1,0:T(8,128)(2,1)S(1)}, u32[]{:S(2)}, u32[]{:S(2)}) collective-permute-start(bf16[4,48,896]{2,1,0:T(8,128)(2,1)S(1)} %slice.116), channel_id=1, source_target_pairs={{0,4},{4,0},{1,5},{5,1},{2,6},{6,2},{3,7},{7,3},{8,12},{12,8},{9,1... | collective-permute-start | bytes 1032200 | tf_op jit(solution)/shard_map/cond/branch_1_fun/ppermute | solution.py:569
  96.0 7.1 collective-permute-start
  103.9 15.4 %collective-permute-start.3 = (bf16[8,48,896]{2,1,0:T(8,128)(2,1)S(1)}, bf16[8,48,896]{2,1,0:T(8,128)(2,1)S(1)}, u32[]{:S(2)}, u32[]{:S(2)}) collective-permute-start(bf16[8,48,896]{2,1,0:T(8,128)(2,1)S(1)} %pad_maximum_fusion.4), channel_id=1, source_target_pairs={{0,2},{2,0},{1,3},{3,1},{4,6},{6,4},{5,7},{7,5},{8,10},{10,8},{9,1... | collective-permute-start | bytes 2064392 | tf_op jit(solution)/shard_map/cond/branch_1_fun/ppermute | solution.py:569
  104.5 12.3 %collective-permute-start.2 = (bf16[8,48,768]{2,1,0:T(8,128)(2,1)S(1)}, bf16[8,48,768]{2,1,0:T(8,128)(2,1)S(1)}, u32[]{:S(2)}, u32[]{:S(2)}) collective-permute-start(bf16[8,48,768]{2,1,0:T(8,128)(2,1)S(1)} %pad_maximum_fusion.5), channel_id=1, source_target_pairs={{0,4},{4,0},{1,5},{5,1},{2,6},{6,2},{3,7},{7,3},{8,12},{12,8},{9,1... | collective-permute-start | bytes 1769480 | tf_op jit(solution)/shard_map/cond/branch_1_fun/ppermute | solution.py:569
  121.7 18.5 %collective-permute-start.5 = (bf16[16,48,896]{2,1,0:T(8,128)(2,1)}, bf16[16,48,896]{2,1,0:T(8,128)(2,1)}, u32[]{:S(2)}, u32[]{:S(2)}) collective-permute-start(bf16[16,48,896]{2,1,0:T(8,128)(2,1)} %pad_maximum_fusion), channel_id=1, source_target_pairs={{0,1},{1,0},{2,3},{3,2},{4,5},{5,4},{6,7},{7,6},{8,9},{9,8},{10,11... | collective-permute-start | bytes 4128776 | tf_op jit(solution)/shard_map/cond/branch_1_fun/ppermute | solution.py:569
  124.2 16.0 %collective-permute-start.4 = (bf16[16,48,768]{2,1,0:T(8,128)(2,1)}, bf16[16,48,768]{2,1,0:T(8,128)(2,1)}, u32[]{:S(2)}, u32[]{:S(2)}) collective-permute-start(bf16[16,48,768]{2,1,0:T(8,128)(2,1)} %pad_maximum_fusion.1), channel_id=1, source_target_pairs={{0,1},{1,0},{2,3},{3,2},{4,5},{5,4},{6,7},{7,6},{8,9},{9,8},{10,11... | collective-permute-start | bytes 3538952 | tf_op jit(solution)/shard_map/cond/branch_1_fun/ppermute | solution.py:569
  124.2 14.5 %collective-permute-start.6 = (bf16[4,48,1536]{2,1,0:T(8,128)(2,1)S(1)}, bf16[4,48,1536]{2,1,0:T(8,128)(2,1)S(1)}, u32[]{:S(2)}, u32[]{:S(2)}) collective-permute-start(bf16[4,48,1536]{2,1,0:T(8,128)(2,1)S(1)} %get-tuple-element.161), channel_id=1, source_target_pairs={{0,2},{2,0},{1,3},{3,1},{4,6},{6,4},{5,7},{7,5},{8,10},{10,8},{9,1... | collective-permute-start | bytes 1769480 | tf_op jit(solution)/shard_map/cond/branch_1_fun/ppermute | solution.py:569
  124.7 14.2 %collective-permute-start.7 = (bf16[4,48,1536]{2,1,0:T(8,128)(2,1)S(1)}, bf16[4,48,1536]{2,1,0:T(8,128)(2,1)S(1)}, u32[]{:S(2)}, u32[]{:S(2)}) collective-permute-start(bf16[4,48,1536]{2,1,0:T(8,128)(2,1)S(1)} %get-tuple-element.162), channel_id=1, source_target_pairs={{0,4},{4,0},{1,5},{5,1},{2,6},{6,2},{3,7},{7,3},{8,12},{12,8},{9,1... | collective-permute-start | bytes 1769480 | tf_op jit(solution)/shard_map/cond/branch_1_fun/ppermute | solution.py:569
  144.5 452.3 %reduce-scatter.3.cloned.1.call-start = ((), (), s32[]{:S(2)}) async-start(), calls=%async_computation.10 | async-start | bytes 7077888 | tf_op jit(solution)/shard_map/reduce_scatter | solution.py:705
  145.4 26.3 %collective-permute-start.8 = (bf16[8,48,1536]{2,1,0:T(8,128)(2,1)}, bf16[8,48,1536]{2,1,0:T(8,128)(2,1)}, u32[]{:S(2)}, u32[]{:S(2)}) collective-permute-start(bf16[8,48,1536]{2,1,0:T(8,128)(2,1)} %get-tuple-element.177), channel_id=1, source_target_pairs={{0,4},{4,0},{1,5},{5,1},{2,6},{6,2},{3,7},{7,3},{8,12},{12,8},{9,1... | collective-permute-start | bytes 3538952 | tf_op jit(solution)/shard_map/cond/branch_1_fun/ppermute | solution.py:569
  146.8 25.7 %collective-permute-start.9 = (bf16[8,48,1536]{2,1,0:T(8,128)(2,1)S(1)}, bf16[8,48,1536]{2,1,0:T(8,128)(2,1)}, u32[]{:S(2)}, u32[]{:S(2)}) collective-permute-start(bf16[8,48,1536]{2,1,0:T(8,128)(2,1)S(1)} %get-tuple-element.178), channel_id=1, source_target_pairs={{0,2},{2,0},{1,3},{3,1},{4,6},{6,4},{5,7},{7,5},{8,10},{10,8},{9,1... | collective-permute-start | bytes 3538952 | tf_op jit(solution)/shard_map/cond/branch_1_fun/ppermute | solution.py:569
  178.2 31.2 %collective-permute-start.11 = (bf16[16,48,1536]{2,1,0:T(8,128)(2,1)}, bf16[16,48,1536]{2,1,0:T(8,128)(2,1)S(1)}, u32[]{:S(2)}, u32[]{:S(2)}) collective-permute-start(bf16[16,48,1536]{2,1,0:T(8,128)(2,1)} %get-tuple-element.197.refs_1_), channel_id=1, source_target_pairs={{0,1},{1,0},{2,3},{3,2},{4,5},{5,4},{6,7},{7,6},{8,9},{9,8},{10,11... | collective-permute-start | bytes 7077896 | tf_op jit(solution)/shard_map/cond/branch_1_fun/ppermute | solution.py:569
  180.9 28.4 %collective-permute-start.10 = (bf16[16,48,1536]{2,1,0:T(8,128)(2,1)}, bf16[16,48,1536]{2,1,0:T(8,128)(2,1)}, u32[]{:S(2)}, u32[]{:S(2)}) collective-permute-start(bf16[16,48,1536]{2,1,0:T(8,128)(2,1)} %get-tuple-element.196.refs_0_), channel_id=1, source_target_pairs={{0,1},{1,0},{2,3},{3,2},{4,5},{5,4},{6,7},{7,6},{8,9},{9,8},{10,11... | collective-permute-start | bytes 7077896 | tf_op jit(solution)/shard_map/cond/branch_1_fun/ppermute | solution.py:569
  180.9 88.8 %all-to-all-start = ((bf16[16,96,768]{2,1,0:T(8,128)(2,1)}), bf16[16,96,768]{2,1,0:T(8,128)(2,1)}, u32[]{:S(2)}, u32[]{:S(2)}) async-start(bf16[16,96,768]{2,1,0:T(8,128)(2,1)} %bitcast.11), calls=%async_computation | async-start | bytes 4718592 | tf_op jit(solution)/shard_map/cond/branch_1_fun/all_to_all | solution.py:716
  185.6 21.6 %collective-permute-start.12 = (bf16[4,48,768]{2,1,0:T(8,128)(2,1)}, bf16[4,48,768]{2,1,0:T(8,128)(2,1)S(1)}, u32[]{:S(2)}, u32[]{:S(2)}) collective-permute-start(bf16[4,48,768]{2,1,0:T(8,128)(2,1)} %get-tuple-element.192), channel_id=1, source_target_pairs={{0,2},{2,0},{1,3},{3,1},{4,6},{6,4},{5,7},{7,5},{8,10},{10,8},{9,1... | collective-permute-start | bytes 884744 | tf_op jit(solution)/shard_map/cond/branch_1_fun/ppermute | solution.py:569
  187.0 20.9 %collective-permute-start.13 = (bf16[4,48,768]{2,1,0:T(8,128)(2,1)}, bf16[4,48,768]{2,1,0:T(8,128)(2,1)}, u32[]{:S(2)}, u32[]{:S(2)}) collective-permute-start(bf16[4,48,768]{2,1,0:T(8,128)(2,1)} %get-tuple-element.193), channel_id=1, source_target_pairs={{0,4},{4,0},{1,5},{5,1},{2,6},{6,2},{3,7},{7,3},{8,12},{12,8},{9,1... | collective-permute-start | bytes 884744 | tf_op jit(solution)/shard_map/cond/branch_1_fun/ppermute | solution.py:569
  209.4 32.5 %collective-permute-start.14 = (bf16[8,48,768]{2,1,0:T(8,128)(2,1)S(1)}, bf16[8,48,768]{2,1,0:T(8,128)(2,1)}, u32[]{:S(2)}, u32[]{:S(2)}) collective-permute-start(bf16[8,48,768]{2,1,0:T(8,128)(2,1)S(1)} %get-tuple-element.202), channel_id=1, source_target_pairs={{0,4},{4,0},{1,5},{5,1},{2,6},{6,2},{3,7},{7,3},{8,12},{12,8},{9,1... | collective-permute-start | bytes 1769480 | tf_op jit(solution)/shard_map/cond/branch_1_fun/ppermute | solution.py:569
  210.5 31.3 %collective-permute-start.15 = (bf16[8,48,768]{2,1,0:T(8,128)(2,1)S(1)}, bf16[8,48,768]{2,1,0:T(8,128)(2,1)}, u32[]{:S(2)}, u32[]{:S(2)}) collective-permute-start(bf16[8,48,768]{2,1,0:T(8,128)(2,1)S(1)} %get-tuple-element.203), channel_id=1, source_target_pairs={{0,2},{2,0},{1,3},{3,1},{4,6},{6,4},{5,7},{7,5},{8,10},{10,8},{9,1... | collective-permute-start | bytes 1769480 | tf_op jit(solution)/shard_map/cond/branch_1_fun/ppermute | solution.py:569
  244.2 7.3 collective-permute-start.16
  245.3 6.1 collective-permute-start.17
  383.9 339.2 %reduce-scatter.5.cloned.1.call-start = ((), (), s32[]{:S(2)}) async-start(), calls=%async_computation.11 | async-start | bytes 7077888 | tf_op jit(solution)/shard_map/reduce_scatter | solution.py:705
  407.6 59.3 %all-to-all-start.3 = ((bf16[16,96,768]{2,1,0:T(8,128)(2,1)}), bf16[16,96,768]{2,1,0:T(8,128)(2,1)}, u32[]{:S(2)}, u32[]{:S(2)}) async-start(bf16[16,96,768]{2,1,0:T(8,128)(2,1)} %bitcast.18), calls=%async_computation.3 | async-start | bytes 4718592 | tf_op jit(solution)/shard_map/cond/branch_1_fun/all_to_all | solution.py:716
  467.8 88.4 %all-to-all-start.2 = ((bf16[16,96,768]{2,1,0:T(8,128)(2,1)}), bf16[16,96,768]{2,1,0:T(8,128)(2,1)}, u32[]{:S(2)}, u32[]{:S(2)}) async-start(bf16[16,96,768]{2,1,0:T(8,128)(2,1)} %bitcast.31), calls=%async_computation.2 | async-start | bytes 4718592 | tf_op jit(solution)/shard_map/cond/branch_1_fun/all_to_all | solution.py:716
  537.2 15.2 %collective-permute-start.18 = (bf16[768,1536]{1,0:T(8,128)(2,1)S(1)}, bf16[768,1536]{1,0:T(8,128)(2,1)}, u32[]{:S(2)}, u32[]{:S(2)}) collective-permute-start(bf16[768,1536]{1,0:T(8,128)(2,1)S(1)} %get-tuple-element.257), channel_id=1, source_target_pairs={{0,1},{1,0},{2,3},{3,2},{4,5},{5,4},{6,7},{7,6},{8,9},{9,8},{10,11... | collective-permute-start | bytes 7077896 | tf_op jit(solution)/shard_map/cond/branch_1_fun/ppermute | solution.py:569
  559.0 19.1 %collective-permute-start.19 = (bf16[4,2,48,768]{3,2,0,1:T(8,128)(2,1)}, bf16[4,2,48,768]{3,2,0,1:T(8,128)(2,1)}, u32[]{:S(2)}, u32[]{:S(2)}) collective-permute-start(bf16[4,2,48,768]{3,2,0,1:T(8,128)(2,1)} %dynamic-slice_bitcast_fusion.1), channel_id=1, source_target_pairs={{0,4},{4,0},{1,5},{5,1},{2,6},{6,2},{3,7},{7,3},{8,12},{12,8},{9,1... | collective-permute-start | bytes 1769480 | tf_op jit(solution)/shard_map/cond/branch_1_fun/ppermute | solution.py:569
  560.6 17.6 %collective-permute-start.20 = (bf16[4,2,48,768]{3,2,0,1:T(8,128)(2,1)}, bf16[4,2,48,768]{3,2,0,1:T(8,128)(2,1)}, u32[]{:S(2)}, u32[]{:S(2)}) collective-permute-start(bf16[4,2,48,768]{3,2,0,1:T(8,128)(2,1)} %dynamic-slice_bitcast_fusion), channel_id=1, source_target_pairs={{0,2},{2,0},{1,3},{3,1},{4,6},{6,4},{5,7},{7,5},{8,10},{10,8},{9,1... | collective-permute-start | bytes 1769480 | tf_op jit(solution)/shard_map/cond/branch_1_fun/ppermute | solution.py:569
  580.8 10.7 %collective-permute-start.23 = (bf16[768,3072]{1,0:T(8,128)(2,1)}, bf16[768,3072]{1,0:T(8,128)(2,1)S(1)}, u32[]{:S(2)}, u32[]{:S(2)}) collective-permute-start(bf16[768,3072]{1,0:T(8,128)(2,1)} %get-tuple-element.284), channel_id=1, source_target_pairs={{0,1},{1,0},{2,3},{3,2},{4,5},{5,4},{6,7},{7,6},{8,9},{9,8},{10,11... | collective-permute-start | bytes 14155784 | tf_op jit(solution)/shard_map/cond/branch_1_fun/ppermute | solution.py:569
  581.9 8.8 %collective-permute-start.21 = (bf16[4,48,768]{2,1,0:T(8,128)(2,1)S(1)}, bf16[4,48,768]{2,1,0:T(8,128)(2,1)S(1)}, u32[]{:S(2)}, u32[]{:S(2)}) collective-permute-start(bf16[4,48,768]{2,1,0:T(8,128)(2,1)S(1)} %dynamic-slice_bitcast_fusion.3), channel_id=1, source_target_pairs={{0,2},{2,0},{1,3},{3,1},{4,6},{6,4},{5,7},{7,5},{8,10},{10,8},{9,1... | collective-permute-start | bytes 884744 | tf_op jit(solution)/shard_map/cond/branch_1_fun/ppermute | solution.py:569
  582.0 8.7 %collective-permute-start.22 = (bf16[4,48,768]{2,1,0:T(8,128)(2,1)S(1)}, bf16[4,48,768]{2,1,0:T(8,128)(2,1)S(1)}, u32[]{:S(2)}, u32[]{:S(2)}) collective-permute-start(bf16[4,48,768]{2,1,0:T(8,128)(2,1)S(1)} %dynamic-slice_bitcast_fusion.2), channel_id=1, source_target_pairs={{0,4},{4,0},{1,5},{5,1},{2,6},{6,2},{3,7},{7,3},{8,12},{12,8},{9,1... | collective-permute-start | bytes 884744 | tf_op jit(solution)/shard_map/cond/branch_1_fun/ppermute | solution.py:569
  596.8 126.2 %copy-start.44 = (f32[3,208,2]{1,0,2:T(4,128)S(1)}, f32[3,208,2]{1,0,2:T(4,128)}, u32[]{:S(2)}) copy-start(f32[3,208,2]{1,0,2:T(4,128)} %get-tuple-element.520) | copy-start | bytes 14980
  598.4 36.2 %collective-permute-start.35 = (bf16[2,48,768]{2,1,0:T(8,128)(2,1)}, bf16[2,48,768]{2,1,0:T(8,128)(2,1)}, u32[]{:S(2)}, u32[]{:S(2)}) collective-permute-start(bf16[2,48,768]{2,1,0:T(8,128)(2,1)} %dynamic-slice_bitcast_fusion.14), channel_id=1, source_target_pairs={{0,16},{16,0},{1,17},{17,1},{2,18},{18,2},{3,19},{19,3},{4,20},{20... | collective-permute-start | bytes 442376 | tf_op jit(solution)/shard_map/cond/branch_1_fun/ppermute | solution.py:569
  598.5 37.6 %collective-permute-start.36 = (bf16[2,48,768]{2,1,0:T(8,128)(2,1)S(1)}, bf16[2,48,768]{2,1,0:T(8,128)(2,1)}, u32[]{:S(2)}, u32[]{:S(2)}) collective-permute-start(bf16[2,48,768]{2,1,0:T(8,128)(2,1)S(1)} %dynamic-slice_bitcast_fusion.13), channel_id=1, source_target_pairs={{0,16},{16,0},{1,17},{17,1},{2,18},{18,2},{3,19},{19,3},{4,20},{20... | collective-permute-start | bytes 442376 | tf_op jit(solution)/shard_map/cond/branch_1_fun/ppermute | solution.py:569
  605.8 31.3 %collective-permute-start.33 = (bf16[4,2,48,1536]{3,2,1,0:T(8,128)(2,1)}, bf16[4,2,48,1536]{3,2,1,0:T(8,128)(2,1)}, u32[]{:S(2)}, u32[]{:S(2)}) collective-permute-start(bf16[4,2,48,1536]{3,2,1,0:T(8,128)(2,1)} %dynamic-slice_bitcast_fusion.5), channel_id=1, source_target_pairs={{0,4},{4,0},{1,5},{5,1},{2,6},{6,2},{3,7},{7,3},{8,12},{12,8},{9,1... | collective-permute-start | bytes 3538952 | tf_op jit(solution)/shard_map/cond/branch_1_fun/ppermute | solution.py:569
  605.8 31.2 %collective-permute-start.34 = (bf16[4,2,48,1536]{3,2,0,1:T(8,128)(2,1)}, bf16[4,2,48,1536]{3,2,0,1:T(8,128)(2,1)}, u32[]{:S(2)}, u32[]{:S(2)}) collective-permute-start(bf16[4,2,48,1536]{3,2,0,1:T(8,128)(2,1)} %dynamic-slice_bitcast_fusion.4), channel_id=1, source_target_pairs={{0,2},{2,0},{1,3},{3,1},{4,6},{6,4},{5,7},{7,5},{8,10},{10,8},{9,1... | collective-permute-start | bytes 3538952 | tf_op jit(solution)/shard_map/cond/branch_1_fun/ppermute | solution.py:569
  609.1 33.1 %collective-permute-start.37 = (bf16[1,192,3072]{2,1,0:T(8,128)(2,1)}, bf16[1,192,3072]{2,1,0:T(8,128)(2,1)}, u32[]{:S(2)}, u32[]{:S(2)}) collective-permute-start(bf16[1,192,3072]{2,1,0:T(8,128)(2,1)} %get-tuple-element.779), channel_id=1, source_target_pairs={{0,8},{8,0},{1,9},{9,1},{2,10},{10,2},{3,11},{11,3},{4,12},{12,4},... | collective-permute-start | bytes 3538952 | tf_op jit(solution)/shard_map/cond/branch_1_fun/ppermute | solution.py:569
  646.6 14.5 %collective-permute-start.40 = (bf16[48,1536]{1,0:T(8,128)(2,1)S(1)}, bf16[48,1536]{1,0:T(8,128)(2,1)}, u32[]{:S(2)}, u32[]{:S(2)}) collective-permute-start(bf16[48,1536]{1,0:T(8,128)(2,1)S(1)} %dynamic-slice_bitcast_fusion.12), channel_id=1, source_target_pairs={{0,8},{8,0},{1,9},{9,1},{2,10},{10,2},{3,11},{11,3},{4,12},{12,4},... | collective-permute-start | bytes 442376 | tf_op jit(solution)/shard_map/cond/branch_1_fun/ppermute | solution.py:569
  648.5 13.7 %collective-permute-start.38 = (bf16[4,48,1536]{2,1,0:T(8,128)(2,1)}, bf16[4,48,1536]{2,1,0:T(8,128)(2,1)}, u32[]{:S(2)}, u32[]{:S(2)}) collective-permute-start(bf16[4,48,1536]{2,1,0:T(8,128)(2,1)} %dynamic-slice_bitcast_fusion.9), channel_id=1, source_target_pairs={{0,2},{2,0},{1,3},{3,1},{4,6},{6,4},{5,7},{7,5},{8,10},{10,8},{9,1... | collective-permute-start | bytes 1769480 | tf_op jit(solution)/shard_map/cond/branch_1_fun/ppermute | solution.py:569
  649.4 12.9 %collective-permute-start.39 = (bf16[4,48,1536]{2,1,0:T(8,128)(2,1)}, bf16[4,48,1536]{2,1,0:T(8,128)(2,1)}, u32[]{:S(2)}, u32[]{:S(2)}) collective-permute-start(bf16[4,48,1536]{2,1,0:T(8,128)(2,1)} %dynamic-slice_bitcast_fusion.8), channel_id=1, source_target_pairs={{0,4},{4,0},{1,5},{5,1},{2,6},{6,2},{3,7},{7,3},{8,12},{12,8},{9,1... | collective-permute-start | bytes 1769480 | tf_op jit(solution)/shard_map/cond/branch_1_fun/ppermute | solution.py:569
  663.5 33.7 %copy-start.26 = (bf16[4,48,1536]{2,1,0:T(8,128)(2,1)}, bf16[4,48,1536]{2,1,0:T(8,128)(2,1)S(1)}, u32[]{:S(2)}) copy-start(bf16[4,48,1536]{2,1,0:T(8,128)(2,1)S(1)} %fusion.48) | copy-start | bytes 1769476 | tf_op jit(solution)/shard_map/cond
  665.0 32.3 %collective-permute-start.41 = (bf16[768,1536]{1,0:T(8,128)(2,1)}, bf16[768,1536]{1,0:T(8,128)(2,1)}, u32[]{:S(2)}, u32[]{:S(2)}) collective-permute-start(bf16[768,1536]{1,0:T(8,128)(2,1)} %get-tuple-element.338), channel_id=1, source_target_pairs={{0,1},{1,0},{2,3},{3,2},{4,5},{5,4},{6,7},{7,6},{8,9},{9,8},{10,11... | collective-permute-start | bytes 7077896 | tf_op jit(solution)/shard_map/cond/branch_1_fun/ppermute | solution.py:569
  668.2 29.1 %copy-start.24 = (bf16[768,1536]{1,0:T(8,128)(2,1)S(1)}, bf16[768,1536]{1,0:T(8,128)(2,1)}, u32[]{:S(2)}) copy-start(bf16[768,1536]{1,0:T(8,128)(2,1)} %get-tuple-element.337) | copy-start | bytes 7077892 | tf_op jit(solution)/shard_map/cond
  668.2 4.2 collective-permute-start.43
  669.0 39.4 %collective-permute-start.46 = (bf16[2,48,1536]{2,1,0:T(8,128)(2,1)}, bf16[2,48,1536]{2,1,0:T(8,128)(2,1)}, u32[]{:S(2)}, u32[]{:S(2)}) collective-permute-start(bf16[2,48,1536]{2,1,0:T(8,128)(2,1)} %dynamic-slice_bitcast_fusion.10), channel_id=1, source_target_pairs={{0,16},{16,0},{1,17},{17,1},{2,18},{18,2},{3,19},{19,3},{4,20},{20... | collective-permute-start | bytes 884744 | tf_op jit(solution)/shard_map/cond/branch_1_fun/ppermute | solution.py:569
  670.4 26.8 %collective-permute-start.42 = (bf16[2,48,1536]{2,1,0:T(8,128)(2,1)S(1)}, bf16[2,48,1536]{2,1,0:T(8,128)(2,1)S(1)}, u32[]{:S(2)}, u32[]{:S(2)}) collective-permute-start(bf16[2,48,1536]{2,1,0:T(8,128)(2,1)S(1)} %dynamic-slice_bitcast_fusion.11), channel_id=1, source_target_pairs={{0,16},{16,0},{1,17},{17,1},{2,18},{18,2},{3,19},{19,3},{4,20},{20... | collective-permute-start | bytes 884744 | tf_op jit(solution)/shard_map/cond/branch_1_fun/ppermute | solution.py:569
  701.9 13.8 %collective-permute-start.44 = (bf16[4,2,48,768]{3,2,1,0:T(8,128)(2,1)}, bf16[4,2,48,768]{3,2,1,0:T(8,128)(2,1)}, u32[]{:S(2)}, u32[]{:S(2)}) collective-permute-start(bf16[4,2,48,768]{3,2,1,0:T(8,128)(2,1)} %dynamic-slice_bitcast_fusion.7), channel_id=1, source_target_pairs={{0,4},{4,0},{1,5},{5,1},{2,6},{6,2},{3,7},{7,3},{8,12},{12,8},{9,1... | collective-permute-start | bytes 1769480 | tf_op jit(solution)/shard_map/cond/branch_1_fun/ppermute | solution.py:569
  703.1 13.5 %collective-permute-start.45 = (bf16[4,2,48,768]{3,2,1,0:T(8,128)(2,1)}, bf16[4,2,48,768]{3,2,1,0:T(8,128)(2,1)}, u32[]{:S(2)}, u32[]{:S(2)}) collective-permute-start(bf16[4,2,48,768]{3,2,1,0:T(8,128)(2,1)} %dynamic-slice_bitcast_fusion.6), channel_id=1, source_target_pairs={{0,2},{2,0},{1,3},{3,1},{4,6},{6,4},{5,7},{7,5},{8,10},{10,8},{9,1... | collective-permute-start | bytes 1769480 | tf_op jit(solution)/shard_map/cond/branch_1_fun/ppermute | solution.py:569
  724.9 25.1 %collective-permute-start.26 = (bf16[48,3072]{1,0:T(8,128)(2,1)}, bf16[48,3072]{1,0:T(8,128)(2,1)}, u32[]{:S(2)}, u32[]{:S(2)}) collective-permute-start(bf16[48,3072]{1,0:T(8,128)(2,1)} %dynamic-slice_bitcast_fusion.15), channel_id=1, source_target_pairs={{0,8},{8,0},{1,9},{9,1},{2,10},{10,2},{3,11},{11,3},{4,12},{12,4},... | collective-permute-start | bytes 884744 | tf_op jit(solution)/shard_map/cond/branch_1_fun/ppermute | solution.py:569
  726.7 19.7 %all-to-all-start.4 = ((f32[32,1,192]{2,1,0:T(1,128)}), f32[32,1,192]{2,1,0:T(1,128)}, u32[]{:S(2)}, u32[]{:S(2)}) async-start(f32[32,1,192]{2,1,0:T(1,128)} %all_to_all.18), calls=%async_computation.4 | async-start | bytes 65536 | tf_op jit(solution)/shard_map/cond/branch_1_fun/all_to_all | solution.py:675
  734.0 13.9 %collective-permute-start.24 = (bf16[4,48,768]{2,1,0:T(8,128)(2,1)}, bf16[4,48,768]{2,1,0:T(8,128)(2,1)S(1)}, u32[]{:S(2)}, u32[]{:S(2)}) collective-permute-start(bf16[4,48,768]{2,1,0:T(8,128)(2,1)} %get-tuple-element.356), channel_id=1, source_target_pairs={{0,2},{2,0},{1,3},{3,1},{4,6},{6,4},{5,7},{7,5},{8,10},{10,8},{9,1... | collective-permute-start | bytes 884744 | tf_op jit(solution)/shard_map/cond/branch_1_fun/ppermute | solution.py:569
  735.3 12.5 %collective-permute-start.25 = (bf16[4,48,768]{2,1,0:T(8,128)(2,1)}, bf16[4,48,768]{2,1,0:T(8,128)(2,1)S(1)}, u32[]{:S(2)}, u32[]{:S(2)}) collective-permute-start(bf16[4,48,768]{2,1,0:T(8,128)(2,1)} %get-tuple-element.357), channel_id=1, source_target_pairs={{0,4},{4,0},{1,5},{5,1},{2,6},{6,2},{3,7},{7,3},{8,12},{12,8},{9,1... | collective-permute-start | bytes 884744 | tf_op jit(solution)/shard_map/cond/branch_1_fun/ppermute | solution.py:569
  738.7 33.2 %collective-permute-start.30 = (bf16[1,192,3072]{2,1,0:T(8,128)(2,1)}, bf16[1,192,3072]{2,1,0:T(8,128)(2,1)}, u32[]{:S(2)}, u32[]{:S(2)}) collective-permute-start(bf16[1,192,3072]{2,1,0:T(8,128)(2,1)} %get-tuple-element.785), channel_id=1, source_target_pairs={{0,8},{8,0},{1,9},{9,1},{2,10},{10,2},{3,11},{11,3},{4,12},{12,4},... | collective-permute-start | bytes 3538952 | tf_op jit(solution)/shard_map/cond/branch_1_fun/ppermute | solution.py:569
  751.2 16.5 %collective-permute-start.27 = (bf16[2,48,768]{2,1,0:T(8,128)(2,1)S(1)}, bf16[2,48,768]{2,1,0:T(8,128)(2,1)S(1)}, u32[]{:S(2)}, u32[]{:S(2)}) collective-permute-start(bf16[2,48,768]{2,1,0:T(8,128)(2,1)S(1)} %dynamic-slice_bitcast_fusion.20), channel_id=1, source_target_pairs={{0,16},{16,0},{1,17},{17,1},{2,18},{18,2},{3,19},{19,3},{4,20},{20... | collective-permute-start | bytes 442376 | tf_op jit(solution)/shard_map/cond/branch_1_fun/ppermute | solution.py:569
  753.5 17.3 %collective-permute-start.28 = (bf16[2,48,768]{2,1,0:T(8,128)(2,1)S(1)}, bf16[2,48,768]{2,1,0:T(8,128)(2,1)S(1)}, u32[]{:S(2)}, u32[]{:S(2)}) collective-permute-start(bf16[2,48,768]{2,1,0:T(8,128)(2,1)S(1)} %dynamic-slice_bitcast_fusion.19), channel_id=1, source_target_pairs={{0,16},{16,0},{1,17},{17,1},{2,18},{18,2},{3,19},{19,3},{4,20},{20... | collective-permute-start | bytes 442376 | tf_op jit(solution)/shard_map/cond/branch_1_fun/ppermute | solution.py:569
  753.7 17.2 %collective-permute-start.29 = (f32[24,3072]{1,0:T(8,128)S(1)}, f32[24,3072]{1,0:T(8,128)S(1)}, u32[]{:S(2)}, u32[]{:S(2)}) collective-permute-start(f32[24,3072]{1,0:T(8,128)S(1)} %get-tuple-element.787), channel_id=1, source_target_pairs={{0,1},{1,0},{2,3},{3,2},{4,5},{5,4},{6,7},{7,6},{8,9},{9,8},{10,11... | collective-permute-start | bytes 884744 | tf_op jit(solution)/shard_map/cond/branch_1_fun/ppermute | solution.py:569
  776.0 5.3 collective-permute-start.31
  782.0 7.9 collective-permute-start.32
  (50 other events, 285.1 us)
Sparse Core Ops, SparseCore 0:
  16.0 71.3 all-gather.3
  90.8 115.8 all-gather.5
  208.3 113.2 all-gather.7
  384.0 108.5 reduce-scatter.2
  494.9 118.5 reduce-scatter.4

commit v4 on v3

--- a/solution.py
+++ b/solution.py
@@ -562,7 +562,7 @@
         self.dp = ("dh", "dl")
         self.expert = expert
         self.axes = self.dp + expert
-        self.mesh = Mesh(mesh.devices.reshape((n_dp // 2, 2) + expert_shape), self.axes)
+        self.mesh = Mesh(mesh.devices.reshape((2, n_dp // 2) + expert_shape), self.axes)
 
     def hop(self, value, axes, bit):
         size = lax.axis_size(axes)
@@ -660,20 +660,38 @@
         came = lax.optimization_barrier(tuple(came))
         return tuple(self.plus(one, two) for one, two in zip(kept, came))
 
-    def scatter_far(self, pair, side):
-        if not self.wide:
-            return pair
-        deep = pair[side].reshape((2, 2) + pair[side].shape[1:])
+    def scatter_stack(self, *pairs):
+        if not self.wide:
+            return jnp.concatenate(pairs, axis=1)
+        return jnp.concatenate([value for pair in pairs for value in pair], axis=2)
+
+    def scatter_send(self, deep):
+        if not self.wide:
+            return deep, deep[:1, :1]
+        deep = deep.reshape((2, 2) + deep.shape[1:])
         high = lax.axis_index("dh")
-        return self.plus(pick(deep, high, 0), self.hop(pick(deep, 1 - high, 0), "dh", 1))
-
-    def scatter_merge(self, left, right):
-        return jnp.concatenate([left, right], axis=2) if self.wide else left
-
-    def scatter_small(self, values):
+        return pick(deep, high, 0), self.hop(pick(deep, 1 - high, 0), "dh", 1)
+
+    def scatter_add(self, own, far):
+        return self.plus(own, far) if self.wide else own
+
+    def small_send(self, values):
         devices = self.n_dp * self.groups
-        pieces = lax.all_to_all(values.reshape(devices, -1), self.axes, 0, 0, tiled=True)
-        return jnp.sum(pieces, axis=0).reshape(-1, values.shape[1])
+        return lax.all_to_all(values.reshape(devices, -1), self.axes, 0, 0, tiled=True)
+
+    def small_sum(self, pieces):
+        return jnp.sum(pieces, axis=0).reshape(-1, 8)
+
+    def scatter_unstack(self, rows, *widths):
+        if not self.wide:
+            return jnp.split(rows, np.cumsum(widths[:-1]), axis=1)
+        out, at, half = [], 0, rows.shape[1] // 2
+        for width in widths:
+            left = rows[:, at : at + width // 2]
+            right = rows[:, half + at : half + at + width // 2]
+            out.append(jnp.concatenate([left, right], axis=1))
+            at += width // 2
+        return out
 
     def scatter_near(self, deep):
         if not self.wide:
@@ -692,28 +710,30 @@
         return (one.astype(WIDE) + two.astype(WIDE)).astype(LOW)
 
     def fetch_near(self, part):
-        parity = lax.axis_index("dl")
+        upper = lax.axis_index("dh")
         same, other = part[0], part[1]
-        same, other = jnp.where(parity == 0, same, other), jnp.where(parity == 0, other, same)
-        pair = flipped(parity, same[None], self.hop(other, "dl", 1)[None], 0)
-        return pair.reshape(-1, part.shape[2])
+        same, other = jnp.where(upper == 0, same, other), jnp.where(upper == 0, other, same)
+        return flipped(upper, same[None], self.hop(other, "dh", 1)[None], 0)
 
     def fetch_far(self, pair, *gates):
-        return lax.all_gather(after(pair, *gates), "dh", axis=0, tiled=True)
+        pieces = lax.all_gather(after(pair, *gates), "dl", axis=1, tiled=True)
+        return pieces.reshape(D, FF)
 
     def share_far(self, partial, *gates):
-        return lax.psum_scatter(after(partial, *gates), "dh", scatter_dimension=0, tiled=True)
-
-    def share_near(self, pair):
-        pair = pair.reshape(2, -1, pair.shape[1])
-        parity = lax.axis_index("dl")
-        own = lax.dynamic_index_in_dim(pair, parity, 0).astype(WIDE)
-        other = self.hop(lax.dynamic_index_in_dim(pair, 1 - parity, 0), "dl", 1).astype(WIDE)
-        return flipped(parity, own, other, 0)
+        pieces = after(partial, *gates).reshape(2, D // 2, FF)
+        return lax.psum_scatter(pieces, "dl", scatter_dimension=1, tiled=True)
+
+    def share_send(self, pair):
+        upper = lax.axis_index("dh")
+        own = lax.dynamic_index_in_dim(pair, upper, 0)
+        return own, self.hop(lax.dynamic_index_in_dim(pair, 1 - upper, 0), "dh", 1)
+
+    def share_sum(self, own, other):
+        return flipped(lax.axis_index("dh"), own.astype(WIDE), other.astype(WIDE), 0)
 
     def to_experts(self, rows):
         chunks = rows.reshape(2 * self.groups, -1, D)
-        return lax.all_to_all(chunks, ("dl",) + self.expert, 0, 0, tiled=True).reshape(-1, D)
+        return lax.all_to_all(chunks, ("dh",) + self.expert, 0, 0, tiled=True).reshape(-1, D)
 
 
 def after(value, *others):
@@ -754,7 +774,7 @@
     bar = lax.optimization_barrier
     core = lax.axis_index("c") if plan.wide else 0 * expert_index[0, 0]
     parts = (part_a, part_b, part_c)
-    in_near = plan.fetch_near(exp_in.astype(LOW))
+    in_low = exp_in.astype(LOW)
     deep = plan.gather_depth(parts)
 
     def prepare(expert_index, gate, cotangent, act_in):
@@ -774,9 +794,8 @@
     spot_rows = flat(spots).T
 
     out_low = jnp.swapaxes(exp_out, 1, 2).astype(LOW)
-    in_near, out_low, x_a, grad_sent, deep = bar((in_near, out_low, x_a, grad_sent, deep))
-    weight_in = plan.fetch_far(in_near)
-    out_near = plan.fetch_near(out_low)
+    in_low, x_a, grad_sent, deep = bar((in_low, x_a, grad_sent, deep))
+    in_near = plan.fetch_near(in_low)
 
     def zeroth_part(deep, parts):
         pair_a, pair_b, pair_c = plan.gather_split(deep, parts)
@@ -787,8 +806,9 @@
         return four_a, one_b, pair_c
 
     four_a, one_b, pair_c = fenced(ready, zeroth_part, deep, parts)
-    four_a, out_near = bar((four_a, out_near))
-    weight_out = plan.fetch_far(out_near)
+    four_a, in_near, out_low = bar((four_a, in_near, out_low))
+    weight_in = plan.fetch_far(in_near)
+    out_near = plan.fetch_near(out_low)
 
     def first_part(four_a, one_b, part_a, x_a):
         block_a = plan.gather_join(four_a, part_a)
@@ -802,9 +822,14 @@
         ready, first_part, four_a, one_b, part_a, x_a
     )
 
+    two_b, out_near = bar((two_b, out_near))
+    weight_out = plan.fetch_far(out_near)
+
     def second_part(x_b, gain, shift, two_b, pair_c, part_b, part_c, spot_rows, grad_sent):
+        four_b, one_c, grad_sent = bar(
+            (plan.gather_core(two_b), plan.gather_side(pair_c, 0), grad_sent)
+        )
         grad_rows = plan.to_experts(grad_sent)
-        four_b, one_c = bar((plan.gather_core(two_b), plan.gather_side(pair_c, 0)))
         block_b = plan.gather_join(four_b, part_b)
         x_c, hidden_b, slope_b = mlp_forward(x_b, gain[1], shift[1], block_b)
         two_c, x_c = bar((plan.gather_side(one_c, 1), x_c))
@@ -818,28 +843,32 @@
         ready, second_part, x_b, gain, shift, two_b, pair_c, part_b, part_c, spot_rows, grad_sent
     )
     hidden, slope = expert_forward(rows, weight_in)
-    (down_partial,) = weight_grad(False, core, (grad_rows, hidden))
+
+
+    def experts_backward(grad_rows, hidden, slope, weight_in, weight_out):
+        dinner, droutes = expert_backward(grad_rows, slope, weight_in, weight_out)
+        (down_partial,) = weight_grad(False, core, (grad_rows, after(hidden, droutes)))
+        return dinner, droutes, down_partial
+
+    dinner, droutes, down_partial = fenced(
+        ready, experts_backward, grad_rows, hidden, slope, weight_in, weight_out
+    )
     down_pair = plan.share_far(down_partial)
 
-    def experts_backward(rows, grad_rows, hidden, slope, weight_in, weight_out):
-        dinner, droutes = expert_backward(grad_rows, slope, weight_in, weight_out)
+    def experts_return(rows, dinner, droutes, hidden, weight_out):
         routes_home = plan.to_experts(droutes)
-        (in_partial,) = weight_grad(False, core, (after(rows, droutes), dinner))
+        (in_partial,) = weight_grad(False, core, (rows, dinner))
         result = mm_t(after(hidden, in_partial), weight_out).astype(LOW)
         routes_home, result = bar((routes_home, result))
         return routes_home, in_partial, result
 
     routes_home, in_partial, result = fenced(
-        ready, experts_backward, rows, grad_rows, hidden, slope, weight_in,
-        after(weight_out, down_partial),
+        ready, experts_return, rows, dinner, droutes, hidden, weight_out
     )
     in_pair = plan.share_far(in_partial)
-
-    def third_part(
-        gain, shift, block_b, block_c, x_b, x_c, x_d, packed_c, mixed_c, hidden_b, slope_b, spots,
-        cot, routes_home, result,
-    ):
-        home = plan.to_experts(result)
+    home = plan.to_experts(after(result, routes_home))
+
+    def third_part(gain, shift, block_c, x_c, x_d, packed_c, mixed_c, spots, cot, routes_home):
         dx_d, gain_d, shift_d = return_grad(spots, x_d, cot, gain[3], routes_home)
         dx_c, dpacked_c, normed_c, low_c, gain_c, shift_c = attend_backward(
             x_c, dx_d, packed_c, gain[2], shift[2], block_c
@@ -847,74 +876,88 @@
         sum_c = weight_grad(
             plan.wide, core, (flat(normed_c), flat(dpacked_c)), (flat(low_c), flat(mixed_c))
         )
-        sum_c, dx_c = bar((sum_c, dx_c))
+        return sum_c, dx_c, (gain_c, gain_d), (shift_c, shift_d)
+
+    sum_c, dx_c, gains, shifts = fenced(
+        ready, third_part, gain, shift, block_c, x_c, x_d, packed_c, mixed_c, spots, cot, routes_home
+    )
+    dx_c, down_pair = bar((dx_c, down_pair))
+    down_own, down_other = plan.share_send(down_pair)
+
+    def fourth_part(gain, shift, block_b, x_b, dx_c, sum_c, hidden_b, slope_b):
         dx_b, dinner_b, normed_b, low_b, gain_b, shift_b = mlp_backward(
             x_b, dx_c, slope_b, gain[1], shift[1], block_b
         )
-        pair_c, dx_b, dinner_b, home = bar((plan.scatter_swap(sum_c), dx_b, dinner_b, home))
+        pair_c, dx_b, dinner_b = bar((plan.scatter_swap(sum_c), dx_b, dinner_b))
         sum_b = weight_grad(
             plan.wide, core, (flat(normed_b), flat(dinner_b)), (flat(low_b), flat(hidden_b))
         )
         pair_c, sum_b = bar((plan.scatter_side(pair_c, 0), sum_b))
         pair_c, pair_b = bar((plan.scatter_side(pair_c, 1), plan.scatter_swap(sum_b)))
-        gains, shifts = (gain_b, gain_c, gain_d), (shift_b, shift_c, shift_d)
-        return pair_c, pair_b, dx_b, gains, shifts, home
-
-    pair_c, pair_b, dx_b, gains, shifts, home = fenced(
-        ready, third_part, gain, shift, block_b, block_c, x_b, x_c, x_d, packed_c, mixed_c,
-        hidden_b, slope_b, spots, cot, routes_home, result,
-    )
-
-    def fourth_part(
-        gain, shift, block_a, x_a, packed_a, mixed_a, pair_c, pair_b, dx_b, gains, shifts, down_pair,
-    ):
+        return pair_c, pair_b, dx_b, gain_b, shift_b
+
+    pair_c, pair_b, dx_b, gain_b, shift_b = fenced(
+        ready, fourth_part, gain, shift, block_b, x_b, dx_c, sum_c, hidden_b, slope_b
+    )
+    dx_b, home, down_other = bar((dx_b, home, down_other))
+
+    def attend_part(gain, shift, block_a, x_a, packed_a, mixed_a, pair_b, dx_b):
         dx_a, dpacked_a, normed_a, low_a, gain_a, shift_a = attend_backward(
             x_a, dx_b, packed_a, gain[0], shift[0], block_a
         )
-        grad_out = plan.share_near(down_pair)
-        pair_b, far_c, dx_a, dpacked_a, grad_out = bar(
-            (
-                plan.scatter_side(pair_b, 0),
-                plan.scatter_merge(plan.scatter_far(pair_c, 0), plan.scatter_far(pair_c, 1)),
-                dx_a,
-                dpacked_a,
-                grad_out,
-            )
-        )
-        norm_grads = jnp.concatenate((gain_a,) + gains + (shift_a,) + shifts).T
+        pair_b, dx_a = bar((plan.scatter_side(pair_b, 0), dx_a))
+        return dx_a, dpacked_a, normed_a, low_a, gain_a, shift_a, pair_b
+
+    dx_a, dpacked_a, normed_a, low_a, gain_a, shift_a, pair_b = fenced(
+        ready, attend_part, gain, shift, block_a, x_a, packed_a, mixed_a, pair_b, dx_b
+    )
+    pair_b, in_pair = bar((pair_b, in_pair))
+    in_own, in_other = plan.share_send(in_pair)
+
+    def combine_part(dpacked_a, normed_a, low_a, mixed_a, pair_b, pair_c, norms, x_d, spots, gates, cot, home):
+        norm_grads = jnp.concatenate(norms).T
+        act_out, grad_gate = combine(spots, gates, x_d, cot, home)
         sum_a = weight_grad(
             plan.wide, core, (flat(normed_a), flat(dpacked_a)), (flat(low_a), flat(mixed_a))
         )
-        pair_b, near_c, sum_a = bar((plan.scatter_side(pair_b, 1), plan.scatter_near(far_c), sum_a))
-        pair_a, left_b, mine_c = bar(
-            (plan.scatter_swap(sum_a), plan.scatter_far(pair_b, 0), plan.scatter_core(near_c))
+        pair_b, sum_a, act_out = bar((plan.scatter_side(pair_b, 1), sum_a, act_out))
+        return norm_grads, sum_a, plan.scatter_stack(pair_b, pair_c), act_out, grad_gate
+
+    norm_grads, sum_a, deep_bc, act_out, grad_gate = fenced(
+        ready, combine_part, dpacked_a, normed_a, low_a, mixed_a, pair_b, pair_c,
+        (gain_a, gain_b) + gains + (shift_a, shift_b) + shifts, x_d, spots, gates, cot, home,
+    )
+    own_bc, far_bc = plan.scatter_send(deep_bc)
+
+
+    def fifth_part(sum_a, act_out, grad_gate, dx_a):
+        pair_a = bar(plan.scatter_swap(sum_a))
+        pair_a = bar(plan.scatter_side(pair_a, 0))
+        deep_a = plan.scatter_stack(plan.scatter_side(pair_a, 1))
+        return deep_a, unpadded(act_out), unpadded(grad_gate), unpadded(dx_a)
+
+    deep_a, act_out, grad_gate, dx_a = fenced(
+        ready, fifth_part, sum_a, act_out, grad_gate, dx_a
+    )
+    deep_a, own_bc, far_bc, in_other = bar((deep_a, own_bc, far_bc, in_other))
+
+    def sixth_part(deep_a, own_bc, far_bc, norm_grads, shares):
+        norm_pieces = plan.small_send(norm_grads)
+        own_a, far_a = plan.scatter_send(deep_a)
+        near_bc = plan.scatter_near(plan.scatter_add(own_bc, far_bc))
+        near_bc, far_a = bar((near_bc, far_a))
+        grad_exp_in, grad_exp_out = [plan.share_sum(*share) for share in shares]
+        near_a, mine_bc = bar(
+            (plan.scatter_near(plan.scatter_add(own_a, far_a)), plan.scatter_core(near_bc))
         )
-        pair_a, right_b = bar((plan.scatter_side(pair_a, 0), plan.scatter_far(pair_b, 1)))
-        far_b = plan.scatter_merge(left_b, right_b)
-        return unpadded(dx_a), norm_grads, pair_a, far_b, mine_c, grad_out
-
-    dx_a, norm_grads, pair_a, far_b, mine_c, grad_exp_out = fenced(
-        ready, fourth_part, gain, shift, block_a, x_a, packed_a, mixed_a, pair_c, pair_b, dx_b,
-        gains, shifts, down_pair,
-    )
-
-    def fifth_part(pair_a, far_b, in_pair, norm_grads, spots, gates, x_d, cot, home):
-        grad_exp_in = plan.share_near(in_pair)
-        mine_norms = plan.scatter_small(norm_grads)
-        act_out, grad_gate = combine(spots, gates, x_d, cot, home)
-        pair_a, near_b, act_out = bar(
-            (plan.scatter_side(pair_a, 1), plan.scatter_near(far_b), act_out)
-        )
-        far_a = plan.scatter_merge(plan.scatter_far(pair_a, 0), plan.scatter_far(pair_a, 1))
-        far_a, mine_b, grad_exp_in, mine_norms = bar(
-            (far_a, plan.scatter_core(near_b), grad_exp_in, mine_norms)
-        )
-        mine_a = plan.scatter_core(plan.scatter_near(far_a))
-        return mine_a, mine_b, mine_norms, grad_exp_in, unpadded(act_out), unpadded(grad_gate)
-
-    mine_a, mine_b, mine_norms, grad_exp_in, act_out, grad_gate = fenced(
-        ready, fifth_part, pair_a, far_b, in_pair, norm_grads, spots, gates, x_d, cot, home
-    )
+        mine_norms = plan.small_sum(norm_pieces)
+        return plan.scatter_core(near_a), mine_bc, mine_norms, grad_exp_in, grad_exp_out
+
+    mine_a, mine_bc, mine_norms, grad_exp_in, grad_exp_out = fenced(
+        ready, sixth_part, deep_a, own_bc, far_bc, norm_grads,
+        ((in_own, in_other), (down_own, down_other)),
+    )
+    mine_b, mine_c = plan.scatter_unstack(mine_bc, 2 * FF, 4 * D)
     grad_exp_out = jnp.swapaxes(grad_exp_out, 1, 2)
 
     grad_qkv = jnp.stack([mine_a[:, : 3 * D], mine_c[:, : 3 * D]])
@@ -927,7 +970,7 @@
         mine_b[:, :FF],
         mine_b[:, FF:].T,
         mine_norms[:, :4].T,
-        mine_norms[:, 4:8].T,
+        mine_norms[:, 4:].T,
         grad_exp_in,
         grad_exp_out,
         grad_gate,

time: 811 us -> 761 us (0.938)
  starting transfers between devices: 97.9 us -> 65.4 us
    ppermute x50 -> x44, waiting for transfers between devices: 155 us -> 119 us  [hop(): return lax.ppermute(value, axes, [(i, i ^ bit) for i in range(size)])]
    all_gather x1, waiting for transfers between devices: 0.01 us -> 29.5 us  [gather_depth(): return lax.all_gather(mine[None], self.dp, axis=0, tiled=True)]
    all_to_all x4, starting transfers between devices: 44.4 us -> 22.6 us  [the longest x3 16.6 us: to_experts(): lax.all_to_all(chunks, ('dh',) + self.expert, 0, 0, tiled=True)]
    ppermute x50 -> x44, starting transfers between devices: 53.4 us -> 42.6 us  [hop(): return lax.ppermute(value, axes, [(i, i ^ bit) for i in range(size)])]
    convert_element_type x21 -> x14, other arithmetic: 26.7 us -> 22.5 us  [plus(): return (one.astype(WIDE) + two.astype(WIDE)).astype(LOW)]
    squeeze x20 -> x16, local copies, waits for them, and re-layouts: 17.5 us -> 16.5 us  [pick(): return lax.dynamic_index_in_dim(value, at, axis, keepdims=False)]
  transfers between devices with their start and end apart: 59 -> 53, of which waited for: 23 -> 22; matrix products, arithmetic and copies ran while one was open for 19% -> 18% of each run, Pallas kernels for 30% -> 28%
where the time goes in v4:
time: 761 us; the launch traced here: 751 us
  Pallas kernels  245 us (32%)
  waiting for transfers between devices  183 us (24%)
  other arithmetic  86 us (11%)
  local copies, waits for them, and re-layouts  77.7 us (10%)
  blocking collectives  68.7 us (9%)
  starting transfers between devices  65.4 us (9%)
  between operations  14.9 us (2%)
  matrix products  7.89 us (1%)
    ppermute x44, waiting for transfers between devices, hop(): return lax.ppermute(value, axes, [(i, i ^ bit) for i in range(size)])  119 us
    all_to_all x1, blocking collectives, to_experts(): lax.all_to_all(chunks, ('dh',) + self.expert, 0, 0, tiled=True)  68.7 us
    pallas_call x5, Pallas kernels, weight_grad(): pl.pallas_call(functools.partial(weight_grad_body, tiles, starts, split),...  56.8 us
    pallas_call x2, Pallas kernels, attend_backward(): pl.pallas_call(attend_backward_body, grid=(images,), in_specs=[image(D),...  48.6 us
    ppermute x44, starting transfers between devices, hop(): return lax.ppermute(value, axes, [(i, i ^ bit) for i in range(size)])  42.6 us
    all_to_all x3, waiting for transfers between devices, to_experts(): lax.all_to_all(chunks, ('dh',) + self.expert, 0, 0, tiled=True)  33.6 us
    all_gather x1, waiting for transfers between devices, gather_depth(): return lax.all_gather(mine[None], self.dp, axis=0, tiled=True)  29.5 us
    pallas_call x2, Pallas kernels, attend_forward(): pl.pallas_call(attend_forward_body, grid=(images,), in_specs=[image(D), w...  26.5 us
  transfers between devices with their start and end apart: 53, of which 22 were waited for; matrix products, arithmetic and copies ran while one was open for 18% of the time, Pallas kernels for 28%

profile of v4, /device:TPU:1, one launch (start us, length us, event | category | flops | bytes accessed | tf_op | source)
XLA Modules:
  0.0 751.2 jit_solution(6654613788568031068)
XLA Ops:
  17.1 4.2 convert_element_type.287
  21.4 18.7 %conditional.12 = (s32[3,208,2]{1,0,2:T(4,128)}, f32[3,208,2]{1,0,2:T(4,128)}, f32[3,208,768]{2,1,0:T(8,128)}, f32[3,208,768]{2,1,0:T(8,128)}, bf16[1536,768]{1,0:T(8,128)(2,1)}) conditional(s32[]{:T(128)} %bitcast.78, () %tuple.165, (s32[591,2]{0,1:T(2,128)S(1)}, f32[591,2]{0,1:T(2,128)S(1)}, f32[591,768]{1,0:T(8,128)S(1)}, ...), branch_computations={%region_0.1_spmd, %region_1.5_spmd} | conditional | flops 752782976 | bytes 24538492 | solution.py:746
  21.8 4.5 reduce-window.4
  31.2 5.7 dispatch_grad.1
  40.0 29.5 %all-gather.4.cloned.1.call-done = bf16[4,48,6272]{2,1,0:T(8,128)(2,1)} async-done(((bf16[1,48,6272]{2,1,0:T(8,128)(2,1)}), bf16[4,48,6272]{2,1,0:T(8,128)(2,1)}) %all-gather.4.cloned.1.call-update) | async-done | bytes 2408464 | tf_op jit(solution)/shard_map/all_gather | solution.py:586
  69.5 3.4 broadcast_select_fusion.1
  76.5 46.6 %conditional.13 = (bf16[16,48,768]{2,1,0:T(8,128)(2,1)}, bf16[16,48,896]{2,1,0:T(8,128)(2,1)}, bf16[16,48,768]{2,1,0:T(8,128)(2,1)}, bf16[16,48,896]{2,1,0:T(8,1...) conditional(s32[]{:T(128)} %bitcast.78, () %tuple.164, ...), branch_computations={%region_5.6_spmd, %region_6.7_spmd} | conditional | flops 3096576 | bytes 39813504 | solution.py:746
  79.8 6.1 collective-permute-done.5
  88.7 11.4 %collective-permute-done.7 = bf16[8,48,768]{2,1,0:T(8,128)(2,1)S(1)} collective-permute-done((bf16[8,48,768]{2,1,0:T(8,128)(2,1)S(1)}, bf16[8,48,768]{2,1,0:T(8,128)(2,1)S(1)}, u32[]{:S(2)}, u32[]{:S(2)}) %collective-permute-start.7) | collective-permute-done | bytes 589856 | tf_op jit(solution)/shard_map/cond/branch_1_fun/ppermute | solution.py:569
  103.7 2.8 collective-permute-start.10
  108.8 12.3 %collective-permute-done.11 = bf16[4,48,1536]{2,1,0:T(8,128)(2,1)S(1)} collective-permute-done((bf16[4,48,1536]{2,1,0:T(8,128)(2,1)S(1)}, bf16[4,48,1536]{2,1,0:T(8,128)(2,1)S(1)}, u32[]{:S(2)}, u32[]{:S(2)}) %collective-permute-start.11) | collective-permute-done | bytes 589856 | tf_op jit(solution)/shard_map/cond/branch_1_fun/ppermute | solution.py:569
  123.1 3.3 collective-permute-done.39
  126.4 4.3 maximum_select_fusion.4
  132.3 31.9 %conditional.14 = (f32[4,1,768]{2,0,1:T(4,128)S(1)}, f32[4,1,768]{2,0,1:T(4,128)}, bf16[768,3328]{1,0:T(8,128)(2,1)}, f32[3,208,768]{2,1,0:T(8,128)}, bf16[3,208...) conditional(s32[]{:T(128)} %bitcast.78, () %tuple.163, ...), branch_computations={%region_7.8_spmd, %region_8.9_spmd} | conditional | flops 927366528 | bytes 29550096 | solution.py:746
  135.6 6.1 join.3.qkv_ref.proj_ref
  142.8 13.4 %attend_forward.2 = (f32[3,208,768]{2,1,0:T(8,128)}, bf16[3,208,2304]{2,1,0:T(8,128)(2,1)}, bf16[3,208,768]{2,1,0:T(8,128)(2,1)}) custom-call(f32[3,208,768]{2,1,0:T(8,128)} %get-tuple-element.235.x_ref, f32[1,768]{1,0:T(1,128)S(1)} %get-tuple-element.908.gain_ref, f32[1,768]{1,0:T(1,128)S(1)} %get-tuple-element.907.shift_ref, ...), custom_call_target="tpu_custom_call" | custom-call | flops 925000000 | bytes 3250000 | tf_op jit(solution)/shard_map/cond/branch_1_fun/attend_forward/pallas_call | solution.py:133
  156.8 3.2 collective-permute-done.13
  161.0 3.2 pad_maximum_fusion.6
  164.3 21.0 %collective-permute-done.40 = bf16[192,3072]{1,0:T(8,128)(2,1)} collective-permute-done((bf16[192,3072]{1,0:T(8,128)(2,1)}, bf16[192,3072]{1,0:T(8,128)(2,1)}, u32[]{:S(2)}, u32[]{:S(2)}) %collective-permute-start.40) | collective-permute-done | bytes 1179680 | tf_op jit(solution)/shard_map/ppermute | solution.py:569
  185.3 4.3 maximum_select_fusion.5
  190.9 158.7 %conditional.15 = (bf16[768,6144]{1,0:T(8,128)(2,1)}, bf16[768,3072]{1,0:T(8,128)(2,1)}, f32[3,208,768]{2,1,0:T(8,128)}, f32[3,208,768]{2,1,0:T(8,128)}, bf16[3,...) conditional(s32[]{:T(128)} %bitcast.78, () %tuple.170, ...), branch_computations={%region_9.10_spmd, %region_10.11_spmd} | conditional | flops 2776771072 | bytes 107157712 | solution.py:746
  195.6 5.6 collective-permute-done.17
  205.1 5.9 all-to-all-start.1
  224.8 7.6 %join.4.up_ref.down_ref = bf16[768,6144]{1,0:T(8,128)(2,1)} custom-call(s32[4,32]{1,0:T(4,128)S(1)} %pad_add_fusion.1.at_ref, bf16[16,48,1536]{2,1,0:T(8,128)(2,1)} %copy-done.12, bf16[16,48,1536]{2,1,0:T(8,128)(2,1)} %get-tuple-element.252.refs_1_, bf16[16,48,1536]{2,1,0:T(8,128)(2,1)S(1)} %collective-permute-done.15.refs_2_, ...), custom_call_target="tpu_custom_call" | custom-call | bytes 4718592 | tf_op jit(solution)/shard_map/cond/branch_1_fun/join/pallas_call | solution.py:531
  232.4 15.7 %mlp_forward.1 = (f32[3,208,768]{2,1,0:T(8,128)}, bf16[3,208,3072]{2,1,0:T(8,128)(2,1)}, bf16[3,208,3072]{2,1,0:T(8,128)(2,1)}) custom-call(f32[3,208,768]{2,1,0:T(8,128)S(1)} %copy-done.10, f32[1,768]{1,0:T(1,128)} %get-tuple-element.937.gain_ref, f32[1,768]{1,0:T(1,128)} %get-tuple-element.921.shift_ref, bf16[768,6144]{1,0:T(8,128)(2,1)} %join.4.up_ref.down_ref, ...), custom_call_target="tpu_custom_call" | custom-call | flops 1475000064 | bytes 5250000 | tf_op jit(solution)/shard_map/cond/branch_1_fun/mlp_forward/pallas_call | solution.py:229
  257.3 5.2 join.5.qkv_ref.proj_ref
  262.5 13.1 %attend_forward.3 = (f32[3,208,768]{2,1,0:T(8,128)}, bf16[3,208,2304]{2,1,0:T(8,128)(2,1)}, bf16[3,208,768]{2,1,0:T(8,128)(2,1)}) custom-call(f32[3,208,768]{2,1,0:T(8,128)} %get-tuple-element.1045.x_ref, f32[1,768]{1,0:T(1,128)S(1)} %get-tuple-element.938.gain_ref, f32[1,768]{1,0:T(1,128)S(1)} %get-tuple-element.920.shift_ref, ...), custom_call_target="tpu_custom_call" | custom-call | flops 925000000 | bytes 3250000 | tf_op jit(solution)/shard_map/cond/branch_1_fun/attend_forward/pallas_call | solution.py:133
  275.6 5.1 dispatch.1
  280.7 68.7 %all_to_all.25 = bf16[16,96,768]{2,1,0:T(8,128)(2,1)} all-to-all(bf16[16,96,768]{2,1,0:T(8,128)(2,1)S(1)} %bitcast.212), channel_id=1, replica_groups=mesh['dh'=2,'dl'=2,'y'=2,'x'=2,'c'=2] {'dh','y','x','c'}, dimensions={0} | all-to-all | bytes 4718592 | tf_op jit(solution)/shard_map/cond/branch_1_fun/all_to_all | solution.py:736
  349.6 18.5 %expert_forward.1 = (bf16[1536,3072]{1,0:T(8,128)(2,1)}, bf16[1536,3072]{1,0:T(8,128)(2,1)}) custom-call(bf16[1536,768]{1,0:T(8,128)(2,1)} %get-tuple-element.586.rows_ref, bf16[768,3072]{1,0:T(8,128)(2,1)} %bitcast.223), custom_call_target="tpu_custom_call" | custom-call | flops 1800000000 | bytes 6500000 | tf_op jit(solution)/shard_map/expert_forward/pallas_call | solution.py:409
  368.1 35.0 %conditional.16 = (bf16[1536,3072]{1,0:T(8,128)(2,1)}, bf16[1536,768]{1,0:T(8,128)(2,1)}, bf16[768,3072]{1,0:T(8,128)(2,1)}) conditional(s32[]{:T(128)} %bitcast.78, () %tuple.174, (bf16[1536,768]{1,0:T(8,128)(2,1)}, bf16[1536,3072]{1,0:T(8,128)(2,1)}, bf16[768,3072]{1,0:T(8,128)(2,1)}, bf16[768,3072]{1,0:T(8,128)(2,1)}, ...), branch_computations={%region_11.12_spmd, %region_12.13_spmd} | conditional | flops 5411939328 | bytes 38331120 | solution.py:746
  368.1 23.1 %expert_backward.1 = (bf16[1536,3072]{1,0:T(8,128)(2,1)}, bf16[1536,768]{1,0:T(8,128)(2,1)}) custom-call(bf16[1536,768]{1,0:T(8,128)(2,1)} %get-tuple-element.281.grad_ref.refs_0_, bf16[1536,3072]{1,0:T(8,128)(2,1)} %get-tuple-element.282.slope_ref, bf16[768,3072]{1,0:T(8,128)(2,1)} %get-tuple-element.283.in_ref, bf16[768,3072]{1,0:T(8,128)(2,1)} %get-tuple-element.284.out_ref), custom_call_target="tpu_custom_call" | custom-call | flops 3600000000 | bytes 8250000 | tf_op jit(solution)/shard_map/cond/branch_1_fun/expert_backward/pallas_call | solution.py:434
  391.2 11.9 %weight_grad.5 = bf16[768,3072]{1,0:T(8,128)(2,1)} custom-call(s32[1]{0:T(128)} %constant.516.clone.at_ref, bf16[1536,768]{1,0:T(8,128)(2,1)} %get-tuple-element.281.grad_ref.refs_0_, bf16[1536,3072]{1,0:T(8,128)(2,1)S(1)} %bitcast.228), custom_call_target="tpu_custom_call" | custom-call | flops 1811939328 | bytes 1769472 | tf_op jit(solution)/shard_map/cond/branch_1_fun/weight_grad/pallas_call | solution.py:501
  403.2 60.5 %conditional.17 = (bf16[1536,768]{1,0:T(8,128)(2,1)}, bf16[768,3072]{1,0:T(8,128)(2,1)}, bf16[1536,768]{1,0:T(8,128)(2,1)S(1)}) conditional(s32[]{:T(128)} %bitcast.78, () %tuple.173, (bf16[1536,768]{1,0:T(8,128)(2,1)}, bf16[1536,768]{1,0:T(8,128)(2,1)}, bf16[1536,3072]{1,0:T(8,128)(2,1)}, bf16[1536,3072]{1,0:T(8,128)(2,1)}, ...), branch_computations={%region_13.14_spmd, %region_14.15_spmd} | conditional | flops 9060876288 | bytes 72548504 | solution.py:746
  403.2 5.6 all-to-all-start.3
  408.9 13.1 %weight_grad.6 = bf16[768,3072]{1,0:T(8,128)(2,1)} custom-call(s32[1]{0:T(128)} %constant.518.clone.at_ref, bf16[1536,768]{1,0:T(8,128)(2,1)} %get-tuple-element.291.refs_0_, bf16[1536,3072]{1,0:T(8,128)(2,1)} %get-tuple-element.292.refs_1_), custom_call_target="tpu_custom_call" | custom-call | flops 1811939328 | bytes 1769472 | tf_op jit(solution)/shard_map/cond/branch_1_fun/weight_grad/pallas_call | solution.py:501
  422.0 7.9 %convolution_convert_fusion = bf16[1536,768]{1,0:T(8,128)(2,1)S(1)} fusion(bf16[1536,3072]{1,0:T(8,128)(2,1)S(1)} %bitcast.230, bf16[768,3072]{1,0:T(8,128)(2,1)S(1)} %copy-done.18), kind=kOutput, calls=%fused_computation.84 | convolution fusion | flops 7248936960 | bytes 16515072 | tf_op jit(solution)/shard_map/cond/branch_1_fun/dot_general | solution.py:38
  429.9 33.6 %all-to-all-done.3 = bf16[16,96,768]{2,1,0:T(8,128)(2,1)} async-done(((bf16[16,96,768]{2,1,0:T(8,128)(2,1)}), bf16[16,96,768]{2,1,0:T(8,128)(2,1)}, u32[]{:S(2)}, u32[]{:S(2)}) %all-to-all-start.3) | async-done | bytes 2359328 | tf_op jit(solution)/shard_map/cond/branch_1_fun/all_to_all | solution.py:736
  465.2 5.0 all-to-all-start.4
  470.2 40.9 %conditional.18 = (bf16[768,1536]{1,0:T(8,128)(2,1)}, bf16[768,1536]{1,0:T(8,128)(2,1)}, f32[3,208,768]{2,1,0:T(8,128)}, f32[1,768]{1,0:T(1,128)S(1)}, f32[1,768...) conditional(s32[]{:T(128)} %bitcast.78, () %tuple.162, (s32[]{:T(128)}, ...), branch_computations={%region_15.16_spmd, %region_16.17_spmd} | conditional | flops 2111100416 | bytes 20848716 | solution.py:746
  471.2 5.6 return_grad.1
  476.8 24.2 %attend_backward.2 = (f32[3,208,768]{2,1,0:T(8,128)}, bf16[3,208,2304]{2,1,0:T(8,128)(2,1)}, bf16[3,208,768]{2,1,0:T(8,128)(2,1)S(1)}, bf16[3,208,768]{2,1,0:T(8...) custom-call(f32[3,208,768]{2,1,0:T(8,128)} %get-tuple-element.298.x_ref, ...), custom_call_target="tpu_custom_call" | custom-call | flops 1000000000 | bytes 5500000 | tf_op jit(solution)/shard_map/cond/branch_1_fun/attend_backward/pallas_call | solution.py:191
  502.7 8.4 %weight_grad.7 = (bf16[768,1536]{1,0:T(8,128)(2,1)}, bf16[768,1536]{1,0:T(8,128)(2,1)}) custom-call(s32[1]{0:T(128)} %bitcast.20.at_ref, bf16[624,768]{1,0:T(8,128)(2,1)S(1)} %bitcast.218, bf16[624,768]{1,0:T(8,128)(2,1)S(1)} %bitcast.219, bf16[624,2304]{1,0:T(8,128)(2,1)S(1)} %bitcast.214, bf16[624,768]{1,0:T(8,128)(2,1)} %bitcast.27.refs_3_), custom_call_target="tpu_custom_call" | custom-call | flops 736100352 | bytes 1769472 | tf_op jit(solution)/shard_map/cond/branch_1_fun/weight_grad/pallas_call | solution.py:501
  515.9 59.4 %conditional.19 = (bf16[4,48,768]{2,1,0:T(8,128)(2,1)S(1)}, bf16[4,48,768]{2,1,0:T(8,128)(2,1)}, bf16[4,2,2,48,1536]{4,3,2,1,0:T(8,128)(2,1)}, bf16[4,2,2,48,153...) conditional(s32[]{:T(128)} %bitcast.78, () %tuple.161, ...), branch_computations={%region_18.19_spmd, %region_19.20_spmd} | conditional | flops 2964895488 | bytes 140792064 | solution.py:746
  518.4 14.4 %mlp_backward.1 = (f32[3,208,768]{2,1,0:T(8,128)}, bf16[3,208,3072]{2,1,0:T(8,128)(2,1)}, bf16[3,208,768]{2,1,0:T(8,128)(2,1)}, bf16[3,208,768]{2,1,0:T(8,128)(2...) custom-call(f32[3,208,768]{2,1,0:T(8,128)S(1)} %get-tuple-element.321.x_ref, f32[3,208,768]{2,1,0:T(8,128)} %get-tuple-element.322.dy_ref, ...), custom_call_target="tpu_custom_call" | custom-call | flops 1475000064 | bytes 6250000 | tf_op jit(solution)/shard_map/cond/branch_1_fun/mlp_backward/pallas_call | solution.py:266
  532.8 3.0 add_convert_fusion.1
  543.2 13.9 %weight_grad.8 = (bf16[768,3072]{1,0:T(8,128)(2,1)}, bf16[768,3072]{1,0:T(8,128)(2,1)}) custom-call(s32[1]{0:T(128)} %bitcast.35.at_ref, bf16[624,768]{1,0:T(8,128)(2,1)S(1)} %bitcast.216, bf16[624,768]{1,0:T(8,128)(2,1)S(1)} %bitcast.217, bf16[624,3072]{1,0:T(8,128)(2,1)S(1)} %bitcast.213, bf16[624,3072]{1,0:T(8,128)(2,1)} %bitcast.39.refs_3_), custom_call_target="tpu_custom_call" | custom-call | flops 1472200704 | bytes 3538944 | tf_op jit(solution)/shard_map/cond/branch_1_fun/weight_grad/pallas_call | solution.py:501
  561.2 8.2 %collective-permute-done.26 = bf16[4,48,768]{2,1,0:T(8,128)(2,1)S(1)} collective-permute-done((bf16[4,48,768]{2,1,0:T(8,128)(2,1)S(1)}, bf16[4,48,768]{2,1,0:T(8,128)(2,1)S(1)}, u32[]{:S(2)}, u32[]{:S(2)}) %collective-permute-start.26) | collective-permute-done | bytes 294944 | tf_op jit(solution)/shard_map/cond/branch_1_fun/ppermute | solution.py:569
  572.4 2.9 fusion.75
  575.3 36.6 %conditional.20 = (f32[3,208,768]{2,1,0:T(8,128)}, bf16[3,208,2304]{2,1,0:T(8,128)(2,1)}, bf16[3,208,768]{2,1,0:T(8,128)(2,1)}, bf16[3,208,768]{2,1,0:T(8,128)(2...) conditional(s32[]{:T(128)} %bitcast.78, () %tuple.160, ...), branch_computations={%region_20.21_spmd, %region_21.22_spmd} | conditional | flops 1004718592 | bytes 38297076 | solution.py:746
  582.6 24.4 %attend_backward.3 = (f32[3,208,768]{2,1,0:T(8,128)}, bf16[3,208,2304]{2,1,0:T(8,128)(2,1)}, bf16[3,208,768]{2,1,0:T(8,128)(2,1)}, bf16[3,208,768]{2,1,0:T(8,128...) custom-call(f32[3,208,768]{2,1,0:T(8,128)} %get-tuple-element.363.x_ref, f32[3,208,768]{2,1,0:T(8,128)} %get-tuple-element.364.dy_ref, ...), custom_call_target="tpu_custom_call" | custom-call | flops 1000000000 | bytes 5500000 | tf_op jit(solution)/shard_map/cond/branch_1_fun/attend_backward/pallas_call | solution.py:191
  607.4 4.4 fusion.44
  615.3 26.8 %conditional.21 = (f32[768,8]{0,1:T(8,128)S(1)}, bf16[768,1536]{1,0:T(8,128)(2,1)}, bf16[768,1536]{1,0:T(8,128)(2,1)}, f32[3,208,768]{2,1,0:T(8,128)}, f32[3,208...) conditional(s32[]{:T(128)} %bitcast.78, () %tuple.159, (f32[1,768]{1,0:T(1,128)S(1)}, f32[1,768]{1,0:T(1,128)S(1)}, ...), branch_computations={%region_23.24_spmd, %region_24.25_spmd} | conditional | flops 1495537536 | bytes 17994760 | solution.py:746
  621.5 9.5 %weight_grad.9 = (bf16[768,1536]{1,0:T(8,128)(2,1)}, bf16[768,1536]{1,0:T(8,128)(2,1)}) custom-call(s32[1]{0:T(128)} %bitcast.56.at_ref, bf16[624,768]{1,0:T(8,128)(2,1)} %bitcast.57.refs_0_, bf16[624,768]{1,0:T(8,128)(2,1)} %bitcast.58.refs_1_, bf16[624,2304]{1,0:T(8,128)(2,1)} %bitcast.59.refs_2_, bf16[624,768]{1,0:T(8,128)(2,1)} %bitcast.60.refs_3_), custom_call_target="tpu_custom_call" | custom-call | flops 736100352 | bytes 1769472 | tf_op jit(solution)/shard_map/cond/branch_1_fun/weight_grad/pallas_call | solution.py:501
  631.0 6.7 combine.1
  642.2 2.8 dynamic-slice_bitcast_fusion.15
  646.5 38.1 %conditional.22 = (bf16[4,48,1536]{2,1,0:T(8,128)(2,1)S(1)}, f32[591,768]{1,0:T(8,128)}, f32[591,2]{0,1:T(2,128)S(1)}, f32[591,768]{1,0:T(8,128)}) conditional(s32[]{:T(128)} %bitcast.78, () %tuple.158, (bf16[768,1536]{1,0:T(8,128)(2,1)}, bf16[768,1536]{1,0:T(8,128)(2,1)}, f32[3,208,768]{2,1,0:T(8,128)}, f32[3,208,2]{2,1,0:T(8,128)}, ...), branch_computations={%region_25.26_spmd, %region_26.27_spmd} | conditional | flops 9437204 | bytes 55262188 | solution.py:746
  646.6 3.4 collective-permute-start.29
  649.9 4.4 collective-permute-done.29
  657.6 14.0 %collective-permute-done.30 = bf16[4,2,48,768]{3,2,0,1:T(8,128)(2,1)} collective-permute-done((bf16[4,2,48,768]{3,2,0,1:T(8,128)(2,1)S(1)}, bf16[4,2,48,768]{3,2,0,1:T(8,128)(2,1)}, u32[]{:S(2)}, u32[]{:S(2)}) %collective-permute-start.30) | collective-permute-done | bytes 589856 | tf_op jit(solution)/shard_map/cond/branch_1_fun/ppermute | solution.py:569
  684.7 21.2 %collective-permute-done.42 = bf16[2,48,4608]{2,1,0:T(8,128)(2,1)} collective-permute-done((bf16[2,48,4608]{2,1,0:T(8,128)(2,1)}, bf16[2,48,4608]{2,1,0:T(8,128)(2,1)}, u32[]{:S(2)}, u32[]{:S(2)}) %collective-permute-start.42) | collective-permute-done | bytes 884768 | tf_op jit(solution)/shard_map/ppermute | solution.py:569
  705.9 35.5 %conditional.23 = (f32[24,3072]{1,0:T(8,128)S(1)}, f32[24,9216]{1,0:T(8,128)S(1)}, f32[24,8]{1,0:T(8,128)S(1)}, f32[2,192,3072]{2,1,0:T(8,128)}, f32[2,192,3072]{2,1,0:T(8,128)}) conditional(s32[]{:T(128)} %bitcast.78, () %tuple.186, (bf16[4,48,1536]{2,1,0:T(8,128)(2,1)S(1)}, bf16[2,48,4608]{2,1,0:T(8,128)(2,1)}, bf16[2,48,4608]{2,1,0:T(8,128)(2,1)}, ...), branch_computations={%region_27.28_spmd, %region_28.30_spmd} | conditional | flops 13571937 | bytes 68734040 | solution.py:746
  710.9 6.1 all-to-all-start
  717.0 2.9 convert_element_type.270
  (349 shorter events, 169.3 us)
Async XLA Ops:
  7.2 62.3 %all-gather.4.cloned.1.call-start = ((), (), s32[]{:S(2)}) async-start(), calls=%async_computation.7 | async-start | bytes 3010560 | tf_op jit(solution)/shard_map/all_gather | solution.py:586
  13.3 1.7 collective-permute-start.38
  15.9 333.7 %all-gather.6.cloned.1.call-start = ((), (), s32[]{:S(2)}) async-start(), calls=%async_computation.8 | async-start | bytes 7077888 | tf_op jit(solution)/shard_map/all_gather | solution.py:719
  72.9 53.4 %collective-permute-start.39 = (bf16[192,3072]{1,0:T(8,128)(2,1)}, bf16[192,3072]{1,0:T(8,128)(2,1)}, u32[]{:S(2)}, u32[]{:S(2)}) collective-permute-start(bf16[192,3072]{1,0:T(8,128)(2,1)} %get-tuple-element.968), channel_id=1, source_target_pairs={{0,16},{16,0},{1,17},{17,1},{2,18},{18,2},{3,19},{19,3},{4,20},{20... | collective-permute-start | bytes 3538952 | tf_op jit(solution)/shard_map/ppermute | solution.py:569
  77.5 8.7 %collective-permute-start.6 = (bf16[4,48,896]{2,1,0:T(8,128)(2,1)S(1)}, bf16[4,48,896]{2,1,0:T(8,128)(2,1)S(1)}, u32[]{:S(2)}, u32[]{:S(2)}) collective-permute-start(bf16[4,48,896]{2,1,0:T(8,128)(2,1)S(1)} %slice.121), channel_id=1, source_target_pairs={{0,4},{4,0},{1,5},{5,1},{2,6},{6,2},{3,7},{7,3},{8,12},{12,8},{9,1... | collective-permute-start | bytes 1032200 | tf_op jit(solution)/shard_map/cond/branch_1_fun/ppermute | solution.py:569
  78.7 7.2 collective-permute-start.5
  86.3 15.1 %collective-permute-start.8 = (bf16[8,48,896]{2,1,0:T(8,128)(2,1)S(1)}, bf16[8,48,896]{2,1,0:T(8,128)(2,1)S(1)}, u32[]{:S(2)}, u32[]{:S(2)}) collective-permute-start(bf16[8,48,896]{2,1,0:T(8,128)(2,1)S(1)} %pad_maximum_fusion.4), channel_id=1, source_target_pairs={{0,2},{2,0},{1,3},{3,1},{4,6},{6,4},{5,7},{7,5},{8,10},{10,8},{9,1... | collective-permute-start | bytes 2064392 | tf_op jit(solution)/shard_map/cond/branch_1_fun/ppermute | solution.py:569
  87.5 12.6 %collective-permute-start.7 = (bf16[8,48,768]{2,1,0:T(8,128)(2,1)S(1)}, bf16[8,48,768]{2,1,0:T(8,128)(2,1)S(1)}, u32[]{:S(2)}, u32[]{:S(2)}) collective-permute-start(bf16[8,48,768]{2,1,0:T(8,128)(2,1)S(1)} %pad_maximum_fusion.5), channel_id=1, source_target_pairs={{0,4},{4,0},{1,5},{5,1},{2,6},{6,2},{3,7},{7,3},{8,12},{12,8},{9,1... | collective-permute-start | bytes 1769480 | tf_op jit(solution)/shard_map/cond/branch_1_fun/ppermute | solution.py:569
  103.7 19.4 %collective-permute-start.10 = (bf16[16,48,896]{2,1,0:T(8,128)(2,1)}, bf16[16,48,896]{2,1,0:T(8,128)(2,1)}, u32[]{:S(2)}, u32[]{:S(2)}) collective-permute-start(bf16[16,48,896]{2,1,0:T(8,128)(2,1)} %pad_maximum_fusion), channel_id=1, source_target_pairs={{0,1},{1,0},{2,3},{3,2},{4,5},{5,4},{6,7},{7,6},{8,9},{9,8},{10,11... | collective-permute-start | bytes 4128776 | tf_op jit(solution)/shard_map/cond/branch_1_fun/ppermute | solution.py:569
  106.5 16.6 %collective-permute-start.9 = (bf16[16,48,768]{2,1,0:T(8,128)(2,1)}, bf16[16,48,768]{2,1,0:T(8,128)(2,1)}, u32[]{:S(2)}, u32[]{:S(2)}) collective-permute-start(bf16[16,48,768]{2,1,0:T(8,128)(2,1)} %pad_maximum_fusion.1), channel_id=1, source_target_pairs={{0,1},{1,0},{2,3},{3,2},{4,5},{5,4},{6,7},{7,6},{8,9},{9,8},{10,11... | collective-permute-start | bytes 3538952 | tf_op jit(solution)/shard_map/cond/branch_1_fun/ppermute | solution.py:569
  106.5 14.5 %collective-permute-start.11 = (bf16[4,48,1536]{2,1,0:T(8,128)(2,1)S(1)}, bf16[4,48,1536]{2,1,0:T(8,128)(2,1)S(1)}, u32[]{:S(2)}, u32[]{:S(2)}) collective-permute-start(bf16[4,48,1536]{2,1,0:T(8,128)(2,1)S(1)} %get-tuple-element.215), channel_id=1, source_target_pairs={{0,2},{2,0},{1,3},{3,1},{4,6},{6,4},{5,7},{7,5},{8,10},{10,8},{9,1... | collective-permute-start | bytes 1769480 | tf_op jit(solution)/shard_map/cond/branch_1_fun/ppermute | solution.py:569
  107.7 14.2 %collective-permute-start.12 = (bf16[4,48,1536]{2,1,0:T(8,128)(2,1)S(1)}, bf16[4,48,1536]{2,1,0:T(8,128)(2,1)S(1)}, u32[]{:S(2)}, u32[]{:S(2)}) collective-permute-start(bf16[4,48,1536]{2,1,0:T(8,128)(2,1)S(1)} %get-tuple-element.216), channel_id=1, source_target_pairs={{0,4},{4,0},{1,5},{5,1},{2,6},{6,2},{3,7},{7,3},{8,12},{12,8},{9,1... | collective-permute-start | bytes 1769480 | tf_op jit(solution)/shard_map/cond/branch_1_fun/ppermute | solution.py:569
  130.7 237.4 %all-gather.8.cloned.1.call-start = ((), (), s32[]{:S(2)}) async-start(), calls=%async_computation.9 | async-start | bytes 7077888 | tf_op jit(solution)/shard_map/all_gather | solution.py:719
  132.3 52.9 %collective-permute-start.40 = (bf16[192,3072]{1,0:T(8,128)(2,1)}, bf16[192,3072]{1,0:T(8,128)(2,1)}, u32[]{:S(2)}, u32[]{:S(2)}) collective-permute-start(bf16[192,3072]{1,0:T(8,128)(2,1)} %get-tuple-element.966), channel_id=1, source_target_pairs={{0,16},{16,0},{1,17},{17,1},{2,18},{18,2},{3,19},{19,3},{4,20},{20... | collective-permute-start | bytes 3538952 | tf_op jit(solution)/shard_map/ppermute | solution.py:569
  132.8 27.2 %collective-permute-start.13 = (bf16[8,48,1536]{2,1,0:T(8,128)(2,1)S(1)}, bf16[8,48,1536]{2,1,0:T(8,128)(2,1)S(1)}, u32[]{:S(2)}, u32[]{:S(2)}) collective-permute-start(bf16[8,48,1536]{2,1,0:T(8,128)(2,1)S(1)} %get-tuple-element.231), channel_id=1, source_target_pairs={{0,4},{4,0},{1,5},{5,1},{2,6},{6,2},{3,7},{7,3},{8,12},{12,8},{9,1... | collective-permute-start | bytes 3538952 | tf_op jit(solution)/shard_map/cond/branch_1_fun/ppermute | solution.py:569
  134.0 27.0 %collective-permute-start.14 = (bf16[8,48,1536]{2,1,0:T(8,128)(2,1)}, bf16[8,48,1536]{2,1,0:T(8,128)(2,1)}, u32[]{:S(2)}, u32[]{:S(2)}) collective-permute-start(bf16[8,48,1536]{2,1,0:T(8,128)(2,1)} %get-tuple-element.232), channel_id=1, source_target_pairs={{0,2},{2,0},{1,3},{3,1},{4,6},{6,4},{5,7},{7,5},{8,10},{10,8},{9,1... | collective-permute-start | bytes 3538952 | tf_op jit(solution)/shard_map/cond/branch_1_fun/ppermute | solution.py:569
  164.2 26.7 %copy-start.26 = (f32[4,1,768]{2,0,1:T(4,128)}, f32[4,1,768]{2,0,1:T(4,128)S(1)}, u32[]{:S(2)}) copy-start(f32[4,1,768]{2,0,1:T(4,128)S(1)} %get-tuple-element.571) | copy-start | bytes 36868
  189.6 321.5 %reduce-scatter.3.cloned.1.call-start = ((), (), s32[]{:S(2)}) async-start(), calls=%async_computation.10 | async-start | bytes 7077888 | tf_op jit(solution)/shard_map/reduce_scatter | solution.py:724
  192.3 11.2 %collective-permute-start.15 = (bf16[16,48,1536]{2,1,0:T(8,128)(2,1)}, bf16[16,48,1536]{2,1,0:T(8,128)(2,1)S(1)}, u32[]{:S(2)}, u32[]{:S(2)}) collective-permute-start(bf16[16,48,1536]{2,1,0:T(8,128)(2,1)} %copy-done.12), channel_id=1, source_target_pairs={{0,1},{1,0},{2,3},{3,2},{4,5},{5,4},{6,7},{7,6},{8,9},{9,8},{10,11... | collective-permute-start | bytes 7077896 | tf_op jit(solution)/shard_map/cond/branch_1_fun/ppermute | solution.py:569
  192.9 10.7 %collective-permute-start.16 = (bf16[16,48,1536]{2,1,0:T(8,128)(2,1)}, bf16[16,48,1536]{2,1,0:T(8,128)(2,1)S(1)}, u32[]{:S(2)}, u32[]{:S(2)}) collective-permute-start(bf16[16,48,1536]{2,1,0:T(8,128)(2,1)} %get-tuple-element.252.refs_1_), channel_id=1, source_target_pairs={{0,1},{1,0},{2,3},{3,2},{4,5},{5,4},{6,7},{7,6},{8,9},{9,8},{10,11... | collective-permute-start | bytes 7077896 | tf_op jit(solution)/shard_map/cond/branch_1_fun/ppermute | solution.py:569
  192.9 8.4 %collective-permute-start.17 = (bf16[4,48,768]{2,1,0:T(8,128)(2,1)}, bf16[4,48,768]{2,1,0:T(8,128)(2,1)S(1)}, u32[]{:S(2)}, u32[]{:S(2)}) collective-permute-start(bf16[4,48,768]{2,1,0:T(8,128)(2,1)} %get-tuple-element.246), channel_id=1, source_target_pairs={{0,2},{2,0},{1,3},{3,1},{4,6},{6,4},{5,7},{7,5},{8,10},{10,8},{9,1... | collective-permute-start | bytes 884744 | tf_op jit(solution)/shard_map/cond/branch_1_fun/ppermute | solution.py:569
  194.4 8.1 %collective-permute-start.18 = (bf16[4,48,768]{2,1,0:T(8,128)(2,1)}, bf16[4,48,768]{2,1,0:T(8,128)(2,1)S(1)}, u32[]{:S(2)}, u32[]{:S(2)}) collective-permute-start(bf16[4,48,768]{2,1,0:T(8,128)(2,1)} %get-tuple-element.247), channel_id=1, source_target_pairs={{0,4},{4,0},{1,5},{5,1},{2,6},{6,2},{3,7},{7,3},{8,12},{12,8},{9,1... | collective-permute-start | bytes 884744 | tf_op jit(solution)/shard_map/cond/branch_1_fun/ppermute | solution.py:569
  205.1 16.0 %copy-start.29 = (f32[4,1,768]{2,0,1:T(4,128)S(1)}, f32[4,1,768]{2,0,1:T(4,128)}, u32[]{:S(2)}) copy-start(f32[4,1,768]{2,0,1:T(4,128)} %copy-done.28) | copy-start | bytes 36868 | tf_op jit(solution)/shard_map/cond
  205.1 70.5 %all-to-all-start.1 = ((bf16[16,96,768]{2,1,0:T(8,128)(2,1)}), bf16[16,96,768]{2,1,0:T(8,128)(2,1)}, u32[]{:S(2)}, u32[]{:S(2)}) async-start(bf16[16,96,768]{2,1,0:T(8,128)(2,1)} %bitcast.11), calls=%async_computation.1 | async-start | bytes 4718592 | tf_op jit(solution)/shard_map/cond/branch_1_fun/all_to_all | solution.py:736
  214.3 33.7 %collective-permute-start.19 = (bf16[8,48,768]{2,1,0:T(8,128)(2,1)S(1)}, bf16[8,48,768]{2,1,0:T(8,128)(2,1)}, u32[]{:S(2)}, u32[]{:S(2)}) collective-permute-start(bf16[8,48,768]{2,1,0:T(8,128)(2,1)S(1)} %get-tuple-element.257), channel_id=1, source_target_pairs={{0,4},{4,0},{1,5},{5,1},{2,6},{6,2},{3,7},{7,3},{8,12},{12,8},{9,1... | collective-permute-start | bytes 1769480 | tf_op jit(solution)/shard_map/cond/branch_1_fun/ppermute | solution.py:569
  215.8 32.3 %collective-permute-start.20 = (bf16[8,48,768]{2,1,0:T(8,128)(2,1)S(1)}, bf16[8,48,768]{2,1,0:T(8,128)(2,1)}, u32[]{:S(2)}, u32[]{:S(2)}) collective-permute-start(bf16[8,48,768]{2,1,0:T(8,128)(2,1)S(1)} %get-tuple-element.258), channel_id=1, source_target_pairs={{0,2},{2,0},{1,3},{3,1},{4,6},{6,4},{5,7},{7,5},{8,10},{10,8},{9,1... | collective-permute-start | bytes 1769480 | tf_op jit(solution)/shard_map/cond/branch_1_fun/ppermute | solution.py:569
  250.4 6.9 collective-permute-start.21
  251.3 6.1 collective-permute-start.22
  262.5 13.1 %copy-start.38 = (s32[2,624]{1,0:T(2,128)S(1)}, s32[2,624]{1,0:T(2,128)}, u32[]{:S(2)}) copy-start(s32[2,624]{1,0:T(2,128)} %get-tuple-element.279.places_ref) | copy-start | bytes 14980 | tf_op jit(solution)/shard_map/cond
  368.1 23.1 %slice-start = ((s8[9437184]{0:T(1024)(128)(4,1)}), s8[4194304]{0:T(1024)(128)(4,1)S(1)}, s32[]{:S(2)}) async-start(s8[9437184]{0:T(1024)(128)(4,1)} %bitcast.227), calls=%async_computation.12 | async-start | bytes 8388608 | tf_op jit(solution)/shard_map/cond
  368.1 23.1 %slice-start.1 = ((s8[9437184]{0:T(1024)(128)(4,1)}), s8[4194304]{0:T(1024)(128)(4,1)S(1)}, s32[]{:S(2)}) async-start(s8[9437184]{0:T(1024)(128)(4,1)} %bitcast.227), calls=%async_computation.13 | async-start | bytes 8388608 | tf_op jit(solution)/shard_map/cond
  368.1 23.1 %slice-start.2 = ((s8[9437184]{0:T(1024)(128)(4,1)}), s8[1048576]{0:T(1024)(128)(4,1)S(1)}, s32[]{:S(2)}) async-start(s8[9437184]{0:T(1024)(128)(4,1)} %bitcast.227), calls=%async_computation.14 | async-start | bytes 2097152 | tf_op jit(solution)/shard_map/cond
  403.2 208.7 %reduce-scatter.5.cloned.1.call-start = ((), (), s32[]{:S(2)}) async-start(), calls=%async_computation.11 | async-start | bytes 7077888 | tf_op jit(solution)/shard_map/reduce_scatter | solution.py:724
  403.2 18.7 %slice-start.3 = ((s8[9437184]{0:T(1024)(128)(4,1)}), s8[1048576]{0:T(1024)(128)(4,1)S(1)}, s32[]{:S(2)}) async-start(s8[9437184]{0:T(1024)(128)(4,1)} %bitcast.229), calls=%async_computation.15 | async-start | bytes 2097152 | tf_op jit(solution)/shard_map/cond
  403.2 60.3 %all-to-all-start.3 = ((bf16[16,96,768]{2,1,0:T(8,128)(2,1)}), bf16[16,96,768]{2,1,0:T(8,128)(2,1)}, u32[]{:S(2)}, u32[]{:S(2)}) async-start(bf16[16,96,768]{2,1,0:T(8,128)(2,1)} %bitcast.18), calls=%async_computation.3 | async-start | bytes 4718592 | tf_op jit(solution)/shard_map/cond/branch_1_fun/all_to_all | solution.py:736
  408.9 13.1 %slice-start.4 = ((s8[9437184]{0:T(1024)(128)(4,1)}), s8[4194304]{0:T(1024)(128)(4,1)S(1)}, s32[]{:S(2)}) async-start(s8[9437184]{0:T(1024)(128)(4,1)} %bitcast.229), calls=%async_computation.16 | async-start | bytes 8388608 | tf_op jit(solution)/shard_map/cond
  408.9 13.1 %slice-start.5 = ((s8[9437184]{0:T(1024)(128)(4,1)}), s8[4194304]{0:T(1024)(128)(4,1)S(1)}, s32[]{:S(2)}) async-start(s8[9437184]{0:T(1024)(128)(4,1)} %bitcast.229), calls=%async_computation.17 | async-start | bytes 8388608 | tf_op jit(solution)/shard_map/cond
  465.2 110.1 %all-to-all-start.4 = ((bf16[16,96,768]{2,1,0:T(8,128)(2,1)}), bf16[16,96,768]{2,1,0:T(8,128)(2,1)}, u32[]{:S(2)}, u32[]{:S(2)}) async-start(bf16[16,96,768]{2,1,0:T(8,128)(2,1)} %bitcast.231), calls=%async_computation.5 | async-start | bytes 4718592 | tf_op jit(solution)/shard_map/all_to_all | solution.py:736
  513.6 61.7 %collective-permute-start.41 = (bf16[1,192,3072]{2,1,0:T(8,128)(2,1)}, bf16[1,192,3072]{2,1,0:T(8,128)(2,1)}, u32[]{:S(2)}, u32[]{:S(2)}) collective-permute-start(bf16[1,192,3072]{2,1,0:T(8,128)(2,1)} %constant_dynamic-slice_fusion.5), channel_id=1, source_target_pairs={{0,16},{16,0},{1,17},{17,1},{2,18},{18,2},{3,19},{19,3},{4,20},{20... | collective-permute-start | bytes 3538952 | tf_op jit(solution)/shard_map/ppermute | solution.py:569
  516.3 16.4 %collective-permute-start.23 = (bf16[768,1536]{1,0:T(8,128)(2,1)}, bf16[768,1536]{1,0:T(8,128)(2,1)}, u32[]{:S(2)}, u32[]{:S(2)}) collective-permute-start(bf16[768,1536]{1,0:T(8,128)(2,1)} %get-tuple-element.320), channel_id=1, source_target_pairs={{0,1},{1,0},{2,3},{3,2},{4,5},{5,4},{6,7},{7,6},{8,9},{9,8},{10,11... | collective-permute-start | bytes 7077896 | tf_op jit(solution)/shard_map/cond/branch_1_fun/ppermute | solution.py:569
  538.7 18.4 %collective-permute-start.24 = (bf16[4,2,48,768]{3,2,1,0:T(8,128)(2,1)}, bf16[4,2,48,768]{3,2,1,0:T(8,128)(2,1)}, u32[]{:S(2)}, u32[]{:S(2)}) collective-permute-start(bf16[4,2,48,768]{3,2,1,0:T(8,128)(2,1)} %dynamic-slice_bitcast_fusion.1), channel_id=1, source_target_pairs={{0,4},{4,0},{1,5},{5,1},{2,6},{6,2},{3,7},{7,3},{8,12},{12,8},{9,1... | collective-permute-start | bytes 1769480 | tf_op jit(solution)/shard_map/cond/branch_1_fun/ppermute | solution.py:569
  539.9 17.2 %collective-permute-start.25 = (bf16[4,2,48,768]{3,2,1,0:T(8,128)(2,1)}, bf16[4,2,48,768]{3,2,1,0:T(8,128)(2,1)}, u32[]{:S(2)}, u32[]{:S(2)}) collective-permute-start(bf16[4,2,48,768]{3,2,1,0:T(8,128)(2,1)} %dynamic-slice_bitcast_fusion), channel_id=1, source_target_pairs={{0,2},{2,0},{1,3},{3,1},{4,6},{6,4},{5,7},{7,5},{8,10},{10,8},{9,1... | collective-permute-start | bytes 1769480 | tf_op jit(solution)/shard_map/cond/branch_1_fun/ppermute | solution.py:569
  543.2 13.9 %copy-start.17 = (bf16[4,2,2,48,768]{4,3,2,1,0:T(8,128)(2,1)S(1)}, bf16[4,2,2,48,768]{4,3,2,1,0:T(8,128)(2,1)}, u32[]{:S(2)}) copy-start(bf16[4,2,2,48,768]{4,3,2,1,0:T(8,128)(2,1)} %copy-done.16) | copy-start | bytes 3538948 | tf_op jit(solution)/shard_map/cond
  559.7 10.6 %collective-permute-start.28 = (bf16[768,3072]{1,0:T(8,128)(2,1)}, bf16[768,3072]{1,0:T(8,128)(2,1)S(1)}, u32[]{:S(2)}, u32[]{:S(2)}) collective-permute-start(bf16[768,3072]{1,0:T(8,128)(2,1)} %get-tuple-element.349), channel_id=1, source_target_pairs={{0,1},{1,0},{2,3},{3,2},{4,5},{5,4},{6,7},{7,6},{8,9},{9,8},{10,11... | collective-permute-start | bytes 14155784 | tf_op jit(solution)/shard_map/cond/branch_1_fun/ppermute | solution.py:569
  560.7 8.8 %collective-permute-start.26 = (bf16[4,48,768]{2,1,0:T(8,128)(2,1)S(1)}, bf16[4,48,768]{2,1,0:T(8,128)(2,1)S(1)}, u32[]{:S(2)}, u32[]{:S(2)}) collective-permute-start(bf16[4,48,768]{2,1,0:T(8,128)(2,1)S(1)} %dynamic-slice_bitcast_fusion.3), channel_id=1, source_target_pairs={{0,2},{2,0},{1,3},{3,1},{4,6},{6,4},{5,7},{7,5},{8,10},{10,8},{9,1... | collective-permute-start | bytes 884744 | tf_op jit(solution)/shard_map/cond/branch_1_fun/ppermute | solution.py:569
  561.1 8.4 %collective-permute-start.27 = (bf16[4,48,768]{2,1,0:T(8,128)(2,1)S(1)}, bf16[4,48,768]{2,1,0:T(8,128)(2,1)S(1)}, u32[]{:S(2)}, u32[]{:S(2)}) collective-permute-start(bf16[4,48,768]{2,1,0:T(8,128)(2,1)S(1)} %dynamic-slice_bitcast_fusion.2), channel_id=1, source_target_pairs={{0,4},{4,0},{1,5},{5,1},{2,6},{6,2},{3,7},{7,3},{8,12},{12,8},{9,1... | collective-permute-start | bytes 884744 | tf_op jit(solution)/shard_map/cond/branch_1_fun/ppermute | solution.py:569
  580.4 26.8 %collective-permute-start.34 = (bf16[4,2,48,1536]{3,2,1,0:T(8,128)(2,1)}, bf16[4,2,48,1536]{3,2,1,0:T(8,128)(2,1)}, u32[]{:S(2)}, u32[]{:S(2)}) collective-permute-start(bf16[4,2,48,1536]{3,2,1,0:T(8,128)(2,1)} %dynamic-slice_bitcast_fusion.5), channel_id=1, source_target_pairs={{0,4},{4,0},{1,5},{5,1},{2,6},{6,2},{3,7},{7,3},{8,12},{12,8},{9,1... | collective-permute-start | bytes 3538952 | tf_op jit(solution)/shard_map/cond/branch_1_fun/ppermute | solution.py:569
  580.7 26.7 %collective-permute-start.35 = (bf16[4,2,48,1536]{3,2,1,0:T(8,128)(2,1)}, bf16[4,2,48,1536]{3,2,1,0:T(8,128)(2,1)}, u32[]{:S(2)}, u32[]{:S(2)}) collective-permute-start(bf16[4,2,48,1536]{3,2,1,0:T(8,128)(2,1)} %dynamic-slice_bitcast_fusion.4), channel_id=1, source_target_pairs={{0,2},{2,0},{1,3},{3,1},{4,6},{6,4},{5,7},{7,5},{8,10},{10,8},{9,1... | collective-permute-start | bytes 3538952 | tf_op jit(solution)/shard_map/cond/branch_1_fun/ppermute | solution.py:569
  614.4 91.5 %collective-permute-start.43 = (bf16[1,192,3072]{2,1,0:T(8,128)(2,1)}, bf16[1,192,3072]{2,1,0:T(8,128)(2,1)}, u32[]{:S(2)}, u32[]{:S(2)}) collective-permute-start(bf16[1,192,3072]{2,1,0:T(8,128)(2,1)} %constant_dynamic-slice_fusion.4), channel_id=1, source_target_pairs={{0,16},{16,0},{1,17},{17,1},{2,18},{18,2},{3,19},{19,3},{4,20},{20... | collective-permute-start | bytes 3538952 | tf_op jit(solution)/shard_map/ppermute | solution.py:569
  619.2 18.6 %collective-permute-start.36 = (bf16[4,48,1536]{2,1,0:T(8,128)(2,1)}, bf16[4,48,1536]{2,1,0:T(8,128)(2,1)}, u32[]{:S(2)}, u32[]{:S(2)}) collective-permute-start(bf16[4,48,1536]{2,1,0:T(8,128)(2,1)} %dynamic-slice_bitcast_fusion.7), channel_id=1, source_target_pairs={{0,2},{2,0},{1,3},{3,1},{4,6},{6,4},{5,7},{7,5},{8,10},{10,8},{9,1... | collective-permute-start | bytes 1769480 | tf_op jit(solution)/shard_map/cond/branch_1_fun/ppermute | solution.py:569
  619.9 17.8 %collective-permute-start.37 = (bf16[4,48,1536]{2,1,0:T(8,128)(2,1)}, bf16[4,48,1536]{2,1,0:T(8,128)(2,1)}, u32[]{:S(2)}, u32[]{:S(2)}) collective-permute-start(bf16[4,48,1536]{2,1,0:T(8,128)(2,1)} %dynamic-slice_bitcast_fusion.6), channel_id=1, source_target_pairs={{0,4},{4,0},{1,5},{5,1},{2,6},{6,2},{3,7},{7,3},{8,12},{12,8},{9,1... | collective-permute-start | bytes 1769480 | tf_op jit(solution)/shard_map/cond/branch_1_fun/ppermute | solution.py:569
  644.9 60.9 %collective-permute-start.42 = (bf16[2,48,4608]{2,1,0:T(8,128)(2,1)}, bf16[2,48,4608]{2,1,0:T(8,128)(2,1)}, u32[]{:S(2)}, u32[]{:S(2)}) collective-permute-start(bf16[2,48,4608]{2,1,0:T(8,128)(2,1)} %get-tuple-element.969), channel_id=1, source_target_pairs={{0,16},{16,0},{1,17},{17,1},{2,18},{18,2},{3,19},{19,3},{4,20},{20... | collective-permute-start | bytes 2654216 | tf_op jit(solution)/shard_map/ppermute | solution.py:569
  646.6 7.7 %collective-permute-start.29 = (bf16[768,1536]{1,0:T(8,128)(2,1)}, bf16[768,1536]{1,0:T(8,128)(2,1)S(1)}, u32[]{:S(2)}, u32[]{:S(2)}) collective-permute-start(bf16[768,1536]{1,0:T(8,128)(2,1)} %get-tuple-element.414), channel_id=1, source_target_pairs={{0,1},{1,0},{2,3},{3,2},{4,5},{5,4},{6,7},{7,6},{8,9},{9,8},{10,11... | collective-permute-start | bytes 7077896 | tf_op jit(solution)/shard_map/cond/branch_1_fun/ppermute | solution.py:569
  656.9 14.7 %collective-permute-start.30 = (bf16[4,2,48,768]{3,2,0,1:T(8,128)(2,1)S(1)}, bf16[4,2,48,768]{3,2,0,1:T(8,128)(2,1)}, u32[]{:S(2)}, u32[]{:S(2)}) collective-permute-start(bf16[4,2,48,768]{3,2,0,1:T(8,128)(2,1)S(1)} %dynamic-slice_bitcast_fusion.9), channel_id=1, source_target_pairs={{0,4},{4,0},{1,5},{5,1},{2,6},{6,2},{3,7},{7,3},{8,12},{12,8},{9,1... | collective-permute-start | bytes 1769480 | tf_op jit(solution)/shard_map/cond/branch_1_fun/ppermute | solution.py:569
  657.2 14.4 %collective-permute-start.31 = (bf16[4,2,48,768]{3,2,1,0:T(8,128)(2,1)S(1)}, bf16[4,2,48,768]{3,2,1,0:T(8,128)(2,1)}, u32[]{:S(2)}, u32[]{:S(2)}) collective-permute-start(bf16[4,2,48,768]{3,2,1,0:T(8,128)(2,1)S(1)} %dynamic-slice_bitcast_fusion.8), channel_id=1, source_target_pairs={{0,2},{2,0},{1,3},{3,1},{4,6},{6,4},{5,7},{7,5},{8,10},{10,8},{9,1... | collective-permute-start | bytes 1769480 | tf_op jit(solution)/shard_map/cond/branch_1_fun/ppermute | solution.py:569
  675.5 7.9 %collective-permute-start.32 = (bf16[4,48,768]{2,1,0:T(8,128)(2,1)}, bf16[4,48,768]{2,1,0:T(8,128)(2,1)}, u32[]{:S(2)}, u32[]{:S(2)}) collective-permute-start(bf16[4,48,768]{2,1,0:T(8,128)(2,1)} %dynamic-slice_bitcast_fusion.11), channel_id=1, source_target_pairs={{0,2},{2,0},{1,3},{3,1},{4,6},{6,4},{5,7},{7,5},{8,10},{10,8},{9,1... | collective-permute-start | bytes 884744 | tf_op jit(solution)/shard_map/cond/branch_1_fun/ppermute | solution.py:569
  675.9 7.5 %collective-permute-start.33 = (bf16[4,48,768]{2,1,0:T(8,128)(2,1)}, bf16[4,48,768]{2,1,0:T(8,128)(2,1)}, u32[]{:S(2)}, u32[]{:S(2)}) collective-permute-start(bf16[4,48,768]{2,1,0:T(8,128)(2,1)} %dynamic-slice_bitcast_fusion.10), channel_id=1, source_target_pairs={{0,4},{4,0},{1,5},{5,1},{2,6},{6,2},{3,7},{7,3},{8,12},{12,8},{9,1... | collective-permute-start | bytes 884744 | tf_op jit(solution)/shard_map/cond/branch_1_fun/ppermute | solution.py:569
  684.7 21.2 %copy-start.41 = (f32[591,2]{0,1:T(2,128)}, f32[591,2]{0,1:T(2,128)S(1)}, u32[]{:S(2)}) copy-start(f32[591,2]{0,1:T(2,128)S(1)} %get-tuple-element.743) | copy-start | bytes 14188
  709.2 18.2 %collective-permute-start = (bf16[48,4608]{1,0:T(8,128)(2,1)}, bf16[48,4608]{1,0:T(8,128)(2,1)}, u32[]{:S(2)}, u32[]{:S(2)}) collective-permute-start(bf16[48,4608]{1,0:T(8,128)(2,1)} %dynamic-slice_bitcast_fusion.12), channel_id=1, source_target_pairs={{0,8},{8,0},{1,9},{9,1},{2,10},{10,2},{3,11},{11,3},{4,12},{12,4},... | collective-permute-start | bytes 1327112 | tf_op jit(solution)/shard_map/cond/branch_1_fun/ppermute | solution.py:569
  709.9 18.5 %collective-permute-start.1 = (bf16[2,48,1536]{2,1,0:T(8,128)(2,1)}, bf16[2,48,1536]{2,1,0:T(8,128)(2,1)S(1)}, u32[]{:S(2)}, u32[]{:S(2)}) collective-permute-start(bf16[2,48,1536]{2,1,0:T(8,128)(2,1)} %dynamic-slice_bitcast_fusion.13), channel_id=1, source_target_pairs={{0,16},{16,0},{1,17},{17,1},{2,18},{18,2},{3,19},{19,3},{4,20},{20... | collective-permute-start | bytes 884744 | tf_op jit(solution)/shard_map/cond/branch_1_fun/ppermute | solution.py:569
  710.9 27.7 %all-to-all-start = ((f32[32,1,192]{2,1,0:T(1,128)}), f32[32,1,192]{2,1,0:T(1,128)}, u32[]{:S(2)}, u32[]{:S(2)}) async-start(f32[32,1,192]{2,1,0:T(1,128)} %all_to_all.19), calls=%async_computation | async-start | bytes 65536 | tf_op jit(solution)/shard_map/cond/branch_1_fun/all_to_all | solution.py:680
  728.5 4.1 collective-permute-start.2
  729.2 3.5 collective-permute-start.3
  733.4 6.1 collective-permute-start.4
  (37 other events, 150.3 us)
Sparse Core Ops, SparseCore 0:
  16.0 53.4 all-gather.3
  130.8 87.8 all-gather.5
  220.3 87.1 all-gather.7
  403.3 91.6 reduce-scatter.2
  497.2 100.3 reduce-scatter.4

commit v5 on v4

--- a/solution.py
+++ b/solution.py
@@ -568,7 +568,8 @@
         size = lax.axis_size(axes)
         return lax.ppermute(value, axes, [(i, i ^ bit) for i in range(size)])
 
-    def gather_depth(self, parts):
+    def gather_depth(self, parts, *gates):
+        parts = after(tuple(parts), *gates)
         if not self.wide:
             return jnp.concatenate(parts, axis=1)
         core = lax.axis_index("c")
@@ -681,6 +682,9 @@
 
     def small_sum(self, pieces):
         return jnp.sum(pieces, axis=0).reshape(-1, 8)
+
+    def scatter_join(self, *values):
+        return jnp.concatenate(values, axis=1)
 
     def scatter_unstack(self, rows, *widths):
         if not self.wide:
@@ -775,7 +779,16 @@
     core = lax.axis_index("c") if plan.wide else 0 * expert_index[0, 0]
     parts = (part_a, part_b, part_c)
     in_low = exp_in.astype(LOW)
-    deep = plan.gather_depth(parts)
+    deep_a = plan.gather_depth(parts[:1])
+    deep_bc = plan.gather_depth(parts[1:], deep_a)
+
+    def zeroth_part(deep_a, part_a):
+        (pair_a,) = plan.gather_split(deep_a, (part_a,))
+        one_a = bar(plan.gather_side(pair_a, 0))
+        return bar(plan.gather_side(one_a, 1))
+
+    two_a = fenced(ready, zeroth_part, deep_a, part_a)
+    expert_index, act_in = after((expert_index, act_in), two_a)
 
     def prepare(expert_index, gate, cotangent, act_in):
         flat_index = expert_index.reshape(-1)
@@ -794,53 +807,50 @@
     spot_rows = flat(spots).T
 
     out_low = jnp.swapaxes(exp_out, 1, 2).astype(LOW)
-    in_low, x_a, grad_sent, deep = bar((in_low, x_a, grad_sent, deep))
+    in_low, x_a, grad_sent, deep_bc = bar((in_low, x_a, grad_sent, deep_bc))
     in_near = plan.fetch_near(in_low)
 
-    def zeroth_part(deep, parts):
-        pair_a, pair_b, pair_c = plan.gather_split(deep, parts)
-        one_a = bar(plan.gather_side(pair_a, 0))
-        two_a = bar(plan.gather_side(one_a, 1))
-        pair_b, two_a = bar((pair_b, two_a))
+    def first_part(two_a, deep_bc, parts, x_a):
+        part_a, part_b, part_c = parts
+        pair_b, pair_c = plan.gather_split(deep_bc, (part_b, part_c))
         four_a, one_b = bar((plan.gather_core(two_a), plan.gather_side(pair_b, 0)))
-        return four_a, one_b, pair_c
-
-    four_a, one_b, pair_c = fenced(ready, zeroth_part, deep, parts)
-    four_a, in_near, out_low = bar((four_a, in_near, out_low))
-    weight_in = plan.fetch_far(in_near)
-    out_near = plan.fetch_near(out_low)
-
-    def first_part(four_a, one_b, part_a, x_a):
         block_a = plan.gather_join(four_a, part_a)
         norms = block_a[:, 4 * D : 4 * D + 8].astype(WIDE).T
         gain, shift = norms[:4, None], norms[4:, None]
         x_b, packed_a, mixed_a = attend_forward(x_a, gain[0], shift[0], block_a)
         two_b, x_b = bar((plan.gather_side(one_b, 1), x_b))
-        return gain, shift, block_a, x_b, packed_a, mixed_a, two_b
-
-    gain, shift, block_a, x_b, packed_a, mixed_a, two_b = fenced(
-        ready, first_part, four_a, one_b, part_a, x_a
-    )
-
-    two_b, out_near = bar((two_b, out_near))
-    weight_out = plan.fetch_far(out_near)
-
-    def second_part(x_b, gain, shift, two_b, pair_c, part_b, part_c, spot_rows, grad_sent):
-        four_b, one_c, grad_sent = bar(
-            (plan.gather_core(two_b), plan.gather_side(pair_c, 0), grad_sent)
-        )
-        grad_rows = plan.to_experts(grad_sent)
+        return gain, shift, block_a, x_b, packed_a, mixed_a, two_b, pair_c
+
+    gain, shift, block_a, x_b, packed_a, mixed_a, two_b, pair_c = fenced(
+        ready, first_part, two_a, deep_bc, parts, x_a
+    )
+    two_b, in_near, out_low = bar((two_b, in_near, out_low))
+    weight_in = plan.fetch_far(in_near)
+    out_near = plan.fetch_near(out_low)
+
+    def second_part(x_b, gain, shift, two_b, pair_c, part_b):
+        four_b, one_c = bar((plan.gather_core(two_b), plan.gather_side(pair_c, 0)))
         block_b = plan.gather_join(four_b, part_b)
         x_c, hidden_b, slope_b = mlp_forward(x_b, gain[1], shift[1], block_b)
         two_c, x_c = bar((plan.gather_side(one_c, 1), x_c))
+        return block_b, x_c, hidden_b, slope_b, two_c
+
+    block_b, x_c, hidden_b, slope_b, two_c = fenced(
+        ready, second_part, x_b, gain, shift, two_b, pair_c, part_b
+    )
+    two_c, out_near = bar((two_c, out_near))
+    weight_out = plan.fetch_far(out_near)
+
+    def rows_part(x_c, gain, shift, two_c, part_c, spot_rows, grad_sent):
+        grad_rows = plan.to_experts(grad_sent)
         block_c = plan.gather_join(bar(plan.gather_core(two_c)), part_c)
         x_d, packed_c, mixed_c = attend_forward(x_c, gain[2], shift[2], block_c)
-        x_d, grad_rows = bar((x_d, grad_rows))
-        rows = plan.to_experts(dispatch(spot_rows, flat(x_d), gain[3], shift[3], slots))
-        return block_b, block_c, x_c, x_d, hidden_b, slope_b, packed_c, mixed_c, rows, grad_rows
-
-    block_b, block_c, x_c, x_d, hidden_b, slope_b, packed_c, mixed_c, rows, grad_rows = fenced(
-        ready, second_part, x_b, gain, shift, two_b, pair_c, part_b, part_c, spot_rows, grad_sent
+        sent = dispatch(spot_rows, flat(x_d), gain[3], shift[3], slots)
+        sent, grad_rows = bar((sent, grad_rows))
+        return block_c, x_d, packed_c, mixed_c, plan.to_experts(sent), grad_rows
+
+    block_c, x_d, packed_c, mixed_c, rows, grad_rows = fenced(
+        ready, rows_part, x_c, gain, shift, two_c, part_c, spot_rows, grad_sent
     )
     hidden, slope = expert_forward(rows, weight_in)
 
@@ -901,15 +911,17 @@
     )
     dx_b, home, down_other = bar((dx_b, home, down_other))
 
-    def attend_part(gain, shift, block_a, x_a, packed_a, mixed_a, pair_b, dx_b):
+    def attend_part(gain, shift, block_a, x_a, packed_a, mixed_a, pair_b, pair_c, dx_b):
+        own_c, far_c = plan.scatter_send(plan.scatter_stack(pair_c))
         dx_a, dpacked_a, normed_a, low_a, gain_a, shift_a = attend_backward(
             x_a, dx_b, packed_a, gain[0], shift[0], block_a
         )
-        pair_b, dx_a = bar((plan.scatter_side(pair_b, 0), dx_a))
-        return dx_a, dpacked_a, normed_a, low_a, gain_a, shift_a, pair_b
-
-    dx_a, dpacked_a, normed_a, low_a, gain_a, shift_a, pair_b = fenced(
-        ready, attend_part, gain, shift, block_a, x_a, packed_a, mixed_a, pair_b, dx_b
+        pair_b, dx_a, far_c = bar((plan.scatter_side(pair_b, 0), dx_a, far_c))
+        pair_c = plan.scatter_add(own_c, far_c)
+        return dx_a, dpacked_a, normed_a, low_a, gain_a, shift_a, pair_b, pair_c
+
+    dx_a, dpacked_a, normed_a, low_a, gain_a, shift_a, pair_b, pair_c = fenced(
+        ready, attend_part, gain, shift, block_a, x_a, packed_a, mixed_a, pair_b, pair_c, dx_b
     )
     pair_b, in_pair = bar((pair_b, in_pair))
     in_own, in_other = plan.share_send(in_pair)
@@ -921,13 +933,13 @@
             plan.wide, core, (flat(normed_a), flat(dpacked_a)), (flat(low_a), flat(mixed_a))
         )
         pair_b, sum_a, act_out = bar((plan.scatter_side(pair_b, 1), sum_a, act_out))
-        return norm_grads, sum_a, plan.scatter_stack(pair_b, pair_c), act_out, grad_gate
-
-    norm_grads, sum_a, deep_bc, act_out, grad_gate = fenced(
+        return norm_grads, sum_a, plan.scatter_stack(pair_b), plan.scatter_near(pair_c), act_out, grad_gate
+
+    norm_grads, sum_a, deep_b, near_c, act_out, grad_gate = fenced(
         ready, combine_part, dpacked_a, normed_a, low_a, mixed_a, pair_b, pair_c,
         (gain_a, gain_b) + gains + (shift_a, shift_b) + shifts, x_d, spots, gates, cot, home,
     )
-    own_bc, far_bc = plan.scatter_send(deep_bc)
+    own_b, far_b = plan.scatter_send(deep_b)
 
 
     def fifth_part(sum_a, act_out, grad_gate, dx_a):
@@ -939,22 +951,22 @@
     deep_a, act_out, grad_gate, dx_a = fenced(
         ready, fifth_part, sum_a, act_out, grad_gate, dx_a
     )
-    deep_a, own_bc, far_bc, in_other = bar((deep_a, own_bc, far_bc, in_other))
-
-    def sixth_part(deep_a, own_bc, far_bc, norm_grads, shares):
+    deep_a, own_b, far_b, in_other = bar((deep_a, own_b, far_b, in_other))
+
+    def sixth_part(deep_a, own_b, far_b, near_c, norm_grads, shares):
         norm_pieces = plan.small_send(norm_grads)
         own_a, far_a = plan.scatter_send(deep_a)
-        near_bc = plan.scatter_near(plan.scatter_add(own_bc, far_bc))
-        near_bc, far_a = bar((near_bc, far_a))
+        near_b = plan.scatter_near(plan.scatter_add(own_b, far_b))
+        near_b, far_a = bar((near_b, far_a))
         grad_exp_in, grad_exp_out = [plan.share_sum(*share) for share in shares]
         near_a, mine_bc = bar(
-            (plan.scatter_near(plan.scatter_add(own_a, far_a)), plan.scatter_core(near_bc))
+            (plan.scatter_near(plan.scatter_add(own_a, far_a)), plan.scatter_core(plan.scatter_join(near_b, near_c)))
         )
         mine_norms = plan.small_sum(norm_pieces)
         return plan.scatter_core(near_a), mine_bc, mine_norms, grad_exp_in, grad_exp_out
 
     mine_a, mine_bc, mine_norms, grad_exp_in, grad_exp_out = fenced(
-        ready, sixth_part, deep_a, own_bc, far_bc, norm_grads,
+        ready, sixth_part, deep_a, own_b, far_b, near_c, norm_grads,
         ((in_own, in_other), (down_own, down_other)),
     )
     mine_b, mine_c = plan.scatter_unstack(mine_bc, 2 * FF, 4 * D)

time: 761 us -> 740 us (0.972)
  waiting for transfers between devices: 183 us -> 146 us
  blocking collectives: 68.7 us -> 77.7 us
  other arithmetic: 86 us -> 94.2 us
    ppermute x44 -> x47, waiting for transfers between devices: 119 us -> 87.2 us  [hop(): return lax.ppermute(value, axes, [(i, i ^ bit) for i in range(size)])]
    all_gather x1, waiting for transfers between devices: 29.5 us -> 0.01 us  [gather_depth(): return lax.all_gather(mine[None], self.dp, axis=0, tiled=True)]
    all_to_all x3, waiting for transfers between devices: 33.6 us -> 58.2 us  [to_experts(): lax.all_to_all(chunks, ('dh',) + self.expert, 0, 0, tiled=True)]
    all_gather x0 -> x1, blocking collectives: none -> 16.9 us  [gather_depth(): return lax.all_gather(mine[None], self.dp, axis=0, tiled=True)]
    all_to_all x1, blocking collectives: 68.7 us -> 60.8 us  [to_experts(): lax.all_to_all(chunks, ('dh',) + self.expert, 0, 0, tiled=True)]
    concatenate x9 -> x10, other arithmetic: 10.4 us -> 16.7 us  [gather_side(): jnp.concatenate([own, new])]
    ppermute x44 -> x47, starting transfers between devices: 42.6 us -> 46.3 us  [hop(): return lax.ppermute(value, axes, [(i, i ^ bit) for i in range(size)])]
    squeeze x16 -> x18, local copies, waits for them, and re-layouts: 16.5 us -> 14.3 us  [pick(): return lax.dynamic_index_in_dim(value, at, axis, keepdims=False)]
  transfers between devices with their start and end apart: 53 -> 56, of which waited for: 22 -> 21; matrix products, arithmetic and copies ran while one was open for 18% -> 19% of each run, Pallas kernels for 28% -> 28%
where the time goes in v5:
time: 740 us; the launch traced here: 732 us
  Pallas kernels  243 us (33%)
  waiting for transfers between devices  146 us (20%)
  other arithmetic  94.2 us (13%)
  blocking collectives  77.7 us (10%)
  local copies, waits for them, and re-layouts  75 us (10%)
  starting transfers between devices  70.4 us (10%)
  between operations  15.1 us (2%)
  matrix products  7.89 us (1%)
    ppermute x47, waiting for transfers between devices, hop(): return lax.ppermute(value, axes, [(i, i ^ bit) for i in range(size)])  87.2 us
    all_to_all x1, blocking collectives, to_experts(): lax.all_to_all(chunks, ('dh',) + self.expert, 0, 0, tiled=True)  60.8 us
    all_to_all x3, waiting for transfers between devices, to_experts(): lax.all_to_all(chunks, ('dh',) + self.expert, 0, 0, tiled=True)  58.2 us
    pallas_call x5, Pallas kernels, weight_grad(): pl.pallas_call(functools.partial(weight_grad_body, tiles, starts, split),...  56.7 us
    pallas_call x2, Pallas kernels, attend_backward(): pl.pallas_call(attend_backward_body, grid=(images,), in_specs=[image(D),...  49 us
    ppermute x47, starting transfers between devices, hop(): return lax.ppermute(value, axes, [(i, i ^ bit) for i in range(size)])  46.3 us
    pallas_call x2, Pallas kernels, attend_forward(): pl.pallas_call(attend_forward_body, grid=(images,), in_specs=[image(D), w...  26.1 us
    pallas_call x1, Pallas kernels, expert_backward(): pl.pallas_call(expert_backward_body, grid=(count // ROW_TILE,), in_specs=...  23 us
  transfers between devices with their start and end apart: 56, of which 21 were waited for; matrix products, arithmetic and copies ran while one was open for 19% of the time, Pallas kernels for 28%

profile of v5, /device:TPU:1, one launch (start us, length us, event | category | flops | bytes accessed | tf_op | source)
XLA Modules:
  0.0 731.7 jit_solution(10087402487226260044)
XLA Ops:
  12.2 16.9 %all_gather.15 = bf16[4,48,1664]{2,1,0:T(8,128)(2,1)S(1)} all-gather(bf16[1,48,1664]{2,1,0:T(8,128)(2,1)S(1)} %maximum_select_fusion.7), channel_id=1, replica_groups=mesh['dh'=2,'dl'=2,'y'=2,'x'=2,'c'=2] {'dh','dl'}, dimensions={0}, use_global_device_ids=true | all-gather | bytes 798720 | tf_op jit(solution)/shard_map/all_gather | solution.py:587
  35.3 4.1 convert_element_type.313
  39.3 27.8 %conditional.13 = (bf16[16,48,768]{2,1,0:T(8,128)(2,1)}, bf16[16,48,896]{2,1,0:T(8,128)(2,1)}) conditional(s32[]{:T(128)} %bitcast.83, () %tuple.172, bf16[4,48,1664]{2,1,0:T(8,128)(2,1)S(1)} %all_gather.15), branch_computations={%region_0.1_spmd, %region_1.2_spmd} | conditional | flops 1916928 | bytes 16613552 | solution.py:750
  41.9 6.8 collective-permute-done
  51.5 12.1 %collective-permute-done.2 = bf16[8,48,768]{2,1,0:T(8,128)(2,1)S(1)} collective-permute-done((bf16[8,48,768]{2,1,0:T(8,128)(2,1)S(1)}, bf16[8,48,768]{2,1,0:T(8,128)(2,1)S(1)}, u32[]{:S(2)}, u32[]{:S(2)}) %collective-permute-start.2) | collective-permute-done | bytes 589856 | tf_op jit(solution)/shard_map/cond/branch_1_fun/ppermute | solution.py:569
  67.1 18.7 %conditional.14 = (s32[3,208,2]{1,0,2:T(4,128)}, f32[3,208,2]{1,0,2:T(4,128)}, f32[3,208,768]{2,1,0:T(8,128)}, f32[3,208,768]{2,1,0:T(8,128)}, bf16[1536,768]{1,0:T(8,128)(2,1)}) conditional(s32[]{:T(128)} %bitcast.83, () %tuple.173, (s32[591,2]{0,1:T(2,128)S(1)}, f32[591,2]{0,1:T(2,128)S(1)}, f32[591,768]{1,0:T(8,128)S(1)}, ...), branch_computations={%region_2.3_spmd, %region_3.7_spmd} | conditional | flops 752782976 | bytes 24538492 | solution.py:750
  67.6 4.6 reduce-window.4
  76.9 5.7 dispatch_grad.1
  85.8 3.2 broadcast_select_fusion.1
  89.5 4.0 convert_bitcast_fusion.1
  93.6 57.4 %conditional.15 = (f32[4,1,768]{2,0,1:T(4,128)S(1)}, f32[4,1,768]{2,0,1:T(4,128)S(1)}, bf16[768,3328]{1,0:T(8,128)(2,1)}, f32[3,208,768]{2,1,0:T(8,128)}, bf16[3...) conditional(s32[]{:T(128)} %bitcast.83, () %tuple.171, ...), branch_computations={%region_7.8_spmd, %region_8.9_spmd} | conditional | flops 928546176 | bytes 48031396 | solution.py:750
  101.4 12.1 %collective-permute-done.11 = bf16[4,48,1536]{2,1,0:T(8,128)(2,1)} collective-permute-done((bf16[4,48,1536]{2,1,0:T(8,128)(2,1)}, bf16[4,48,1536]{2,1,0:T(8,128)(2,1)}, u32[]{:S(2)}, u32[]{:S(2)}) %collective-permute-start.11) | collective-permute-done | bytes 589856 | tf_op jit(solution)/shard_map/cond/branch_1_fun/ppermute | solution.py:569
  114.2 3.0 pad_maximum_fusion.6
  121.0 4.6 join.3.qkv_ref.proj_ref
  126.7 13.0 %attend_forward.2 = (f32[3,208,768]{2,1,0:T(8,128)}, bf16[3,208,2304]{2,1,0:T(8,128)(2,1)}, bf16[3,208,768]{2,1,0:T(8,128)(2,1)}) custom-call(f32[3,208,768]{2,1,0:T(8,128)} %get-tuple-element.234.x_ref, f32[1,768]{1,0:T(1,128)S(1)} %get-tuple-element.933.gain_ref, f32[1,768]{1,0:T(1,128)S(1)} %get-tuple-element.932.shift_ref, ...), custom_call_target="tpu_custom_call" | custom-call | flops 925000000 | bytes 3250000 | tf_op jit(solution)/shard_map/cond/branch_1_fun/attend_forward/pallas_call | solution.py:133
  139.8 3.7 collective-permute-done.13
  144.4 3.3 pad_maximum_fusion.5
  147.7 3.2 pad_maximum_fusion.4
  150.9 4.2 maximum_select_fusion.4
  160.3 48.6 %conditional.16 = (bf16[768,6144]{1,0:T(8,128)(2,1)}, f32[3,208,768]{2,1,0:T(8,128)}, bf16[3,208,3072]{2,1,0:T(8,128)(2,1)}, bf16[3,208,3072]{2,1,0:T(8,128)(2,1...) conditional(s32[]{:T(128)} %bitcast.83, () %tuple.180, (bf16[16,48,1536]{2,1,0:T(8,128)(2,1)}, ...), branch_computations={%region_9.10_spmd, %region_10.11_spmd} | conditional | flops 1476770688 | bytes 50191248 | solution.py:750
  160.3 3.1 collective-permute-start.15
  165.4 6.3 collective-permute-done.17
  182.9 7.5 %join.4.up_ref.down_ref = bf16[768,6144]{1,0:T(8,128)(2,1)} custom-call(s32[4,32]{1,0:T(4,128)S(1)} %pad_add_fusion.1.at_ref, bf16[16,48,1536]{2,1,0:T(8,128)(2,1)} %get-tuple-element.249.refs_0_, bf16[16,48,1536]{2,1,0:T(8,128)(2,1)} %get-tuple-element.250.refs_1_, bf16[16,48,1536]{2,1,0:T(8,128)(2,1)S(1)} %collective-permute-done.15.refs_2_, ...), custom_call_target="tpu_custom_call" | custom-call | bytes 4718592 | tf_op jit(solution)/shard_map/cond/branch_1_fun/join/pallas_call | solution.py:531
  190.4 15.1 %mlp_forward.1 = (f32[3,208,768]{2,1,0:T(8,128)}, bf16[3,208,3072]{2,1,0:T(8,128)(2,1)}, bf16[3,208,3072]{2,1,0:T(8,128)(2,1)}) custom-call(f32[3,208,768]{2,1,0:T(8,128)} %get-tuple-element.259.x_ref, f32[1,768]{1,0:T(1,128)} %get-tuple-element.953.gain_ref, f32[1,768]{1,0:T(1,128)} %get-tuple-element.952.shift_ref, bf16[768,6144]{1,0:T(8,128)(2,1)} %join.4.up_ref.down_ref, ...), custom_call_target="tpu_custom_call" | custom-call | flops 1475000064 | bytes 5250000 | tf_op jit(solution)/shard_map/cond/branch_1_fun/mlp_forward/pallas_call | solution.py:229
  210.4 4.2 maximum_select_fusion.5
  216.0 124.0 %conditional.17 = (bf16[768,3072]{1,0:T(8,128)(2,1)}, f32[3,208,768]{2,1,0:T(8,128)}, bf16[3,208,2304]{2,1,0:T(8,128)(2,1)}, bf16[3,208,768]{2,1,0:T(8,128)(2,1)...) conditional(s32[]{:T(128)} %bitcast.83, () %tuple.179, (bf16[16,48,768]{2,1,0:T(8,128)(2,1)S(1)}, ...), branch_computations={%region_11.12_spmd, %region_12.13_spmd} | conditional | flops 1300001024 | bytes 28065448 | solution.py:750
  216.1 7.2 all-to-all-start.1
  232.6 4.5 join.5.qkv_ref.proj_ref
  237.1 13.1 %attend_forward.3 = (f32[3,208,768]{2,1,0:T(8,128)}, bf16[3,208,2304]{2,1,0:T(8,128)(2,1)}, bf16[3,208,768]{2,1,0:T(8,128)(2,1)}) custom-call(f32[3,208,768]{2,1,0:T(8,128)} %get-tuple-element.274.x_ref, f32[1,768]{1,0:T(1,128)S(1)} %get-tuple-element.964.gain_ref, f32[1,768]{1,0:T(1,128)S(1)} %get-tuple-element.955.shift_ref, ...), custom_call_target="tpu_custom_call" | custom-call | flops 925000000 | bytes 3250000 | tf_op jit(solution)/shard_map/cond/branch_1_fun/attend_forward/pallas_call | solution.py:133
  250.1 5.1 dispatch.1
  255.3 24.0 %all-to-all-done.1 = bf16[16,96,768]{2,1,0:T(8,128)(2,1)} async-done(((bf16[16,96,768]{2,1,0:T(8,128)(2,1)}), bf16[16,96,768]{2,1,0:T(8,128)(2,1)}, u32[]{:S(2)}, u32[]{:S(2)}) %all-to-all-start.1) | async-done | bytes 2359328 | tf_op jit(solution)/shard_map/cond/branch_1_fun/all_to_all | solution.py:740
  279.2 60.8 %all_to_all.25 = bf16[16,96,768]{2,1,0:T(8,128)(2,1)} all-to-all(bf16[16,96,768]{2,1,0:T(8,128)(2,1)S(1)} %bitcast.226), channel_id=1, replica_groups=mesh['dh'=2,'dl'=2,'y'=2,'x'=2,'c'=2] {'dh','y','x','c'}, dimensions={0} | all-to-all | bytes 4718592 | tf_op jit(solution)/shard_map/cond/branch_1_fun/all_to_all | solution.py:740
  340.0 18.5 %expert_forward.1 = (bf16[1536,3072]{1,0:T(8,128)(2,1)}, bf16[1536,3072]{1,0:T(8,128)(2,1)}) custom-call(bf16[1536,768]{1,0:T(8,128)(2,1)} %get-tuple-element.595.rows_ref, bf16[768,3072]{1,0:T(8,128)(2,1)} %bitcast.237), custom_call_target="tpu_custom_call" | custom-call | flops 1800000000 | bytes 6500000 | tf_op jit(solution)/shard_map/expert_forward/pallas_call | solution.py:409
  358.5 35.2 %conditional.18 = (bf16[1536,3072]{1,0:T(8,128)(2,1)}, bf16[1536,768]{1,0:T(8,128)(2,1)}, bf16[768,3072]{1,0:T(8,128)(2,1)}) conditional(s32[]{:T(128)} %bitcast.83, () %tuple.186, (bf16[1536,768]{1,0:T(8,128)(2,1)}, bf16[1536,3072]{1,0:T(8,128)(2,1)}, bf16[768,3072]{1,0:T(8,128)(2,1)}, bf16[768,3072]{1,0:T(8,128)(2,1)}, ...), branch_computations={%region_13.14_spmd, %region_14.15_spmd} | conditional | flops 5411939328 | bytes 38331120 | solution.py:750
  358.7 23.0 %expert_backward.1 = (bf16[1536,3072]{1,0:T(8,128)(2,1)}, bf16[1536,768]{1,0:T(8,128)(2,1)}) custom-call(bf16[1536,768]{1,0:T(8,128)(2,1)} %get-tuple-element.284.grad_ref.refs_0_, bf16[1536,3072]{1,0:T(8,128)(2,1)} %get-tuple-element.285.slope_ref, bf16[768,3072]{1,0:T(8,128)(2,1)} %get-tuple-element.286.in_ref, bf16[768,3072]{1,0:T(8,128)(2,1)} %get-tuple-element.287.out_ref), custom_call_target="tpu_custom_call" | custom-call | flops 3600000000 | bytes 8250000 | tf_op jit(solution)/shard_map/cond/branch_1_fun/expert_backward/pallas_call | solution.py:434
  381.8 11.9 %weight_grad.5 = bf16[768,3072]{1,0:T(8,128)(2,1)} custom-call(s32[1]{0:T(128)} %constant.597.clone.at_ref, bf16[1536,768]{1,0:T(8,128)(2,1)} %get-tuple-element.284.grad_ref.refs_0_, bf16[1536,3072]{1,0:T(8,128)(2,1)S(1)} %bitcast.242), custom_call_target="tpu_custom_call" | custom-call | flops 1811939328 | bytes 1769472 | tf_op jit(solution)/shard_map/cond/branch_1_fun/weight_grad/pallas_call | solution.py:501
  393.8 60.9 %conditional.19 = (bf16[1536,768]{1,0:T(8,128)(2,1)}, bf16[768,3072]{1,0:T(8,128)(2,1)}, bf16[1536,768]{1,0:T(8,128)(2,1)S(1)}) conditional(s32[]{:T(128)} %bitcast.83, () %tuple.185, (bf16[1536,768]{1,0:T(8,128)(2,1)}, bf16[1536,768]{1,0:T(8,128)(2,1)}, bf16[1536,3072]{1,0:T(8,128)(2,1)}, bf16[1536,3072]{1,0:T(8,128)(2,1)}, ...), branch_computations={%region_15.16_spmd, %region_16.17_spmd} | conditional | flops 9060876288 | bytes 72548504 | solution.py:750
  393.9 5.6 all-to-all-start.3
  399.5 13.1 %weight_grad.6 = bf16[768,3072]{1,0:T(8,128)(2,1)} custom-call(s32[1]{0:T(128)} %constant.599.clone.at_ref, bf16[1536,768]{1,0:T(8,128)(2,1)} %get-tuple-element.294.refs_0_, bf16[1536,3072]{1,0:T(8,128)(2,1)} %get-tuple-element.295.refs_1_), custom_call_target="tpu_custom_call" | custom-call | flops 1811939328 | bytes 1769472 | tf_op jit(solution)/shard_map/cond/branch_1_fun/weight_grad/pallas_call | solution.py:501
  412.6 7.9 %convolution_convert_fusion = bf16[1536,768]{1,0:T(8,128)(2,1)S(1)} fusion(bf16[1536,3072]{1,0:T(8,128)(2,1)S(1)} %bitcast.244, bf16[768,3072]{1,0:T(8,128)(2,1)S(1)} %copy-done.15), kind=kOutput, calls=%fused_computation.114 | convolution fusion | flops 7248936960 | bytes 16515072 | tf_op jit(solution)/shard_map/cond/branch_1_fun/dot_general | solution.py:38
  420.5 34.3 %all-to-all-done.3 = bf16[16,96,768]{2,1,0:T(8,128)(2,1)} async-done(((bf16[16,96,768]{2,1,0:T(8,128)(2,1)}), bf16[16,96,768]{2,1,0:T(8,128)(2,1)}, u32[]{:S(2)}, u32[]{:S(2)}) %all-to-all-start.3) | async-done | bytes 2359328 | tf_op jit(solution)/shard_map/cond/branch_1_fun/all_to_all | solution.py:740
  456.2 5.4 all-to-all-start.4
  461.6 40.5 %conditional.20 = (bf16[768,1536]{1,0:T(8,128)(2,1)}, bf16[768,1536]{1,0:T(8,128)(2,1)}, f32[3,208,768]{2,1,0:T(8,128)}, f32[1,768]{1,0:T(1,128)S(1)}, f32[1,768...) conditional(s32[]{:T(128)} %bitcast.83, () %tuple.170, (s32[]{:T(128)}, ...), branch_computations={%region_17.18_spmd, %region_18.19_spmd} | conditional | flops 2111100416 | bytes 20848716 | solution.py:750
  462.3 5.5 return_grad.1
  467.8 24.2 %attend_backward.2 = (f32[3,208,768]{2,1,0:T(8,128)}, bf16[3,208,2304]{2,1,0:T(8,128)(2,1)}, bf16[3,208,768]{2,1,0:T(8,128)(2,1)S(1)}, bf16[3,208,768]{2,1,0:T(8...) custom-call(f32[3,208,768]{2,1,0:T(8,128)} %get-tuple-element.301.x_ref, ...), custom_call_target="tpu_custom_call" | custom-call | flops 1000000000 | bytes 5500000 | tf_op jit(solution)/shard_map/cond/branch_1_fun/attend_backward/pallas_call | solution.py:191
  493.8 8.3 %weight_grad.7 = (bf16[768,1536]{1,0:T(8,128)(2,1)}, bf16[768,1536]{1,0:T(8,128)(2,1)}) custom-call(s32[1]{0:T(128)} %bitcast.20.at_ref, bf16[624,768]{1,0:T(8,128)(2,1)S(1)} %bitcast.232, bf16[624,768]{1,0:T(8,128)(2,1)S(1)} %bitcast.233, bf16[624,2304]{1,0:T(8,128)(2,1)S(1)} %bitcast.228, bf16[624,768]{1,0:T(8,128)(2,1)} %bitcast.27.refs_3_), custom_call_target="tpu_custom_call" | custom-call | flops 736100352 | bytes 1769472 | tf_op jit(solution)/shard_map/cond/branch_1_fun/weight_grad/pallas_call | solution.py:501
  506.8 58.0 %conditional.21 = (bf16[4,48,768]{2,1,0:T(8,128)(2,1)S(1)}, bf16[4,48,768]{2,1,0:T(8,128)(2,1)}, bf16[4,2,2,48,1536]{4,3,2,1,0:T(8,128)(2,1)}, bf16[4,2,2,48,153...) conditional(s32[]{:T(128)} %bitcast.83, () %tuple.169, ...), branch_computations={%region_20.21_spmd, %region_21.22_spmd} | conditional | flops 2964895488 | bytes 140792064 | solution.py:750
  508.3 14.7 %mlp_backward.1 = (f32[3,208,768]{2,1,0:T(8,128)}, bf16[3,208,3072]{2,1,0:T(8,128)(2,1)}, bf16[3,208,768]{2,1,0:T(8,128)(2,1)}, bf16[3,208,768]{2,1,0:T(8,128)(2...) custom-call(f32[3,208,768]{2,1,0:T(8,128)} %get-tuple-element.324.x_ref, f32[3,208,768]{2,1,0:T(8,128)} %get-tuple-element.325.dy_ref, ...), custom_call_target="tpu_custom_call" | custom-call | flops 1475000064 | bytes 6250000 | tf_op jit(solution)/shard_map/cond/branch_1_fun/mlp_backward/pallas_call | solution.py:266
  532.7 13.9 %weight_grad.8 = (bf16[768,3072]{1,0:T(8,128)(2,1)}, bf16[768,3072]{1,0:T(8,128)(2,1)}) custom-call(s32[1]{0:T(128)} %bitcast.35.at_ref, bf16[624,768]{1,0:T(8,128)(2,1)S(1)} %bitcast.230, bf16[624,768]{1,0:T(8,128)(2,1)S(1)} %bitcast.231, bf16[624,3072]{1,0:T(8,128)(2,1)S(1)} %bitcast.227, bf16[624,3072]{1,0:T(8,128)(2,1)} %bitcast.39.refs_3_), custom_call_target="tpu_custom_call" | custom-call | flops 1472200704 | bytes 3538944 | tf_op jit(solution)/shard_map/cond/branch_1_fun/weight_grad/pallas_call | solution.py:501
  550.8 8.2 %collective-permute-done.26 = bf16[4,48,768]{2,1,0:T(8,128)(2,1)S(1)} collective-permute-done((bf16[4,48,768]{2,1,0:T(8,128)(2,1)S(1)}, bf16[4,48,768]{2,1,0:T(8,128)(2,1)S(1)}, u32[]{:S(2)}, u32[]{:S(2)}) %collective-permute-start.26) | collective-permute-done | bytes 294944 | tf_op jit(solution)/shard_map/cond/branch_1_fun/ppermute | solution.py:569
  566.1 37.9 %conditional.22 = (f32[3,208,768]{2,1,0:T(8,128)}, bf16[3,208,2304]{2,1,0:T(8,128)(2,1)}, bf16[3,208,768]{2,1,0:T(8,128)(2,1)}, bf16[3,208,768]{2,1,0:T(8,128)(2...) conditional(s32[]{:T(128)} %bitcast.83, () %tuple.168, ...), branch_computations={%region_22.23_spmd, %region_23.24_spmd} | conditional | flops 1006488064 | bytes 31809184 | solution.py:750
  573.3 24.8 %attend_backward.3 = (f32[3,208,768]{2,1,0:T(8,128)}, bf16[3,208,2304]{2,1,0:T(8,128)(2,1)}, bf16[3,208,768]{2,1,0:T(8,128)(2,1)}, bf16[3,208,768]{2,1,0:T(8,128...) custom-call(f32[3,208,768]{2,1,0:T(8,128)} %get-tuple-element.366.x_ref, f32[3,208,768]{2,1,0:T(8,128)} %get-tuple-element.367.dy_ref, ...), custom_call_target="tpu_custom_call" | custom-call | flops 1000000000 | bytes 5500000 | tf_op jit(solution)/shard_map/cond/branch_1_fun/attend_backward/pallas_call | solution.py:191
  598.2 4.1 fusion.64
  608.9 30.9 %conditional.23 = (f32[768,8]{0,1:T(8,128)S(1)}, bf16[768,1536]{1,0:T(8,128)(2,1)}, bf16[768,1536]{1,0:T(8,128)(2,1)}, f32[48,1536]{1,0:T(8,128)S(1)}, f32[3,208...) conditional(s32[]{:T(128)} %bitcast.83, () %tuple.167, (f32[1,768]{1,0:T(1,128)S(1)}, ...), branch_computations={%region_25.26_spmd, %region_26.27_spmd} | conditional | flops 1491040128 | bytes 30086432 | solution.py:750
  613.7 9.5 %weight_grad.9 = (bf16[768,1536]{1,0:T(8,128)(2,1)}, bf16[768,1536]{1,0:T(8,128)(2,1)}) custom-call(s32[1]{0:T(128)} %bitcast.59.at_ref, bf16[624,768]{1,0:T(8,128)(2,1)} %bitcast.60.refs_0_, bf16[624,768]{1,0:T(8,128)(2,1)} %bitcast.61.refs_1_, bf16[624,2304]{1,0:T(8,128)(2,1)} %bitcast.62.refs_2_, bf16[624,768]{1,0:T(8,128)(2,1)} %bitcast.248), custom_call_target="tpu_custom_call" | custom-call | flops 736100352 | bytes 1769472 | tf_op jit(solution)/shard_map/cond/branch_1_fun/weight_grad/pallas_call | solution.py:501
  623.2 6.9 combine.1
  630.1 5.8 collective-permute-done.39
  644.5 37.6 %conditional.24 = (bf16[4,48,1536]{2,1,0:T(8,128)(2,1)S(1)}, f32[591,768]{1,0:T(8,128)}, f32[591,2]{0,1:T(2,128)S(1)}, f32[591,768]{1,0:T(8,128)}) conditional(s32[]{:T(128)} %bitcast.83, () %tuple.166, (bf16[768,1536]{1,0:T(8,128)(2,1)}, bf16[768,1536]{1,0:T(8,128)(2,1)}, f32[3,208,768]{2,1,0:T(8,128)}, f32[3,208,2]{2,1,0:T(8,128)}, ...), branch_computations={%region_27.28_spmd, %region_28.29_spmd} | conditional | flops 9437204 | bytes 55262188 | solution.py:750
  647.4 4.4 collective-permute-done.29
  654.9 14.2 %collective-permute-done.30 = bf16[4,2,48,768]{3,2,0,1:T(8,128)(2,1)} collective-permute-done((bf16[4,2,48,768]{3,2,0,1:T(8,128)(2,1)S(1)}, bf16[4,2,48,768]{3,2,0,1:T(8,128)(2,1)}, u32[]{:S(2)}, u32[]{:S(2)}) %collective-permute-start.30) | collective-permute-done | bytes 589856 | tf_op jit(solution)/shard_map/cond/branch_1_fun/ppermute | solution.py:569
  682.1 3.0 collective-permute-done.45
  685.1 34.7 %conditional.25 = (f32[24,3072]{1,0:T(8,128)}, f32[24,9216]{1,0:T(8,128)S(1)}, f32[24,8]{1,0:T(8,128)S(1)}, f32[2,192,3072]{2,1,0:T(8,128)}, f32[2,192,3072]{2,1,0:T(8,128)}) conditional(s32[]{:T(128)} %bitcast.83, () %tuple.198, (bf16[4,48,1536]{2,1,0:T(8,128)(2,1)S(1)}, bf16[2,48,3072]{2,1,0:T(8,128)(2,1)}, bf16[2,48,3072]{2,1,0:T(8,128)(2,1)}, ...), branch_computations={%region_29.30_spmd, %region_30.32_spmd} | conditional | flops 12760929 | bytes 66374716 | solution.py:750
  690.7 5.8 all-to-all-start
  696.5 2.9 convert_element_type.292
  (381 shorter events, 182.5 us)
Async XLA Ops:
  7.2 78.6 %all-gather.4.cloned.1.call-start = ((), (), s32[]{:S(2)}) async-start(), calls=%async_computation.7 | async-start | bytes 2211840 | tf_op jit(solution)/shard_map/all_gather | solution.py:587
  10.8 1.3 collective-permute-start.40
  11.0 23.0 %copy-start.42 = (s32[591,2]{0,1:T(2,128)S(1)}, s32[591,2]{0,1:T(2,128)}, u32[]{:S(2)}) copy-start(s32[591,2]{0,1:T(2,128)} %param.48) | copy-start | bytes 14188
  29.2 4.0 collective-permute-start.41
  34.0 306.0 %all-gather.6.cloned.1.call-start = ((), (), s32[]{:S(2)}) async-start(), calls=%async_computation.8 | async-start | bytes 7077888 | tf_op jit(solution)/shard_map/all_gather | solution.py:723
  39.3 27.8 %copy-start.20 = (f32[591,768]{1,0:T(8,128)S(1)}, f32[591,768]{1,0:T(8,128)}, u32[]{:S(2)}) copy-start(f32[591,768]{1,0:T(8,128)} %param.49) | copy-start | bytes 5446660
  39.3 27.8 %copy-start.43 = (f32[591,2]{0,1:T(2,128)S(1)}, f32[591,2]{0,1:T(2,128)}, u32[]{:S(2)}) copy-start(f32[591,2]{0,1:T(2,128)} %param.47) | copy-start | bytes 14188
  39.4 9.4 %collective-permute-start.1 = (bf16[4,48,896]{2,1,0:T(8,128)(2,1)S(1)}, bf16[4,48,896]{2,1,0:T(8,128)(2,1)S(1)}, u32[]{:S(2)}, u32[]{:S(2)}) collective-permute-start(bf16[4,48,896]{2,1,0:T(8,128)(2,1)S(1)} %slice.116), channel_id=1, source_target_pairs={{0,4},{4,0},{1,5},{5,1},{2,6},{6,2},{3,7},{7,3},{8,12},{12,8},{9,1... | collective-permute-start | bytes 1032200 | tf_op jit(solution)/shard_map/cond/branch_1_fun/ppermute | solution.py:569
  40.7 8.0 %collective-permute-start = (bf16[4,48,768]{2,1,0:T(8,128)(2,1)S(1)}, bf16[4,48,768]{2,1,0:T(8,128)(2,1)S(1)}, u32[]{:S(2)}, u32[]{:S(2)}) collective-permute-start(bf16[4,48,768]{2,1,0:T(8,128)(2,1)S(1)} %slice.115), channel_id=1, source_target_pairs={{0,2},{2,0},{1,3},{3,1},{4,6},{6,4},{5,7},{7,5},{8,10},{10,8},{9,1... | collective-permute-start | bytes 884744 | tf_op jit(solution)/shard_map/cond/branch_1_fun/ppermute | solution.py:569
  49.0 15.8 %collective-permute-start.3 = (bf16[8,48,896]{2,1,0:T(8,128)(2,1)S(1)}, bf16[8,48,896]{2,1,0:T(8,128)(2,1)S(1)}, u32[]{:S(2)}, u32[]{:S(2)}) collective-permute-start(bf16[8,48,896]{2,1,0:T(8,128)(2,1)S(1)} %pad_maximum_fusion.2), channel_id=1, source_target_pairs={{0,2},{2,0},{1,3},{3,1},{4,6},{6,4},{5,7},{7,5},{8,10},{10,8},{9,1... | collective-permute-start | bytes 2064392 | tf_op jit(solution)/shard_map/cond/branch_1_fun/ppermute | solution.py:569
  50.3 13.4 %collective-permute-start.2 = (bf16[8,48,768]{2,1,0:T(8,128)(2,1)S(1)}, bf16[8,48,768]{2,1,0:T(8,128)(2,1)S(1)}, u32[]{:S(2)}, u32[]{:S(2)}) collective-permute-start(bf16[8,48,768]{2,1,0:T(8,128)(2,1)S(1)} %pad_maximum_fusion.3), channel_id=1, source_target_pairs={{0,4},{4,0},{1,5},{5,1},{2,6},{6,2},{3,7},{7,3},{8,12},{12,8},{9,1... | collective-permute-start | bytes 1769480 | tf_op jit(solution)/shard_map/cond/branch_1_fun/ppermute | solution.py:569
  89.0 61.9 %collective-permute-start.42 = (bf16[192,3072]{1,0:T(8,128)(2,1)}, bf16[192,3072]{1,0:T(8,128)(2,1)}, u32[]{:S(2)}, u32[]{:S(2)}) collective-permute-start(bf16[192,3072]{1,0:T(8,128)(2,1)} %get-tuple-element.994), channel_id=1, source_target_pairs={{0,16},{16,0},{1,17},{17,1},{2,18},{18,2},{3,19},{19,3},{4,20},{20... | collective-permute-start | bytes 3538952 | tf_op jit(solution)/shard_map/ppermute | solution.py:569
  94.0 23.2 %collective-permute-start.10 = (bf16[16,48,896]{2,1,0:T(8,128)(2,1)}, bf16[16,48,896]{2,1,0:T(8,128)(2,1)S(1)}, u32[]{:S(2)}, u32[]{:S(2)}) collective-permute-start(bf16[16,48,896]{2,1,0:T(8,128)(2,1)} %get-tuple-element.225.refs_1_), channel_id=1, source_target_pairs={{0,1},{1,0},{2,3},{3,2},{4,5},{5,4},{6,7},{7,6},{8,9},{9,8},{10,11... | collective-permute-start | bytes 4128776 | tf_op jit(solution)/shard_map/cond/branch_1_fun/ppermute | solution.py:569
  96.5 20.7 %collective-permute-start.9 = (bf16[16,48,768]{2,1,0:T(8,128)(2,1)}, bf16[16,48,768]{2,1,0:T(8,128)(2,1)S(1)}, u32[]{:S(2)}, u32[]{:S(2)}) collective-permute-start(bf16[16,48,768]{2,1,0:T(8,128)(2,1)} %get-tuple-element.224.refs_0_), channel_id=1, source_target_pairs={{0,1},{1,0},{2,3},{3,2},{4,5},{5,4},{6,7},{7,6},{8,9},{9,8},{10,11... | collective-permute-start | bytes 3538952 | tf_op jit(solution)/shard_map/cond/branch_1_fun/ppermute | solution.py:569
  98.7 14.8 %collective-permute-start.11 = (bf16[4,48,1536]{2,1,0:T(8,128)(2,1)}, bf16[4,48,1536]{2,1,0:T(8,128)(2,1)}, u32[]{:S(2)}, u32[]{:S(2)}) collective-permute-start(bf16[4,48,1536]{2,1,0:T(8,128)(2,1)} %get-tuple-element.220), channel_id=1, source_target_pairs={{0,2},{2,0},{1,3},{3,1},{4,6},{6,4},{5,7},{7,5},{8,10},{10,8},{9,1... | collective-permute-start | bytes 1769480 | tf_op jit(solution)/shard_map/cond/branch_1_fun/ppermute | solution.py:569
  99.9 14.3 %collective-permute-start.12 = (bf16[4,48,1536]{2,1,0:T(8,128)(2,1)S(1)}, bf16[4,48,1536]{2,1,0:T(8,128)(2,1)}, u32[]{:S(2)}, u32[]{:S(2)}) collective-permute-start(bf16[4,48,1536]{2,1,0:T(8,128)(2,1)S(1)} %get-tuple-element.221), channel_id=1, source_target_pairs={{0,4},{4,0},{1,5},{5,1},{2,6},{6,2},{3,7},{7,3},{8,12},{12,8},{9,1... | collective-permute-start | bytes 1769480 | tf_op jit(solution)/shard_map/cond/branch_1_fun/ppermute | solution.py:569
  117.2 26.2 %collective-permute-start.13 = (bf16[8,48,1536]{2,1,0:T(8,128)(2,1)}, bf16[8,48,1536]{2,1,0:T(8,128)(2,1)}, u32[]{:S(2)}, u32[]{:S(2)}) collective-permute-start(bf16[8,48,1536]{2,1,0:T(8,128)(2,1)} %get-tuple-element.230), channel_id=1, source_target_pairs={{0,4},{4,0},{1,5},{5,1},{2,6},{6,2},{3,7},{7,3},{8,12},{12,8},{9,1... | collective-permute-start | bytes 3538952 | tf_op jit(solution)/shard_map/cond/branch_1_fun/ppermute | solution.py:569
  118.5 25.9 %collective-permute-start.14 = (bf16[8,48,1536]{2,1,0:T(8,128)(2,1)}, bf16[8,48,1536]{2,1,0:T(8,128)(2,1)}, u32[]{:S(2)}, u32[]{:S(2)}) collective-permute-start(bf16[8,48,1536]{2,1,0:T(8,128)(2,1)} %get-tuple-element.231), channel_id=1, source_target_pairs={{0,2},{2,0},{1,3},{3,1},{4,6},{6,4},{5,7},{7,5},{8,10},{10,8},{9,1... | collective-permute-start | bytes 3538952 | tf_op jit(solution)/shard_map/cond/branch_1_fun/ppermute | solution.py:569
  155.2 203.3 %all-gather.8.cloned.1.call-start = ((), (), s32[]{:S(2)}) async-start(), calls=%async_computation.9 | async-start | bytes 7077888 | tf_op jit(solution)/shard_map/all_gather | solution.py:723
  158.4 52.0 %collective-permute-start.43 = (bf16[192,3072]{1,0:T(8,128)(2,1)}, bf16[192,3072]{1,0:T(8,128)(2,1)}, u32[]{:S(2)}, u32[]{:S(2)}) collective-permute-start(bf16[192,3072]{1,0:T(8,128)(2,1)} %get-tuple-element.992), channel_id=1, source_target_pairs={{0,16},{16,0},{1,17},{17,1},{2,18},{18,2},{3,19},{19,3},{4,20},{20... | collective-permute-start | bytes 3538952 | tf_op jit(solution)/shard_map/ppermute | solution.py:569
  160.3 13.5 %collective-permute-start.15 = (bf16[16,48,1536]{2,1,0:T(8,128)(2,1)}, bf16[16,48,1536]{2,1,0:T(8,128)(2,1)S(1)}, u32[]{:S(2)}, u32[]{:S(2)}) collective-permute-start(bf16[16,48,1536]{2,1,0:T(8,128)(2,1)} %get-tuple-element.249.refs_0_), channel_id=1, source_target_pairs={{0,1},{1,0},{2,3},{3,2},{4,5},{5,4},{6,7},{7,6},{8,9},{9,8},{10,11... | collective-permute-start | bytes 7077896 | tf_op jit(solution)/shard_map/cond/branch_1_fun/ppermute | solution.py:569
  163.4 10.4 %collective-permute-start.16 = (bf16[16,48,1536]{2,1,0:T(8,128)(2,1)}, bf16[16,48,1536]{2,1,0:T(8,128)(2,1)}, u32[]{:S(2)}, u32[]{:S(2)}) collective-permute-start(bf16[16,48,1536]{2,1,0:T(8,128)(2,1)} %get-tuple-element.250.refs_1_), channel_id=1, source_target_pairs={{0,1},{1,0},{2,3},{3,2},{4,5},{5,4},{6,7},{7,6},{8,9},{9,8},{10,11... | collective-permute-start | bytes 7077896 | tf_op jit(solution)/shard_map/cond/branch_1_fun/ppermute | solution.py:569
  163.4 8.3 %collective-permute-start.17 = (bf16[4,48,768]{2,1,0:T(8,128)(2,1)S(1)}, bf16[4,48,768]{2,1,0:T(8,128)(2,1)S(1)}, u32[]{:S(2)}, u32[]{:S(2)}) collective-permute-start(bf16[4,48,768]{2,1,0:T(8,128)(2,1)S(1)} %get-tuple-element.245), channel_id=1, source_target_pairs={{0,2},{2,0},{1,3},{3,1},{4,6},{6,4},{5,7},{7,5},{8,10},{10,8},{9,1... | collective-permute-start | bytes 884744 | tf_op jit(solution)/shard_map/cond/branch_1_fun/ppermute | solution.py:569
  164.0 8.4 %collective-permute-start.18 = (bf16[4,48,768]{2,1,0:T(8,128)(2,1)}, bf16[4,48,768]{2,1,0:T(8,128)(2,1)}, u32[]{:S(2)}, u32[]{:S(2)}) collective-permute-start(bf16[4,48,768]{2,1,0:T(8,128)(2,1)} %get-tuple-element.246), channel_id=1, source_target_pairs={{0,4},{4,0},{1,5},{5,1},{2,6},{6,2},{3,7},{7,3},{8,12},{12,8},{9,1... | collective-permute-start | bytes 884744 | tf_op jit(solution)/shard_map/cond/branch_1_fun/ppermute | solution.py:569
  173.7 16.6 %copy-start.18 = (bf16[8,48,768]{2,1,0:T(8,128)(2,1)}, bf16[8,48,768]{2,1,0:T(8,128)(2,1)S(1)}, u32[]{:S(2)}) copy-start(bf16[8,48,768]{2,1,0:T(8,128)(2,1)S(1)} %get-tuple-element.255) | copy-start | bytes 1769476 | tf_op jit(solution)/shard_map/cond
  173.8 31.7 %collective-permute-start.19 = (bf16[8,48,768]{2,1,0:T(8,128)(2,1)S(1)}, bf16[8,48,768]{2,1,0:T(8,128)(2,1)}, u32[]{:S(2)}, u32[]{:S(2)}) collective-permute-start(bf16[8,48,768]{2,1,0:T(8,128)(2,1)S(1)} %get-tuple-element.255), channel_id=1, source_target_pairs={{0,4},{4,0},{1,5},{5,1},{2,6},{6,2},{3,7},{7,3},{8,12},{12,8},{9,1... | collective-permute-start | bytes 1769480 | tf_op jit(solution)/shard_map/cond/branch_1_fun/ppermute | solution.py:569
  174.1 31.4 %collective-permute-start.20 = (bf16[8,48,768]{2,1,0:T(8,128)(2,1)S(1)}, bf16[8,48,768]{2,1,0:T(8,128)(2,1)}, u32[]{:S(2)}, u32[]{:S(2)}) collective-permute-start(bf16[8,48,768]{2,1,0:T(8,128)(2,1)S(1)} %get-tuple-element.256), channel_id=1, source_target_pairs={{0,2},{2,0},{1,3},{3,1},{4,6},{6,4},{5,7},{7,5},{8,10},{10,8},{9,1... | collective-permute-start | bytes 1769480 | tf_op jit(solution)/shard_map/cond/branch_1_fun/ppermute | solution.py:569
  214.6 287.5 %reduce-scatter.3.cloned.1.call-start = ((), (), s32[]{:S(2)}) async-start(), calls=%async_computation.10 | async-start | bytes 7077888 | tf_op jit(solution)/shard_map/reduce_scatter | solution.py:728
  216.1 63.1 %all-to-all-start.1 = ((bf16[16,96,768]{2,1,0:T(8,128)(2,1)}), bf16[16,96,768]{2,1,0:T(8,128)(2,1)}, u32[]{:S(2)}, u32[]{:S(2)}) async-start(bf16[16,96,768]{2,1,0:T(8,128)(2,1)} %bitcast.14), calls=%async_computation.1 | async-start | bytes 4718592 | tf_op jit(solution)/shard_map/cond/branch_1_fun/all_to_all | solution.py:740
  223.3 9.2 %collective-permute-start.21 = (bf16[16,48,768]{2,1,0:T(8,128)(2,1)S(1)}, bf16[16,48,768]{2,1,0:T(8,128)(2,1)S(1)}, u32[]{:S(2)}, u32[]{:S(2)}) collective-permute-start(bf16[16,48,768]{2,1,0:T(8,128)(2,1)S(1)} %get-tuple-element.270.refs_0_), channel_id=1, source_target_pairs={{0,1},{1,0},{2,3},{3,2},{4,5},{5,4},{6,7},{7,6},{8,9},{9,8},{10,11... | collective-permute-start | bytes 3538952 | tf_op jit(solution)/shard_map/cond/branch_1_fun/ppermute | solution.py:569
  223.7 8.9 %collective-permute-start.22 = (bf16[16,48,768]{2,1,0:T(8,128)(2,1)}, bf16[16,48,768]{2,1,0:T(8,128)(2,1)S(1)}, u32[]{:S(2)}, u32[]{:S(2)}) collective-permute-start(bf16[16,48,768]{2,1,0:T(8,128)(2,1)} %get-tuple-element.271.refs_1_), channel_id=1, source_target_pairs={{0,1},{1,0},{2,3},{3,2},{4,5},{5,4},{6,7},{7,6},{8,9},{9,8},{10,11... | collective-permute-start | bytes 3538952 | tf_op jit(solution)/shard_map/cond/branch_1_fun/ppermute | solution.py:569
  358.7 23.1 %slice-start = ((s8[9437184]{0:T(1024)(128)(4,1)}), s8[4194304]{0:T(1024)(128)(4,1)S(1)}, s32[]{:S(2)}) async-start(s8[9437184]{0:T(1024)(128)(4,1)} %bitcast.241), calls=%async_computation.12 | async-start | bytes 8388608 | tf_op jit(solution)/shard_map/cond
  358.7 23.1 %slice-start.1 = ((s8[9437184]{0:T(1024)(128)(4,1)}), s8[4194304]{0:T(1024)(128)(4,1)S(1)}, s32[]{:S(2)}) async-start(s8[9437184]{0:T(1024)(128)(4,1)} %bitcast.241), calls=%async_computation.13 | async-start | bytes 8388608 | tf_op jit(solution)/shard_map/cond
  358.7 23.1 %slice-start.2 = ((s8[9437184]{0:T(1024)(128)(4,1)}), s8[1048576]{0:T(1024)(128)(4,1)S(1)}, s32[]{:S(2)}) async-start(s8[9437184]{0:T(1024)(128)(4,1)} %bitcast.241), calls=%async_computation.14 | async-start | bytes 2097152 | tf_op jit(solution)/shard_map/cond
  393.8 210.2 %reduce-scatter.5.cloned.1.call-start = ((), (), s32[]{:S(2)}) async-start(), calls=%async_computation.11 | async-start | bytes 7077888 | tf_op jit(solution)/shard_map/reduce_scatter | solution.py:728
  393.8 18.7 %slice-start.3 = ((s8[9437184]{0:T(1024)(128)(4,1)}), s8[1048576]{0:T(1024)(128)(4,1)S(1)}, s32[]{:S(2)}) async-start(s8[9437184]{0:T(1024)(128)(4,1)} %bitcast.243), calls=%async_computation.15 | async-start | bytes 2097152 | tf_op jit(solution)/shard_map/cond
  393.9 60.9 %all-to-all-start.3 = ((bf16[16,96,768]{2,1,0:T(8,128)(2,1)}), bf16[16,96,768]{2,1,0:T(8,128)(2,1)}, u32[]{:S(2)}, u32[]{:S(2)}) async-start(bf16[16,96,768]{2,1,0:T(8,128)(2,1)} %bitcast.18), calls=%async_computation.3 | async-start | bytes 4718592 | tf_op jit(solution)/shard_map/cond/branch_1_fun/all_to_all | solution.py:740
  456.2 108.6 %all-to-all-start.4 = ((bf16[16,96,768]{2,1,0:T(8,128)(2,1)}), bf16[16,96,768]{2,1,0:T(8,128)(2,1)}, u32[]{:S(2)}, u32[]{:S(2)}) async-start(bf16[16,96,768]{2,1,0:T(8,128)(2,1)} %bitcast.245), calls=%async_computation.5 | async-start | bytes 4718592 | tf_op jit(solution)/shard_map/all_to_all | solution.py:740
  504.4 61.7 %collective-permute-start.44 = (bf16[1,192,3072]{2,1,0:T(8,128)(2,1)}, bf16[1,192,3072]{2,1,0:T(8,128)(2,1)}, u32[]{:S(2)}, u32[]{:S(2)}) collective-permute-start(bf16[1,192,3072]{2,1,0:T(8,128)(2,1)} %constant_dynamic-slice_fusion.5), channel_id=1, source_target_pairs={{0,16},{16,0},{1,17},{17,1},{2,18},{18,2},{3,19},{19,3},{4,20},{20... | collective-permute-start | bytes 3538952 | tf_op jit(solution)/shard_map/ppermute | solution.py:569
  507.0 16.1 %collective-permute-start.23 = (bf16[768,1536]{1,0:T(8,128)(2,1)}, bf16[768,1536]{1,0:T(8,128)(2,1)S(1)}, u32[]{:S(2)}, u32[]{:S(2)}) collective-permute-start(bf16[768,1536]{1,0:T(8,128)(2,1)} %get-tuple-element.323), channel_id=1, source_target_pairs={{0,1},{1,0},{2,3},{3,2},{4,5},{5,4},{6,7},{7,6},{8,9},{9,8},{10,11... | collective-permute-start | bytes 7077896 | tf_op jit(solution)/shard_map/cond/branch_1_fun/ppermute | solution.py:569
  528.2 18.4 %collective-permute-start.24 = (bf16[4,2,48,768]{3,2,1,0:T(8,128)(2,1)}, bf16[4,2,48,768]{3,2,1,0:T(8,128)(2,1)}, u32[]{:S(2)}, u32[]{:S(2)}) collective-permute-start(bf16[4,2,48,768]{3,2,1,0:T(8,128)(2,1)} %dynamic-slice_bitcast_fusion.1), channel_id=1, source_target_pairs={{0,4},{4,0},{1,5},{5,1},{2,6},{6,2},{3,7},{7,3},{8,12},{12,8},{9,1... | collective-permute-start | bytes 1769480 | tf_op jit(solution)/shard_map/cond/branch_1_fun/ppermute | solution.py:569
  529.5 17.2 %collective-permute-start.25 = (bf16[4,2,48,768]{3,2,1,0:T(8,128)(2,1)}, bf16[4,2,48,768]{3,2,1,0:T(8,128)(2,1)}, u32[]{:S(2)}, u32[]{:S(2)}) collective-permute-start(bf16[4,2,48,768]{3,2,1,0:T(8,128)(2,1)} %dynamic-slice_bitcast_fusion), channel_id=1, source_target_pairs={{0,2},{2,0},{1,3},{3,1},{4,6},{6,4},{5,7},{7,5},{8,10},{10,8},{9,1... | collective-permute-start | bytes 1769480 | tf_op jit(solution)/shard_map/cond/branch_1_fun/ppermute | solution.py:569
  549.3 10.6 %collective-permute-start.28 = (bf16[768,3072]{1,0:T(8,128)(2,1)}, bf16[768,3072]{1,0:T(8,128)(2,1)S(1)}, u32[]{:S(2)}, u32[]{:S(2)}) collective-permute-start(bf16[768,3072]{1,0:T(8,128)(2,1)} %get-tuple-element.352), channel_id=1, source_target_pairs={{0,1},{1,0},{2,3},{3,2},{4,5},{5,4},{6,7},{7,6},{8,9},{9,8},{10,11... | collective-permute-start | bytes 14155784 | tf_op jit(solution)/shard_map/cond/branch_1_fun/ppermute | solution.py:569
  550.2 8.8 %collective-permute-start.26 = (bf16[4,48,768]{2,1,0:T(8,128)(2,1)S(1)}, bf16[4,48,768]{2,1,0:T(8,128)(2,1)S(1)}, u32[]{:S(2)}, u32[]{:S(2)}) collective-permute-start(bf16[4,48,768]{2,1,0:T(8,128)(2,1)S(1)} %dynamic-slice_bitcast_fusion.3), channel_id=1, source_target_pairs={{0,2},{2,0},{1,3},{3,1},{4,6},{6,4},{5,7},{7,5},{8,10},{10,8},{9,1... | collective-permute-start | bytes 884744 | tf_op jit(solution)/shard_map/cond/branch_1_fun/ppermute | solution.py:569
  550.5 8.5 %collective-permute-start.27 = (bf16[4,48,768]{2,1,0:T(8,128)(2,1)S(1)}, bf16[4,48,768]{2,1,0:T(8,128)(2,1)S(1)}, u32[]{:S(2)}, u32[]{:S(2)}) collective-permute-start(bf16[4,48,768]{2,1,0:T(8,128)(2,1)S(1)} %dynamic-slice_bitcast_fusion.2), channel_id=1, source_target_pairs={{0,4},{4,0},{1,5},{5,1},{2,6},{6,2},{3,7},{7,3},{8,12},{12,8},{9,1... | collective-permute-start | bytes 884744 | tf_op jit(solution)/shard_map/cond/branch_1_fun/ppermute | solution.py:569
  569.1 29.1 %collective-permute-start.34 = (bf16[4,2,48,1536]{3,2,1,0:T(8,128)(2,1)S(1)}, bf16[4,2,48,1536]{3,2,1,0:T(8,128)(2,1)}, u32[]{:S(2)}, u32[]{:S(2)}) collective-permute-start(bf16[4,2,48,1536]{3,2,1,0:T(8,128)(2,1)S(1)} %dynamic-slice_bitcast_fusion.5), channel_id=1, source_target_pairs={{0,4},{4,0},{1,5},{5,1},{2,6},{6,2},{3,7},{7,3},{8,12},{12,8},{9,1... | collective-permute-start | bytes 3538952 | tf_op jit(solution)/shard_map/cond/branch_1_fun/ppermute | solution.py:569
  570.4 27.8 %collective-permute-start.35 = (bf16[4,2,48,1536]{3,2,1,0:T(8,128)(2,1)S(1)}, bf16[4,2,48,1536]{3,2,1,0:T(8,128)(2,1)}, u32[]{:S(2)}, u32[]{:S(2)}) collective-permute-start(bf16[4,2,48,1536]{3,2,1,0:T(8,128)(2,1)S(1)} %dynamic-slice_bitcast_fusion.4), channel_id=1, source_target_pairs={{0,2},{2,0},{1,3},{3,1},{4,6},{6,4},{5,7},{7,5},{8,10},{10,8},{9,1... | collective-permute-start | bytes 3538952 | tf_op jit(solution)/shard_map/cond/branch_1_fun/ppermute | solution.py:569
  573.3 29.0 %collective-permute-start.36 = (bf16[2,48,1536]{2,1,0:T(8,128)(2,1)}, bf16[2,48,1536]{2,1,0:T(8,128)(2,1)S(1)}, u32[]{:S(2)}, u32[]{:S(2)}) collective-permute-start(bf16[2,48,1536]{2,1,0:T(8,128)(2,1)} %dynamic-slice_bitcast_fusion.6), channel_id=1, source_target_pairs={{0,16},{16,0},{1,17},{17,1},{2,18},{18,2},{3,19},{19,3},{4,20},{20... | collective-permute-start | bytes 884744 | tf_op jit(solution)/shard_map/cond/branch_1_fun/ppermute | solution.py:569
  606.6 78.5 %collective-permute-start.46 = (bf16[1,192,3072]{2,1,0:T(8,128)(2,1)}, bf16[1,192,3072]{2,1,0:T(8,128)(2,1)}, u32[]{:S(2)}, u32[]{:S(2)}) collective-permute-start(bf16[1,192,3072]{2,1,0:T(8,128)(2,1)} %constant_dynamic-slice_fusion.4), channel_id=1, source_target_pairs={{0,16},{16,0},{1,17},{17,1},{2,18},{18,2},{3,19},{19,3},{4,20},{20... | collective-permute-start | bytes 3538952 | tf_op jit(solution)/shard_map/ppermute | solution.py:569
  609.9 26.0 %collective-permute-start.39 = (bf16[48,1536]{1,0:T(8,128)(2,1)}, bf16[48,1536]{1,0:T(8,128)(2,1)}, u32[]{:S(2)}, u32[]{:S(2)}) collective-permute-start(bf16[48,1536]{1,0:T(8,128)(2,1)} %dynamic-slice_bitcast_fusion.9), channel_id=1, source_target_pairs={{0,8},{8,0},{1,9},{9,1},{2,10},{10,2},{3,11},{11,3},{4,12},{12,4},... | collective-permute-start | bytes 442376 | tf_op jit(solution)/shard_map/cond/branch_1_fun/ppermute | solution.py:569
  612.7 24.2 %collective-permute-start.37 = (bf16[4,48,1536]{2,1,0:T(8,128)(2,1)}, bf16[4,48,1536]{2,1,0:T(8,128)(2,1)}, u32[]{:S(2)}, u32[]{:S(2)}) collective-permute-start(bf16[4,48,1536]{2,1,0:T(8,128)(2,1)} %dynamic-slice_bitcast_fusion.8), channel_id=1, source_target_pairs={{0,2},{2,0},{1,3},{3,1},{4,6},{6,4},{5,7},{7,5},{8,10},{10,8},{9,1... | collective-permute-start | bytes 1769480 | tf_op jit(solution)/shard_map/cond/branch_1_fun/ppermute | solution.py:569
  613.0 23.9 %collective-permute-start.38 = (bf16[4,48,1536]{2,1,0:T(8,128)(2,1)}, bf16[4,48,1536]{2,1,0:T(8,128)(2,1)}, u32[]{:S(2)}, u32[]{:S(2)}) collective-permute-start(bf16[4,48,1536]{2,1,0:T(8,128)(2,1)} %dynamic-slice_bitcast_fusion.7), channel_id=1, source_target_pairs={{0,4},{4,0},{1,5},{5,1},{2,6},{6,2},{3,7},{7,3},{8,12},{12,8},{9,1... | collective-permute-start | bytes 1769480 | tf_op jit(solution)/shard_map/cond/branch_1_fun/ppermute | solution.py:569
  642.2 42.9 %collective-permute-start.45 = (bf16[2,48,3072]{2,1,0:T(8,128)(2,1)}, bf16[2,48,3072]{2,1,0:T(8,128)(2,1)}, u32[]{:S(2)}, u32[]{:S(2)}) collective-permute-start(bf16[2,48,3072]{2,1,0:T(8,128)(2,1)} %get-tuple-element.995), channel_id=1, source_target_pairs={{0,16},{16,0},{1,17},{17,1},{2,18},{18,2},{3,19},{19,3},{4,20},{20... | collective-permute-start | bytes 1769480 | tf_op jit(solution)/shard_map/ppermute | solution.py:569
  644.5 7.3 collective-permute-start.29
  654.4 14.7 %collective-permute-start.30 = (bf16[4,2,48,768]{3,2,0,1:T(8,128)(2,1)S(1)}, bf16[4,2,48,768]{3,2,0,1:T(8,128)(2,1)}, u32[]{:S(2)}, u32[]{:S(2)}) collective-permute-start(bf16[4,2,48,768]{3,2,0,1:T(8,128)(2,1)S(1)} %dynamic-slice_bitcast_fusion.11), channel_id=1, source_target_pairs={{0,4},{4,0},{1,5},{5,1},{2,6},{6,2},{3,7},{7,3},{8,12},{12,8},{9,1... | collective-permute-start | bytes 1769480 | tf_op jit(solution)/shard_map/cond/branch_1_fun/ppermute | solution.py:569
  654.8 14.4 %collective-permute-start.31 = (bf16[4,2,48,768]{3,2,1,0:T(8,128)(2,1)S(1)}, bf16[4,2,48,768]{3,2,1,0:T(8,128)(2,1)}, u32[]{:S(2)}, u32[]{:S(2)}) collective-permute-start(bf16[4,2,48,768]{3,2,1,0:T(8,128)(2,1)S(1)} %dynamic-slice_bitcast_fusion.10), channel_id=1, source_target_pairs={{0,2},{2,0},{1,3},{3,1},{4,6},{6,4},{5,7},{7,5},{8,10},{10,8},{9,1... | collective-permute-start | bytes 1769480 | tf_op jit(solution)/shard_map/cond/branch_1_fun/ppermute | solution.py:569
  673.0 7.8 %collective-permute-start.32 = (bf16[4,48,768]{2,1,0:T(8,128)(2,1)}, bf16[4,48,768]{2,1,0:T(8,128)(2,1)}, u32[]{:S(2)}, u32[]{:S(2)}) collective-permute-start(bf16[4,48,768]{2,1,0:T(8,128)(2,1)} %dynamic-slice_bitcast_fusion.13), channel_id=1, source_target_pairs={{0,2},{2,0},{1,3},{3,1},{4,6},{6,4},{5,7},{7,5},{8,10},{10,8},{9,1... | collective-permute-start | bytes 884744 | tf_op jit(solution)/shard_map/cond/branch_1_fun/ppermute | solution.py:569
  673.3 7.5 %collective-permute-start.33 = (bf16[4,48,768]{2,1,0:T(8,128)(2,1)}, bf16[4,48,768]{2,1,0:T(8,128)(2,1)}, u32[]{:S(2)}, u32[]{:S(2)}) collective-permute-start(bf16[4,48,768]{2,1,0:T(8,128)(2,1)} %dynamic-slice_bitcast_fusion.12), channel_id=1, source_target_pairs={{0,4},{4,0},{1,5},{5,1},{2,6},{6,2},{3,7},{7,3},{8,12},{12,8},{9,1... | collective-permute-start | bytes 884744 | tf_op jit(solution)/shard_map/cond/branch_1_fun/ppermute | solution.py:569
  688.1 17.8 %collective-permute-start.4 = (bf16[48,3072]{1,0:T(8,128)(2,1)}, bf16[48,3072]{1,0:T(8,128)(2,1)}, u32[]{:S(2)}, u32[]{:S(2)}) collective-permute-start(bf16[48,3072]{1,0:T(8,128)(2,1)} %dynamic-slice_bitcast_fusion.15), channel_id=1, source_target_pairs={{0,8},{8,0},{1,9},{9,1},{2,10},{10,2},{3,11},{11,3},{4,12},{12,4},... | collective-permute-start | bytes 884744 | tf_op jit(solution)/shard_map/cond/branch_1_fun/ppermute | solution.py:569
  688.9 18.1 %collective-permute-start.5 = (bf16[2,48,1536]{2,1,0:T(8,128)(2,1)}, bf16[2,48,1536]{2,1,0:T(8,128)(2,1)}, u32[]{:S(2)}, u32[]{:S(2)}) collective-permute-start(bf16[2,48,1536]{2,1,0:T(8,128)(2,1)} %dynamic-slice_bitcast_fusion.14), channel_id=1, source_target_pairs={{0,16},{16,0},{1,17},{17,1},{2,18},{18,2},{3,19},{19,3},{4,20},{20... | collective-permute-start | bytes 884744 | tf_op jit(solution)/shard_map/cond/branch_1_fun/ppermute | solution.py:569
  690.7 26.5 %all-to-all-start = ((f32[32,1,192]{2,1,0:T(1,128)}), f32[32,1,192]{2,1,0:T(1,128)}, u32[]{:S(2)}, u32[]{:S(2)}) async-start(f32[32,1,192]{2,1,0:T(1,128)} %all_to_all.19), calls=%async_computation | async-start | bytes 65536 | tf_op jit(solution)/shard_map/cond/branch_1_fun/all_to_all | solution.py:681
  708.1 5.0 collective-permute-start.6
  709.7 3.4 collective-permute-start.7
  713.3 4.8 collective-permute-start.8
  (43 other events, 253.9 us)
Sparse Core Ops, SparseCore 0:
  34.1 40.1 all-gather.3
  155.3 99.4 all-gather.5
  256.4 97.1 all-gather.7
  393.9 93.3 reduce-scatter.2
  489.6 105.4 reduce-scatter.4

commit v6 on v5

--- a/solution.py
+++ b/solution.py
@@ -713,10 +713,13 @@
     def plus(self, one, two):
         return (one.astype(WIDE) + two.astype(WIDE)).astype(LOW)
 
-    def fetch_near(self, part):
+    def choose(self, part):
         upper = lax.axis_index("dh")
-        same, other = part[0], part[1]
-        same, other = jnp.where(upper == 0, same, other), jnp.where(upper == 0, other, same)
+        first, second = part[0].astype(LOW), part[1].astype(LOW)
+        return jnp.where(upper == 0, first, second), jnp.where(upper == 0, second, first)
+
+    def fetch_near(self, same, other):
+        upper = lax.axis_index("dh")
         return flipped(upper, same[None], self.hop(other, "dh", 1)[None], 0)
 
     def fetch_far(self, pair, *gates):
@@ -778,19 +781,16 @@
     bar = lax.optimization_barrier
     core = lax.axis_index("c") if plan.wide else 0 * expert_index[0, 0]
     parts = (part_a, part_b, part_c)
-    in_low = exp_in.astype(LOW)
     deep_a = plan.gather_depth(parts[:1])
     deep_bc = plan.gather_depth(parts[1:], deep_a)
 
-    def zeroth_part(deep_a, part_a):
+    def zeroth_part(deep_a, part_a, exp_in, exp_out, expert_index, gate, cotangent, act_in):
+        in_pair = plan.choose(exp_in)
+        out_pair = plan.choose(jnp.swapaxes(exp_out, 1, 2))
         (pair_a,) = plan.gather_split(deep_a, (part_a,))
-        one_a = bar(plan.gather_side(pair_a, 0))
-        return bar(plan.gather_side(one_a, 1))
-
-    two_a = fenced(ready, zeroth_part, deep_a, part_a)
-    expert_index, act_in = after((expert_index, act_in), two_a)
-
-    def prepare(expert_index, gate, cotangent, act_in):
+        one_a, in_pair, out_pair = bar((plan.gather_side(pair_a, 0), in_pair, out_pair))
+        two_a = plan.gather_side(one_a, 1)
+        expert_index, cotangent, act_in = after((expert_index, cotangent, act_in), one_a)
         flat_index = expert_index.reshape(-1)
         onehot = (flat_index[:, None] == jnp.arange(experts_all, dtype=jnp.int32)).astype(jnp.int32)
         before = jnp.cumsum(onehot, axis=0) - onehot
@@ -799,16 +799,14 @@
         spots = padded(spots, -1)
         gates, cot, x_a = padded(gate), padded(cotangent), padded(act_in)
         grad_sent = dispatch_grad(flat(spots).T, flat(gates), flat(cot), slots)
-        return spots, gates, cot, x_a, grad_sent
-
-    spots, gates, cot, x_a, grad_sent = fenced(
-        ready, prepare, expert_index, gate, cotangent, act_in
+        return two_a, in_pair, out_pair, spots, gates, cot, x_a, grad_sent
+
+    two_a, in_pair, out_pair, spots, gates, cot, x_a, grad_sent = fenced(
+        ready, zeroth_part, deep_a, part_a, exp_in, exp_out, expert_index, gate, cotangent, act_in
     )
     spot_rows = flat(spots).T
-
-    out_low = jnp.swapaxes(exp_out, 1, 2).astype(LOW)
-    in_low, x_a, grad_sent, deep_bc = bar((in_low, x_a, grad_sent, deep_bc))
-    in_near = plan.fetch_near(in_low)
+    in_pair, x_a, deep_bc = bar((in_pair, x_a, deep_bc))
+    in_near = plan.fetch_near(*in_pair)
 
     def first_part(two_a, deep_bc, parts, x_a):
         part_a, part_b, part_c = parts
@@ -824,9 +822,9 @@
     gain, shift, block_a, x_b, packed_a, mixed_a, two_b, pair_c = fenced(
         ready, first_part, two_a, deep_bc, parts, x_a
     )
-    two_b, in_near, out_low = bar((two_b, in_near, out_low))
+    two_b, in_near, out_pair = bar((two_b, in_near, out_pair))
     weight_in = plan.fetch_far(in_near)
-    out_near = plan.fetch_near(out_low)
+    out_near = plan.fetch_near(*out_pair)
 
     def second_part(x_b, gain, shift, two_b, pair_c, part_b):
         four_b, one_c = bar((plan.gather_core(two_b), plan.gather_side(pair_c, 0)))

time: 740 us -> 726 us (0.981)
  waiting for transfers between devices: 146 us -> 126 us
    ppermute x47, waiting for transfers between devices: 87.2 us -> 67.8 us  [hop(): return lax.ppermute(value, axes, [(i, i ^ bit) for i in range(size)])]
    convert_element_type x2 -> x0, other arithmetic: 8.13 us -> none  [the longest x1 4.08 us: local(): in_low = exp_in.astype(LOW)]
  transfers between devices with their start and end apart: 56 -> 56, of which waited for: 21 -> 17; matrix products, arithmetic and copies ran while one was open for 19% -> 21% of each run, Pallas kernels for 28% -> 29%
where the time goes in v6:
time: 726 us; the launch traced here: 717 us
  Pallas kernels  243 us (33%)
  waiting for transfers between devices  126 us (17%)
  other arithmetic  95.8 us (13%)
  local copies, waits for them, and re-layouts  81.4 us (11%)
  blocking collectives  77.6 us (11%)
  starting transfers between devices  67.2 us (9%)
  between operations  15.1 us (2%)
  matrix products  7.88 us (1%)
    ppermute x47, waiting for transfers between devices, hop(): return lax.ppermute(value, axes, [(i, i ^ bit) for i in range(size)])  67.8 us
    all_to_all x1, blocking collectives, to_experts(): lax.all_to_all(chunks, ('dh',) + self.expert, 0, 0, tiled=True)  60.7 us
    all_to_all x3, waiting for transfers between devices, to_experts(): lax.all_to_all(chunks, ('dh',) + self.expert, 0, 0, tiled=True)  58.1 us
    pallas_call x5, Pallas kernels, weight_grad(): pl.pallas_call(functools.partial(weight_grad_body, tiles, starts, split),...  56.8 us
    pallas_call x2, Pallas kernels, attend_backward(): pl.pallas_call(attend_backward_body, grid=(images,), in_specs=[image(D),...  49 us
    ppermute x47, starting transfers between devices, hop(): return lax.ppermute(value, axes, [(i, i ^ bit) for i in range(size)])  44 us
    pallas_call x2, Pallas kernels, attend_forward(): pl.pallas_call(attend_forward_body, grid=(images,), in_specs=[image(D), w...  26.1 us
    concatenate x10, other arithmetic, gather_side(): jnp.concatenate([own, new])  23.2 us
  transfers between devices with their start and end apart: 56, of which 17 were waited for; matrix products, arithmetic and copies ran while one was open for 21% of the time, Pallas kernels for 29%

profile of v6, /device:TPU:1, one launch (start us, length us, event | category | flops | bytes accessed | tf_op | source)
XLA Modules:
  0.0 716.8 jit_solution(8359476168611300519)
XLA Ops:
  12.2 16.9 %all_gather.12 = bf16[4,48,1664]{2,1,0:T(8,128)(2,1)S(1)} all-gather(bf16[1,48,1664]{2,1,0:T(8,128)(2,1)S(1)} %maximum_select_fusion.7), channel_id=1, replica_groups=mesh['dh'=2,'dl'=2,'y'=2,'x'=2,'c'=2] {'dh','dl'}, dimensions={0}, use_global_device_ids=true | all-gather | bytes 798720 | tf_op jit(solution)/shard_map/all_gather | solution.py:587
  35.3 46.2 %conditional.12 = (bf16[16,48,768]{2,1,0:T(8,128)(2,1)}, bf16[16,48,896]{2,1,0:T(8,128)(2,1)}, bf16[192,3072]{1,0:T(8,128)(2,1)S(1)}, bf16[192,3072]{1,0:T(8,128...) conditional(s32[]{:T(128)} %bitcast.88, () %tuple.165, ...), branch_computations={%region_0.1_spmd, %region_1.5_spmd} | conditional | flops 759418496 | bytes 83628928 | solution.py:753
  39.2 3.0 convert.33
  45.1 3.6 select_bitcast_fusion
  53.3 4.5 reduce-window.4
  59.7 2.9 reshape.747
  64.3 3.6 reshape.748
  67.9 2.9 pad.33
  70.9 5.6 dispatch_grad.1
  82.4 56.8 %conditional.13 = (f32[4,1,768]{2,0,1:T(4,128)S(1)}, f32[4,1,768]{2,0,1:T(4,128)S(1)}, bf16[768,3328]{1,0:T(8,128)(2,1)}, f32[3,208,768]{2,1,0:T(8,128)}, bf16[3...) conditional(s32[]{:T(128)} %bitcast.88, () %tuple.164, ...), branch_computations={%region_5.6_spmd, %region_6.7_spmd} | conditional | flops 928546176 | bytes 48031396 | solution.py:753
  89.7 11.8 %collective-permute-done.11 = bf16[4,48,1536]{2,1,0:T(8,128)(2,1)} collective-permute-done((bf16[4,48,1536]{2,1,0:T(8,128)(2,1)}, bf16[4,48,1536]{2,1,0:T(8,128)(2,1)}, u32[]{:S(2)}, u32[]{:S(2)}) %collective-permute-start.11) | collective-permute-done | bytes 589856 | tf_op jit(solution)/shard_map/cond/branch_1_fun/ppermute | solution.py:569
  102.4 3.0 pad_maximum_fusion.2
  109.4 4.6 join.3.qkv_ref.proj_ref
  115.1 13.1 %attend_forward.2 = (f32[3,208,768]{2,1,0:T(8,128)}, bf16[3,208,2304]{2,1,0:T(8,128)(2,1)}, bf16[3,208,768]{2,1,0:T(8,128)(2,1)}) custom-call(f32[3,208,768]{2,1,0:T(8,128)} %get-tuple-element.251.x_ref, f32[1,768]{1,0:T(1,128)S(1)} %get-tuple-element.971.gain_ref, f32[1,768]{1,0:T(1,128)S(1)} %get-tuple-element.970.shift_ref, ...), custom_call_target="tpu_custom_call" | custom-call | flops 925000000 | bytes 3250000 | tf_op jit(solution)/shard_map/cond/branch_1_fun/attend_forward/pallas_call | solution.py:133
  128.2 3.5 collective-permute-done.13
  132.8 3.3 pad_maximum_fusion.1
  136.0 3.2 pad_maximum_fusion
  139.3 4.2 maximum_select_fusion.4
  145.2 48.5 %conditional.14 = (bf16[768,6144]{1,0:T(8,128)(2,1)}, f32[3,208,768]{2,1,0:T(8,128)}, bf16[3,208,3072]{2,1,0:T(8,128)(2,1)}, bf16[3,208,3072]{2,1,0:T(8,128)(2,1...) conditional(s32[]{:T(128)} %bitcast.88, () %tuple.171, (bf16[16,48,1536]{2,1,0:T(8,128)(2,1)}, ...), branch_computations={%region_7.8_spmd, %region_8.9_spmd} | conditional | flops 1476770688 | bytes 50191248 | solution.py:753
  145.2 3.1 collective-permute-start.15
  150.2 6.4 collective-permute-done.17
  167.8 7.5 %join.4.up_ref.down_ref = bf16[768,6144]{1,0:T(8,128)(2,1)} custom-call(s32[4,32]{1,0:T(4,128)S(1)} %pad_add_fusion.1.at_ref, bf16[16,48,1536]{2,1,0:T(8,128)(2,1)} %get-tuple-element.266.refs_0_, bf16[16,48,1536]{2,1,0:T(8,128)(2,1)} %get-tuple-element.267.refs_1_, bf16[16,48,1536]{2,1,0:T(8,128)(2,1)S(1)} %collective-permute-done.15.refs_2_, ...), custom_call_target="tpu_custom_call" | custom-call | bytes 4718592 | tf_op jit(solution)/shard_map/cond/branch_1_fun/join/pallas_call | solution.py:531
  175.2 15.1 %mlp_forward.1 = (f32[3,208,768]{2,1,0:T(8,128)}, bf16[3,208,3072]{2,1,0:T(8,128)(2,1)}, bf16[3,208,3072]{2,1,0:T(8,128)(2,1)}) custom-call(f32[3,208,768]{2,1,0:T(8,128)} %get-tuple-element.276.x_ref, f32[1,768]{1,0:T(1,128)} %get-tuple-element.991.gain_ref, f32[1,768]{1,0:T(1,128)} %get-tuple-element.990.shift_ref, bf16[768,6144]{1,0:T(8,128)(2,1)} %join.4.up_ref.down_ref, ...), custom_call_target="tpu_custom_call" | custom-call | flops 1475000064 | bytes 5250000 | tf_op jit(solution)/shard_map/cond/branch_1_fun/mlp_forward/pallas_call | solution.py:229
  196.5 4.1 maximum_select_fusion.5
  202.0 123.0 %conditional.15 = (bf16[768,3072]{1,0:T(8,128)(2,1)}, f32[3,208,768]{2,1,0:T(8,128)}, bf16[3,208,2304]{2,1,0:T(8,128)(2,1)}, bf16[3,208,768]{2,1,0:T(8,128)(2,1)...) conditional(s32[]{:T(128)} %bitcast.88, () %tuple.170, (bf16[16,48,768]{2,1,0:T(8,128)(2,1)S(1)}, ...), branch_computations={%region_9.10_spmd, %region_10.11_spmd} | conditional | flops 1300001024 | bytes 28065448 | solution.py:753
  202.2 6.2 all-to-all-start.1
  217.6 4.5 join.5.qkv_ref.proj_ref
  222.1 13.1 %attend_forward.3 = (f32[3,208,768]{2,1,0:T(8,128)}, bf16[3,208,2304]{2,1,0:T(8,128)(2,1)}, bf16[3,208,768]{2,1,0:T(8,128)(2,1)}) custom-call(f32[3,208,768]{2,1,0:T(8,128)} %get-tuple-element.291.x_ref, f32[1,768]{1,0:T(1,128)S(1)} %get-tuple-element.1002.gain_ref, f32[1,768]{1,0:T(1,128)S(1)} %get-tuple-element.993.shift_ref, ...), custom_call_target="tpu_custom_call" | custom-call | flops 925000000 | bytes 3250000 | tf_op jit(solution)/shard_map/cond/branch_1_fun/attend_forward/pallas_call | solution.py:133
  235.2 5.1 dispatch.1
  240.3 24.1 %all-to-all-done.1 = bf16[16,96,768]{2,1,0:T(8,128)(2,1)} async-done(((bf16[16,96,768]{2,1,0:T(8,128)(2,1)}), bf16[16,96,768]{2,1,0:T(8,128)(2,1)}, u32[]{:S(2)}, u32[]{:S(2)}) %all-to-all-start.1) | async-done | bytes 2359328 | tf_op jit(solution)/shard_map/cond/branch_1_fun/all_to_all | solution.py:743
  264.4 60.7 %all_to_all.25 = bf16[16,96,768]{2,1,0:T(8,128)(2,1)} all-to-all(bf16[16,96,768]{2,1,0:T(8,128)(2,1)S(1)} %bitcast.232), channel_id=1, replica_groups=mesh['dh'=2,'dl'=2,'y'=2,'x'=2,'c'=2] {'dh','y','x','c'}, dimensions={0} | all-to-all | bytes 4718592 | tf_op jit(solution)/shard_map/cond/branch_1_fun/all_to_all | solution.py:743
  325.1 18.5 %expert_forward.1 = (bf16[1536,3072]{1,0:T(8,128)(2,1)}, bf16[1536,3072]{1,0:T(8,128)(2,1)}) custom-call(bf16[1536,768]{1,0:T(8,128)(2,1)} %get-tuple-element.618.rows_ref, bf16[768,3072]{1,0:T(8,128)(2,1)} %bitcast.243), custom_call_target="tpu_custom_call" | custom-call | flops 1800000000 | bytes 6500000 | tf_op jit(solution)/shard_map/expert_forward/pallas_call | solution.py:409
  343.6 35.3 %conditional.16 = (bf16[1536,3072]{1,0:T(8,128)(2,1)}, bf16[1536,768]{1,0:T(8,128)(2,1)}, bf16[768,3072]{1,0:T(8,128)(2,1)}) conditional(s32[]{:T(128)} %bitcast.88, () %tuple.177, (bf16[1536,768]{1,0:T(8,128)(2,1)}, bf16[1536,3072]{1,0:T(8,128)(2,1)}, bf16[768,3072]{1,0:T(8,128)(2,1)}, bf16[768,3072]{1,0:T(8,128)(2,1)}, ...), branch_computations={%region_11.12_spmd, %region_12.13_spmd} | conditional | flops 5411939328 | bytes 38331120 | solution.py:753
  343.8 23.1 %expert_backward.1 = (bf16[1536,3072]{1,0:T(8,128)(2,1)}, bf16[1536,768]{1,0:T(8,128)(2,1)}) custom-call(bf16[1536,768]{1,0:T(8,128)(2,1)} %get-tuple-element.301.grad_ref.refs_0_, bf16[1536,3072]{1,0:T(8,128)(2,1)} %get-tuple-element.302.slope_ref, bf16[768,3072]{1,0:T(8,128)(2,1)} %get-tuple-element.303.in_ref, bf16[768,3072]{1,0:T(8,128)(2,1)} %get-tuple-element.304.out_ref), custom_call_target="tpu_custom_call" | custom-call | flops 3600000000 | bytes 8250000 | tf_op jit(solution)/shard_map/cond/branch_1_fun/expert_backward/pallas_call | solution.py:434
  366.9 11.9 %weight_grad.5 = bf16[768,3072]{1,0:T(8,128)(2,1)} custom-call(s32[1]{0:T(128)} %constant.603.clone.at_ref, bf16[1536,768]{1,0:T(8,128)(2,1)} %get-tuple-element.301.grad_ref.refs_0_, bf16[1536,3072]{1,0:T(8,128)(2,1)S(1)} %bitcast.248), custom_call_target="tpu_custom_call" | custom-call | flops 1811939328 | bytes 1769472 | tf_op jit(solution)/shard_map/cond/branch_1_fun/weight_grad/pallas_call | solution.py:501
  378.9 60.8 %conditional.17 = (bf16[1536,768]{1,0:T(8,128)(2,1)}, bf16[768,3072]{1,0:T(8,128)(2,1)}, bf16[1536,768]{1,0:T(8,128)(2,1)S(1)}) conditional(s32[]{:T(128)} %bitcast.88, () %tuple.176, (bf16[1536,768]{1,0:T(8,128)(2,1)}, bf16[1536,768]{1,0:T(8,128)(2,1)}, bf16[1536,3072]{1,0:T(8,128)(2,1)}, bf16[1536,3072]{1,0:T(8,128)(2,1)}, ...), branch_computations={%region_13.14_spmd, %region_14.15_spmd} | conditional | flops 9060876288 | bytes 72548504 | solution.py:753
  378.9 5.7 all-to-all-start.3
  384.6 13.1 %weight_grad.6 = bf16[768,3072]{1,0:T(8,128)(2,1)} custom-call(s32[1]{0:T(128)} %constant.605.clone.at_ref, bf16[1536,768]{1,0:T(8,128)(2,1)} %get-tuple-element.311.refs_0_, bf16[1536,3072]{1,0:T(8,128)(2,1)} %get-tuple-element.312.refs_1_), custom_call_target="tpu_custom_call" | custom-call | flops 1811939328 | bytes 1769472 | tf_op jit(solution)/shard_map/cond/branch_1_fun/weight_grad/pallas_call | solution.py:501
  397.7 7.9 %convolution_convert_fusion = bf16[1536,768]{1,0:T(8,128)(2,1)S(1)} fusion(bf16[1536,3072]{1,0:T(8,128)(2,1)S(1)} %bitcast.250, bf16[768,3072]{1,0:T(8,128)(2,1)S(1)} %copy-done.16), kind=kOutput, calls=%fused_computation.110 | convolution fusion | flops 7248936960 | bytes 16515072 | tf_op jit(solution)/shard_map/cond/branch_1_fun/dot_general | solution.py:38
  405.6 34.0 %all-to-all-done.3 = bf16[16,96,768]{2,1,0:T(8,128)(2,1)} async-done(((bf16[16,96,768]{2,1,0:T(8,128)(2,1)}), bf16[16,96,768]{2,1,0:T(8,128)(2,1)}, u32[]{:S(2)}, u32[]{:S(2)}) %all-to-all-start.3) | async-done | bytes 2359328 | tf_op jit(solution)/shard_map/cond/branch_1_fun/all_to_all | solution.py:743
  441.1 5.5 all-to-all-start.4
  446.6 40.5 %conditional.18 = (bf16[768,1536]{1,0:T(8,128)(2,1)}, bf16[768,1536]{1,0:T(8,128)(2,1)}, f32[3,208,768]{2,1,0:T(8,128)}, f32[1,768]{1,0:T(1,128)S(1)}, f32[1,768...) conditional(s32[]{:T(128)} %bitcast.88, () %tuple.163, (s32[]{:T(128)}, ...), branch_computations={%region_15.16_spmd, %region_16.17_spmd} | conditional | flops 2111100416 | bytes 20848716 | solution.py:753
  447.2 5.5 return_grad.1
  452.7 24.2 %attend_backward.2 = (f32[3,208,768]{2,1,0:T(8,128)}, bf16[3,208,2304]{2,1,0:T(8,128)(2,1)}, bf16[3,208,768]{2,1,0:T(8,128)(2,1)S(1)}, bf16[3,208,768]{2,1,0:T(8...) custom-call(f32[3,208,768]{2,1,0:T(8,128)} %get-tuple-element.318.x_ref, ...), custom_call_target="tpu_custom_call" | custom-call | flops 1000000000 | bytes 5500000 | tf_op jit(solution)/shard_map/cond/branch_1_fun/attend_backward/pallas_call | solution.py:191
  478.7 8.4 %weight_grad.7 = (bf16[768,1536]{1,0:T(8,128)(2,1)}, bf16[768,1536]{1,0:T(8,128)(2,1)}) custom-call(s32[1]{0:T(128)} %bitcast.25.at_ref, bf16[624,768]{1,0:T(8,128)(2,1)S(1)} %bitcast.238, bf16[624,768]{1,0:T(8,128)(2,1)S(1)} %bitcast.239, bf16[624,2304]{1,0:T(8,128)(2,1)S(1)} %bitcast.234, bf16[624,768]{1,0:T(8,128)(2,1)} %bitcast.32.refs_3_), custom_call_target="tpu_custom_call" | custom-call | flops 736100352 | bytes 1769472 | tf_op jit(solution)/shard_map/cond/branch_1_fun/weight_grad/pallas_call | solution.py:501
  491.8 58.0 %conditional.19 = (bf16[4,48,768]{2,1,0:T(8,128)(2,1)S(1)}, bf16[4,48,768]{2,1,0:T(8,128)(2,1)}, bf16[4,2,2,48,1536]{4,3,2,1,0:T(8,128)(2,1)}, bf16[4,2,2,48,153...) conditional(s32[]{:T(128)} %bitcast.88, () %tuple.162, ...), branch_computations={%region_18.19_spmd, %region_19.20_spmd} | conditional | flops 2964895488 | bytes 140792064 | solution.py:753
  493.3 14.7 %mlp_backward.1 = (f32[3,208,768]{2,1,0:T(8,128)}, bf16[3,208,3072]{2,1,0:T(8,128)(2,1)}, bf16[3,208,768]{2,1,0:T(8,128)(2,1)}, bf16[3,208,768]{2,1,0:T(8,128)(2...) custom-call(f32[3,208,768]{2,1,0:T(8,128)} %get-tuple-element.341.x_ref, f32[3,208,768]{2,1,0:T(8,128)} %get-tuple-element.342.dy_ref, ...), custom_call_target="tpu_custom_call" | custom-call | flops 1475000064 | bytes 6250000 | tf_op jit(solution)/shard_map/cond/branch_1_fun/mlp_backward/pallas_call | solution.py:266
  517.7 13.9 %weight_grad.8 = (bf16[768,3072]{1,0:T(8,128)(2,1)}, bf16[768,3072]{1,0:T(8,128)(2,1)}) custom-call(s32[1]{0:T(128)} %bitcast.40.at_ref, bf16[624,768]{1,0:T(8,128)(2,1)S(1)} %bitcast.236, bf16[624,768]{1,0:T(8,128)(2,1)S(1)} %bitcast.237, bf16[624,3072]{1,0:T(8,128)(2,1)S(1)} %bitcast.233, bf16[624,3072]{1,0:T(8,128)(2,1)} %bitcast.44.refs_3_), custom_call_target="tpu_custom_call" | custom-call | flops 1472200704 | bytes 3538944 | tf_op jit(solution)/shard_map/cond/branch_1_fun/weight_grad/pallas_call | solution.py:501
  535.8 8.2 %collective-permute-done.26 = bf16[4,48,768]{2,1,0:T(8,128)(2,1)S(1)} collective-permute-done((bf16[4,48,768]{2,1,0:T(8,128)(2,1)S(1)}, bf16[4,48,768]{2,1,0:T(8,128)(2,1)S(1)}, u32[]{:S(2)}, u32[]{:S(2)}) %collective-permute-start.26) | collective-permute-done | bytes 294944 | tf_op jit(solution)/shard_map/cond/branch_1_fun/ppermute | solution.py:569
  547.0 2.9 fusion.94
  551.1 37.9 %conditional.20 = (f32[3,208,768]{2,1,0:T(8,128)}, bf16[3,208,2304]{2,1,0:T(8,128)(2,1)}, bf16[3,208,768]{2,1,0:T(8,128)(2,1)}, bf16[3,208,768]{2,1,0:T(8,128)(2...) conditional(s32[]{:T(128)} %bitcast.88, () %tuple.161, ...), branch_computations={%region_20.21_spmd, %region_21.22_spmd} | conditional | flops 1006488064 | bytes 31809184 | solution.py:753
  558.4 24.8 %attend_backward.3 = (f32[3,208,768]{2,1,0:T(8,128)}, bf16[3,208,2304]{2,1,0:T(8,128)(2,1)}, bf16[3,208,768]{2,1,0:T(8,128)(2,1)}, bf16[3,208,768]{2,1,0:T(8,128...) custom-call(f32[3,208,768]{2,1,0:T(8,128)} %get-tuple-element.383.x_ref, f32[3,208,768]{2,1,0:T(8,128)} %get-tuple-element.384.dy_ref, ...), custom_call_target="tpu_custom_call" | custom-call | flops 1000000000 | bytes 5500000 | tf_op jit(solution)/shard_map/cond/branch_1_fun/attend_backward/pallas_call | solution.py:191
  583.2 4.1 fusion.64
  593.9 30.9 %conditional.21 = (f32[768,8]{0,1:T(8,128)S(1)}, bf16[768,1536]{1,0:T(8,128)(2,1)}, bf16[768,1536]{1,0:T(8,128)(2,1)}, f32[48,1536]{1,0:T(8,128)S(1)}, f32[3,208...) conditional(s32[]{:T(128)} %bitcast.88, () %tuple.160, (f32[1,768]{1,0:T(1,128)S(1)}, ...), branch_computations={%region_23.24_spmd, %region_24.25_spmd} | conditional | flops 1491040128 | bytes 30086432 | solution.py:753
  599.0 9.5 %weight_grad.9 = (bf16[768,1536]{1,0:T(8,128)(2,1)}, bf16[768,1536]{1,0:T(8,128)(2,1)}) custom-call(s32[1]{0:T(128)} %bitcast.64.at_ref, bf16[624,768]{1,0:T(8,128)(2,1)} %bitcast.65.refs_0_, bf16[624,768]{1,0:T(8,128)(2,1)} %bitcast.66.refs_1_, bf16[624,2304]{1,0:T(8,128)(2,1)} %bitcast.67.refs_2_, bf16[624,768]{1,0:T(8,128)(2,1)} %bitcast.255), custom_call_target="tpu_custom_call" | custom-call | flops 736100352 | bytes 1769472 | tf_op jit(solution)/shard_map/cond/branch_1_fun/weight_grad/pallas_call | solution.py:501
  608.5 6.8 combine.1
  615.4 5.6 collective-permute-done.39
  629.6 37.6 %conditional.22 = (bf16[4,48,1536]{2,1,0:T(8,128)(2,1)S(1)}, f32[591,768]{1,0:T(8,128)}, f32[591,2]{0,1:T(2,128)S(1)}, f32[591,768]{1,0:T(8,128)}) conditional(s32[]{:T(128)} %bitcast.88, () %tuple.159, (bf16[768,1536]{1,0:T(8,128)(2,1)}, bf16[768,1536]{1,0:T(8,128)(2,1)}, f32[3,208,768]{2,1,0:T(8,128)}, f32[3,208,2]{2,1,0:T(8,128)}, ...), branch_computations={%region_25.26_spmd, %region_26.27_spmd} | conditional | flops 9437204 | bytes 55262188 | solution.py:753
  629.6 2.9 collective-permute-start.29
  632.5 4.4 collective-permute-done.29
  640.1 14.2 %collective-permute-done.30 = bf16[4,2,48,768]{3,2,0,1:T(8,128)(2,1)} collective-permute-done((bf16[4,2,48,768]{3,2,0,1:T(8,128)(2,1)S(1)}, bf16[4,2,48,768]{3,2,0,1:T(8,128)(2,1)}, u32[]{:S(2)}, u32[]{:S(2)}) %collective-permute-start.30) | collective-permute-done | bytes 589856 | tf_op jit(solution)/shard_map/cond/branch_1_fun/ppermute | solution.py:569
  670.0 35.0 %conditional.23 = (f32[24,3072]{1,0:T(8,128)}, f32[24,9216]{1,0:T(8,128)S(1)}, f32[24,8]{1,0:T(8,128)S(1)}, f32[2,192,3072]{2,1,0:T(8,128)}, f32[2,192,3072]{2,1,0:T(8,128)}) conditional(s32[]{:T(128)} %bitcast.88, () %tuple.189, (bf16[4,48,1536]{2,1,0:T(8,128)(2,1)S(1)}, bf16[2,48,3072]{2,1,0:T(8,128)(2,1)}, bf16[2,48,3072]{2,1,0:T(8,128)(2,1)}, ...), branch_computations={%region_27.28_spmd, %region_28.30_spmd} | conditional | flops 12760929 | bytes 66374716 | solution.py:753
  676.0 5.7 all-to-all-start
  681.7 2.9 convert_element_type.293
  (380 shorter events, 181.1 us)
Async XLA Ops:
  7.2 74.2 %all-gather.4.cloned.1.call-start = ((), (), s32[]{:S(2)}) async-start(), calls=%async_computation.7 | async-start | bytes 2211840 | tf_op jit(solution)/shard_map/all_gather | solution.py:587
  10.8 1.3 collective-permute-start.40
  11.0 23.0 %copy-start.44 = (s32[591,2]{0,1:T(2,128)S(1)}, s32[591,2]{0,1:T(2,128)}, u32[]{:S(2)}) copy-start(s32[591,2]{0,1:T(2,128)} %param.46) | copy-start | bytes 14188
  11.1 24.2 %copy-start.42 = (f32[591,2]{0,1:T(2,128)S(1)}, f32[591,2]{0,1:T(2,128)}, u32[]{:S(2)}) copy-start(f32[591,2]{0,1:T(2,128)} %param.45) | copy-start | bytes 14188
  29.2 4.0 collective-permute-start.41
  34.0 291.1 %all-gather.6.cloned.1.call-start = ((), (), s32[]{:S(2)}) async-start(), calls=%async_computation.8 | async-start | bytes 7077888 | tf_op jit(solution)/shard_map/all_gather | solution.py:726
  36.8 12.3 %collective-permute-start.6 = (bf16[4,48,896]{2,1,0:T(8,128)(2,1)}, bf16[4,48,896]{2,1,0:T(8,128)(2,1)}, u32[]{:S(2)}, u32[]{:S(2)}) collective-permute-start(bf16[4,48,896]{2,1,0:T(8,128)(2,1)} %slice.120), channel_id=1, source_target_pairs={{0,4},{4,0},{1,5},{5,1},{2,6},{6,2},{3,7},{7,3},{8,12},{12,8},{9,1... | collective-permute-start | bytes 1032200 | tf_op jit(solution)/shard_map/cond/branch_1_fun/ppermute | solution.py:569
  38.0 11.1 %collective-permute-start.5 = (bf16[4,48,768]{2,1,0:T(8,128)(2,1)}, bf16[4,48,768]{2,1,0:T(8,128)(2,1)}, u32[]{:S(2)}, u32[]{:S(2)}) collective-permute-start(bf16[4,48,768]{2,1,0:T(8,128)(2,1)} %slice.119), channel_id=1, source_target_pairs={{0,2},{2,0},{1,3},{3,1},{4,6},{6,4},{5,7},{7,5},{8,10},{10,8},{9,1... | collective-permute-start | bytes 884744 | tf_op jit(solution)/shard_map/cond/branch_1_fun/ppermute | solution.py:569
  57.9 18.7 %collective-permute-start.8 = (bf16[8,48,896]{2,1,0:T(8,128)(2,1)}, bf16[8,48,896]{2,1,0:T(8,128)(2,1)}, u32[]{:S(2)}, u32[]{:S(2)}) collective-permute-start(bf16[8,48,896]{2,1,0:T(8,128)(2,1)} %pad_maximum_fusion.13), channel_id=1, source_target_pairs={{0,2},{2,0},{1,3},{3,1},{4,6},{6,4},{5,7},{7,5},{8,10},{10,8},{9,1... | collective-permute-start | bytes 2064392 | tf_op jit(solution)/shard_map/cond/branch_1_fun/ppermute | solution.py:569
  58.7 17.8 %collective-permute-start.7 = (bf16[8,48,768]{2,1,0:T(8,128)(2,1)}, bf16[8,48,768]{2,1,0:T(8,128)(2,1)}, u32[]{:S(2)}, u32[]{:S(2)}) collective-permute-start(bf16[8,48,768]{2,1,0:T(8,128)(2,1)} %pad_maximum_fusion.14), channel_id=1, source_target_pairs={{0,4},{4,0},{1,5},{5,1},{2,6},{6,2},{3,7},{7,3},{8,12},{12,8},{9,1... | collective-permute-start | bytes 1769480 | tf_op jit(solution)/shard_map/cond/branch_1_fun/ppermute | solution.py:569
  81.4 57.9 %collective-permute-start.42 = (bf16[192,3072]{1,0:T(8,128)(2,1)}, bf16[192,3072]{1,0:T(8,128)(2,1)}, u32[]{:S(2)}, u32[]{:S(2)}) collective-permute-start(bf16[192,3072]{1,0:T(8,128)(2,1)} %get-tuple-element.598), channel_id=1, source_target_pairs={{0,16},{16,0},{1,17},{17,1},{2,18},{18,2},{3,19},{19,3},{4,20},{20... | collective-permute-start | bytes 3538952 | tf_op jit(solution)/shard_map/ppermute | solution.py:569
  82.9 22.5 %collective-permute-start.10 = (bf16[16,48,896]{2,1,0:T(8,128)(2,1)}, bf16[16,48,896]{2,1,0:T(8,128)(2,1)S(1)}, u32[]{:S(2)}, u32[]{:S(2)}) collective-permute-start(bf16[16,48,896]{2,1,0:T(8,128)(2,1)} %get-tuple-element.242.refs_1_), channel_id=1, source_target_pairs={{0,1},{1,0},{2,3},{3,2},{4,5},{5,4},{6,7},{7,6},{8,9},{9,8},{10,11... | collective-permute-start | bytes 4128776 | tf_op jit(solution)/shard_map/cond/branch_1_fun/ppermute | solution.py:569
  84.5 20.9 %collective-permute-start.9 = (bf16[16,48,768]{2,1,0:T(8,128)(2,1)}, bf16[16,48,768]{2,1,0:T(8,128)(2,1)S(1)}, u32[]{:S(2)}, u32[]{:S(2)}) collective-permute-start(bf16[16,48,768]{2,1,0:T(8,128)(2,1)} %get-tuple-element.241.refs_0_), channel_id=1, source_target_pairs={{0,1},{1,0},{2,3},{3,2},{4,5},{5,4},{6,7},{7,6},{8,9},{9,8},{10,11... | collective-permute-start | bytes 3538952 | tf_op jit(solution)/shard_map/cond/branch_1_fun/ppermute | solution.py:569
  86.7 14.8 %collective-permute-start.11 = (bf16[4,48,1536]{2,1,0:T(8,128)(2,1)}, bf16[4,48,1536]{2,1,0:T(8,128)(2,1)}, u32[]{:S(2)}, u32[]{:S(2)}) collective-permute-start(bf16[4,48,1536]{2,1,0:T(8,128)(2,1)} %get-tuple-element.237), channel_id=1, source_target_pairs={{0,2},{2,0},{1,3},{3,1},{4,6},{6,4},{5,7},{7,5},{8,10},{10,8},{9,1... | collective-permute-start | bytes 1769480 | tf_op jit(solution)/shard_map/cond/branch_1_fun/ppermute | solution.py:569
  88.1 14.3 %collective-permute-start.12 = (bf16[4,48,1536]{2,1,0:T(8,128)(2,1)S(1)}, bf16[4,48,1536]{2,1,0:T(8,128)(2,1)}, u32[]{:S(2)}, u32[]{:S(2)}) collective-permute-start(bf16[4,48,1536]{2,1,0:T(8,128)(2,1)S(1)} %get-tuple-element.238), channel_id=1, source_target_pairs={{0,4},{4,0},{1,5},{5,1},{2,6},{6,2},{3,7},{7,3},{8,12},{12,8},{9,1... | collective-permute-start | bytes 1769480 | tf_op jit(solution)/shard_map/cond/branch_1_fun/ppermute | solution.py:569
  105.4 26.2 %collective-permute-start.13 = (bf16[8,48,1536]{2,1,0:T(8,128)(2,1)}, bf16[8,48,1536]{2,1,0:T(8,128)(2,1)}, u32[]{:S(2)}, u32[]{:S(2)}) collective-permute-start(bf16[8,48,1536]{2,1,0:T(8,128)(2,1)} %get-tuple-element.247), channel_id=1, source_target_pairs={{0,4},{4,0},{1,5},{5,1},{2,6},{6,2},{3,7},{7,3},{8,12},{12,8},{9,1... | collective-permute-start | bytes 3538952 | tf_op jit(solution)/shard_map/cond/branch_1_fun/ppermute | solution.py:569
  106.9 25.9 %collective-permute-start.14 = (bf16[8,48,1536]{2,1,0:T(8,128)(2,1)}, bf16[8,48,1536]{2,1,0:T(8,128)(2,1)}, u32[]{:S(2)}, u32[]{:S(2)}) collective-permute-start(bf16[8,48,1536]{2,1,0:T(8,128)(2,1)} %get-tuple-element.248), channel_id=1, source_target_pairs={{0,2},{2,0},{1,3},{3,1},{4,6},{6,4},{5,7},{7,5},{8,10},{10,8},{9,1... | collective-permute-start | bytes 3538952 | tf_op jit(solution)/shard_map/cond/branch_1_fun/ppermute | solution.py:569
  143.5 200.1 %all-gather.8.cloned.1.call-start = ((), (), s32[]{:S(2)}) async-start(), calls=%async_computation.9 | async-start | bytes 7077888 | tf_op jit(solution)/shard_map/all_gather | solution.py:726
  143.5 53.0 %collective-permute-start.43 = (bf16[192,3072]{1,0:T(8,128)(2,1)}, bf16[192,3072]{1,0:T(8,128)(2,1)}, u32[]{:S(2)}, u32[]{:S(2)}) collective-permute-start(bf16[192,3072]{1,0:T(8,128)(2,1)} %get-tuple-element.610), channel_id=1, source_target_pairs={{0,16},{16,0},{1,17},{17,1},{2,18},{18,2},{3,19},{19,3},{4,20},{20... | collective-permute-start | bytes 3538952 | tf_op jit(solution)/shard_map/ppermute | solution.py:569
  145.2 13.6 %collective-permute-start.15 = (bf16[16,48,1536]{2,1,0:T(8,128)(2,1)}, bf16[16,48,1536]{2,1,0:T(8,128)(2,1)S(1)}, u32[]{:S(2)}, u32[]{:S(2)}) collective-permute-start(bf16[16,48,1536]{2,1,0:T(8,128)(2,1)} %get-tuple-element.266.refs_0_), channel_id=1, source_target_pairs={{0,1},{1,0},{2,3},{3,2},{4,5},{5,4},{6,7},{7,6},{8,9},{9,8},{10,11... | collective-permute-start | bytes 7077896 | tf_op jit(solution)/shard_map/cond/branch_1_fun/ppermute | solution.py:569
  148.3 10.5 %collective-permute-start.16 = (bf16[16,48,1536]{2,1,0:T(8,128)(2,1)}, bf16[16,48,1536]{2,1,0:T(8,128)(2,1)}, u32[]{:S(2)}, u32[]{:S(2)}) collective-permute-start(bf16[16,48,1536]{2,1,0:T(8,128)(2,1)} %get-tuple-element.267.refs_1_), channel_id=1, source_target_pairs={{0,1},{1,0},{2,3},{3,2},{4,5},{5,4},{6,7},{7,6},{8,9},{9,8},{10,11... | collective-permute-start | bytes 7077896 | tf_op jit(solution)/shard_map/cond/branch_1_fun/ppermute | solution.py:569
  148.4 8.3 %collective-permute-start.17 = (bf16[4,48,768]{2,1,0:T(8,128)(2,1)S(1)}, bf16[4,48,768]{2,1,0:T(8,128)(2,1)S(1)}, u32[]{:S(2)}, u32[]{:S(2)}) collective-permute-start(bf16[4,48,768]{2,1,0:T(8,128)(2,1)S(1)} %get-tuple-element.262), channel_id=1, source_target_pairs={{0,2},{2,0},{1,3},{3,1},{4,6},{6,4},{5,7},{7,5},{8,10},{10,8},{9,1... | collective-permute-start | bytes 884744 | tf_op jit(solution)/shard_map/cond/branch_1_fun/ppermute | solution.py:569
  148.9 8.4 %collective-permute-start.18 = (bf16[4,48,768]{2,1,0:T(8,128)(2,1)}, bf16[4,48,768]{2,1,0:T(8,128)(2,1)}, u32[]{:S(2)}, u32[]{:S(2)}) collective-permute-start(bf16[4,48,768]{2,1,0:T(8,128)(2,1)} %get-tuple-element.263), channel_id=1, source_target_pairs={{0,4},{4,0},{1,5},{5,1},{2,6},{6,2},{3,7},{7,3},{8,12},{12,8},{9,1... | collective-permute-start | bytes 884744 | tf_op jit(solution)/shard_map/cond/branch_1_fun/ppermute | solution.py:569
  158.8 16.5 %copy-start.19 = (bf16[8,48,768]{2,1,0:T(8,128)(2,1)}, bf16[8,48,768]{2,1,0:T(8,128)(2,1)S(1)}, u32[]{:S(2)}) copy-start(bf16[8,48,768]{2,1,0:T(8,128)(2,1)S(1)} %get-tuple-element.272) | copy-start | bytes 1769476 | tf_op jit(solution)/shard_map/cond
  158.8 31.5 %collective-permute-start.19 = (bf16[8,48,768]{2,1,0:T(8,128)(2,1)S(1)}, bf16[8,48,768]{2,1,0:T(8,128)(2,1)}, u32[]{:S(2)}, u32[]{:S(2)}) collective-permute-start(bf16[8,48,768]{2,1,0:T(8,128)(2,1)S(1)} %get-tuple-element.272), channel_id=1, source_target_pairs={{0,4},{4,0},{1,5},{5,1},{2,6},{6,2},{3,7},{7,3},{8,12},{12,8},{9,1... | collective-permute-start | bytes 1769480 | tf_op jit(solution)/shard_map/cond/branch_1_fun/ppermute | solution.py:569
  159.0 31.4 %collective-permute-start.20 = (bf16[8,48,768]{2,1,0:T(8,128)(2,1)S(1)}, bf16[8,48,768]{2,1,0:T(8,128)(2,1)}, u32[]{:S(2)}, u32[]{:S(2)}) collective-permute-start(bf16[8,48,768]{2,1,0:T(8,128)(2,1)S(1)} %get-tuple-element.273), channel_id=1, source_target_pairs={{0,2},{2,0},{1,3},{3,1},{4,6},{6,4},{5,7},{7,5},{8,10},{10,8},{9,1... | collective-permute-start | bytes 1769480 | tf_op jit(solution)/shard_map/cond/branch_1_fun/ppermute | solution.py:569
  200.7 286.4 %reduce-scatter.3.cloned.1.call-start = ((), (), s32[]{:S(2)}) async-start(), calls=%async_computation.10 | async-start | bytes 7077888 | tf_op jit(solution)/shard_map/reduce_scatter | solution.py:731
  202.2 62.2 %all-to-all-start.1 = ((bf16[16,96,768]{2,1,0:T(8,128)(2,1)}), bf16[16,96,768]{2,1,0:T(8,128)(2,1)}, u32[]{:S(2)}, u32[]{:S(2)}) async-start(bf16[16,96,768]{2,1,0:T(8,128)(2,1)} %bitcast.19), calls=%async_computation.1 | async-start | bytes 4718592 | tf_op jit(solution)/shard_map/cond/branch_1_fun/all_to_all | solution.py:743
  208.4 9.2 %collective-permute-start.21 = (bf16[16,48,768]{2,1,0:T(8,128)(2,1)S(1)}, bf16[16,48,768]{2,1,0:T(8,128)(2,1)S(1)}, u32[]{:S(2)}, u32[]{:S(2)}) collective-permute-start(bf16[16,48,768]{2,1,0:T(8,128)(2,1)S(1)} %get-tuple-element.287.refs_0_), channel_id=1, source_target_pairs={{0,1},{1,0},{2,3},{3,2},{4,5},{5,4},{6,7},{7,6},{8,9},{9,8},{10,11... | collective-permute-start | bytes 3538952 | tf_op jit(solution)/shard_map/cond/branch_1_fun/ppermute | solution.py:569
  208.7 8.9 %collective-permute-start.22 = (bf16[16,48,768]{2,1,0:T(8,128)(2,1)}, bf16[16,48,768]{2,1,0:T(8,128)(2,1)S(1)}, u32[]{:S(2)}, u32[]{:S(2)}) collective-permute-start(bf16[16,48,768]{2,1,0:T(8,128)(2,1)} %get-tuple-element.288.refs_1_), channel_id=1, source_target_pairs={{0,1},{1,0},{2,3},{3,2},{4,5},{5,4},{6,7},{7,6},{8,9},{9,8},{10,11... | collective-permute-start | bytes 3538952 | tf_op jit(solution)/shard_map/cond/branch_1_fun/ppermute | solution.py:569
  343.8 23.1 %slice-start = ((s8[9437184]{0:T(1024)(128)(4,1)}), s8[4194304]{0:T(1024)(128)(4,1)S(1)}, s32[]{:S(2)}) async-start(s8[9437184]{0:T(1024)(128)(4,1)} %bitcast.247), calls=%async_computation.12 | async-start | bytes 8388608 | tf_op jit(solution)/shard_map/cond
  343.8 23.1 %slice-start.1 = ((s8[9437184]{0:T(1024)(128)(4,1)}), s8[4194304]{0:T(1024)(128)(4,1)S(1)}, s32[]{:S(2)}) async-start(s8[9437184]{0:T(1024)(128)(4,1)} %bitcast.247), calls=%async_computation.13 | async-start | bytes 8388608 | tf_op jit(solution)/shard_map/cond
  343.8 23.1 %slice-start.2 = ((s8[9437184]{0:T(1024)(128)(4,1)}), s8[1048576]{0:T(1024)(128)(4,1)S(1)}, s32[]{:S(2)}) async-start(s8[9437184]{0:T(1024)(128)(4,1)} %bitcast.247), calls=%async_computation.14 | async-start | bytes 2097152 | tf_op jit(solution)/shard_map/cond
  378.8 210.2 %reduce-scatter.5.cloned.1.call-start = ((), (), s32[]{:S(2)}) async-start(), calls=%async_computation.11 | async-start | bytes 7077888 | tf_op jit(solution)/shard_map/reduce_scatter | solution.py:731
  378.9 18.8 %slice-start.3 = ((s8[9437184]{0:T(1024)(128)(4,1)}), s8[1048576]{0:T(1024)(128)(4,1)S(1)}, s32[]{:S(2)}) async-start(s8[9437184]{0:T(1024)(128)(4,1)} %bitcast.249), calls=%async_computation.15 | async-start | bytes 2097152 | tf_op jit(solution)/shard_map/cond
  378.9 60.7 %all-to-all-start.3 = ((bf16[16,96,768]{2,1,0:T(8,128)(2,1)}), bf16[16,96,768]{2,1,0:T(8,128)(2,1)}, u32[]{:S(2)}, u32[]{:S(2)}) async-start(bf16[16,96,768]{2,1,0:T(8,128)(2,1)} %bitcast.23), calls=%async_computation.3 | async-start | bytes 4718592 | tf_op jit(solution)/shard_map/cond/branch_1_fun/all_to_all | solution.py:743
  441.1 108.7 %all-to-all-start.4 = ((bf16[16,96,768]{2,1,0:T(8,128)(2,1)}), bf16[16,96,768]{2,1,0:T(8,128)(2,1)}, u32[]{:S(2)}, u32[]{:S(2)}) async-start(bf16[16,96,768]{2,1,0:T(8,128)(2,1)} %bitcast.251), calls=%async_computation.5 | async-start | bytes 4718592 | tf_op jit(solution)/shard_map/all_to_all | solution.py:743
  489.4 61.7 %collective-permute-start.44 = (bf16[1,192,3072]{2,1,0:T(8,128)(2,1)}, bf16[1,192,3072]{2,1,0:T(8,128)(2,1)}, u32[]{:S(2)}, u32[]{:S(2)}) collective-permute-start(bf16[1,192,3072]{2,1,0:T(8,128)(2,1)} %constant_dynamic-slice_fusion.5), channel_id=1, source_target_pairs={{0,16},{16,0},{1,17},{17,1},{2,18},{18,2},{3,19},{19,3},{4,20},{20... | collective-permute-start | bytes 3538952 | tf_op jit(solution)/shard_map/ppermute | solution.py:569
  491.9 16.1 %collective-permute-start.23 = (bf16[768,1536]{1,0:T(8,128)(2,1)}, bf16[768,1536]{1,0:T(8,128)(2,1)S(1)}, u32[]{:S(2)}, u32[]{:S(2)}) collective-permute-start(bf16[768,1536]{1,0:T(8,128)(2,1)} %get-tuple-element.340), channel_id=1, source_target_pairs={{0,1},{1,0},{2,3},{3,2},{4,5},{5,4},{6,7},{7,6},{8,9},{9,8},{10,11... | collective-permute-start | bytes 7077896 | tf_op jit(solution)/shard_map/cond/branch_1_fun/ppermute | solution.py:569
  513.2 18.4 %collective-permute-start.24 = (bf16[4,2,48,768]{3,2,1,0:T(8,128)(2,1)}, bf16[4,2,48,768]{3,2,1,0:T(8,128)(2,1)}, u32[]{:S(2)}, u32[]{:S(2)}) collective-permute-start(bf16[4,2,48,768]{3,2,1,0:T(8,128)(2,1)} %dynamic-slice_bitcast_fusion.1), channel_id=1, source_target_pairs={{0,4},{4,0},{1,5},{5,1},{2,6},{6,2},{3,7},{7,3},{8,12},{12,8},{9,1... | collective-permute-start | bytes 1769480 | tf_op jit(solution)/shard_map/cond/branch_1_fun/ppermute | solution.py:569
  514.5 17.2 %collective-permute-start.25 = (bf16[4,2,48,768]{3,2,1,0:T(8,128)(2,1)}, bf16[4,2,48,768]{3,2,1,0:T(8,128)(2,1)}, u32[]{:S(2)}, u32[]{:S(2)}) collective-permute-start(bf16[4,2,48,768]{3,2,1,0:T(8,128)(2,1)} %dynamic-slice_bitcast_fusion), channel_id=1, source_target_pairs={{0,2},{2,0},{1,3},{3,1},{4,6},{6,4},{5,7},{7,5},{8,10},{10,8},{9,1... | collective-permute-start | bytes 1769480 | tf_op jit(solution)/shard_map/cond/branch_1_fun/ppermute | solution.py:569
  534.3 10.6 %collective-permute-start.28 = (bf16[768,3072]{1,0:T(8,128)(2,1)}, bf16[768,3072]{1,0:T(8,128)(2,1)S(1)}, u32[]{:S(2)}, u32[]{:S(2)}) collective-permute-start(bf16[768,3072]{1,0:T(8,128)(2,1)} %get-tuple-element.369), channel_id=1, source_target_pairs={{0,1},{1,0},{2,3},{3,2},{4,5},{5,4},{6,7},{7,6},{8,9},{9,8},{10,11... | collective-permute-start | bytes 14155784 | tf_op jit(solution)/shard_map/cond/branch_1_fun/ppermute | solution.py:569
  535.2 8.8 %collective-permute-start.26 = (bf16[4,48,768]{2,1,0:T(8,128)(2,1)S(1)}, bf16[4,48,768]{2,1,0:T(8,128)(2,1)S(1)}, u32[]{:S(2)}, u32[]{:S(2)}) collective-permute-start(bf16[4,48,768]{2,1,0:T(8,128)(2,1)S(1)} %dynamic-slice_bitcast_fusion.3), channel_id=1, source_target_pairs={{0,2},{2,0},{1,3},{3,1},{4,6},{6,4},{5,7},{7,5},{8,10},{10,8},{9,1... | collective-permute-start | bytes 884744 | tf_op jit(solution)/shard_map/cond/branch_1_fun/ppermute | solution.py:569
  535.6 8.4 %collective-permute-start.27 = (bf16[4,48,768]{2,1,0:T(8,128)(2,1)S(1)}, bf16[4,48,768]{2,1,0:T(8,128)(2,1)S(1)}, u32[]{:S(2)}, u32[]{:S(2)}) collective-permute-start(bf16[4,48,768]{2,1,0:T(8,128)(2,1)S(1)} %dynamic-slice_bitcast_fusion.2), channel_id=1, source_target_pairs={{0,4},{4,0},{1,5},{5,1},{2,6},{6,2},{3,7},{7,3},{8,12},{12,8},{9,1... | collective-permute-start | bytes 884744 | tf_op jit(solution)/shard_map/cond/branch_1_fun/ppermute | solution.py:569
  554.1 29.1 %collective-permute-start.34 = (bf16[4,2,48,1536]{3,2,1,0:T(8,128)(2,1)S(1)}, bf16[4,2,48,1536]{3,2,1,0:T(8,128)(2,1)}, u32[]{:S(2)}, u32[]{:S(2)}) collective-permute-start(bf16[4,2,48,1536]{3,2,1,0:T(8,128)(2,1)S(1)} %dynamic-slice_bitcast_fusion.5), channel_id=1, source_target_pairs={{0,4},{4,0},{1,5},{5,1},{2,6},{6,2},{3,7},{7,3},{8,12},{12,8},{9,1... | collective-permute-start | bytes 3538952 | tf_op jit(solution)/shard_map/cond/branch_1_fun/ppermute | solution.py:569
  555.4 27.8 %collective-permute-start.35 = (bf16[4,2,48,1536]{3,2,1,0:T(8,128)(2,1)S(1)}, bf16[4,2,48,1536]{3,2,1,0:T(8,128)(2,1)}, u32[]{:S(2)}, u32[]{:S(2)}) collective-permute-start(bf16[4,2,48,1536]{3,2,1,0:T(8,128)(2,1)S(1)} %dynamic-slice_bitcast_fusion.4), channel_id=1, source_target_pairs={{0,2},{2,0},{1,3},{3,1},{4,6},{6,4},{5,7},{7,5},{8,10},{10,8},{9,1... | collective-permute-start | bytes 3538952 | tf_op jit(solution)/shard_map/cond/branch_1_fun/ppermute | solution.py:569
  558.3 29.0 %collective-permute-start.36 = (bf16[2,48,1536]{2,1,0:T(8,128)(2,1)}, bf16[2,48,1536]{2,1,0:T(8,128)(2,1)S(1)}, u32[]{:S(2)}, u32[]{:S(2)}) collective-permute-start(bf16[2,48,1536]{2,1,0:T(8,128)(2,1)} %dynamic-slice_bitcast_fusion.6), channel_id=1, source_target_pairs={{0,16},{16,0},{1,17},{17,1},{2,18},{18,2},{3,19},{19,3},{4,20},{20... | collective-permute-start | bytes 884744 | tf_op jit(solution)/shard_map/cond/branch_1_fun/ppermute | solution.py:569
  591.6 78.4 %collective-permute-start.46 = (bf16[1,192,3072]{2,1,0:T(8,128)(2,1)}, bf16[1,192,3072]{2,1,0:T(8,128)(2,1)}, u32[]{:S(2)}, u32[]{:S(2)}) collective-permute-start(bf16[1,192,3072]{2,1,0:T(8,128)(2,1)} %constant_dynamic-slice_fusion.4), channel_id=1, source_target_pairs={{0,16},{16,0},{1,17},{17,1},{2,18},{18,2},{3,19},{19,3},{4,20},{20... | collective-permute-start | bytes 3538952 | tf_op jit(solution)/shard_map/ppermute | solution.py:569
  594.2 14.3 %copy-start.25 = (bf16[2,48,1536]{2,1,0:T(8,128)(2,1)}, bf16[2,48,1536]{2,1,0:T(8,128)(2,1)S(1)}, u32[]{:S(2)}) copy-start(bf16[2,48,1536]{2,1,0:T(8,128)(2,1)S(1)} %get-tuple-element.430) | copy-start | bytes 884740 | tf_op jit(solution)/shard_map/cond
  594.9 26.0 %collective-permute-start.39 = (bf16[48,1536]{1,0:T(8,128)(2,1)}, bf16[48,1536]{1,0:T(8,128)(2,1)}, u32[]{:S(2)}, u32[]{:S(2)}) collective-permute-start(bf16[48,1536]{1,0:T(8,128)(2,1)} %dynamic-slice_bitcast_fusion.9), channel_id=1, source_target_pairs={{0,8},{8,0},{1,9},{9,1},{2,10},{10,2},{3,11},{11,3},{4,12},{12,4},... | collective-permute-start | bytes 442376 | tf_op jit(solution)/shard_map/cond/branch_1_fun/ppermute | solution.py:569
  597.7 24.2 %collective-permute-start.37 = (bf16[4,48,1536]{2,1,0:T(8,128)(2,1)}, bf16[4,48,1536]{2,1,0:T(8,128)(2,1)}, u32[]{:S(2)}, u32[]{:S(2)}) collective-permute-start(bf16[4,48,1536]{2,1,0:T(8,128)(2,1)} %dynamic-slice_bitcast_fusion.8), channel_id=1, source_target_pairs={{0,2},{2,0},{1,3},{3,1},{4,6},{6,4},{5,7},{7,5},{8,10},{10,8},{9,1... | collective-permute-start | bytes 1769480 | tf_op jit(solution)/shard_map/cond/branch_1_fun/ppermute | solution.py:569
  598.0 23.9 %collective-permute-start.38 = (bf16[4,48,1536]{2,1,0:T(8,128)(2,1)}, bf16[4,48,1536]{2,1,0:T(8,128)(2,1)}, u32[]{:S(2)}, u32[]{:S(2)}) collective-permute-start(bf16[4,48,1536]{2,1,0:T(8,128)(2,1)} %dynamic-slice_bitcast_fusion.7), channel_id=1, source_target_pairs={{0,4},{4,0},{1,5},{5,1},{2,6},{6,2},{3,7},{7,3},{8,12},{12,8},{9,1... | collective-permute-start | bytes 1769480 | tf_op jit(solution)/shard_map/cond/branch_1_fun/ppermute | solution.py:569
  627.3 42.8 %collective-permute-start.45 = (bf16[2,48,3072]{2,1,0:T(8,128)(2,1)}, bf16[2,48,3072]{2,1,0:T(8,128)(2,1)}, u32[]{:S(2)}, u32[]{:S(2)}) collective-permute-start(bf16[2,48,3072]{2,1,0:T(8,128)(2,1)} %get-tuple-element.1035), channel_id=1, source_target_pairs={{0,16},{16,0},{1,17},{17,1},{2,18},{18,2},{3,19},{19,3},{4,20},{20... | collective-permute-start | bytes 1769480 | tf_op jit(solution)/shard_map/ppermute | solution.py:569
  629.6 7.3 %collective-permute-start.29 = (bf16[768,1536]{1,0:T(8,128)(2,1)}, bf16[768,1536]{1,0:T(8,128)(2,1)S(1)}, u32[]{:S(2)}, u32[]{:S(2)}) collective-permute-start(bf16[768,1536]{1,0:T(8,128)(2,1)} %get-tuple-element.436), channel_id=1, source_target_pairs={{0,1},{1,0},{2,3},{3,2},{4,5},{5,4},{6,7},{7,6},{8,9},{9,8},{10,11... | collective-permute-start | bytes 7077896 | tf_op jit(solution)/shard_map/cond/branch_1_fun/ppermute | solution.py:569
  639.6 14.7 %collective-permute-start.30 = (bf16[4,2,48,768]{3,2,0,1:T(8,128)(2,1)S(1)}, bf16[4,2,48,768]{3,2,0,1:T(8,128)(2,1)}, u32[]{:S(2)}, u32[]{:S(2)}) collective-permute-start(bf16[4,2,48,768]{3,2,0,1:T(8,128)(2,1)S(1)} %dynamic-slice_bitcast_fusion.11), channel_id=1, source_target_pairs={{0,4},{4,0},{1,5},{5,1},{2,6},{6,2},{3,7},{7,3},{8,12},{12,8},{9,1... | collective-permute-start | bytes 1769480 | tf_op jit(solution)/shard_map/cond/branch_1_fun/ppermute | solution.py:569
  639.9 14.4 %collective-permute-start.31 = (bf16[4,2,48,768]{3,2,1,0:T(8,128)(2,1)S(1)}, bf16[4,2,48,768]{3,2,1,0:T(8,128)(2,1)}, u32[]{:S(2)}, u32[]{:S(2)}) collective-permute-start(bf16[4,2,48,768]{3,2,1,0:T(8,128)(2,1)S(1)} %dynamic-slice_bitcast_fusion.10), channel_id=1, source_target_pairs={{0,2},{2,0},{1,3},{3,1},{4,6},{6,4},{5,7},{7,5},{8,10},{10,8},{9,1... | collective-permute-start | bytes 1769480 | tf_op jit(solution)/shard_map/cond/branch_1_fun/ppermute | solution.py:569
  658.2 7.8 %collective-permute-start.32 = (bf16[4,48,768]{2,1,0:T(8,128)(2,1)}, bf16[4,48,768]{2,1,0:T(8,128)(2,1)}, u32[]{:S(2)}, u32[]{:S(2)}) collective-permute-start(bf16[4,48,768]{2,1,0:T(8,128)(2,1)} %dynamic-slice_bitcast_fusion.13), channel_id=1, source_target_pairs={{0,2},{2,0},{1,3},{3,1},{4,6},{6,4},{5,7},{7,5},{8,10},{10,8},{9,1... | collective-permute-start | bytes 884744 | tf_op jit(solution)/shard_map/cond/branch_1_fun/ppermute | solution.py:569
  658.5 7.5 %collective-permute-start.33 = (bf16[4,48,768]{2,1,0:T(8,128)(2,1)}, bf16[4,48,768]{2,1,0:T(8,128)(2,1)}, u32[]{:S(2)}, u32[]{:S(2)}) collective-permute-start(bf16[4,48,768]{2,1,0:T(8,128)(2,1)} %dynamic-slice_bitcast_fusion.12), channel_id=1, source_target_pairs={{0,4},{4,0},{1,5},{5,1},{2,6},{6,2},{3,7},{7,3},{8,12},{12,8},{9,1... | collective-permute-start | bytes 884744 | tf_op jit(solution)/shard_map/cond/branch_1_fun/ppermute | solution.py:569
  673.0 18.0 %collective-permute-start = (bf16[48,3072]{1,0:T(8,128)(2,1)}, bf16[48,3072]{1,0:T(8,128)(2,1)}, u32[]{:S(2)}, u32[]{:S(2)}) collective-permute-start(bf16[48,3072]{1,0:T(8,128)(2,1)} %dynamic-slice_bitcast_fusion.15), channel_id=1, source_target_pairs={{0,8},{8,0},{1,9},{9,1},{2,10},{10,2},{3,11},{11,3},{4,12},{12,4},... | collective-permute-start | bytes 884744 | tf_op jit(solution)/shard_map/cond/branch_1_fun/ppermute | solution.py:569
  673.8 18.4 %collective-permute-start.1 = (bf16[2,48,1536]{2,1,0:T(8,128)(2,1)}, bf16[2,48,1536]{2,1,0:T(8,128)(2,1)}, u32[]{:S(2)}, u32[]{:S(2)}) collective-permute-start(bf16[2,48,1536]{2,1,0:T(8,128)(2,1)} %dynamic-slice_bitcast_fusion.14), channel_id=1, source_target_pairs={{0,16},{16,0},{1,17},{17,1},{2,18},{18,2},{3,19},{19,3},{4,20},{20... | collective-permute-start | bytes 884744 | tf_op jit(solution)/shard_map/cond/branch_1_fun/ppermute | solution.py:569
  676.0 26.4 %all-to-all-start = ((f32[32,1,192]{2,1,0:T(1,128)}), f32[32,1,192]{2,1,0:T(1,128)}, u32[]{:S(2)}, u32[]{:S(2)}) async-start(f32[32,1,192]{2,1,0:T(1,128)} %all_to_all.19), calls=%async_computation | async-start | bytes 65536 | tf_op jit(solution)/shard_map/cond/branch_1_fun/all_to_all | solution.py:681
  693.3 5.0 collective-permute-start.2
  694.9 3.4 collective-permute-start.3
  698.4 4.8 collective-permute-start.4
  (43 other events, 246.5 us)
Sparse Core Ops, SparseCore 0:
  34.1 40.1 all-gather.3
  143.6 99.4 all-gather.5
  244.6 94.0 all-gather.7
  379.0 93.7 reduce-scatter.2
  475.0 104.7 reduce-scatter.4

commit v7 on v6

--- a/solution.py
+++ b/solution.py
@@ -940,32 +940,33 @@
     own_b, far_b = plan.scatter_send(deep_b)
 
 
-    def fifth_part(sum_a, act_out, grad_gate, dx_a):
+    def fifth_part(sum_a, act_out, grad_gate, dx_a, down_share):
+        grad_exp_out = plan.share_sum(*down_share)
         pair_a = bar(plan.scatter_swap(sum_a))
         pair_a = bar(plan.scatter_side(pair_a, 0))
         deep_a = plan.scatter_stack(plan.scatter_side(pair_a, 1))
-        return deep_a, unpadded(act_out), unpadded(grad_gate), unpadded(dx_a)
-
-    deep_a, act_out, grad_gate, dx_a = fenced(
-        ready, fifth_part, sum_a, act_out, grad_gate, dx_a
+        return deep_a, unpadded(act_out), unpadded(grad_gate), unpadded(dx_a), grad_exp_out
+
+    deep_a, act_out, grad_gate, dx_a, grad_exp_out = fenced(
+        ready, fifth_part, sum_a, act_out, grad_gate, dx_a, (down_own, down_other)
     )
     deep_a, own_b, far_b, in_other = bar((deep_a, own_b, far_b, in_other))
 
-    def sixth_part(deep_a, own_b, far_b, near_c, norm_grads, shares):
+    def sixth_part(deep_a, own_b, far_b, near_c, norm_grads, in_share):
         norm_pieces = plan.small_send(norm_grads)
         own_a, far_a = plan.scatter_send(deep_a)
         near_b = plan.scatter_near(plan.scatter_add(own_b, far_b))
         near_b, far_a = bar((near_b, far_a))
-        grad_exp_in, grad_exp_out = [plan.share_sum(*share) for share in shares]
+        grad_exp_in = plan.share_sum(*in_share)
         near_a, mine_bc = bar(
             (plan.scatter_near(plan.scatter_add(own_a, far_a)), plan.scatter_core(plan.scatter_join(near_b, near_c)))
         )
         mine_norms = plan.small_sum(norm_pieces)
-        return plan.scatter_core(near_a), mine_bc, mine_norms, grad_exp_in, grad_exp_out
-
-    mine_a, mine_bc, mine_norms, grad_exp_in, grad_exp_out = fenced(
+        return plan.scatter_core(near_a), mine_bc, mine_norms, grad_exp_in
+
+    mine_a, mine_bc, mine_norms, grad_exp_in = fenced(
         ready, sixth_part, deep_a, own_b, far_b, near_c, norm_grads,
-        ((in_own, in_other), (down_own, down_other)),
+        (in_own, in_other),
     )
     mine_b, mine_c = plan.scatter_unstack(mine_bc, 2 * FF, 4 * D)
     grad_exp_out = jnp.swapaxes(grad_exp_out, 1, 2)

time: 726 us -> 725 us (level)
  waiting for transfers between devices: 126 us -> 111 us
  local copies, waits for them, and re-layouts: 81.4 us -> 89.2 us
    ppermute x47, waiting for transfers between devices: 67.8 us -> 53 us  [hop(): return lax.ppermute(value, axes, [(i, i ^ bit) for i in range(size)])]
  transfers between devices with their start and end apart: 56 -> 56, of which waited for: 17 -> 17; matrix products, arithmetic and copies ran while one was open for 21% -> 22% of each run, Pallas kernels for 29% -> 29%
where the time goes in v7:
time: 725 us; the launch traced here: 716 us
  Pallas kernels  243 us (34%)
  waiting for transfers between devices  111 us (15%)
  other arithmetic  94.9 us (13%)
  local copies, waits for them, and re-layouts  89.2 us (12%)
  blocking collectives  77.5 us (11%)
  starting transfers between devices  74.2 us (10%)
  between operations  15.1 us (2%)
  matrix products  7.89 us (1%)
    all_to_all x1, blocking collectives, to_experts(): lax.all_to_all(chunks, ('dh',) + self.expert, 0, 0, tiled=True)  60.6 us
    all_to_all x3, waiting for transfers between devices, to_experts(): lax.all_to_all(chunks, ('dh',) + self.expert, 0, 0, tiled=True)  58 us
    pallas_call x5, Pallas kernels, weight_grad(): pl.pallas_call(functools.partial(weight_grad_body, tiles, starts, split),...  56.8 us
    ppermute x47, waiting for transfers between devices, hop(): return lax.ppermute(value, axes, [(i, i ^ bit) for i in range(size)])  53 us
    ppermute x47, starting transfers between devices, hop(): return lax.ppermute(value, axes, [(i, i ^ bit) for i in range(size)])  51.2 us
    pallas_call x2, Pallas kernels, attend_backward(): pl.pallas_call(attend_backward_body, grid=(images,), in_specs=[image(D),...  49 us
    pallas_call x2, Pallas kernels, attend_forward(): pl.pallas_call(attend_forward_body, grid=(images,), in_specs=[image(D), w...  26.1 us
    concatenate x10, other arithmetic, gather_side(): jnp.concatenate([own, new])  23.2 us
  transfers between devices with their start and end apart: 56, of which 17 were waited for; matrix products, arithmetic and copies ran while one was open for 22% of the time, Pallas kernels for 29%

profile of v7, /device:TPU:1, one launch (start us, length us, event | category | flops | bytes accessed | tf_op | source)
XLA Modules:
  0.0 715.8 jit_solution(9249152841790332470)
XLA Ops:
  12.2 16.9 %all_gather.12 = bf16[4,48,1664]{2,1,0:T(8,128)(2,1)S(1)} all-gather(bf16[1,48,1664]{2,1,0:T(8,128)(2,1)S(1)} %maximum_select_fusion.7), channel_id=1, replica_groups=mesh['dh'=2,'dl'=2,'y'=2,'x'=2,'c'=2] {'dh','dl'}, dimensions={0}, use_global_device_ids=true | all-gather | bytes 798720 | tf_op jit(solution)/shard_map/all_gather | solution.py:587
  35.3 46.1 %conditional.12 = (bf16[16,48,768]{2,1,0:T(8,128)(2,1)}, bf16[16,48,896]{2,1,0:T(8,128)(2,1)}, bf16[192,3072]{1,0:T(8,128)(2,1)S(1)}, bf16[192,3072]{1,0:T(8,128...) conditional(s32[]{:T(128)} %bitcast.88, () %tuple.165, ...), branch_computations={%region_0.1_spmd, %region_1.5_spmd} | conditional | flops 759418496 | bytes 83628928 | solution.py:753
  39.2 3.0 convert.33
  45.1 3.6 select_bitcast_fusion
  53.3 4.5 reduce-window.4
  59.6 2.9 reshape.747
  64.3 3.6 reshape.748
  67.9 2.9 pad.33
  70.9 5.6 dispatch_grad.1
  82.4 56.8 %conditional.13 = (f32[4,1,768]{2,0,1:T(4,128)S(1)}, f32[4,1,768]{2,0,1:T(4,128)S(1)}, bf16[768,3328]{1,0:T(8,128)(2,1)}, f32[3,208,768]{2,1,0:T(8,128)}, bf16[3...) conditional(s32[]{:T(128)} %bitcast.88, () %tuple.164, ...), branch_computations={%region_5.6_spmd, %region_6.7_spmd} | conditional | flops 928546176 | bytes 48031396 | solution.py:753
  89.7 11.8 %collective-permute-done.11 = bf16[4,48,1536]{2,1,0:T(8,128)(2,1)} collective-permute-done((bf16[4,48,1536]{2,1,0:T(8,128)(2,1)}, bf16[4,48,1536]{2,1,0:T(8,128)(2,1)}, u32[]{:S(2)}, u32[]{:S(2)}) %collective-permute-start.11) | collective-permute-done | bytes 589856 | tf_op jit(solution)/shard_map/cond/branch_1_fun/ppermute | solution.py:569
  102.3 3.0 pad_maximum_fusion.2
  109.4 4.6 join.3.qkv_ref.proj_ref
  115.0 13.1 %attend_forward.2 = (f32[3,208,768]{2,1,0:T(8,128)}, bf16[3,208,2304]{2,1,0:T(8,128)(2,1)}, bf16[3,208,768]{2,1,0:T(8,128)(2,1)}) custom-call(f32[3,208,768]{2,1,0:T(8,128)} %get-tuple-element.252.x_ref, f32[1,768]{1,0:T(1,128)S(1)} %get-tuple-element.978.gain_ref, f32[1,768]{1,0:T(1,128)S(1)} %get-tuple-element.977.shift_ref, ...), custom_call_target="tpu_custom_call" | custom-call | flops 925000000 | bytes 3250000 | tf_op jit(solution)/shard_map/cond/branch_1_fun/attend_forward/pallas_call | solution.py:133
  128.1 3.5 collective-permute-done.13
  132.7 3.3 pad_maximum_fusion.1
  136.0 3.2 pad_maximum_fusion
  139.2 4.2 maximum_select_fusion.4
  145.2 48.6 %conditional.14 = (bf16[768,6144]{1,0:T(8,128)(2,1)}, f32[3,208,768]{2,1,0:T(8,128)}, bf16[3,208,3072]{2,1,0:T(8,128)(2,1)}, bf16[3,208,3072]{2,1,0:T(8,128)(2,1...) conditional(s32[]{:T(128)} %bitcast.88, () %tuple.171, (bf16[16,48,1536]{2,1,0:T(8,128)(2,1)}, ...), branch_computations={%region_7.8_spmd, %region_8.9_spmd} | conditional | flops 1476770688 | bytes 50191248 | solution.py:753
  145.2 3.1 collective-permute-start.15
  150.2 6.4 collective-permute-done.17
  167.8 7.5 %join.4.up_ref.down_ref = bf16[768,6144]{1,0:T(8,128)(2,1)} custom-call(s32[4,32]{1,0:T(4,128)S(1)} %pad_add_fusion.1.at_ref, bf16[16,48,1536]{2,1,0:T(8,128)(2,1)} %get-tuple-element.267.refs_0_, bf16[16,48,1536]{2,1,0:T(8,128)(2,1)} %get-tuple-element.268.refs_1_, bf16[16,48,1536]{2,1,0:T(8,128)(2,1)S(1)} %collective-permute-done.15.refs_2_, ...), custom_call_target="tpu_custom_call" | custom-call | bytes 4718592 | tf_op jit(solution)/shard_map/cond/branch_1_fun/join/pallas_call | solution.py:531
  175.3 15.1 %mlp_forward.1 = (f32[3,208,768]{2,1,0:T(8,128)}, bf16[3,208,3072]{2,1,0:T(8,128)(2,1)}, bf16[3,208,3072]{2,1,0:T(8,128)(2,1)}) custom-call(f32[3,208,768]{2,1,0:T(8,128)} %get-tuple-element.277.x_ref, f32[1,768]{1,0:T(1,128)} %get-tuple-element.998.gain_ref, f32[1,768]{1,0:T(1,128)} %get-tuple-element.997.shift_ref, bf16[768,6144]{1,0:T(8,128)(2,1)} %join.4.up_ref.down_ref, ...), custom_call_target="tpu_custom_call" | custom-call | flops 1475000064 | bytes 5250000 | tf_op jit(solution)/shard_map/cond/branch_1_fun/mlp_forward/pallas_call | solution.py:229
  196.5 4.1 maximum_select_fusion.5
  202.0 123.0 %conditional.15 = (bf16[768,3072]{1,0:T(8,128)(2,1)}, f32[3,208,768]{2,1,0:T(8,128)}, bf16[3,208,2304]{2,1,0:T(8,128)(2,1)}, bf16[3,208,768]{2,1,0:T(8,128)(2,1)...) conditional(s32[]{:T(128)} %bitcast.88, () %tuple.170, (bf16[16,48,768]{2,1,0:T(8,128)(2,1)S(1)}, ...), branch_computations={%region_9.10_spmd, %region_10.11_spmd} | conditional | flops 1300001024 | bytes 28065448 | solution.py:753
  202.2 6.2 all-to-all-start.1
  217.6 4.5 join.5.qkv_ref.proj_ref
  222.1 13.1 %attend_forward.3 = (f32[3,208,768]{2,1,0:T(8,128)}, bf16[3,208,2304]{2,1,0:T(8,128)(2,1)}, bf16[3,208,768]{2,1,0:T(8,128)(2,1)}) custom-call(f32[3,208,768]{2,1,0:T(8,128)} %get-tuple-element.292.x_ref, f32[1,768]{1,0:T(1,128)S(1)} %get-tuple-element.1009.gain_ref, f32[1,768]{1,0:T(1,128)S(1)} %get-tuple-element.1000.shift_ref, ...), custom_call_target="tpu_custom_call" | custom-call | flops 925000000 | bytes 3250000 | tf_op jit(solution)/shard_map/cond/branch_1_fun/attend_forward/pallas_call | solution.py:133
  235.2 5.1 dispatch.1
  240.3 24.1 %all-to-all-done.1 = bf16[16,96,768]{2,1,0:T(8,128)(2,1)} async-done(((bf16[16,96,768]{2,1,0:T(8,128)(2,1)}), bf16[16,96,768]{2,1,0:T(8,128)(2,1)}, u32[]{:S(2)}, u32[]{:S(2)}) %all-to-all-start.1) | async-done | bytes 2359328 | tf_op jit(solution)/shard_map/cond/branch_1_fun/all_to_all | solution.py:743
  264.4 60.6 %all_to_all.25 = bf16[16,96,768]{2,1,0:T(8,128)(2,1)} all-to-all(bf16[16,96,768]{2,1,0:T(8,128)(2,1)S(1)} %bitcast.232), channel_id=1, replica_groups=mesh['dh'=2,'dl'=2,'y'=2,'x'=2,'c'=2] {'dh','y','x','c'}, dimensions={0} | all-to-all | bytes 4718592 | tf_op jit(solution)/shard_map/cond/branch_1_fun/all_to_all | solution.py:743
  325.0 18.5 %expert_forward.1 = (bf16[1536,3072]{1,0:T(8,128)(2,1)}, bf16[1536,3072]{1,0:T(8,128)(2,1)}) custom-call(bf16[1536,768]{1,0:T(8,128)(2,1)} %get-tuple-element.620.rows_ref, bf16[768,3072]{1,0:T(8,128)(2,1)} %bitcast.243), custom_call_target="tpu_custom_call" | custom-call | flops 1800000000 | bytes 6500000 | tf_op jit(solution)/shard_map/expert_forward/pallas_call | solution.py:409
  343.5 35.3 %conditional.16 = (bf16[1536,3072]{1,0:T(8,128)(2,1)}, bf16[1536,768]{1,0:T(8,128)(2,1)}, bf16[768,3072]{1,0:T(8,128)(2,1)}) conditional(s32[]{:T(128)} %bitcast.88, () %tuple.177, (bf16[1536,768]{1,0:T(8,128)(2,1)}, bf16[1536,3072]{1,0:T(8,128)(2,1)}, bf16[768,3072]{1,0:T(8,128)(2,1)}, bf16[768,3072]{1,0:T(8,128)(2,1)}, ...), branch_computations={%region_11.12_spmd, %region_12.13_spmd} | conditional | flops 5411939328 | bytes 38331120 | solution.py:753
  343.8 23.1 %expert_backward.1 = (bf16[1536,3072]{1,0:T(8,128)(2,1)}, bf16[1536,768]{1,0:T(8,128)(2,1)}) custom-call(bf16[1536,768]{1,0:T(8,128)(2,1)} %get-tuple-element.302.grad_ref.refs_0_, bf16[1536,3072]{1,0:T(8,128)(2,1)} %get-tuple-element.303.slope_ref, bf16[768,3072]{1,0:T(8,128)(2,1)} %get-tuple-element.304.in_ref, bf16[768,3072]{1,0:T(8,128)(2,1)} %get-tuple-element.305.out_ref), custom_call_target="tpu_custom_call" | custom-call | flops 3600000000 | bytes 8250000 | tf_op jit(solution)/shard_map/cond/branch_1_fun/expert_backward/pallas_call | solution.py:434
  366.8 11.9 %weight_grad.5 = bf16[768,3072]{1,0:T(8,128)(2,1)} custom-call(s32[1]{0:T(128)} %constant.608.clone.at_ref, bf16[1536,768]{1,0:T(8,128)(2,1)} %get-tuple-element.302.grad_ref.refs_0_, bf16[1536,3072]{1,0:T(8,128)(2,1)S(1)} %bitcast.248), custom_call_target="tpu_custom_call" | custom-call | flops 1811939328 | bytes 1769472 | tf_op jit(solution)/shard_map/cond/branch_1_fun/weight_grad/pallas_call | solution.py:501
  378.9 60.6 %conditional.17 = (bf16[1536,768]{1,0:T(8,128)(2,1)}, bf16[768,3072]{1,0:T(8,128)(2,1)}, bf16[1536,768]{1,0:T(8,128)(2,1)S(1)}) conditional(s32[]{:T(128)} %bitcast.88, () %tuple.176, (bf16[1536,768]{1,0:T(8,128)(2,1)}, bf16[1536,768]{1,0:T(8,128)(2,1)}, bf16[1536,3072]{1,0:T(8,128)(2,1)}, bf16[1536,3072]{1,0:T(8,128)(2,1)}, ...), branch_computations={%region_13.14_spmd, %region_14.15_spmd} | conditional | flops 9060876288 | bytes 72548504 | solution.py:753
  378.9 5.7 all-to-all-start.3
  384.6 13.1 %weight_grad.6 = bf16[768,3072]{1,0:T(8,128)(2,1)} custom-call(s32[1]{0:T(128)} %constant.610.clone.at_ref, bf16[1536,768]{1,0:T(8,128)(2,1)} %get-tuple-element.312.refs_0_, bf16[1536,3072]{1,0:T(8,128)(2,1)} %get-tuple-element.313.refs_1_), custom_call_target="tpu_custom_call" | custom-call | flops 1811939328 | bytes 1769472 | tf_op jit(solution)/shard_map/cond/branch_1_fun/weight_grad/pallas_call | solution.py:501
  397.7 7.9 %convolution_convert_fusion = bf16[1536,768]{1,0:T(8,128)(2,1)S(1)} fusion(bf16[1536,3072]{1,0:T(8,128)(2,1)S(1)} %bitcast.250, bf16[768,3072]{1,0:T(8,128)(2,1)S(1)} %copy-done.17), kind=kOutput, calls=%fused_computation.110 | convolution fusion | flops 7248936960 | bytes 16515072 | tf_op jit(solution)/shard_map/cond/branch_1_fun/dot_general | solution.py:38
  405.6 33.9 %all-to-all-done.3 = bf16[16,96,768]{2,1,0:T(8,128)(2,1)} async-done(((bf16[16,96,768]{2,1,0:T(8,128)(2,1)}), bf16[16,96,768]{2,1,0:T(8,128)(2,1)}, u32[]{:S(2)}, u32[]{:S(2)}) %all-to-all-start.3) | async-done | bytes 2359328 | tf_op jit(solution)/shard_map/cond/branch_1_fun/all_to_all | solution.py:743
  440.9 5.5 all-to-all-start.4
  446.5 40.5 %conditional.18 = (bf16[768,1536]{1,0:T(8,128)(2,1)}, bf16[768,1536]{1,0:T(8,128)(2,1)}, f32[3,208,768]{2,1,0:T(8,128)}, f32[1,768]{1,0:T(1,128)S(1)}, f32[1,768...) conditional(s32[]{:T(128)} %bitcast.88, () %tuple.163, (s32[]{:T(128)}, ...), branch_computations={%region_15.16_spmd, %region_16.17_spmd} | conditional | flops 2111100416 | bytes 20848716 | solution.py:753
  447.1 5.5 return_grad.1
  452.6 24.1 %attend_backward.2 = (f32[3,208,768]{2,1,0:T(8,128)}, bf16[3,208,2304]{2,1,0:T(8,128)(2,1)}, bf16[3,208,768]{2,1,0:T(8,128)(2,1)S(1)}, bf16[3,208,768]{2,1,0:T(8...) custom-call(f32[3,208,768]{2,1,0:T(8,128)} %get-tuple-element.319.x_ref, ...), custom_call_target="tpu_custom_call" | custom-call | flops 1000000000 | bytes 5500000 | tf_op jit(solution)/shard_map/cond/branch_1_fun/attend_backward/pallas_call | solution.py:191
  478.6 8.4 %weight_grad.7 = (bf16[768,1536]{1,0:T(8,128)(2,1)}, bf16[768,1536]{1,0:T(8,128)(2,1)}) custom-call(s32[1]{0:T(128)} %bitcast.25.at_ref, bf16[624,768]{1,0:T(8,128)(2,1)S(1)} %bitcast.238, bf16[624,768]{1,0:T(8,128)(2,1)S(1)} %bitcast.239, bf16[624,2304]{1,0:T(8,128)(2,1)S(1)} %bitcast.234, bf16[624,768]{1,0:T(8,128)(2,1)} %bitcast.32.refs_3_), custom_call_target="tpu_custom_call" | custom-call | flops 736100352 | bytes 1769472 | tf_op jit(solution)/shard_map/cond/branch_1_fun/weight_grad/pallas_call | solution.py:501
  491.7 58.0 %conditional.19 = (bf16[4,48,768]{2,1,0:T(8,128)(2,1)S(1)}, bf16[4,48,768]{2,1,0:T(8,128)(2,1)}, bf16[4,2,2,48,1536]{4,3,2,1,0:T(8,128)(2,1)}, bf16[4,2,2,48,153...) conditional(s32[]{:T(128)} %bitcast.88, () %tuple.162, ...), branch_computations={%region_18.19_spmd, %region_19.20_spmd} | conditional | flops 2964895488 | bytes 140792064 | solution.py:753
  493.2 14.7 %mlp_backward.1 = (f32[3,208,768]{2,1,0:T(8,128)}, bf16[3,208,3072]{2,1,0:T(8,128)(2,1)}, bf16[3,208,768]{2,1,0:T(8,128)(2,1)}, bf16[3,208,768]{2,1,0:T(8,128)(2...) custom-call(f32[3,208,768]{2,1,0:T(8,128)} %get-tuple-element.342.x_ref, f32[3,208,768]{2,1,0:T(8,128)} %get-tuple-element.343.dy_ref, ...), custom_call_target="tpu_custom_call" | custom-call | flops 1475000064 | bytes 6250000 | tf_op jit(solution)/shard_map/cond/branch_1_fun/mlp_backward/pallas_call | solution.py:266
  517.6 13.9 %weight_grad.8 = (bf16[768,3072]{1,0:T(8,128)(2,1)}, bf16[768,3072]{1,0:T(8,128)(2,1)}) custom-call(s32[1]{0:T(128)} %bitcast.40.at_ref, bf16[624,768]{1,0:T(8,128)(2,1)S(1)} %bitcast.236, bf16[624,768]{1,0:T(8,128)(2,1)S(1)} %bitcast.237, bf16[624,3072]{1,0:T(8,128)(2,1)S(1)} %bitcast.233, bf16[624,3072]{1,0:T(8,128)(2,1)} %bitcast.44.refs_3_), custom_call_target="tpu_custom_call" | custom-call | flops 1472200704 | bytes 3538944 | tf_op jit(solution)/shard_map/cond/branch_1_fun/weight_grad/pallas_call | solution.py:501
  535.7 8.2 %collective-permute-done.26 = bf16[4,48,768]{2,1,0:T(8,128)(2,1)S(1)} collective-permute-done((bf16[4,48,768]{2,1,0:T(8,128)(2,1)S(1)}, bf16[4,48,768]{2,1,0:T(8,128)(2,1)S(1)}, u32[]{:S(2)}, u32[]{:S(2)}) %collective-permute-start.26) | collective-permute-done | bytes 294944 | tf_op jit(solution)/shard_map/cond/branch_1_fun/ppermute | solution.py:569
  551.0 37.9 %conditional.20 = (f32[3,208,768]{2,1,0:T(8,128)}, bf16[3,208,2304]{2,1,0:T(8,128)(2,1)}, bf16[3,208,768]{2,1,0:T(8,128)(2,1)}, bf16[3,208,768]{2,1,0:T(8,128)(2...) conditional(s32[]{:T(128)} %bitcast.88, () %tuple.161, ...), branch_computations={%region_20.21_spmd, %region_21.22_spmd} | conditional | flops 1006488064 | bytes 31809184 | solution.py:753
  558.2 24.8 %attend_backward.3 = (f32[3,208,768]{2,1,0:T(8,128)}, bf16[3,208,2304]{2,1,0:T(8,128)(2,1)}, bf16[3,208,768]{2,1,0:T(8,128)(2,1)}, bf16[3,208,768]{2,1,0:T(8,128...) custom-call(f32[3,208,768]{2,1,0:T(8,128)} %get-tuple-element.384.x_ref, f32[3,208,768]{2,1,0:T(8,128)} %get-tuple-element.385.dy_ref, ...), custom_call_target="tpu_custom_call" | custom-call | flops 1000000000 | bytes 5500000 | tf_op jit(solution)/shard_map/cond/branch_1_fun/attend_backward/pallas_call | solution.py:191
  583.1 4.1 fusion.64
  593.9 30.9 %conditional.21 = (f32[768,8]{0,1:T(8,128)S(1)}, bf16[768,1536]{1,0:T(8,128)(2,1)}, bf16[768,1536]{1,0:T(8,128)(2,1)}, f32[48,1536]{1,0:T(8,128)S(1)}, f32[3,208...) conditional(s32[]{:T(128)} %bitcast.88, () %tuple.160, (f32[1,768]{1,0:T(1,128)S(1)}, ...), branch_computations={%region_23.24_spmd, %region_24.25_spmd} | conditional | flops 1491040128 | bytes 30086432 | solution.py:753
  599.1 9.5 %weight_grad.9 = (bf16[768,1536]{1,0:T(8,128)(2,1)}, bf16[768,1536]{1,0:T(8,128)(2,1)}) custom-call(s32[1]{0:T(128)} %bitcast.64.at_ref, bf16[624,768]{1,0:T(8,128)(2,1)} %bitcast.65.refs_0_, bf16[624,768]{1,0:T(8,128)(2,1)} %bitcast.66.refs_1_, bf16[624,2304]{1,0:T(8,128)(2,1)} %bitcast.67.refs_2_, bf16[624,768]{1,0:T(8,128)(2,1)} %bitcast.255), custom_call_target="tpu_custom_call" | custom-call | flops 736100352 | bytes 1769472 | tf_op jit(solution)/shard_map/cond/branch_1_fun/weight_grad/pallas_call | solution.py:501
  608.6 6.8 combine.1
  615.4 5.5 collective-permute-done.39
  629.8 40.5 %conditional.22 = (bf16[4,48,1536]{2,1,0:T(8,128)(2,1)}, f32[591,768]{1,0:T(8,128)}, f32[591,2]{0,1:T(2,128)S(1)}, f32[591,768]{1,0:T(8,128)}, f32[2,192,3072]{2,1,0:T(8,128)}) conditional(s32[]{:T(128)} %bitcast.88, () %tuple.159, (bf16[768,1536]{1,0:T(8,128)(2,1)}, bf16[768,1536]{1,0:T(8,128)(2,1)}, f32[3,208,768]{2,1,0:T(8,128)}, ...), branch_computations={%region_25.26_spmd, %region_26.27_spmd} | conditional | flops 14155800 | bytes 81194568 | solution.py:753
  632.6 4.4 collective-permute-done.29
  646.4 2.9 reshape.792
  652.2 2.9 reshape.794
  670.9 33.0 %conditional.23 = (f32[24,3072]{1,0:T(8,128)}, f32[24,9216]{1,0:T(8,128)S(1)}, f32[24,8]{1,0:T(8,128)S(1)}, f32[2,192,3072]{2,1,0:T(8,128)}) conditional(s32[]{:T(128)} %bitcast.88, () %tuple.189, (bf16[4,48,1536]{2,1,0:T(8,128)(2,1)}, bf16[2,48,3072]{2,1,0:T(8,128)(2,1)}, bf16[2,48,3072]{2,1,0:T(8,128)(2,1)}, f32[48,1536]{1,0:T(8,128)}, ...), branch_computations={%region_27.28_spmd, %region_28.30_spmd} | conditional | flops 8042337 | bytes 35703776 | solution.py:753
  677.9 5.4 all-to-all-start
  690.2 3.4 collective-permute-start.3
  695.1 3.6 collective-permute-start.4
  (377 shorter events, 190.5 us)
Async XLA Ops:
  7.2 74.2 %all-gather.4.cloned.1.call-start = ((), (), s32[]{:S(2)}) async-start(), calls=%async_computation.7 | async-start | bytes 2211840 | tf_op jit(solution)/shard_map/all_gather | solution.py:587
  10.8 1.3 collective-permute-start.40
  11.0 23.0 %copy-start.42 = (s32[591,2]{0,1:T(2,128)S(1)}, s32[591,2]{0,1:T(2,128)}, u32[]{:S(2)}) copy-start(s32[591,2]{0,1:T(2,128)} %param.46) | copy-start | bytes 14188
  11.1 24.2 %copy-start.40 = (f32[591,2]{0,1:T(2,128)S(1)}, f32[591,2]{0,1:T(2,128)}, u32[]{:S(2)}) copy-start(f32[591,2]{0,1:T(2,128)} %param.45) | copy-start | bytes 14188
  29.2 4.0 collective-permute-start.41
  34.0 291.0 %all-gather.6.cloned.1.call-start = ((), (), s32[]{:S(2)}) async-start(), calls=%async_computation.8 | async-start | bytes 7077888 | tf_op jit(solution)/shard_map/all_gather | solution.py:726
  36.8 12.3 %collective-permute-start.6 = (bf16[4,48,896]{2,1,0:T(8,128)(2,1)}, bf16[4,48,896]{2,1,0:T(8,128)(2,1)}, u32[]{:S(2)}, u32[]{:S(2)}) collective-permute-start(bf16[4,48,896]{2,1,0:T(8,128)(2,1)} %slice.120), channel_id=1, source_target_pairs={{0,4},{4,0},{1,5},{5,1},{2,6},{6,2},{3,7},{7,3},{8,12},{12,8},{9,1... | collective-permute-start | bytes 1032200 | tf_op jit(solution)/shard_map/cond/branch_1_fun/ppermute | solution.py:569
  38.0 11.1 %collective-permute-start.5 = (bf16[4,48,768]{2,1,0:T(8,128)(2,1)}, bf16[4,48,768]{2,1,0:T(8,128)(2,1)}, u32[]{:S(2)}, u32[]{:S(2)}) collective-permute-start(bf16[4,48,768]{2,1,0:T(8,128)(2,1)} %slice.119), channel_id=1, source_target_pairs={{0,2},{2,0},{1,3},{3,1},{4,6},{6,4},{5,7},{7,5},{8,10},{10,8},{9,1... | collective-permute-start | bytes 884744 | tf_op jit(solution)/shard_map/cond/branch_1_fun/ppermute | solution.py:569
  57.8 18.7 %collective-permute-start.8 = (bf16[8,48,896]{2,1,0:T(8,128)(2,1)}, bf16[8,48,896]{2,1,0:T(8,128)(2,1)}, u32[]{:S(2)}, u32[]{:S(2)}) collective-permute-start(bf16[8,48,896]{2,1,0:T(8,128)(2,1)} %pad_maximum_fusion.13), channel_id=1, source_target_pairs={{0,2},{2,0},{1,3},{3,1},{4,6},{6,4},{5,7},{7,5},{8,10},{10,8},{9,1... | collective-permute-start | bytes 2064392 | tf_op jit(solution)/shard_map/cond/branch_1_fun/ppermute | solution.py:569
  58.7 17.8 %collective-permute-start.7 = (bf16[8,48,768]{2,1,0:T(8,128)(2,1)}, bf16[8,48,768]{2,1,0:T(8,128)(2,1)}, u32[]{:S(2)}, u32[]{:S(2)}) collective-permute-start(bf16[8,48,768]{2,1,0:T(8,128)(2,1)} %pad_maximum_fusion.14), channel_id=1, source_target_pairs={{0,4},{4,0},{1,5},{5,1},{2,6},{6,2},{3,7},{7,3},{8,12},{12,8},{9,1... | collective-permute-start | bytes 1769480 | tf_op jit(solution)/shard_map/cond/branch_1_fun/ppermute | solution.py:569
  81.4 57.9 %collective-permute-start.42 = (bf16[192,3072]{1,0:T(8,128)(2,1)}, bf16[192,3072]{1,0:T(8,128)(2,1)}, u32[]{:S(2)}, u32[]{:S(2)}) collective-permute-start(bf16[192,3072]{1,0:T(8,128)(2,1)} %get-tuple-element.600), channel_id=1, source_target_pairs={{0,16},{16,0},{1,17},{17,1},{2,18},{18,2},{3,19},{19,3},{4,20},{20... | collective-permute-start | bytes 3538952 | tf_op jit(solution)/shard_map/ppermute | solution.py:569
  82.9 22.5 %collective-permute-start.10 = (bf16[16,48,896]{2,1,0:T(8,128)(2,1)}, bf16[16,48,896]{2,1,0:T(8,128)(2,1)S(1)}, u32[]{:S(2)}, u32[]{:S(2)}) collective-permute-start(bf16[16,48,896]{2,1,0:T(8,128)(2,1)} %get-tuple-element.243.refs_1_), channel_id=1, source_target_pairs={{0,1},{1,0},{2,3},{3,2},{4,5},{5,4},{6,7},{7,6},{8,9},{9,8},{10,11... | collective-permute-start | bytes 4128776 | tf_op jit(solution)/shard_map/cond/branch_1_fun/ppermute | solution.py:569
  84.4 20.9 %collective-permute-start.9 = (bf16[16,48,768]{2,1,0:T(8,128)(2,1)}, bf16[16,48,768]{2,1,0:T(8,128)(2,1)S(1)}, u32[]{:S(2)}, u32[]{:S(2)}) collective-permute-start(bf16[16,48,768]{2,1,0:T(8,128)(2,1)} %get-tuple-element.242.refs_0_), channel_id=1, source_target_pairs={{0,1},{1,0},{2,3},{3,2},{4,5},{5,4},{6,7},{7,6},{8,9},{9,8},{10,11... | collective-permute-start | bytes 3538952 | tf_op jit(solution)/shard_map/cond/branch_1_fun/ppermute | solution.py:569
  86.7 14.8 %collective-permute-start.11 = (bf16[4,48,1536]{2,1,0:T(8,128)(2,1)}, bf16[4,48,1536]{2,1,0:T(8,128)(2,1)}, u32[]{:S(2)}, u32[]{:S(2)}) collective-permute-start(bf16[4,48,1536]{2,1,0:T(8,128)(2,1)} %get-tuple-element.238), channel_id=1, source_target_pairs={{0,2},{2,0},{1,3},{3,1},{4,6},{6,4},{5,7},{7,5},{8,10},{10,8},{9,1... | collective-permute-start | bytes 1769480 | tf_op jit(solution)/shard_map/cond/branch_1_fun/ppermute | solution.py:569
  88.1 14.3 %collective-permute-start.12 = (bf16[4,48,1536]{2,1,0:T(8,128)(2,1)S(1)}, bf16[4,48,1536]{2,1,0:T(8,128)(2,1)}, u32[]{:S(2)}, u32[]{:S(2)}) collective-permute-start(bf16[4,48,1536]{2,1,0:T(8,128)(2,1)S(1)} %get-tuple-element.239), channel_id=1, source_target_pairs={{0,4},{4,0},{1,5},{5,1},{2,6},{6,2},{3,7},{7,3},{8,12},{12,8},{9,1... | collective-permute-start | bytes 1769480 | tf_op jit(solution)/shard_map/cond/branch_1_fun/ppermute | solution.py:569
  105.4 26.2 %collective-permute-start.13 = (bf16[8,48,1536]{2,1,0:T(8,128)(2,1)}, bf16[8,48,1536]{2,1,0:T(8,128)(2,1)}, u32[]{:S(2)}, u32[]{:S(2)}) collective-permute-start(bf16[8,48,1536]{2,1,0:T(8,128)(2,1)} %get-tuple-element.248), channel_id=1, source_target_pairs={{0,4},{4,0},{1,5},{5,1},{2,6},{6,2},{3,7},{7,3},{8,12},{12,8},{9,1... | collective-permute-start | bytes 3538952 | tf_op jit(solution)/shard_map/cond/branch_1_fun/ppermute | solution.py:569
  106.8 25.9 %collective-permute-start.14 = (bf16[8,48,1536]{2,1,0:T(8,128)(2,1)}, bf16[8,48,1536]{2,1,0:T(8,128)(2,1)}, u32[]{:S(2)}, u32[]{:S(2)}) collective-permute-start(bf16[8,48,1536]{2,1,0:T(8,128)(2,1)} %get-tuple-element.249), channel_id=1, source_target_pairs={{0,2},{2,0},{1,3},{3,1},{4,6},{6,4},{5,7},{7,5},{8,10},{10,8},{9,1... | collective-permute-start | bytes 3538952 | tf_op jit(solution)/shard_map/cond/branch_1_fun/ppermute | solution.py:569
  143.5 200.1 %all-gather.8.cloned.1.call-start = ((), (), s32[]{:S(2)}) async-start(), calls=%async_computation.9 | async-start | bytes 7077888 | tf_op jit(solution)/shard_map/all_gather | solution.py:726
  143.5 53.0 %collective-permute-start.43 = (bf16[192,3072]{1,0:T(8,128)(2,1)}, bf16[192,3072]{1,0:T(8,128)(2,1)}, u32[]{:S(2)}, u32[]{:S(2)}) collective-permute-start(bf16[192,3072]{1,0:T(8,128)(2,1)} %get-tuple-element.612), channel_id=1, source_target_pairs={{0,16},{16,0},{1,17},{17,1},{2,18},{18,2},{3,19},{19,3},{4,20},{20... | collective-permute-start | bytes 3538952 | tf_op jit(solution)/shard_map/ppermute | solution.py:569
  145.2 13.6 %collective-permute-start.15 = (bf16[16,48,1536]{2,1,0:T(8,128)(2,1)}, bf16[16,48,1536]{2,1,0:T(8,128)(2,1)S(1)}, u32[]{:S(2)}, u32[]{:S(2)}) collective-permute-start(bf16[16,48,1536]{2,1,0:T(8,128)(2,1)} %get-tuple-element.267.refs_0_), channel_id=1, source_target_pairs={{0,1},{1,0},{2,3},{3,2},{4,5},{5,4},{6,7},{7,6},{8,9},{9,8},{10,11... | collective-permute-start | bytes 7077896 | tf_op jit(solution)/shard_map/cond/branch_1_fun/ppermute | solution.py:569
  148.3 10.5 %collective-permute-start.16 = (bf16[16,48,1536]{2,1,0:T(8,128)(2,1)}, bf16[16,48,1536]{2,1,0:T(8,128)(2,1)}, u32[]{:S(2)}, u32[]{:S(2)}) collective-permute-start(bf16[16,48,1536]{2,1,0:T(8,128)(2,1)} %get-tuple-element.268.refs_1_), channel_id=1, source_target_pairs={{0,1},{1,0},{2,3},{3,2},{4,5},{5,4},{6,7},{7,6},{8,9},{9,8},{10,11... | collective-permute-start | bytes 7077896 | tf_op jit(solution)/shard_map/cond/branch_1_fun/ppermute | solution.py:569
  148.4 8.3 %collective-permute-start.17 = (bf16[4,48,768]{2,1,0:T(8,128)(2,1)S(1)}, bf16[4,48,768]{2,1,0:T(8,128)(2,1)S(1)}, u32[]{:S(2)}, u32[]{:S(2)}) collective-permute-start(bf16[4,48,768]{2,1,0:T(8,128)(2,1)S(1)} %get-tuple-element.263), channel_id=1, source_target_pairs={{0,2},{2,0},{1,3},{3,1},{4,6},{6,4},{5,7},{7,5},{8,10},{10,8},{9,1... | collective-permute-start | bytes 884744 | tf_op jit(solution)/shard_map/cond/branch_1_fun/ppermute | solution.py:569
  148.9 8.4 %collective-permute-start.18 = (bf16[4,48,768]{2,1,0:T(8,128)(2,1)}, bf16[4,48,768]{2,1,0:T(8,128)(2,1)}, u32[]{:S(2)}, u32[]{:S(2)}) collective-permute-start(bf16[4,48,768]{2,1,0:T(8,128)(2,1)} %get-tuple-element.264), channel_id=1, source_target_pairs={{0,4},{4,0},{1,5},{5,1},{2,6},{6,2},{3,7},{7,3},{8,12},{12,8},{9,1... | collective-permute-start | bytes 884744 | tf_op jit(solution)/shard_map/cond/branch_1_fun/ppermute | solution.py:569
  158.8 16.5 %copy-start.18 = (bf16[8,48,768]{2,1,0:T(8,128)(2,1)}, bf16[8,48,768]{2,1,0:T(8,128)(2,1)S(1)}, u32[]{:S(2)}) copy-start(bf16[8,48,768]{2,1,0:T(8,128)(2,1)S(1)} %get-tuple-element.273) | copy-start | bytes 1769476 | tf_op jit(solution)/shard_map/cond
  158.8 31.6 %collective-permute-start.19 = (bf16[8,48,768]{2,1,0:T(8,128)(2,1)S(1)}, bf16[8,48,768]{2,1,0:T(8,128)(2,1)}, u32[]{:S(2)}, u32[]{:S(2)}) collective-permute-start(bf16[8,48,768]{2,1,0:T(8,128)(2,1)S(1)} %get-tuple-element.273), channel_id=1, source_target_pairs={{0,4},{4,0},{1,5},{5,1},{2,6},{6,2},{3,7},{7,3},{8,12},{12,8},{9,1... | collective-permute-start | bytes 1769480 | tf_op jit(solution)/shard_map/cond/branch_1_fun/ppermute | solution.py:569
  159.0 31.4 %collective-permute-start.20 = (bf16[8,48,768]{2,1,0:T(8,128)(2,1)S(1)}, bf16[8,48,768]{2,1,0:T(8,128)(2,1)}, u32[]{:S(2)}, u32[]{:S(2)}) collective-permute-start(bf16[8,48,768]{2,1,0:T(8,128)(2,1)S(1)} %get-tuple-element.274), channel_id=1, source_target_pairs={{0,2},{2,0},{1,3},{3,1},{4,6},{6,4},{5,7},{7,5},{8,10},{10,8},{9,1... | collective-permute-start | bytes 1769480 | tf_op jit(solution)/shard_map/cond/branch_1_fun/ppermute | solution.py:569
  200.6 286.3 %reduce-scatter.3.cloned.1.call-start = ((), (), s32[]{:S(2)}) async-start(), calls=%async_computation.10 | async-start | bytes 7077888 | tf_op jit(solution)/shard_map/reduce_scatter | solution.py:731
  202.2 62.2 %all-to-all-start.1 = ((bf16[16,96,768]{2,1,0:T(8,128)(2,1)}), bf16[16,96,768]{2,1,0:T(8,128)(2,1)}, u32[]{:S(2)}, u32[]{:S(2)}) async-start(bf16[16,96,768]{2,1,0:T(8,128)(2,1)} %bitcast.19), calls=%async_computation.1 | async-start | bytes 4718592 | tf_op jit(solution)/shard_map/cond/branch_1_fun/all_to_all | solution.py:743
  208.4 9.2 %collective-permute-start.21 = (bf16[16,48,768]{2,1,0:T(8,128)(2,1)S(1)}, bf16[16,48,768]{2,1,0:T(8,128)(2,1)S(1)}, u32[]{:S(2)}, u32[]{:S(2)}) collective-permute-start(bf16[16,48,768]{2,1,0:T(8,128)(2,1)S(1)} %get-tuple-element.288.refs_0_), channel_id=1, source_target_pairs={{0,1},{1,0},{2,3},{3,2},{4,5},{5,4},{6,7},{7,6},{8,9},{9,8},{10,11... | collective-permute-start | bytes 3538952 | tf_op jit(solution)/shard_map/cond/branch_1_fun/ppermute | solution.py:569
  208.7 8.9 %collective-permute-start.22 = (bf16[16,48,768]{2,1,0:T(8,128)(2,1)}, bf16[16,48,768]{2,1,0:T(8,128)(2,1)S(1)}, u32[]{:S(2)}, u32[]{:S(2)}) collective-permute-start(bf16[16,48,768]{2,1,0:T(8,128)(2,1)} %get-tuple-element.289.refs_1_), channel_id=1, source_target_pairs={{0,1},{1,0},{2,3},{3,2},{4,5},{5,4},{6,7},{7,6},{8,9},{9,8},{10,11... | collective-permute-start | bytes 3538952 | tf_op jit(solution)/shard_map/cond/branch_1_fun/ppermute | solution.py:569
  343.7 23.1 %slice-start = ((s8[9437184]{0:T(1024)(128)(4,1)}), s8[4194304]{0:T(1024)(128)(4,1)S(1)}, s32[]{:S(2)}) async-start(s8[9437184]{0:T(1024)(128)(4,1)} %bitcast.247), calls=%async_computation.12 | async-start | bytes 8388608 | tf_op jit(solution)/shard_map/cond
  343.7 23.1 %slice-start.1 = ((s8[9437184]{0:T(1024)(128)(4,1)}), s8[4194304]{0:T(1024)(128)(4,1)S(1)}, s32[]{:S(2)}) async-start(s8[9437184]{0:T(1024)(128)(4,1)} %bitcast.247), calls=%async_computation.13 | async-start | bytes 8388608 | tf_op jit(solution)/shard_map/cond
  343.7 23.1 %slice-start.2 = ((s8[9437184]{0:T(1024)(128)(4,1)}), s8[1048576]{0:T(1024)(128)(4,1)S(1)}, s32[]{:S(2)}) async-start(s8[9437184]{0:T(1024)(128)(4,1)} %bitcast.247), calls=%async_computation.14 | async-start | bytes 2097152 | tf_op jit(solution)/shard_map/cond
  378.8 210.2 %reduce-scatter.5.cloned.1.call-start = ((), (), s32[]{:S(2)}) async-start(), calls=%async_computation.11 | async-start | bytes 7077888 | tf_op jit(solution)/shard_map/reduce_scatter | solution.py:731
  378.9 18.8 %slice-start.3 = ((s8[9437184]{0:T(1024)(128)(4,1)}), s8[1048576]{0:T(1024)(128)(4,1)S(1)}, s32[]{:S(2)}) async-start(s8[9437184]{0:T(1024)(128)(4,1)} %bitcast.249), calls=%async_computation.15 | async-start | bytes 2097152 | tf_op jit(solution)/shard_map/cond
  378.9 60.6 %all-to-all-start.3 = ((bf16[16,96,768]{2,1,0:T(8,128)(2,1)}), bf16[16,96,768]{2,1,0:T(8,128)(2,1)}, u32[]{:S(2)}, u32[]{:S(2)}) async-start(bf16[16,96,768]{2,1,0:T(8,128)(2,1)} %bitcast.23), calls=%async_computation.3 | async-start | bytes 4718592 | tf_op jit(solution)/shard_map/cond/branch_1_fun/all_to_all | solution.py:743
  440.9 108.8 %all-to-all-start.4 = ((bf16[16,96,768]{2,1,0:T(8,128)(2,1)}), bf16[16,96,768]{2,1,0:T(8,128)(2,1)}, u32[]{:S(2)}, u32[]{:S(2)}) async-start(bf16[16,96,768]{2,1,0:T(8,128)(2,1)} %bitcast.251), calls=%async_computation.5 | async-start | bytes 4718592 | tf_op jit(solution)/shard_map/all_to_all | solution.py:743
  489.3 61.7 %collective-permute-start.44 = (bf16[1,192,3072]{2,1,0:T(8,128)(2,1)}, bf16[1,192,3072]{2,1,0:T(8,128)(2,1)}, u32[]{:S(2)}, u32[]{:S(2)}) collective-permute-start(bf16[1,192,3072]{2,1,0:T(8,128)(2,1)} %constant_dynamic-slice_fusion.5), channel_id=1, source_target_pairs={{0,16},{16,0},{1,17},{17,1},{2,18},{18,2},{3,19},{19,3},{4,20},{20... | collective-permute-start | bytes 3538952 | tf_op jit(solution)/shard_map/ppermute | solution.py:569
  491.8 16.1 %collective-permute-start.23 = (bf16[768,1536]{1,0:T(8,128)(2,1)}, bf16[768,1536]{1,0:T(8,128)(2,1)S(1)}, u32[]{:S(2)}, u32[]{:S(2)}) collective-permute-start(bf16[768,1536]{1,0:T(8,128)(2,1)} %get-tuple-element.341), channel_id=1, source_target_pairs={{0,1},{1,0},{2,3},{3,2},{4,5},{5,4},{6,7},{7,6},{8,9},{9,8},{10,11... | collective-permute-start | bytes 7077896 | tf_op jit(solution)/shard_map/cond/branch_1_fun/ppermute | solution.py:569
  513.1 18.4 %collective-permute-start.24 = (bf16[4,2,48,768]{3,2,1,0:T(8,128)(2,1)}, bf16[4,2,48,768]{3,2,1,0:T(8,128)(2,1)}, u32[]{:S(2)}, u32[]{:S(2)}) collective-permute-start(bf16[4,2,48,768]{3,2,1,0:T(8,128)(2,1)} %dynamic-slice_bitcast_fusion.1), channel_id=1, source_target_pairs={{0,4},{4,0},{1,5},{5,1},{2,6},{6,2},{3,7},{7,3},{8,12},{12,8},{9,1... | collective-permute-start | bytes 1769480 | tf_op jit(solution)/shard_map/cond/branch_1_fun/ppermute | solution.py:569
  514.4 17.2 %collective-permute-start.25 = (bf16[4,2,48,768]{3,2,1,0:T(8,128)(2,1)}, bf16[4,2,48,768]{3,2,1,0:T(8,128)(2,1)}, u32[]{:S(2)}, u32[]{:S(2)}) collective-permute-start(bf16[4,2,48,768]{3,2,1,0:T(8,128)(2,1)} %dynamic-slice_bitcast_fusion), channel_id=1, source_target_pairs={{0,2},{2,0},{1,3},{3,1},{4,6},{6,4},{5,7},{7,5},{8,10},{10,8},{9,1... | collective-permute-start | bytes 1769480 | tf_op jit(solution)/shard_map/cond/branch_1_fun/ppermute | solution.py:569
  534.2 10.6 %collective-permute-start.28 = (bf16[768,3072]{1,0:T(8,128)(2,1)}, bf16[768,3072]{1,0:T(8,128)(2,1)S(1)}, u32[]{:S(2)}, u32[]{:S(2)}) collective-permute-start(bf16[768,3072]{1,0:T(8,128)(2,1)} %get-tuple-element.370), channel_id=1, source_target_pairs={{0,1},{1,0},{2,3},{3,2},{4,5},{5,4},{6,7},{7,6},{8,9},{9,8},{10,11... | collective-permute-start | bytes 14155784 | tf_op jit(solution)/shard_map/cond/branch_1_fun/ppermute | solution.py:569
  535.1 8.8 %collective-permute-start.26 = (bf16[4,48,768]{2,1,0:T(8,128)(2,1)S(1)}, bf16[4,48,768]{2,1,0:T(8,128)(2,1)S(1)}, u32[]{:S(2)}, u32[]{:S(2)}) collective-permute-start(bf16[4,48,768]{2,1,0:T(8,128)(2,1)S(1)} %dynamic-slice_bitcast_fusion.3), channel_id=1, source_target_pairs={{0,2},{2,0},{1,3},{3,1},{4,6},{6,4},{5,7},{7,5},{8,10},{10,8},{9,1... | collective-permute-start | bytes 884744 | tf_op jit(solution)/shard_map/cond/branch_1_fun/ppermute | solution.py:569
  535.5 8.4 %collective-permute-start.27 = (bf16[4,48,768]{2,1,0:T(8,128)(2,1)S(1)}, bf16[4,48,768]{2,1,0:T(8,128)(2,1)S(1)}, u32[]{:S(2)}, u32[]{:S(2)}) collective-permute-start(bf16[4,48,768]{2,1,0:T(8,128)(2,1)S(1)} %dynamic-slice_bitcast_fusion.2), channel_id=1, source_target_pairs={{0,4},{4,0},{1,5},{5,1},{2,6},{6,2},{3,7},{7,3},{8,12},{12,8},{9,1... | collective-permute-start | bytes 884744 | tf_op jit(solution)/shard_map/cond/branch_1_fun/ppermute | solution.py:569
  554.0 29.1 %collective-permute-start.34 = (bf16[4,2,48,1536]{3,2,1,0:T(8,128)(2,1)S(1)}, bf16[4,2,48,1536]{3,2,1,0:T(8,128)(2,1)}, u32[]{:S(2)}, u32[]{:S(2)}) collective-permute-start(bf16[4,2,48,1536]{3,2,1,0:T(8,128)(2,1)S(1)} %dynamic-slice_bitcast_fusion.5), channel_id=1, source_target_pairs={{0,4},{4,0},{1,5},{5,1},{2,6},{6,2},{3,7},{7,3},{8,12},{12,8},{9,1... | collective-permute-start | bytes 3538952 | tf_op jit(solution)/shard_map/cond/branch_1_fun/ppermute | solution.py:569
  555.3 27.8 %collective-permute-start.35 = (bf16[4,2,48,1536]{3,2,1,0:T(8,128)(2,1)S(1)}, bf16[4,2,48,1536]{3,2,1,0:T(8,128)(2,1)}, u32[]{:S(2)}, u32[]{:S(2)}) collective-permute-start(bf16[4,2,48,1536]{3,2,1,0:T(8,128)(2,1)S(1)} %dynamic-slice_bitcast_fusion.4), channel_id=1, source_target_pairs={{0,2},{2,0},{1,3},{3,1},{4,6},{6,4},{5,7},{7,5},{8,10},{10,8},{9,1... | collective-permute-start | bytes 3538952 | tf_op jit(solution)/shard_map/cond/branch_1_fun/ppermute | solution.py:569
  558.2 29.0 %collective-permute-start.36 = (bf16[2,48,1536]{2,1,0:T(8,128)(2,1)}, bf16[2,48,1536]{2,1,0:T(8,128)(2,1)S(1)}, u32[]{:S(2)}, u32[]{:S(2)}) collective-permute-start(bf16[2,48,1536]{2,1,0:T(8,128)(2,1)} %dynamic-slice_bitcast_fusion.6), channel_id=1, source_target_pairs={{0,16},{16,0},{1,17},{17,1},{2,18},{18,2},{3,19},{19,3},{4,20},{20... | collective-permute-start | bytes 884744 | tf_op jit(solution)/shard_map/cond/branch_1_fun/ppermute | solution.py:569
  591.6 78.7 %collective-permute-start.46 = (bf16[1,192,3072]{2,1,0:T(8,128)(2,1)}, bf16[1,192,3072]{2,1,0:T(8,128)(2,1)}, u32[]{:S(2)}, u32[]{:S(2)}) collective-permute-start(bf16[1,192,3072]{2,1,0:T(8,128)(2,1)} %constant_dynamic-slice_fusion.4), channel_id=1, source_target_pairs={{0,16},{16,0},{1,17},{17,1},{2,18},{18,2},{3,19},{19,3},{4,20},{20... | collective-permute-start | bytes 3538952 | tf_op jit(solution)/shard_map/ppermute | solution.py:569
  594.1 14.5 %copy-start.23 = (bf16[2,48,1536]{2,1,0:T(8,128)(2,1)}, bf16[2,48,1536]{2,1,0:T(8,128)(2,1)S(1)}, u32[]{:S(2)}) copy-start(bf16[2,48,1536]{2,1,0:T(8,128)(2,1)S(1)} %get-tuple-element.431) | copy-start | bytes 884740 | tf_op jit(solution)/shard_map/cond
  594.9 26.0 %collective-permute-start.39 = (bf16[48,1536]{1,0:T(8,128)(2,1)}, bf16[48,1536]{1,0:T(8,128)(2,1)}, u32[]{:S(2)}, u32[]{:S(2)}) collective-permute-start(bf16[48,1536]{1,0:T(8,128)(2,1)} %dynamic-slice_bitcast_fusion.9), channel_id=1, source_target_pairs={{0,8},{8,0},{1,9},{9,1},{2,10},{10,2},{3,11},{11,3},{4,12},{12,4},... | collective-permute-start | bytes 442376 | tf_op jit(solution)/shard_map/cond/branch_1_fun/ppermute | solution.py:569
  597.7 24.2 %collective-permute-start.37 = (bf16[4,48,1536]{2,1,0:T(8,128)(2,1)}, bf16[4,48,1536]{2,1,0:T(8,128)(2,1)}, u32[]{:S(2)}, u32[]{:S(2)}) collective-permute-start(bf16[4,48,1536]{2,1,0:T(8,128)(2,1)} %dynamic-slice_bitcast_fusion.8), channel_id=1, source_target_pairs={{0,2},{2,0},{1,3},{3,1},{4,6},{6,4},{5,7},{7,5},{8,10},{10,8},{9,1... | collective-permute-start | bytes 1769480 | tf_op jit(solution)/shard_map/cond/branch_1_fun/ppermute | solution.py:569
  598.0 23.9 %collective-permute-start.38 = (bf16[4,48,1536]{2,1,0:T(8,128)(2,1)}, bf16[4,48,1536]{2,1,0:T(8,128)(2,1)}, u32[]{:S(2)}, u32[]{:S(2)}) collective-permute-start(bf16[4,48,1536]{2,1,0:T(8,128)(2,1)} %dynamic-slice_bitcast_fusion.7), channel_id=1, source_target_pairs={{0,4},{4,0},{1,5},{5,1},{2,6},{6,2},{3,7},{7,3},{8,12},{12,8},{9,1... | collective-permute-start | bytes 1769480 | tf_op jit(solution)/shard_map/cond/branch_1_fun/ppermute | solution.py:569
  627.2 43.0 %collective-permute-start.45 = (bf16[2,48,3072]{2,1,0:T(8,128)(2,1)}, bf16[2,48,3072]{2,1,0:T(8,128)(2,1)}, u32[]{:S(2)}, u32[]{:S(2)}) collective-permute-start(bf16[2,48,3072]{2,1,0:T(8,128)(2,1)} %get-tuple-element.1040), channel_id=1, source_target_pairs={{0,16},{16,0},{1,17},{17,1},{2,18},{18,2},{3,19},{19,3},{4,20},{20... | collective-permute-start | bytes 1769480 | tf_op jit(solution)/shard_map/ppermute | solution.py:569
  629.8 7.2 %collective-permute-start.29 = (bf16[768,1536]{1,0:T(8,128)(2,1)}, bf16[768,1536]{1,0:T(8,128)(2,1)S(1)}, u32[]{:S(2)}, u32[]{:S(2)}) collective-permute-start(bf16[768,1536]{1,0:T(8,128)(2,1)} %get-tuple-element.437), channel_id=1, source_target_pairs={{0,1},{1,0},{2,3},{3,2},{4,5},{5,4},{6,7},{7,6},{8,9},{9,8},{10,11... | collective-permute-start | bytes 7077896 | tf_op jit(solution)/shard_map/cond/branch_1_fun/ppermute | solution.py:569
  641.5 16.5 %collective-permute-start.30 = (bf16[4,2,48,768]{3,2,0,1:T(8,128)(2,1)}, bf16[4,2,48,768]{3,2,0,1:T(8,128)(2,1)}, u32[]{:S(2)}, u32[]{:S(2)}) collective-permute-start(bf16[4,2,48,768]{3,2,0,1:T(8,128)(2,1)} %dynamic-slice_bitcast_fusion.11), channel_id=1, source_target_pairs={{0,4},{4,0},{1,5},{5,1},{2,6},{6,2},{3,7},{7,3},{8,12},{12,8},{9,1... | collective-permute-start | bytes 1769480 | tf_op jit(solution)/shard_map/cond/branch_1_fun/ppermute | solution.py:569
  641.8 16.2 %collective-permute-start.31 = (bf16[4,2,48,768]{3,2,1,0:T(8,128)(2,1)}, bf16[4,2,48,768]{3,2,1,0:T(8,128)(2,1)}, u32[]{:S(2)}, u32[]{:S(2)}) collective-permute-start(bf16[4,2,48,768]{3,2,1,0:T(8,128)(2,1)} %dynamic-slice_bitcast_fusion.10), channel_id=1, source_target_pairs={{0,2},{2,0},{1,3},{3,1},{4,6},{6,4},{5,7},{7,5},{8,10},{10,8},{9,1... | collective-permute-start | bytes 1769480 | tf_op jit(solution)/shard_map/cond/branch_1_fun/ppermute | solution.py:569
  660.6 7.7 %collective-permute-start.32 = (bf16[4,48,768]{2,1,0:T(8,128)(2,1)S(1)}, bf16[4,48,768]{2,1,0:T(8,128)(2,1)S(1)}, u32[]{:S(2)}, u32[]{:S(2)}) collective-permute-start(bf16[4,48,768]{2,1,0:T(8,128)(2,1)S(1)} %dynamic-slice_bitcast_fusion.13), channel_id=1, source_target_pairs={{0,2},{2,0},{1,3},{3,1},{4,6},{6,4},{5,7},{7,5},{8,10},{10,8},{9,1... | collective-permute-start | bytes 884744 | tf_op jit(solution)/shard_map/cond/branch_1_fun/ppermute | solution.py:569
  661.9 7.4 %collective-permute-start.33 = (bf16[4,48,768]{2,1,0:T(8,128)(2,1)S(1)}, bf16[4,48,768]{2,1,0:T(8,128)(2,1)S(1)}, u32[]{:S(2)}, u32[]{:S(2)}) collective-permute-start(bf16[4,48,768]{2,1,0:T(8,128)(2,1)S(1)} %dynamic-slice_bitcast_fusion.12), channel_id=1, source_target_pairs={{0,4},{4,0},{1,5},{5,1},{2,6},{6,2},{3,7},{7,3},{8,12},{12,8},{9,1... | collective-permute-start | bytes 884744 | tf_op jit(solution)/shard_map/cond/branch_1_fun/ppermute | solution.py:569
  673.0 13.4 %collective-permute-start = (bf16[48,3072]{1,0:T(8,128)(2,1)}, bf16[48,3072]{1,0:T(8,128)(2,1)}, u32[]{:S(2)}, u32[]{:S(2)}) collective-permute-start(bf16[48,3072]{1,0:T(8,128)(2,1)} %dynamic-slice_bitcast_fusion.15), channel_id=1, source_target_pairs={{0,8},{8,0},{1,9},{9,1},{2,10},{10,2},{3,11},{11,3},{4,12},{12,4},... | collective-permute-start | bytes 884744 | tf_op jit(solution)/shard_map/cond/branch_1_fun/ppermute | solution.py:569
  674.7 12.7 %collective-permute-start.1 = (bf16[2,48,1536]{2,1,0:T(8,128)(2,1)}, bf16[2,48,1536]{2,1,0:T(8,128)(2,1)S(1)}, u32[]{:S(2)}, u32[]{:S(2)}) collective-permute-start(bf16[2,48,1536]{2,1,0:T(8,128)(2,1)} %dynamic-slice_bitcast_fusion.14), channel_id=1, source_target_pairs={{0,16},{16,0},{1,17},{17,1},{2,18},{18,2},{3,19},{19,3},{4,20},{20... | collective-permute-start | bytes 884744 | tf_op jit(solution)/shard_map/cond/branch_1_fun/ppermute | solution.py:569
  677.9 23.4 %all-to-all-start = ((f32[32,1,192]{2,1,0:T(1,128)}), f32[32,1,192]{2,1,0:T(1,128)}, u32[]{:S(2)}, u32[]{:S(2)}) async-start(f32[32,1,192]{2,1,0:T(1,128)} %all_to_all.19), calls=%async_computation | async-start | bytes 65536 | tf_op jit(solution)/shard_map/cond/branch_1_fun/all_to_all | solution.py:681
  688.6 5.0 collective-permute-start.2
  690.2 4.8 collective-permute-start.3
  695.1 7.1 collective-permute-start.4
  (41 other events, 242.8 us)
Sparse Core Ops, SparseCore 0:
  34.1 40.1 all-gather.3
  143.6 99.5 all-gather.5
  244.7 93.9 all-gather.7
  378.9 93.9 reduce-scatter.2
  475.2 104.4 reduce-scatter.4
